TPU v7x, 32 devices: a whole 2x2x4 slice. The times are simulated.
32 devices in a mesh: gx: 8 (over z, core), gy: 4 (over y, x).
Axes of the slice: x: 2, y: 2, z: 4, core: 2. Of those that a mesh axis runs over, the one named last changes fastest.
Arguments:
- source: float32 [128, 64, 512], P('gx', 'gy'), may hold values from -20 to 20
- reaction: float32 [128, 64, 512], P('gx', 'gy'), may hold values from 0.005 to 0.5
- boundary_kind: int32 [128, 64, 512], P('gx', 'gy'), may hold values from 0 to 2
- disk_id: int32 [128, 64, 512], P('gx', 'gy'), may hold values from 0 to 119
- disk_mask: int32 [128, 64, 512], P('gx', 'gy'), may hold values 0 or 1
- thrust: float32 [120], replicated, may hold values from -16 to 16
Outputs:
- pressure: float32 [128, 64, 512], P('gx', 'gy')
- coarse_correction: float32 [32, 16, 128], P('gx')
All inputs are finite; a program needn't handle non-finite values. No bound on the sum of `disk_mask` on one device may be relied on, other than what follows from the above.
Results may differ from a plain program's by a relative error of at most 0.00002.
Values sent between devices are 32-bit elements; how exact they have to be, the bound alone decides.
No kernel may reach another device: no remote copies, remote signals or barrier semaphores. Data moves between devices by JAX's collectives and lax.ppermute only.
A program may use at most 64 MiB of HBM per device.

v0:
```python
from functools import partial

import jax
import jax.numpy as jnp
from jax import lax
from jax.sharding import PartitionSpec as P

SWEEPS = 4


OMEGA = 0.8
WALL_PENALTY = 0.4
INFLOW_PENALTY = 0.2
CHEB_LOW = 0.1
CHEB_HIGH = 2.0


def extended(array, sides, width):
    for axis, dim in sides:
        size, length = (lax.axis_size(axis), array.shape[dim])
        up = [(i, (i + 1) % size) for i in range(size - 1)]
        down = [(j, i) for i, j in up]
        last = lax.slice_in_dim(array, length - width, length, axis=dim)
        initial = lax.slice_in_dim(array, 0, width, axis=dim)
        before = lax.ppermute(last, axis, up)
        after = lax.ppermute(initial, axis, down)
        array = jnp.concatenate([before, array, after], axis=dim)
    return array


def beside_all(padded):
    inside = padded[1:-1, 1:-1]
    zero_plane = jnp.zeros(inside.shape[:2] + (1,), inside.dtype)
    plane_above = jnp.concatenate([inside[:, :, 1:], zero_plane], axis=2)
    plane_below = jnp.concatenate([zero_plane, inside[:, :, :-1]], axis=2)
    summed = padded[2:, 1:-1] + padded[:-2, 1:-1]
    summed = summed + padded[1:-1, 2:] + padded[1:-1, :-2]
    return summed + plane_above + plane_below


def fine_faces(values):
    return extended(values, (("gx", 0), ("gy", 1)), 1)


def relax_once(values, right_side, diagonal):
    applied = diagonal * values - beside_all(fine_faces(values))
    return values + OMEGA * (right_side - applied) / diagonal


def plane_source(thrust, planes):
    plane_ids, plane_mask = planes
    matches = jnp.arange(thrust.shape[0], dtype=jnp.int32)[:, None, None] == plane_ids[None]
    picked = jnp.sum(jnp.where(matches, thrust[:, None, None], 0.0), axis=0)
    return picked * plane_mask.astype(jnp.float32)


def restrict(values):
    rows, cols, depth = values.shape
    return values.reshape(rows // 4, 4, cols // 4, 4, depth // 4, 4).sum(axis=(1, 3, 5))


def prolong(values):
    return jnp.repeat(jnp.repeat(jnp.repeat(values, 4, axis=0), 4, axis=1), 4, axis=2)


def slab_image(direction, coarse_diagonal):
    padded = extended(direction, (("gx", 0),), 1)
    padded = jnp.pad(padded, ((0, 0), (1, 1), (0, 0)))
    return 16.0 * (coarse_diagonal * direction - beside_all(padded))


def chebyshev(residual, coarse_diagonal, image_fn):
    centre = (CHEB_HIGH + CHEB_LOW) / 2.0
    half_range = (CHEB_HIGH - CHEB_LOW) / 2.0
    aspect = centre / half_range
    factor = 1.0 / aspect
    inverse = 1.0 / (16.0 * coarse_diagonal)
    direction = inverse * residual / centre
    solution = jnp.zeros_like(residual)
    for number in range(SWEEPS):
        solution = solution + direction
        if number + 1 < SWEEPS:
            residual = residual - image_fn(direction, coarse_diagonal)
            factor_next = 1.0 / (2.0 * aspect - factor)
            direction = (
                factor_next * factor * direction
                + 2.0 * factor_next / half_range * inverse * residual
            )
            factor = factor_next
    return solution


def local(source, reaction, boundary_kind, disk_id, disk_mask, thrust):
    penalty = jnp.where(
        boundary_kind == 1, WALL_PENALTY, jnp.where(boundary_kind == 2, INFLOW_PENALTY, 0.0)
    )
    absorb = reaction + penalty
    diagonal = 6.0 + absorb
    right_side = source + lax.map(partial(plane_source, thrust), (disk_id, disk_mask))
    first = OMEGA * right_side / diagonal
    second = relax_once(first, right_side, diagonal)
    fine_residual = right_side - (diagonal * second - beside_all(fine_faces(second)))
    coarse_residual = restrict(fine_residual)
    coarse_absorb = restrict(absorb) / 16.0
    slab_residual, slab_absorb = (
        lax.all_gather(coarse_residual, "gy", axis=1, tiled=True),
        lax.all_gather(coarse_absorb, "gy", axis=1, tiled=True),
    )
    slab_correction = chebyshev(slab_residual, 6.0 + slab_absorb, slab_image)
    coarse_span = coarse_residual.shape[1]
    correction = lax.dynamic_slice_in_dim(
        slab_correction, lax.axis_index("gy") * coarse_span, coarse_span, 1
    )
    third = second + prolong(correction)
    fourth = relax_once(third, right_side, diagonal)
    pressure = relax_once(fourth, right_side, diagonal)
    return (pressure, slab_correction)


def solution(mesh):
    return jax.shard_map(
        local,
        mesh=mesh,
        in_specs=(
            P("gx", "gy", None),
            P("gx", "gy", None),
            P("gx", "gy", None),
            P("gx", "gy", None),
            P("gx", "gy", None),
            P(),
        ),
        out_specs=(P("gx", "gy", None), P("gx", None, None)),
        check_vma=False,
    )
```

profile of v0, /device:TPU:12, one launch (start us, length us, event | category | flops | bytes accessed | tf_op | source)
XLA Modules:
  0.0 201.6 jit_solution(1878352295562181736)
XLA Ops:
  0.6 42.3 %while.11 = (s32[]{:T(128)}, f32[16,16,512]{2,1,0:T(8,128)S(1)}, s32[16,16,512]{2,1,0:T(8,128)}, f32[120]{0:T(128)}, s32[16,16,512]{2,1,0:T(8,128)}) while((s32[]{:T(128)}, f32[16,16,512]{2,1,0:T(8,128)S(1)}, s32[16,16,512]{2,1,0:T(8,128)}, f32[120]{0:T(128)}, s32[16,16,512]{2,1,0:T(8,128)}) %tuple.59), condition=%wide.region_2.3_spmd.clone, body=%wide.region_0.2_spmd.sunk.clone | while | flops 2957314 | bytes 229925 | solution.py:99
  48.9 2.8 %collective-permute-done.1 = f32[1,16,512]{2,1,0:T(8,128)S(1)} collective-permute-done((f32[1,16,512]{2,1,0:T(8,128)S(1)}, f32[1,16,512]{2,1,0:T(8,128)S(1)}, u32[]{:S(2)}, u32[]{:S(2)}) %collective-permute-start.1) | collective-permute-done | bytes 32800 | tf_op jit(solution)/shard_map/ppermute | solution.py:25
  51.8 3.3 %collective-permute-start.2 = (f32[18,1,512]{2,1,0:T(1,128)S(1)}, f32[18,1,512]{2,1,0:T(1,128)S(1)}, u32[]{:S(2)}, u32[]{:S(2)}) collective-permute-start(f32[18,1,512]{2,1,0:T(1,128)S(1)} %get-tuple-element.92), channel_id=1, source_target_pairs={{1,0},{2,1},{3,2},{5,4},{6,5},{7,6},{9,8},{10,9},{11,10},{13,12},{... | collective-permute-start | bytes 110600 | tf_op jit(solution)/shard_map/ppermute | solution.py:26
  55.1 2.5 %collective-permute-start.3 = (f32[18,1,512]{2,1,0:T(1,128)S(1)}, f32[18,1,512]{2,1,0:T(1,128)S(1)}, u32[]{:S(2)}, u32[]{:S(2)}) collective-permute-start(f32[18,1,512]{2,1,0:T(1,128)S(1)} %get-tuple-element.93), channel_id=1, source_target_pairs={{0,1},{1,2},{2,3},{4,5},{5,6},{6,7},{8,9},{9,10},{10,11},{12,13},{... | collective-permute-start | bytes 110600 | tf_op jit(solution)/shard_map/ppermute | solution.py:25
  57.9 18.6 %reshape.21 = f32[4,4,4,4,128,4]{5,4,3,2,1,0:T(8,128)} reshape(f32[16,16,512]{2,1,0:T(8,128)S(1)} %get-tuple-element.84) | data formatting | bytes 1048576 | tf_op jit(solution)/shard_map/reshape | solution.py:59
  76.5 6.9 %reduce_sum.29 = f32[4,4,128]{2,1,0:T(4,128)S(1)} reduce(f32[4,4,4,4,128,4]{5,4,3,2,1,0:T(8,128)} %reshape.21, f32[]{:T(128)} %constant.30.clone.1), dimensions={1,3,5}, to_apply=%region_3.4 | reduce | flops 129024 | bytes 532484 | tf_op jit(solution)/shard_map/reduce_sum | solution.py:59
  88.3 7.5 %all_gather.6 = f32[4,16,128]{2,0,1:T(4,128)S(1)} all-gather(f32[4,4,128]{2,0,1:T(4,128)S(1)} %copy.291), channel_id=1, replica_groups=mesh['gx'=8,'gy'=4] {'gy'}, dimensions={1}, use_global_device_ids=true | all-gather | bytes 40960 | tf_op jit(solution)/shard_map/all_gather | solution.py:107
  95.9 3.4 %collective-permute-start.6 = (f32[18,1,512]{2,1,0:T(1,128)S(1)}, f32[18,1,512]{2,1,0:T(1,128)S(1)}, u32[]{:S(2)}, u32[]{:S(2)}) collective-permute-start(f32[18,1,512]{2,1,0:T(1,128)S(1)} %get-tuple-element.90), channel_id=1, source_target_pairs={{1,0},{2,1},{3,2},{5,4},{6,5},{7,6},{9,8},{10,9},{11,10},{13,12},{... | collective-permute-start | bytes 110600 | tf_op jit(solution)/shard_map/ppermute | solution.py:26
  99.2 2.5 %collective-permute-start.7 = (f32[18,1,512]{2,1,0:T(1,128)S(1)}, f32[18,1,512]{2,1,0:T(1,128)S(1)}, u32[]{:S(2)}, u32[]{:S(2)}) collective-permute-start(f32[18,1,512]{2,1,0:T(1,128)S(1)} %get-tuple-element.91), channel_id=1, source_target_pairs={{0,1},{1,2},{2,3},{4,5},{5,6},{6,7},{8,9},{9,10},{10,11},{12,13},{... | collective-permute-start | bytes 110600 | tf_op jit(solution)/shard_map/ppermute | solution.py:25
  101.9 4.1 %collective-permute-done.7 = f32[18,1,512]{2,1,0:T(1,128)S(1)} collective-permute-done((f32[18,1,512]{2,1,0:T(1,128)S(1)}, f32[18,1,512]{2,1,0:T(1,128)S(1)}, u32[]{:S(2)}, u32[]{:S(2)}) %collective-permute-start.7) | collective-permute-done | bytes 36896 | tf_op jit(solution)/shard_map/ppermute | solution.py:25
  106.4 18.6 %reshape.22 = f32[4,4,4,4,128,4]{5,4,3,2,1,0:T(8,128)} reshape(f32[16,16,512]{2,1,0:T(8,128)S(1)} %fusion.25) | data formatting | bytes 1048576 | tf_op jit(solution)/shard_map/reshape | solution.py:59
  125.0 6.9 %reduce_sum.30 = f32[4,4,128]{2,1,0:T(4,128)S(1)} reduce(f32[4,4,4,4,128,4]{5,4,3,2,1,0:T(8,128)} %reshape.22, f32[]{:T(128)} %constant.30.clone.1), dimensions={1,3,5}, to_apply=%region_4.5 | reduce | flops 129024 | bytes 532484 | tf_op jit(solution)/shard_map/reduce_sum | solution.py:59
  132.0 6.6 %all_gather.7 = f32[4,16,128]{2,0,1:T(4,128)S(1)} all-gather(f32[4,4,128]{2,0,1:T(4,128)S(1)} %copy.292), channel_id=1, replica_groups=mesh['gx'=8,'gy'=4] {'gy'}, dimensions={1}, use_global_device_ids=true | all-gather | bytes 40960 | tf_op jit(solution)/shard_map/all_gather | solution.py:106
  143.1 2.5 %collective-permute-done.9 = f32[1,16,128]{2,0,1:T(1,128)S(1)} collective-permute-done((f32[1,16,128]{2,0,1:T(1,128)S(1)}, f32[1,16,128]{2,0,1:T(1,128)S(1)}, u32[]{:S(2)}, u32[]{:S(2)}) %collective-permute-start.9) | collective-permute-done | bytes 8224 | tf_op jit(solution)/shard_map/ppermute | solution.py:25
  150.1 2.5 %collective-permute-done.11 = f32[1,16,128]{2,0,1:T(1,128)S(1)} collective-permute-done((f32[1,16,128]{2,0,1:T(1,128)S(1)}, f32[1,16,128]{2,0,1:T(1,128)S(1)}, u32[]{:S(2)}, u32[]{:S(2)}) %collective-permute-start.11) | collective-permute-done | bytes 8224 | tf_op jit(solution)/shard_map/ppermute | solution.py:25
  157.2 2.5 %collective-permute-done.13 = f32[1,16,128]{2,0,1:T(1,128)S(1)} collective-permute-done((f32[1,16,128]{2,0,1:T(1,128)S(1)}, f32[1,16,128]{2,0,1:T(1,128)S(1)}, u32[]{:S(2)}, u32[]{:S(2)}) %collective-permute-start.13) | collective-permute-done | bytes 8224 | tf_op jit(solution)/shard_map/ppermute | solution.py:25
  162.7 2.8 %copy.294 = f32[16,16,512]{2,1,0:T(8,128)S(1)} copy(f32[16,16,512]{1,0,2:T(8,128)} %bitcast.15) | data formatting | bytes 1048576 | tf_op jit(solution)/shard_map/reshape | solution.py:63
  169.9 2.8 %collective-permute-done.15 = f32[1,16,512]{2,1,0:T(8,128)S(1)} collective-permute-done((f32[1,16,512]{2,1,0:T(8,128)S(1)}, f32[1,16,512]{2,1,0:T(8,128)S(1)}, u32[]{:S(2)}, u32[]{:S(2)}) %collective-permute-start.15) | collective-permute-done | bytes 32800 | tf_op jit(solution)/shard_map/ppermute | solution.py:25
  172.8 3.4 %collective-permute-start.16 = (f32[18,1,512]{2,1,0:T(1,128)S(1)}, f32[18,1,512]{2,1,0:T(1,128)S(1)}, u32[]{:S(2)}, u32[]{:S(2)}) collective-permute-start(f32[18,1,512]{2,1,0:T(1,128)S(1)} %get-tuple-element.88), channel_id=1, source_target_pairs={{1,0},{2,1},{3,2},{5,4},{6,5},{7,6},{9,8},{10,9},{11,10},{13,12},{... | collective-permute-start | bytes 110600 | tf_op jit(solution)/shard_map/ppermute | solution.py:26
  176.2 2.5 %collective-permute-start.17 = (f32[18,1,512]{2,1,0:T(1,128)S(1)}, f32[18,1,512]{2,1,0:T(1,128)S(1)}, u32[]{:S(2)}, u32[]{:S(2)}) collective-permute-start(f32[18,1,512]{2,1,0:T(1,128)S(1)} %get-tuple-element.89), channel_id=1, source_target_pairs={{0,1},{1,2},{2,3},{4,5},{5,6},{6,7},{8,9},{9,10},{10,11},{12,13},{... | collective-permute-start | bytes 110600 | tf_op jit(solution)/shard_map/ppermute | solution.py:25
  178.9 4.1 %collective-permute-done.17 = f32[18,1,512]{2,1,0:T(1,128)S(1)} collective-permute-done((f32[18,1,512]{2,1,0:T(1,128)S(1)}, f32[18,1,512]{2,1,0:T(1,128)S(1)}, u32[]{:S(2)}, u32[]{:S(2)}) %collective-permute-start.17) | collective-permute-done | bytes 36896 | tf_op jit(solution)/shard_map/ppermute | solution.py:25
  190.6 3.0 %collective-permute-start.20 = (f32[18,1,512]{2,1,0:T(1,128)S(1)}, f32[18,1,512]{2,1,0:T(1,128)S(1)}, u32[]{:S(2)}, u32[]{:S(2)}) collective-permute-start(f32[18,1,512]{2,1,0:T(1,128)S(1)} %get-tuple-element.86), channel_id=1, source_target_pairs={{1,0},{2,1},{3,2},{5,4},{6,5},{7,6},{9,8},{10,9},{11,10},{13,12},{... | collective-permute-start | bytes 110600 | tf_op jit(solution)/shard_map/ppermute | solution.py:26
  193.7 2.8 %collective-permute-start.21 = (f32[18,1,512]{2,1,0:T(1,128)S(1)}, f32[18,1,512]{2,1,0:T(1,128)S(1)}, u32[]{:S(2)}, u32[]{:S(2)}) collective-permute-start(f32[18,1,512]{2,1,0:T(1,128)S(1)} %get-tuple-element.87), channel_id=1, source_target_pairs={{0,1},{1,2},{2,3},{4,5},{5,6},{6,7},{8,9},{9,10},{10,11},{12,13},{... | collective-permute-start | bytes 110600 | tf_op jit(solution)/shard_map/ppermute | solution.py:25
  196.7 3.7 %collective-permute-done.21 = f32[18,1,512]{2,1,0:T(1,128)S(1)} collective-permute-done((f32[18,1,512]{2,1,0:T(1,128)S(1)}, f32[18,1,512]{2,1,0:T(1,128)S(1)}, u32[]{:S(2)}, u32[]{:S(2)}) %collective-permute-start.21) | collective-permute-done | bytes 36896 | tf_op jit(solution)/shard_map/ppermute | solution.py:25
  (117 shorter events, 84.1 us)
Async XLA Ops:
  44.6 4.3 %collective-permute-start = (f32[1,16,512]{2,1,0:T(8,128)S(1)}, f32[1,16,512]{2,1,0:T(8,128)S(1)}, u32[]{:S(2)}, u32[]{:S(2)}) collective-permute-start(f32[1,16,512]{2,1,0:T(8,128)S(1)} %get-tuple-element.109), channel_id=1, source_target_pairs={{4,0},{8,4},{12,8},{16,12},{20,16},{24,20},{28,24},{5,1},{9,5},{13... | collective-permute-start | bytes 98312 | tf_op jit(solution)/shard_map/ppermute | solution.py:26
  46.5 5.2 %collective-permute-start.1 = (f32[1,16,512]{2,1,0:T(8,128)S(1)}, f32[1,16,512]{2,1,0:T(8,128)S(1)}, u32[]{:S(2)}, u32[]{:S(2)}) collective-permute-start(f32[1,16,512]{2,1,0:T(8,128)S(1)} %get-tuple-element.108), channel_id=1, source_target_pairs={{0,4},{4,8},{8,12},{12,16},{16,20},{20,24},{24,28},{1,5},{5,9},{9,... | collective-permute-start | bytes 98312 | tf_op jit(solution)/shard_map/ppermute | solution.py:25
  51.8 31.6 %collective-permute-start.2 = (f32[18,1,512]{2,1,0:T(1,128)S(1)}, f32[18,1,512]{2,1,0:T(1,128)S(1)}, u32[]{:S(2)}, u32[]{:S(2)}) collective-permute-start(f32[18,1,512]{2,1,0:T(1,128)S(1)} %get-tuple-element.92), channel_id=1, source_target_pairs={{1,0},{2,1},{3,2},{5,4},{6,5},{7,6},{9,8},{10,9},{11,10},{13,12},{... | collective-permute-start | bytes 110600 | tf_op jit(solution)/shard_map/ppermute | solution.py:26
  55.1 28.3 %collective-permute-start.3 = (f32[18,1,512]{2,1,0:T(1,128)S(1)}, f32[18,1,512]{2,1,0:T(1,128)S(1)}, u32[]{:S(2)}, u32[]{:S(2)}) collective-permute-start(f32[18,1,512]{2,1,0:T(1,128)S(1)} %get-tuple-element.93), channel_id=1, source_target_pairs={{0,1},{1,2},{2,3},{4,5},{5,6},{6,7},{8,9},{9,10},{10,11},{12,13},{... | collective-permute-start | bytes 110600 | tf_op jit(solution)/shard_map/ppermute | solution.py:25
  83.9 11.9 %collective-permute-start.4 = (f32[1,16,512]{2,1,0:T(8,128)S(1)}, f32[1,16,512]{2,1,0:T(8,128)S(1)}, u32[]{:S(2)}, u32[]{:S(2)}) collective-permute-start(f32[1,16,512]{2,1,0:T(8,128)S(1)} %get-tuple-element.105), channel_id=1, source_target_pairs={{4,0},{8,4},{12,8},{16,12},{20,16},{24,20},{28,24},{5,1},{9,5},{13... | collective-permute-start | bytes 98312 | tf_op jit(solution)/shard_map/ppermute | solution.py:26
  85.8 10.0 %collective-permute-start.5 = (f32[1,16,512]{2,1,0:T(8,128)S(1)}, f32[1,16,512]{2,1,0:T(8,128)S(1)}, u32[]{:S(2)}, u32[]{:S(2)}) collective-permute-start(f32[1,16,512]{2,1,0:T(8,128)S(1)} %get-tuple-element.104), channel_id=1, source_target_pairs={{0,4},{4,8},{8,12},{12,16},{16,20},{20,24},{24,28},{1,5},{5,9},{9,... | collective-permute-start | bytes 98312 | tf_op jit(solution)/shard_map/ppermute | solution.py:25
  95.9 6.1 %collective-permute-start.6 = (f32[18,1,512]{2,1,0:T(1,128)S(1)}, f32[18,1,512]{2,1,0:T(1,128)S(1)}, u32[]{:S(2)}, u32[]{:S(2)}) collective-permute-start(f32[18,1,512]{2,1,0:T(1,128)S(1)} %get-tuple-element.90), channel_id=1, source_target_pairs={{1,0},{2,1},{3,2},{5,4},{6,5},{7,6},{9,8},{10,9},{11,10},{13,12},{... | collective-permute-start | bytes 110600 | tf_op jit(solution)/shard_map/ppermute | solution.py:26
  99.2 6.8 %collective-permute-start.7 = (f32[18,1,512]{2,1,0:T(1,128)S(1)}, f32[18,1,512]{2,1,0:T(1,128)S(1)}, u32[]{:S(2)}, u32[]{:S(2)}) collective-permute-start(f32[18,1,512]{2,1,0:T(1,128)S(1)} %get-tuple-element.91), channel_id=1, source_target_pairs={{0,1},{1,2},{2,3},{4,5},{5,6},{6,7},{8,9},{9,10},{10,11},{12,13},{... | collective-permute-start | bytes 110600 | tf_op jit(solution)/shard_map/ppermute | solution.py:25
  138.7 4.4 %collective-permute-start.8 = (f32[1,16,128]{2,0,1:T(1,128)S(1)}, f32[1,16,128]{2,0,1:T(1,128)S(1)}, u32[]{:S(2)}, u32[]{:S(2)}) collective-permute-start(f32[1,16,128]{2,0,1:T(1,128)S(1)} %get-tuple-element.119), channel_id=1, source_target_pairs={{4,0},{8,4},{12,8},{16,12},{20,16},{24,20},{28,24},{5,1},{9,5},{13... | collective-permute-start | bytes 24584 | tf_op jit(solution)/shard_map/ppermute | solution.py:26
  140.6 5.0 %collective-permute-start.9 = (f32[1,16,128]{2,0,1:T(1,128)S(1)}, f32[1,16,128]{2,0,1:T(1,128)S(1)}, u32[]{:S(2)}, u32[]{:S(2)}) collective-permute-start(f32[1,16,128]{2,0,1:T(1,128)S(1)} %get-tuple-element.118), channel_id=1, source_target_pairs={{0,4},{4,8},{8,12},{12,16},{16,20},{20,24},{24,28},{1,5},{5,9},{9,... | collective-permute-start | bytes 24584 | tf_op jit(solution)/shard_map/ppermute | solution.py:25
  145.7 4.4 %collective-permute-start.10 = (f32[1,16,128]{2,0,1:T(1,128)S(1)}, f32[1,16,128]{2,0,1:T(1,128)S(1)}, u32[]{:S(2)}, u32[]{:S(2)}) collective-permute-start(f32[1,16,128]{2,0,1:T(1,128)S(1)} %get-tuple-element.115), channel_id=1, source_target_pairs={{4,0},{8,4},{12,8},{16,12},{20,16},{24,20},{28,24},{5,1},{9,5},{13... | collective-permute-start | bytes 24584 | tf_op jit(solution)/shard_map/ppermute | solution.py:26
  147.6 5.0 %collective-permute-start.11 = (f32[1,16,128]{2,0,1:T(1,128)S(1)}, f32[1,16,128]{2,0,1:T(1,128)S(1)}, u32[]{:S(2)}, u32[]{:S(2)}) collective-permute-start(f32[1,16,128]{2,0,1:T(1,128)S(1)} %get-tuple-element.114), channel_id=1, source_target_pairs={{0,4},{4,8},{8,12},{12,16},{16,20},{20,24},{24,28},{1,5},{5,9},{9,... | collective-permute-start | bytes 24584 | tf_op jit(solution)/shard_map/ppermute | solution.py:25
  152.8 4.4 %collective-permute-start.12 = (f32[1,16,128]{2,0,1:T(1,128)S(1)}, f32[1,16,128]{2,0,1:T(1,128)S(1)}, u32[]{:S(2)}, u32[]{:S(2)}) collective-permute-start(f32[1,16,128]{2,0,1:T(1,128)S(1)} %get-tuple-element.113), channel_id=1, source_target_pairs={{4,0},{8,4},{12,8},{16,12},{20,16},{24,20},{28,24},{5,1},{9,5},{13... | collective-permute-start | bytes 24584 | tf_op jit(solution)/shard_map/ppermute | solution.py:26
  154.7 5.0 %collective-permute-start.13 = (f32[1,16,128]{2,0,1:T(1,128)S(1)}, f32[1,16,128]{2,0,1:T(1,128)S(1)}, u32[]{:S(2)}, u32[]{:S(2)}) collective-permute-start(f32[1,16,128]{2,0,1:T(1,128)S(1)} %get-tuple-element.112), channel_id=1, source_target_pairs={{0,4},{4,8},{8,12},{12,16},{16,20},{20,24},{24,28},{1,5},{5,9},{9,... | collective-permute-start | bytes 24584 | tf_op jit(solution)/shard_map/ppermute | solution.py:25
  165.6 4.3 %collective-permute-start.14 = (f32[1,16,512]{2,1,0:T(8,128)S(1)}, f32[1,16,512]{2,1,0:T(8,128)S(1)}, u32[]{:S(2)}, u32[]{:S(2)}) collective-permute-start(f32[1,16,512]{2,1,0:T(8,128)S(1)} %get-tuple-element.101), channel_id=1, source_target_pairs={{4,0},{8,4},{12,8},{16,12},{20,16},{24,20},{28,24},{5,1},{9,5},{13... | collective-permute-start | bytes 98312 | tf_op jit(solution)/shard_map/ppermute | solution.py:26
  167.5 5.2 %collective-permute-start.15 = (f32[1,16,512]{2,1,0:T(8,128)S(1)}, f32[1,16,512]{2,1,0:T(8,128)S(1)}, u32[]{:S(2)}, u32[]{:S(2)}) collective-permute-start(f32[1,16,512]{2,1,0:T(8,128)S(1)} %get-tuple-element.100), channel_id=1, source_target_pairs={{0,4},{4,8},{8,12},{12,16},{16,20},{20,24},{24,28},{1,5},{5,9},{9,... | collective-permute-start | bytes 98312 | tf_op jit(solution)/shard_map/ppermute | solution.py:25
  172.8 6.1 %collective-permute-start.16 = (f32[18,1,512]{2,1,0:T(1,128)S(1)}, f32[18,1,512]{2,1,0:T(1,128)S(1)}, u32[]{:S(2)}, u32[]{:S(2)}) collective-permute-start(f32[18,1,512]{2,1,0:T(1,128)S(1)} %get-tuple-element.88), channel_id=1, source_target_pairs={{1,0},{2,1},{3,2},{5,4},{6,5},{7,6},{9,8},{10,9},{11,10},{13,12},{... | collective-permute-start | bytes 110600 | tf_op jit(solution)/shard_map/ppermute | solution.py:26
  176.2 6.8 %collective-permute-start.17 = (f32[18,1,512]{2,1,0:T(1,128)S(1)}, f32[18,1,512]{2,1,0:T(1,128)S(1)}, u32[]{:S(2)}, u32[]{:S(2)}) collective-permute-start(f32[18,1,512]{2,1,0:T(1,128)S(1)} %get-tuple-element.89), channel_id=1, source_target_pairs={{0,1},{1,2},{2,3},{4,5},{5,6},{6,7},{8,9},{9,10},{10,11},{12,13},{... | collective-permute-start | bytes 110600 | tf_op jit(solution)/shard_map/ppermute | solution.py:25
  183.4 5.0 %collective-permute-start.18 = (f32[1,16,512]{2,1,0:T(8,128)S(1)}, f32[1,16,512]{2,1,0:T(8,128)S(1)}, u32[]{:S(2)}, u32[]{:S(2)}) collective-permute-start(f32[1,16,512]{2,1,0:T(8,128)S(1)} %get-tuple-element.97), channel_id=1, source_target_pairs={{4,0},{8,4},{12,8},{16,12},{20,16},{24,20},{28,24},{5,1},{9,5},{13... | collective-permute-start | bytes 98312 | tf_op jit(solution)/shard_map/ppermute | solution.py:26
  185.3 5.2 %collective-permute-start.19 = (f32[1,16,512]{2,1,0:T(8,128)S(1)}, f32[1,16,512]{2,1,0:T(8,128)S(1)}, u32[]{:S(2)}, u32[]{:S(2)}) collective-permute-start(f32[1,16,512]{2,1,0:T(8,128)S(1)} %get-tuple-element.96), channel_id=1, source_target_pairs={{0,4},{4,8},{8,12},{12,16},{16,20},{20,24},{24,28},{1,5},{5,9},{9,... | collective-permute-start | bytes 98312 | tf_op jit(solution)/shard_map/ppermute | solution.py:25
  190.6 6.1 %collective-permute-start.20 = (f32[18,1,512]{2,1,0:T(1,128)S(1)}, f32[18,1,512]{2,1,0:T(1,128)S(1)}, u32[]{:S(2)}, u32[]{:S(2)}) collective-permute-start(f32[18,1,512]{2,1,0:T(1,128)S(1)} %get-tuple-element.86), channel_id=1, source_target_pairs={{1,0},{2,1},{3,2},{5,4},{6,5},{7,6},{9,8},{10,9},{11,10},{13,12},{... | collective-permute-start | bytes 110600 | tf_op jit(solution)/shard_map/ppermute | solution.py:26
  193.7 6.8 %collective-permute-start.21 = (f32[18,1,512]{2,1,0:T(1,128)S(1)}, f32[18,1,512]{2,1,0:T(1,128)S(1)}, u32[]{:S(2)}, u32[]{:S(2)}) collective-permute-start(f32[18,1,512]{2,1,0:T(1,128)S(1)} %get-tuple-element.87), channel_id=1, source_target_pairs={{0,1},{1,2},{2,3},{4,5},{5,6},{6,7},{8,9},{9,10},{10,11},{12,13},{... | collective-permute-start | bytes 110600 | tf_op jit(solution)/shard_map/ppermute | solution.py:25
where the time goes:
time: 205 us; the launch traced here: 202 us
  local copies, waits for them, and re-layouts  56.8 us (28%)
  starting transfers between devices  53.7 us (26%)
  other arithmetic  48.7 us (24%)
  waiting for transfers between devices  27.1 us (13%)
  blocking collectives  14.1 us (7%)
    reshape x2, local copies, waits for them, and re-layouts, restrict(): values.reshape(rows // 4, 4, cols // 4, 4, depth // 4, 4)  37.3 us
    ppermute x11, starting transfers between devices, extended(): before = lax.ppermute(last, axis, up)  27.1 us
    ppermute x11, waiting for transfers between devices, extended(): before = lax.ppermute(last, axis, up)  27.1 us
    ppermute x11, starting transfers between devices, extended(): after = lax.ppermute(initial, axis, down)  26.6 us
    reduce_sum x16, other arithmetic, plane_source(): picked = jnp.sum(jnp.where(matches, thrust[:, None, None], 0.0), axis=0)  17.6 us
    reduce_sum x2, other arithmetic, restrict(): values.reshape(rows // 4, 4, cols // 4, 4, depth // 4, 4)  13.9 us
    dynamic_update_slice x16, other arithmetic, local(): lax.map(partial(plane_source, thrust), (disk_id, disk_mask))  12.4 us
    eq x16, local copies, waits for them, and re-layouts, plane_source(): jnp.arange(thrust.shape[0], dtype=jnp.int32)[:, None, None]  12.2 us
  transfers between devices with their start and end apart: 22, of which 9 were waited for; matrix products, arithmetic and copies ran while one was open for 14% of the time, Pallas kernels for 0%

commit v1 on v0

v1 whole, which is shorter than its diff:
```python
import jax
import jax.numpy as jnp
from jax import lax
from jax.experimental import pallas as pl
from jax.experimental.pallas import tpu as pltpu
from jax.sharding import PartitionSpec as P

SWEEPS = 4
OMEGA = 0.8
WALL_PENALTY = 0.4
INFLOW_PENALTY = 0.2
CHEB_LOW = 0.1
CHEB_HIGH = 2.0
F32 = jnp.float32
VMEM = pl.BlockSpec(memory_space=pltpu.VMEM)


def call(kernel, outs, *args, scratch=(), name=None):
    return pl.pallas_call(
        kernel,
        out_shape=[jax.ShapeDtypeStruct(s, F32) for s in outs],
        in_specs=[VMEM] * len(args),
        out_specs=[VMEM] * len(outs),
        scratch_shapes=[pltpu.VMEM(s, F32) for s in scratch],
        compiler_params=pltpu.CompilerParams(vmem_limit_bytes=16 << 20),
        name=name,
    )(*args)


def pairs_core(nx, ny):
    return [(x * ny + y, (x ^ 1) * ny + y) for x in range(nx) for y in range(ny)]


def pairs_chip(nx, ny):
    found = []
    for x in range(nx):
        for y in range(ny):
            if x in (0, nx - 1):
                found.append((x * ny + y, x * ny + (y ^ 1)))
            else:
                found.append((x * ny + y, (x + 1 if x % 2 else x - 1) * ny + y))
    return found


def pairs_row(nx, ny, step):
    return [(x * ny + y, x * ny + (y ^ step)) for x in range(nx) for y in range(ny)]


def pairs_odd(nx, ny):
    return [
        (x * ny + y, x * ny + (y + 1 if y % 2 else y - 1) % ny) for x in range(nx) for y in range(ny)
    ]


def put(ref, row, slab):
    rows = slab.shape[0]
    for j in range(slab.shape[1] // 128):
        ref[row + rows * j : row + rows * (j + 1), :] = slab[:, 128 * j : 128 * (j + 1)]


def get(ref, row, rows, width):
    return jnp.concatenate(
        [ref[row + rows * j : row + rows * (j + 1), :] for j in range(width // 128)], axis=1
    )


def iota(shape, dim):
    return lax.broadcasted_iota(jnp.int32, shape, dim)


def beside_z(slab):
    depth = slab.shape[1]
    lane = iota(slab.shape, 1)
    above = jnp.where(lane == depth - 1, 0.0, pltpu.roll(slab, depth - 1, 1))
    below = jnp.where(lane == 0, 0.0, pltpu.roll(slab, 1, 1))
    return above + below


def beside_rows(slab, low, high):
    rows = slab.shape[0]
    row = iota(slab.shape, 0)
    above = jnp.where(row == rows - 1, jnp.broadcast_to(high, slab.shape), pltpu.roll(slab, rows - 1, 0))
    below = jnp.where(row == 0, jnp.broadcast_to(low, slab.shape), pltpu.roll(slab, 1, 0))
    return above + below


def dot(left, right):
    return lax.dot_general(
        left,
        right,
        (((1,), (0,)), ((), ())),
        precision=lax.Precision.HIGHEST,
        preferred_element_type=F32,
    )


def group_lanes(depth):
    return (iota((depth, depth // 4), 0) // 4 == iota((depth, depth // 4), 1)).astype(F32)


def spread_lanes(rows):
    count, lanes = rows.shape
    pad = -count % 8
    if pad:
        rows = jnp.concatenate([rows, jnp.zeros((pad, lanes), F32)], axis=0)
    parts = []
    for j in range(4):
        index = iota(rows.shape, 1) // 4 + (lanes // 4) * j
        parts.append(jnp.take_along_axis(rows, index, axis=1, mode="promise_in_bounds"))
    return jnp.concatenate(parts, axis=1)[:count]


def spread_rows(ref, plane, start):
    row = iota((16, 128), 0) // 4
    value = jnp.zeros((16, 128), F32)
    for q in range(4):
        value = jnp.where(row == q, jnp.broadcast_to(ref[plane, start + q : start + q + 1, :], (16, 128)), value)
    return value


def spread_planes(ref, plane, column):
    row = iota((16, 128), 0) // 4
    value = jnp.zeros((16, 128), F32)
    for q in range(4):
        value = jnp.where(row == q, jnp.broadcast_to(ref[plane + q, column : column + 1, :], (16, 128)), value)
    return value


def solution(mesh):
    nx, ny = mesh.shape["gx"], mesh.shape["gy"]
    assert nx % 2 == 0 and ny % 2 == 0 and ny & (ny - 1) == 0
    axes = ("gx", "gy")

    def where_am_i():
        x, y = lax.axis_index("gx"), lax.axis_index("gy")
        return x, y, x % 2 == 0, y % 2 == 0

    def set_up(source, reaction, kind, disk_id, disk_mask, thrust, f, g, d, absorb, core, chip, row, odd, table, y_low, y_high):
        _, _, x_even, y_even = where_am_i()
        table[...] = jnp.zeros(table.shape, F32)
        table[0:1, 0 : thrust.shape[1]] = thrust[...]
        lookup = jnp.broadcast_to(table[0:1, :], (16, 128))

        def group(k, carry):
            total = jnp.zeros((16, 512), F32)
            for q in range(4):
                x = 4 * k + q
                kinds = kind[x]
                a = reaction[x] + jnp.where(kinds == 1, WALL_PENALTY, jnp.where(kinds == 2, INFLOW_PENALTY, 0.0))
                total = total + a
                diagonal = 6.0 + a
                scale = OMEGA / diagonal
                ids = disk_id[x]
                picked = jnp.concatenate(
                    [
                        jnp.take_along_axis(lookup, ids[:, 128 * j : 128 * (j + 1)], axis=1, mode="promise_in_bounds")
                        for j in range(4)
                    ],
                    axis=1,
                )
                first = (source[x] + disk_mask[x].astype(F32) * picked) * scale
                f[x] = first
                g[x] = scale
                d[x] = diagonal
                y_low[pl.ds(x, 1), :] = first[0:1, :]
                y_high[pl.ds(x, 1), :] = first[15:16, :]
            absorb[pl.ds(pl.multiple_of(16 * k, 16), 16), :] = total
            return carry

        lax.fori_loop(0, 4, group, 0)
        near, far = jnp.where(x_even, 15, 0), jnp.where(x_even, 0, 15)
        put(core, 0, f[near])
        put(core, 64, g[near])
        put(chip, 0, f[far])
        put(chip, 64, g[far])
        low, high = y_low[...], y_high[...]
        put(row, 0, jnp.where(y_even, high, low))
        put(odd, 0, jnp.where(y_even, low, high))

    def halo_x(core, chip, row, x, x_even):
        a, b = get(core, row, 16, 512), get(chip, row, 16, 512)
        left = jnp.where(x > 0, jnp.where(x_even, b, a), 0.0)
        right = jnp.where(x < nx - 1, jnp.where(x_even, a, b), 0.0)
        return left, right

    def halo_y(row, odd, at, y, y_even):
        a, b = get(row, at, 16, 512), get(odd, at, 16, 512)
        low = jnp.where(y > 0, jnp.where(y_even, b, a), 0.0)
        high = jnp.where(y < ny - 1, jnp.where(y_even, a, b), 0.0)
        return low, high

    def smooth(f, g, d, absorb, core, chip, row, odd, s, to_core, to_row, to_odd, block, F, lo, hi, S, V, y0, y1, y14, y15, g0, g15):
        x_at, y_at, x_even, y_even = where_am_i()
        left, right = halo_x(core, chip, 0, x_at, x_even)
        F[0], F[17] = left, right
        lo[...], hi[...] = halo_y(row, odd, 0, y_at, y_even)
        zero = jnp.zeros((16, 512), F32)
        S[0], S[17] = zero, zero

        def fill(x, carry):
            F[x + 1] = f[x]
            return carry

        lax.fori_loop(0, 16, fill, 0)

        def sweep(x, carry):
            here = F[x + 1]
            scale = g[x]
            total = F[x] + F[x + 2] + beside_rows(here, lo[pl.ds(x, 1), :], hi[pl.ds(x, 1), :]) + beside_z(here)
            value = 1.2 * here + scale * total
            S[x + 1] = value
            s[x] = value
            y0[pl.ds(x, 1), :] = value[0:1, :]
            y1[pl.ds(x, 1), :] = value[1:2, :]
            y14[pl.ds(x, 1), :] = value[14:15, :]
            y15[pl.ds(x, 1), :] = value[15:16, :]
            g0[pl.ds(x, 1), :] = scale[0:1, :]
            g15[pl.ds(x, 1), :] = scale[15:16, :]
            return carry

        lax.fori_loop(0, 16, sweep, 0)
        nothing = jnp.zeros((1, 512), F32)

        def residual(k, carry):
            total = jnp.zeros((16, 512), F32)
            for q in range(4):
                x = 4 * k + q
                here = S[x + 1]
                total = total + d[x] * (1.25 * F[x + 1] - here) + S[x] + S[x + 2]
                total = total + beside_rows(here, nothing, nothing) + beside_z(here)
            V[pl.ds(pl.multiple_of(16 * k, 16), 16), :] = total
            return carry

        lax.fori_loop(0, 4, residual, 0)
        V[64:128, :] = absorb[...]
        V[128:144, :] = S[1]
        V[144:160, :] = S[16]
        V[160:176, :] = y0[...]
        V[176:192, :] = y15[...]
        out, src = iota((48, 192), 0), iota((48, 192), 1)
        cx, cy = out % 4, out // 8
        in_bulk = (out < 32) & (src < 128) & (src // 64 == (out // 4) % 2)
        bulk = in_bulk & ((src % 64) // 16 == cx) & ((src % 16) // 4 == cy)
        faces = (out >= 32) & (src >= 128) & ((out - 32) // 4 == (src - 128) // 16) & ((src % 16) // 4 == cx)
        picked = dot((bulk | faces).astype(F32), V[...])
        block[...] = dot(picked, group_lanes(512))
        near = jnp.where(x_even, 16, 1)
        inner = jnp.where(x_even, 15, 2)
        put(to_core, 0, S[near])
        put(to_core, 64, S[inner])
        to_core[128:132, :] = jnp.where(x_even, block[36:40, :], block[32:36, :])
        to_core[132:136, :] = jnp.zeros((4, 128), F32)
        for at, (low, high) in enumerate(((y0, y15), (y1, y14), (g0, g15))):
            a, b = low[...], high[...]
            put(to_row, 64 * at, jnp.where(y_even, b, a))
            put(to_odd, 64 * at, jnp.where(y_even, a, b))

    def to_chip_kernel(block, core, s, mine, to_chip):
        _, _, x_even, _ = where_am_i()
        mine[...] = jnp.concatenate([block[0:32, :], block[40:48, :]], axis=0)
        face = core[128:136, :]
        for cy in range(4):
            line = face[cy : cy + 1, :]
            mine[8 * cy : 8 * cy + 1, :] = block[8 * cy : 8 * cy + 1, :] + jnp.where(x_even, 0.0, line)
            mine[8 * cy + 3 : 8 * cy + 4, :] = block[8 * cy + 3 : 8 * cy + 4, :] + jnp.where(x_even, line, 0.0)
        put(to_chip, 0, s[jnp.where(x_even, 0, 15)])
        put(to_chip, 64, s[jnp.where(x_even, 1, 14)])
        to_chip[128:168, :] = mine[...]
        to_chip[168:172, :] = jnp.where(x_even, block[32:36, :], block[36:40, :])
        to_chip[172:176, :] = jnp.zeros((4, 128), F32)

    def from_chip_kernel(mine, block, chip, full, beyond):
        x_at, _, x_even, _ = where_am_i()
        has = jnp.where(x_even, x_at > 0, x_at < nx - 1)
        full[...] = mine[...]
        beyond[...] = chip[128:168, :]
        mine_face = jnp.where(x_even, block[32:36, :], block[36:40, :])
        face = chip[168:176, :]
        for cy in range(4):
            line = jnp.where(has, face[cy : cy + 1, :], 0.0)
            own = mine_face[cy : cy + 1, :]
            a, b = 8 * cy, 8 * cy + 3
            full[a : a + 1, :] = mine[a : a + 1, :] + jnp.where(x_even, line, 0.0)
            full[b : b + 1, :] = mine[b : b + 1, :] + jnp.where(x_even, 0.0, line)
            beyond[a : a + 1, :] = chip[128 + a : 129 + a, :] + jnp.where(x_even, 0.0, own)
            beyond[b : b + 1, :] = chip[128 + b : 129 + b, :] + jnp.where(x_even, own, 0.0)

    def window_kernel(full, beyond, core, chip, s_core, s, window):
        x_at, _, x_even, _ = where_am_i()
        mid = full[...]
        a, b = core[...], beyond[...]
        left, right = jnp.where(x_even, b, a), jnp.where(x_even, a, b)
        for at, block in enumerate((left, mid, right)):
            for cy in range(4):
                window[24 * cy + 4 * at : 24 * cy + 4 * at + 4, :] = block[8 * cy : 8 * cy + 4, :]
                window[24 * cy + 12 + 4 * at : 24 * cy + 16 + 4 * at, :] = block[8 * cy + 4 : 8 * cy + 8, :]
            window[96 + 4 * at : 100 + 4 * at, :] = block[32:36, :]
            window[108 + 4 * at : 112 + 4 * at, :] = block[36:40, :]
        low, high = halo_x(s_core, chip, 0, x_at, x_even)
        for at, line in enumerate((low[0:1, :], low[15:16, :], high[0:1, :], high[15:16, :])):
            put(window, 120 + 4 * at, line)

    planes = 4 * ny

    def finish(*refs):
        f, g, s, a_core, a_chip, a_row, a_odd, s_core, s_chip, s_row, s_odd = refs[:11]
        windows = refs[11 : 11 + ny]
        pressure, coarse = refs[11 + ny : 13 + ny]
        every, res, diag, inv, one, two, sol, Pc, T, U, yl, yh, tl, th, ul, uh = refs[13 + ny :]
        x_at, y_at, x_even, y_even = where_am_i()
        for step, window in enumerate(windows):
            every[jnp.bitwise_xor(y_at, step)] = window[...]

        row = iota((16, 128), 0)
        valid = ((row >= 4) | (x_at > 0)) & ((row < 8) | (x_at < nx - 1)) & (row < 12)
        blank = jnp.zeros((4, 128), F32)

        def twelve(value):
            return jnp.concatenate([value, blank], axis=0)

        centre = (CHEB_HIGH + CHEB_LOW) / 2.0
        half_range = (CHEB_HIGH - CHEB_LOW) / 2.0
        aspect = centre / half_range
        factor = 1.0 / aspect
        empty = jnp.zeros((16, 128), F32)
        for ref in (one, two, sol):
            ref[0] = empty
            ref[planes + 1] = empty
        for at in range(ny):
            for cy in range(4):
                plane = 4 * at + cy
                value = every[at, 24 * cy : 24 * cy + 12, :]
                if cy == 0 and at > 0:
                    value = value + every[at - 1, 108:120, :]
                if cy == 3 and at < ny - 1:
                    value = value + every[at + 1, 96:108, :]
                value = jnp.where(valid, twelve(value), 0.0)
                centre_value = 6.0 + twelve(every[at, 24 * cy + 12 : 24 * cy + 24, :]) / 16.0
                inverse = jnp.where(valid, 1.0 / (16.0 * centre_value), 0.0)
                res[plane] = value
                diag[plane] = centre_value
                inv[plane] = inverse
                direction = inverse * value / centre
                one[plane + 1] = direction
                sol[plane + 1] = direction
        now, later = one, two
        for number in range(1, SWEEPS):
            factor_next = 1.0 / (2.0 * aspect - factor)
            keep, gain = factor_next * factor, 2.0 * factor_next / half_range

            def step(plane, carry, now=now, later=later, keep=keep, gain=gain):
                here = now[plane + 1]
                lane = iota((16, 128), 1)
                total = now[plane] + now[plane + 2]
                total = total + pltpu.roll(here, 15, 0) + pltpu.roll(here, 1, 0)
                total = total + jnp.where(lane == 127, 0.0, pltpu.roll(here, 127, 1))
                total = total + jnp.where(lane == 0, 0.0, pltpu.roll(here, 1, 1))
                residual = res[plane] - 16.0 * (diag[plane] * here - total)
                res[plane] = residual
                direction = keep * here + gain * inv[plane] * residual
                later[plane + 1] = direction
                sol[plane + 1] = sol[plane + 1] + direction
                return carry

            lax.fori_loop(0, planes, step, 0)
            now, later = later, now
            factor = factor_next
        for plane in range(planes):
            for cx in range(4):
                coarse[cx, plane : plane + 1, :] = sol[plane + 1, 4 + cx : 5 + cx, :]

        first_plane = 4 * y_at + 1
        for at in range(6):
            Pc[at] = spread_lanes(spread_planes(sol, first_plane, 3 + at))
        s_left, s_right = halo_x(s_core, s_chip, 0, x_at, x_even)
        s_left2, s_right2 = halo_x(s_core, s_chip, 64, x_at, x_even)
        T[0], T[1] = s_left2 + Pc[0], s_left + Pc[0]
        T[18], T[19] = s_right + Pc[5], s_right2 + Pc[5]

        def third(x, carry):
            T[x + 2] = s[x] + Pc[x // 4 + 1]
            return carry

        lax.fori_loop(0, 16, third, 0)
        below, above = first_plane - 1, first_plane + 4
        y1_low, y1_high = halo_y(s_row, s_odd, 0, y_at, y_even)
        y2_low, y2_high = halo_y(s_row, s_odd, 64, y_at, y_even)
        g_low, g_high = halo_y(s_row, s_odd, 128, y_at, y_even)
        f_low, f_high = halo_y(a_row, a_odd, 0, y_at, y_even)
        before, after = jnp.maximum(y_at - 1, 0), jnp.minimum(y_at + 1, ny - 1)
        outer = {}
        for name, ref, plane, s1, s2, who, inside, line in (
            ("low", tl, below, y1_low, y2_low, before, y_at > 0, 1),
            ("high", th, above, y1_high, y2_high, after, y_at < ny - 1, 0),
        ):
            spread = spread_lanes(spread_rows(sol, plane, 4))
            ref[8:24, :] = s1 + spread
            outer[name] = s2 + spread
            for at, cx, base, there in ((7, 3, 0, x_at > 0), (24, 8, 2, x_at < nx - 1)):
                corner = jnp.concatenate(
                    [every[who, pl.ds(120 + 4 * (base + line) + j, 1), :] for j in range(4)], axis=1
                )
                corner = jnp.where(inside & there, corner, 0.0)
                ref[at : at + 1, :] = corner + spread_lanes(sol[plane, cx : cx + 1, :])

        f_left, f_right = halo_x(a_core, a_chip, 0, x_at, x_even)
        g_left, g_right = halo_x(a_core, a_chip, 64, x_at, x_even)

        def fourth_at(at, forcing, scale):
            here = T[at + 1]
            total = T[at] + T[at + 2] + beside_z(here)
            total = total + beside_rows(here, tl[pl.ds(at + 7, 1), :], th[pl.ds(at + 7, 1), :])
            return 0.2 * here + forcing + scale * total

        U[0] = fourth_at(0, f_left, g_left)
        U[17] = fourth_at(17, f_right, g_right)

        def fourth(x, carry):
            U[x + 1] = fourth_at(x + 1, f[x], g[x])
            here = T[x + 2]
            yl[pl.ds(x, 1), :] = here[0:1, :]
            yh[pl.ds(x, 1), :] = here[15:16, :]
            return carry

        lax.fori_loop(0, 16, fourth, 0)
        for ref, out, edge, far, forcing, scale in (
            (tl, ul, yl, outer["low"], f_low, g_low),
            (th, uh, yh, outer["high"], f_high, g_high),
        ):
            here = ref[8:24, :]
            total = far + edge[...] + ref[7:23, :] + ref[9:25, :] + beside_z(here)
            out[...] = 0.2 * here + forcing + scale * total

        def fifth(x, carry):
            here = U[x + 1]
            total = U[x] + U[x + 2] + beside_z(here)
            total = total + beside_rows(here, ul[pl.ds(x, 1), :], uh[pl.ds(x, 1), :])
            pressure[x] = 0.2 * here + f[x] + g[x] * total
            return carry

        lax.fori_loop(0, 16, fifth, 0)

    slab, field, long = (16, 512), (16, 16, 512), (18, 16, 512)
    core_pairs, chip_pairs = pairs_core(nx, ny), pairs_chip(nx, ny)
    row_pairs = [pairs_row(nx, ny, step) for step in range(1, ny)]
    odd_pairs = pairs_odd(nx, ny)

    def swap(array, pairs):
        return lax.ppermute(array, axes, pairs)

    def local(source, reaction, boundary_kind, disk_id, disk_mask, thrust):
        f, g, d, absorb, core, chip, row, odd = call(
            set_up,
            [field, field, field, (64, 512), (128, 128), (128, 128), (64, 128), (64, 128)],
            source, reaction, boundary_kind, disk_id, disk_mask, thrust.reshape(1, -1),
            scratch=[(8, 128), slab, slab],
            name="set_up",
        )
        a_row, a_odd = swap(row, row_pairs[0]), swap(odd, odd_pairs)
        a_chip, a_core = swap(chip, chip_pairs), swap(core, core_pairs)
        s, to_core, to_row, to_odd, block = call(
            smooth,
            [field, (136, 128), (192, 128), (192, 128), (48, 128)],
            f, g, d, absorb, a_core, a_chip, a_row, a_odd,
            scratch=[long, slab, slab, long, (192, 512), slab, slab, slab, slab, slab, slab],
            name="smooth",
        )
        s_core = swap(to_core, core_pairs)
        s_row, s_odd = swap(to_row, row_pairs[0]), swap(to_odd, odd_pairs)
        mine, to_chip = call(to_chip_kernel, [(40, 128), (176, 128)], block, s_core, s, name="to_chip")
        s_chip = swap(to_chip, chip_pairs)
        full, beyond = call(from_chip_kernel, [(40, 128), (40, 128)], mine, block, s_chip, name="from_chip")
        c_core = swap(full, core_pairs)
        (window,) = call(window_kernel, [(136, 128)], full, beyond, c_core, s_chip, s_core, s, name="window")
        windows = [window] + [swap(window, pairs) for pairs in row_pairs]
        pressure, coarse = call(
            finish,
            [field, (4, planes, 128)],
            f, g, s, a_core, a_chip, a_row, a_odd, s_core, s_chip, s_row, s_odd, *windows,
            scratch=[(ny, 136, 128)]
            + [(planes, 16, 128)] * 3
            + [(planes + 2, 16, 128)] * 3
            + [(6, 16, 512), (20, 16, 512), long, slab, slab, (32, 512), (32, 512), slab, slab],
            name="finish",
        )
        return pressure, coarse

    spec = P("gx", "gy", None)
    return jax.shard_map(
        local,
        mesh=mesh,
        in_specs=(spec, spec, spec, spec, spec, P()),
        out_specs=(spec, P("gx", None, None)),
        check_vma=False,
    )
```

time: 205 us -> 42.6 us (0.21)
  the two profiles are of different devices: /device:TPU:12 before, /device:TPU:0 now
where the time goes in v1:
time: 42.6 us; the launch traced here: 42.2 us
  starting transfers between devices  14.2 us (33%)
  Pallas kernels  11.8 us (28%)
  waiting for transfers between devices  9.63 us (23%)
  local copies, waits for them, and re-layouts  5.85 us (14%)
  between operations  0.68 us (2%)
    ppermute x12, starting transfers between devices, swap(): return lax.ppermute(array, axes, pairs)  14.2 us
    pallas_call x6, Pallas kernels, call(): pl.pallas_call(kernel, out_shape=[jax.ShapeDtypeStruct(s, F32) for s in o...  11.8 us
    ppermute x12, waiting for transfers between devices, swap(): return lax.ppermute(array, axes, pairs)  9.63 us
    unnamed x12, local copies, waits for them, and re-layouts  5.85 us
  transfers between devices with their start and end apart: 12, of which 8 were waited for; matrix products, arithmetic and copies ran while one was open for 0% of the time, Pallas kernels for 0%

profile of v1, /device:TPU:0, one launch (start us, length us, event | category | flops | bytes accessed | tf_op | source)
XLA Modules:
  0.0 42.2 jit_solution(14959686154850554777)
XLA Ops:
  0.6 0.6 %copy-done.5 = f32[120]{0:T(128)S(1)} copy-done((f32[120]{0:T(128)S(1)}, f32[120]{0:T(128)}, u32[]{:S(2)}) %copy-start.5) | copy-done | bytes 504
  1.3 1.0 %copy-done = f32[16,16,512]{2,1,0:T(8,128)S(1)} copy-done((f32[16,16,512]{2,1,0:T(8,128)S(1)}, f32[16,16,512]{2,1,0:T(8,128)}, u32[]{:S(2)}) %copy-start) | copy-done | bytes 524312
  2.3 1.0 %copy-done.1 = f32[16,16,512]{2,1,0:T(8,128)S(1)} copy-done((f32[16,16,512]{2,1,0:T(8,128)S(1)}, f32[16,16,512]{2,1,0:T(8,128)}, u32[]{:S(2)}) %copy-start.1) | copy-done | bytes 524312
  3.4 1.0 %copy-done.2 = s32[16,16,512]{2,1,0:T(8,128)S(1)} copy-done((s32[16,16,512]{2,1,0:T(8,128)S(1)}, s32[16,16,512]{2,1,0:T(8,128)}, u32[]{:S(2)}) %copy-start.2) | copy-done | bytes 524312
  4.4 1.0 %copy-done.3 = s32[16,16,512]{2,1,0:T(8,128)S(1)} copy-done((s32[16,16,512]{2,1,0:T(8,128)S(1)}, s32[16,16,512]{2,1,0:T(8,128)}, u32[]{:S(2)}) %copy-start.3) | copy-done | bytes 524312
  5.5 1.0 %copy-done.4 = s32[16,16,512]{2,1,0:T(8,128)S(1)} copy-done((s32[16,16,512]{2,1,0:T(8,128)S(1)}, s32[16,16,512]{2,1,0:T(8,128)}, u32[]{:S(2)}) %copy-start.4) | copy-done | bytes 524312
  6.5 0.7 %set_up.1 = (f32[16,16,512]{2,1,0:T(8,128)S(1)}, f32[16,16,512]{2,1,0:T(8,128)S(1)}, f32[16,16,512]{2,1,0:T(8,128)S(1)}, f32[64,512]{1,0:T(8,128)S(1)}, f32[128,...) custom-call(f32[16,16,512]{2,1,0:T(8,128)S(1)} %copy-done, ...), custom_call_target="tpu_custom_call" | custom-call | tf_op jit(solution)/shard_map/set_up/pallas_call | solution.py:19
  7.2 0.5 %collective-permute-start = (f32[128,128]{1,0:T(8,128)S(1)}, f32[128,128]{1,0:T(8,128)S(1)}, u32[]{:S(2)}, u32[]{:S(2)}) collective-permute-start(f32[128,128]{1,0:T(8,128)S(1)} %get-tuple-element.23), channel_id=1, source_target_pairs={{0,4},{1,5},{2,6},{3,7},{4,0},{5,1},{6,2},{7,3},{8,12},{9,13},{10,... | collective-permute-start | bytes 196616 | tf_op jit(solution)/shard_map/ppermute | solution.py:449
  7.7 2.6 %collective-permute-start.1 = (f32[128,128]{1,0:T(8,128)S(1)}, f32[128,128]{1,0:T(8,128)S(1)}, u32[]{:S(2)}, u32[]{:S(2)}) collective-permute-start(f32[128,128]{1,0:T(8,128)S(1)} %get-tuple-element.24), channel_id=1, source_target_pairs={{0,1},{1,0},{2,3},{3,2},{4,8},{5,9},{6,10},{7,11},{8,4},{9,5},{10,... | collective-permute-start | bytes 196616 | tf_op jit(solution)/shard_map/ppermute | solution.py:449
  10.3 2.9 %collective-permute-start.3 = (f32[64,128]{1,0:T(8,128)S(1)}, f32[64,128]{1,0:T(8,128)S(1)}, u32[]{:S(2)}, u32[]{:S(2)}) collective-permute-start(f32[64,128]{1,0:T(8,128)S(1)} %get-tuple-element.26), channel_id=1, source_target_pairs={{0,3},{1,2},{2,1},{3,0},{4,7},{5,6},{6,5},{7,4},{8,11},{9,10},{10,... | collective-permute-start | bytes 98312 | tf_op jit(solution)/shard_map/ppermute | solution.py:449
  13.2 0.9 %collective-permute-done.2.row.refs_5_ = f32[64,128]{1,0:T(8,128)S(1)} collective-permute-done((f32[64,128]{1,0:T(8,128)S(1)}, f32[64,128]{1,0:T(8,128)S(1)}, u32[]{:S(2)}, u32[]{:S(2)}) %collective-permute-start.2) | collective-permute-done | bytes 32800 | tf_op jit(solution)/shard_map/ppermute | solution.py:449
  14.2 1.7 %collective-permute-done.3.odd.refs_6_ = f32[64,128]{1,0:T(8,128)S(1)} collective-permute-done((f32[64,128]{1,0:T(8,128)S(1)}, f32[64,128]{1,0:T(8,128)S(1)}, u32[]{:S(2)}, u32[]{:S(2)}) %collective-permute-start.3) | collective-permute-done | bytes 32800 | tf_op jit(solution)/shard_map/ppermute | solution.py:449
  15.8 2.8 %smooth.1 = (f32[16,16,512]{2,1,0:T(8,128)S(1)}, f32[136,128]{1,0:T(8,128)S(1)}, f32[192,128]{1,0:T(8,128)S(1)}, f32[192,128]{1,0:T(8,128)S(1)}, f32[48,128]{1,0:T(8,128)S(1)}) custom-call(f32[16,16,512]{2,1,0:T(8,128)S(1)} %get-tuple-element.19.f.refs_0_, f32[16,16,512]{2,1,0:T(8,128)S(1)} %get-tuple-element.20.g.refs_1_, ...), custom_call_target="tpu_custom_call" | custom-call | tf_op jit(solution)/shard_map/smooth/pallas_call | solution.py:19
  18.8 1.2 %collective-permute-done.4.core.s_core.refs_7_ = f32[136,128]{1,0:T(8,128)S(1)} collective-permute-done((f32[136,128]{1,0:T(8,128)S(1)}, f32[136,128]{1,0:T(8,128)S(1)}, u32[]{:S(2)}, u32[]{:S(2)}) %collective-permute-start.4) | collective-permute-done | bytes 69664 | tf_op jit(solution)/shard_map/ppermute | solution.py:449
  20.0 1.3 %collective-permute-start.5 = (f32[176,128]{1,0:T(8,128)S(1)}, f32[176,128]{1,0:T(8,128)S(1)}, u32[]{:S(2)}, u32[]{:S(2)}) collective-permute-start(f32[176,128]{1,0:T(8,128)S(1)} %get-tuple-element.30), channel_id=1, source_target_pairs={{0,1},{1,0},{2,3},{3,2},{4,8},{5,9},{6,10},{7,11},{8,4},{9,5},{10,... | collective-permute-start | bytes 270344 | tf_op jit(solution)/shard_map/ppermute | solution.py:449
  21.3 0.8 %collective-permute-start.6 = (f32[192,128]{1,0:T(8,128)S(1)}, f32[192,128]{1,0:T(8,128)S(1)}, u32[]{:S(2)}, u32[]{:S(2)}) collective-permute-start(f32[192,128]{1,0:T(8,128)S(1)} %get-tuple-element.31), channel_id=1, source_target_pairs={{0,1},{1,0},{2,3},{3,2},{4,5},{5,4},{6,7},{7,6},{8,9},{9,8},{10,11... | collective-permute-start | bytes 294920 | tf_op jit(solution)/shard_map/ppermute | solution.py:449
  22.1 2.2 %collective-permute-start.7 = (f32[192,128]{1,0:T(8,128)S(1)}, f32[192,128]{1,0:T(8,128)S(1)}, u32[]{:S(2)}, u32[]{:S(2)}) collective-permute-start(f32[192,128]{1,0:T(8,128)S(1)} %get-tuple-element.32), channel_id=1, source_target_pairs={{0,3},{1,2},{2,1},{3,0},{4,7},{5,6},{6,5},{7,4},{8,11},{9,10},{10,... | collective-permute-start | bytes 294920 | tf_op jit(solution)/shard_map/ppermute | solution.py:449
  24.3 0.5 %collective-permute-done.5.chip.refs_8_ = f32[176,128]{1,0:T(8,128)S(1)} collective-permute-done((f32[176,128]{1,0:T(8,128)S(1)}, f32[176,128]{1,0:T(8,128)S(1)}, u32[]{:S(2)}, u32[]{:S(2)}) %collective-permute-start.5) | collective-permute-done | bytes 90144 | tf_op jit(solution)/shard_map/ppermute | solution.py:449
  24.9 1.2 %collective-permute-done.8.core = f32[40,128]{1,0:T(8,128)S(1)} collective-permute-done((f32[40,128]{1,0:T(8,128)S(1)}, f32[40,128]{1,0:T(8,128)S(1)}, u32[]{:S(2)}, u32[]{:S(2)}) %collective-permute-start.8) | collective-permute-done | bytes 20512 | tf_op jit(solution)/shard_map/ppermute | solution.py:449
  26.1 3.0 %collective-permute-start.11 = (f32[136,128]{1,0:T(8,128)S(1)}, f32[136,128]{1,0:T(8,128)S(1)}, u32[]{:S(2)}, u32[]{:S(2)}) collective-permute-start(f32[136,128]{1,0:T(8,128)S(1)} %window.1.refs_11_), channel_id=1, source_target_pairs={{0,3},{1,2},{2,1},{3,0},{4,7},{5,6},{6,5},{7,4},{8,11},{9,10},{10,... | collective-permute-start | bytes 208904 | tf_op jit(solution)/shard_map/ppermute | solution.py:449
  29.1 0.5 %collective-permute-start.10 = (f32[136,128]{1,0:T(8,128)S(1)}, f32[136,128]{1,0:T(8,128)S(1)}, u32[]{:S(2)}, u32[]{:S(2)}) collective-permute-start(f32[136,128]{1,0:T(8,128)S(1)} %window.1.refs_11_), channel_id=1, source_target_pairs={{0,2},{1,3},{2,0},{3,1},{4,6},{5,7},{6,4},{7,5},{8,10},{9,11},{10,... | collective-permute-start | bytes 208904 | tf_op jit(solution)/shard_map/ppermute | solution.py:449
  29.8 1.9 %collective-permute-done.11.refs_14_ = f32[136,128]{1,0:T(8,128)S(1)} collective-permute-done((f32[136,128]{1,0:T(8,128)S(1)}, f32[136,128]{1,0:T(8,128)S(1)}, u32[]{:S(2)}, u32[]{:S(2)}) %collective-permute-start.11) | collective-permute-done | bytes 69664 | tf_op jit(solution)/shard_map/ppermute | solution.py:449
  31.6 1.8 %collective-permute-done.10.refs_13_ = f32[136,128]{1,0:T(8,128)S(1)} collective-permute-done((f32[136,128]{1,0:T(8,128)S(1)}, f32[136,128]{1,0:T(8,128)S(1)}, u32[]{:S(2)}, u32[]{:S(2)}) %collective-permute-start.10) | collective-permute-done | bytes 69664 | tf_op jit(solution)/shard_map/ppermute | solution.py:449
  33.9 8.3 %finish.1 = (f32[16,16,512]{2,1,0:T(8,128)}, f32[4,16,128]{2,1,0:T(8,128)}) custom-call(f32[16,16,512]{2,1,0:T(8,128)S(1)} %get-tuple-element.19.f.refs_0_, f32[16,16,512]{2,1,0:T(8,128)S(1)} %get-tuple-element.20.g.refs_1_, f32[16,16,512]{2,1,0:T(8,128)S(1)} %get-tuple-element.27.s.refs_2_, f32[128,128]{1,0:T(8,128)S(1)} %collective-permute-done.core.refs_3_, ...), custom_call_target="tpu_custom_call" | custom-call | tf_op jit(solution)/shard_map/finish/pallas_call | solution.py:19
  (18 shorter events, 1.0 us)
Async XLA Ops:
  0.6 0.7 %copy-start.5 = (f32[120]{0:T(128)S(1)}, f32[120]{0:T(128)}, u32[]{:S(2)}) copy-start(f32[120]{0:T(128)} %param.11) | copy-start | bytes 1444
  1.3 1.0 %copy-start = (f32[16,16,512]{2,1,0:T(8,128)S(1)}, f32[16,16,512]{2,1,0:T(8,128)}, u32[]{:S(2)}) copy-start(f32[16,16,512]{2,1,0:T(8,128)} %source.1) | copy-start | bytes 1572868
  2.3 1.0 %copy-start.1 = (f32[16,16,512]{2,1,0:T(8,128)S(1)}, f32[16,16,512]{2,1,0:T(8,128)}, u32[]{:S(2)}) copy-start(f32[16,16,512]{2,1,0:T(8,128)} %reaction.1) | copy-start | bytes 1572868
  3.4 1.0 %copy-start.2 = (s32[16,16,512]{2,1,0:T(8,128)S(1)}, s32[16,16,512]{2,1,0:T(8,128)}, u32[]{:S(2)}) copy-start(s32[16,16,512]{2,1,0:T(8,128)} %kind.1) | copy-start | bytes 1572868
  4.4 1.0 %copy-start.3 = (s32[16,16,512]{2,1,0:T(8,128)S(1)}, s32[16,16,512]{2,1,0:T(8,128)}, u32[]{:S(2)}) copy-start(s32[16,16,512]{2,1,0:T(8,128)} %disk_id.1) | copy-start | bytes 1572868
  5.5 1.0 %copy-start.4 = (s32[16,16,512]{2,1,0:T(8,128)S(1)}, s32[16,16,512]{2,1,0:T(8,128)}, u32[]{:S(2)}) copy-start(s32[16,16,512]{2,1,0:T(8,128)} %disk_mask.1) | copy-start | bytes 1572868
  7.2 8.7 %collective-permute-start = (f32[128,128]{1,0:T(8,128)S(1)}, f32[128,128]{1,0:T(8,128)S(1)}, u32[]{:S(2)}, u32[]{:S(2)}) collective-permute-start(f32[128,128]{1,0:T(8,128)S(1)} %get-tuple-element.23), channel_id=1, source_target_pairs={{0,4},{1,5},{2,6},{3,7},{4,0},{5,1},{6,2},{7,3},{8,12},{9,13},{10,... | collective-permute-start | bytes 196616 | tf_op jit(solution)/shard_map/ppermute | solution.py:449
  7.7 8.1 %collective-permute-start.1 = (f32[128,128]{1,0:T(8,128)S(1)}, f32[128,128]{1,0:T(8,128)S(1)}, u32[]{:S(2)}, u32[]{:S(2)}) collective-permute-start(f32[128,128]{1,0:T(8,128)S(1)} %get-tuple-element.24), channel_id=1, source_target_pairs={{0,1},{1,0},{2,3},{3,2},{4,8},{5,9},{6,10},{7,11},{8,4},{9,5},{10,... | collective-permute-start | bytes 196616 | tf_op jit(solution)/shard_map/ppermute | solution.py:449
  10.3 3.9 %collective-permute-start.2 = (f32[64,128]{1,0:T(8,128)S(1)}, f32[64,128]{1,0:T(8,128)S(1)}, u32[]{:S(2)}, u32[]{:S(2)}) collective-permute-start(f32[64,128]{1,0:T(8,128)S(1)} %get-tuple-element.25), channel_id=1, source_target_pairs={{0,1},{1,0},{2,3},{3,2},{4,5},{5,4},{6,7},{7,6},{8,9},{9,8},{10,11... | collective-permute-start | bytes 98312 | tf_op jit(solution)/shard_map/ppermute | solution.py:449
  10.3 5.5 %collective-permute-start.3 = (f32[64,128]{1,0:T(8,128)S(1)}, f32[64,128]{1,0:T(8,128)S(1)}, u32[]{:S(2)}, u32[]{:S(2)}) collective-permute-start(f32[64,128]{1,0:T(8,128)S(1)} %get-tuple-element.26), channel_id=1, source_target_pairs={{0,3},{1,2},{2,1},{3,0},{4,7},{5,6},{6,5},{7,4},{8,11},{9,10},{10,... | collective-permute-start | bytes 98312 | tf_op jit(solution)/shard_map/ppermute | solution.py:449
  18.6 1.3 %collective-permute-start.4 = (f32[136,128]{1,0:T(8,128)S(1)}, f32[136,128]{1,0:T(8,128)S(1)}, u32[]{:S(2)}, u32[]{:S(2)}) collective-permute-start(f32[136,128]{1,0:T(8,128)S(1)} %get-tuple-element.28), channel_id=1, source_target_pairs={{0,4},{1,5},{2,6},{3,7},{4,0},{5,1},{6,2},{7,3},{8,12},{9,13},{10,... | collective-permute-start | bytes 208904 | tf_op jit(solution)/shard_map/ppermute | solution.py:449
  20.0 4.8 %collective-permute-start.5 = (f32[176,128]{1,0:T(8,128)S(1)}, f32[176,128]{1,0:T(8,128)S(1)}, u32[]{:S(2)}, u32[]{:S(2)}) collective-permute-start(f32[176,128]{1,0:T(8,128)S(1)} %get-tuple-element.30), channel_id=1, source_target_pairs={{0,1},{1,0},{2,3},{3,2},{4,8},{5,9},{6,10},{7,11},{8,4},{9,5},{10,... | collective-permute-start | bytes 270344 | tf_op jit(solution)/shard_map/ppermute | solution.py:449
  21.3 8.4 %collective-permute-start.6 = (f32[192,128]{1,0:T(8,128)S(1)}, f32[192,128]{1,0:T(8,128)S(1)}, u32[]{:S(2)}, u32[]{:S(2)}) collective-permute-start(f32[192,128]{1,0:T(8,128)S(1)} %get-tuple-element.31), channel_id=1, source_target_pairs={{0,1},{1,0},{2,3},{3,2},{4,5},{5,4},{6,7},{7,6},{8,9},{9,8},{10,11... | collective-permute-start | bytes 294920 | tf_op jit(solution)/shard_map/ppermute | solution.py:449
  22.1 7.7 %collective-permute-start.7 = (f32[192,128]{1,0:T(8,128)S(1)}, f32[192,128]{1,0:T(8,128)S(1)}, u32[]{:S(2)}, u32[]{:S(2)}) collective-permute-start(f32[192,128]{1,0:T(8,128)S(1)} %get-tuple-element.32), channel_id=1, source_target_pairs={{0,3},{1,2},{2,1},{3,0},{4,7},{5,6},{6,5},{7,4},{8,11},{9,10},{10,... | collective-permute-start | bytes 294920 | tf_op jit(solution)/shard_map/ppermute | solution.py:449
  24.8 1.3 %collective-permute-start.8 = (f32[40,128]{1,0:T(8,128)S(1)}, f32[40,128]{1,0:T(8,128)S(1)}, u32[]{:S(2)}, u32[]{:S(2)}) collective-permute-start(f32[40,128]{1,0:T(8,128)S(1)} %get-tuple-element.34.full), channel_id=1, source_target_pairs={{0,4},{1,5},{2,6},{3,7},{4,0},{5,1},{6,2},{7,3},{8,12},{9,13},{10,... | collective-permute-start | bytes 61448 | tf_op jit(solution)/shard_map/ppermute | solution.py:449
  26.1 5.5 %collective-permute-start.11 = (f32[136,128]{1,0:T(8,128)S(1)}, f32[136,128]{1,0:T(8,128)S(1)}, u32[]{:S(2)}, u32[]{:S(2)}) collective-permute-start(f32[136,128]{1,0:T(8,128)S(1)} %window.1.refs_11_), channel_id=1, source_target_pairs={{0,3},{1,2},{2,1},{3,0},{4,7},{5,6},{6,5},{7,4},{8,11},{9,10},{10,... | collective-permute-start | bytes 208904 | tf_op jit(solution)/shard_map/ppermute | solution.py:449
  29.1 4.3 %collective-permute-start.10 = (f32[136,128]{1,0:T(8,128)S(1)}, f32[136,128]{1,0:T(8,128)S(1)}, u32[]{:S(2)}, u32[]{:S(2)}) collective-permute-start(f32[136,128]{1,0:T(8,128)S(1)} %window.1.refs_11_), channel_id=1, source_target_pairs={{0,2},{1,3},{2,0},{3,1},{4,6},{5,7},{6,4},{7,5},{8,10},{9,11},{10,... | collective-permute-start | bytes 208904 | tf_op jit(solution)/shard_map/ppermute | solution.py:449
  29.6 4.3 %collective-permute-start.9 = (f32[136,128]{1,0:T(8,128)S(1)}, f32[136,128]{1,0:T(8,128)S(1)}, u32[]{:S(2)}, u32[]{:S(2)}) collective-permute-start(f32[136,128]{1,0:T(8,128)S(1)} %window.1.refs_11_), channel_id=1, source_target_pairs={{0,1},{1,0},{2,3},{3,2},{4,5},{5,4},{6,7},{7,6},{8,9},{9,8},{10,11... | collective-permute-start | bytes 208904 | tf_op jit(solution)/shard_map/ppermute | solution.py:449

commit v2 on v1

--- a/solution.py
+++ b/solution.py
@@ -15,13 +15,16 @@
 VMEM = pl.BlockSpec(memory_space=pltpu.VMEM)
 
 
-def call(kernel, outs, *args, scratch=(), name=None):
+HBM = pl.BlockSpec(memory_space=pltpu.HBM)
+
+
+def call(kernel, outs, *args, scratch=(), name=None, in_specs=None, out_specs=None):
     return pl.pallas_call(
         kernel,
         out_shape=[jax.ShapeDtypeStruct(s, F32) for s in outs],
-        in_specs=[VMEM] * len(args),
-        out_specs=[VMEM] * len(outs),
-        scratch_shapes=[pltpu.VMEM(s, F32) for s in scratch],
+        in_specs=in_specs or [VMEM] * len(args),
+        out_specs=out_specs or [VMEM] * len(outs),
+        scratch_shapes=[pltpu.VMEM(s, F32) if isinstance(s, tuple) else s for s in scratch],
         compiler_params=pltpu.CompilerParams(vmem_limit_bytes=16 << 20),
         name=name,
     )(*args)
@@ -135,16 +138,34 @@
         x, y = lax.axis_index("gx"), lax.axis_index("gy")
         return x, y, x % 2 == 0, y % 2 == 0
 
-    def set_up(source, reaction, kind, disk_id, disk_mask, thrust, f, g, d, absorb, core, chip, row, odd, table, y_low, y_high):
+    def set_up(
+        source_hbm, reaction_hbm, kind_hbm, id_hbm, mask_hbm, thrust_hbm,
+        f, g, d, absorb, core, chip, row, odd,
+        source, reaction, kind, disk_id, disk_mask, table, y_low, y_high, sems, table_sem,
+    ):
         _, _, x_even, y_even = where_am_i()
-        table[...] = jnp.zeros(table.shape, F32)
-        table[0:1, 0 : thrust.shape[1]] = thrust[...]
-        lookup = jnp.broadcast_to(table[0:1, :], (16, 128))
-
-        def group(k, carry):
+        moves = []
+        arrays = (
+            (source_hbm, source), (reaction_hbm, reaction), (kind_hbm, kind), (id_hbm, disk_id), (mask_hbm, disk_mask)
+        )
+        table_move = pltpu.make_async_copy(thrust_hbm, table, table_sem)
+        table_move.start()
+        for k in range(4):
+            part = pl.ds(4 * k, 4)
+            moves.append(
+                [pltpu.make_async_copy(a.at[part], b.at[part], sems.at[k, i]) for i, (a, b) in enumerate(arrays)]
+            )
+            for move in moves[k]:
+                move.start()
+        table_move.wait()
+        spare = jnp.zeros((1, 128 - table.shape[1]), F32)
+        lookup = jnp.broadcast_to(jnp.concatenate([table[...], spare], axis=1), (16, 128))
+
+        for k in range(4):
+            for move in moves[k]:
+                move.wait()
             total = jnp.zeros((16, 512), F32)
-            for q in range(4):
-                x = 4 * k + q
+            for x in range(4 * k, 4 * k + 4):
                 kinds = kind[x]
                 a = reaction[x] + jnp.where(kinds == 1, WALL_PENALTY, jnp.where(kinds == 2, INFLOW_PENALTY, 0.0))
                 total = total + a
@@ -162,12 +183,9 @@
                 f[x] = first
                 g[x] = scale
                 d[x] = diagonal
-                y_low[pl.ds(x, 1), :] = first[0:1, :]
-                y_high[pl.ds(x, 1), :] = first[15:16, :]
-            absorb[pl.ds(pl.multiple_of(16 * k, 16), 16), :] = total
-            return carry
-
-        lax.fori_loop(0, 4, group, 0)
+                y_low[x : x + 1, :] = first[0:1, :]
+                y_high[x : x + 1, :] = first[15:16, :]
+            absorb[16 * k : 16 * k + 16, :] = total
         near, far = jnp.where(x_even, 15, 0), jnp.where(x_even, 0, 15)
         put(core, 0, f[near])
         put(core, 64, g[near])
@@ -189,52 +207,38 @@
         high = jnp.where(y < ny - 1, jnp.where(y_even, a, b), 0.0)
         return low, high
 
-    def smooth(f, g, d, absorb, core, chip, row, odd, s, to_core, to_row, to_odd, block, F, lo, hi, S, V, y0, y1, y14, y15, g0, g15):
+    def smooth(f, g, d, absorb, core, chip, row, odd, s, to_core, to_row, to_odd, block, lo, hi, V, y0, y1, y14, y15, g0, g15):
         x_at, y_at, x_even, y_even = where_am_i()
         left, right = halo_x(core, chip, 0, x_at, x_even)
-        F[0], F[17] = left, right
         lo[...], hi[...] = halo_y(row, odd, 0, y_at, y_even)
-        zero = jnp.zeros((16, 512), F32)
-        S[0], S[17] = zero, zero
-
-        def fill(x, carry):
-            F[x + 1] = f[x]
-            return carry
-
-        lax.fori_loop(0, 16, fill, 0)
-
-        def sweep(x, carry):
-            here = F[x + 1]
+        for x in range(16):
+            here = f[x]
             scale = g[x]
-            total = F[x] + F[x + 2] + beside_rows(here, lo[pl.ds(x, 1), :], hi[pl.ds(x, 1), :]) + beside_z(here)
+            total = (f[x - 1] if x > 0 else left) + (f[x + 1] if x < 15 else right)
+            total = total + beside_rows(here, lo[x : x + 1, :], hi[x : x + 1, :]) + beside_z(here)
             value = 1.2 * here + scale * total
-            S[x + 1] = value
             s[x] = value
-            y0[pl.ds(x, 1), :] = value[0:1, :]
-            y1[pl.ds(x, 1), :] = value[1:2, :]
-            y14[pl.ds(x, 1), :] = value[14:15, :]
-            y15[pl.ds(x, 1), :] = value[15:16, :]
-            g0[pl.ds(x, 1), :] = scale[0:1, :]
-            g15[pl.ds(x, 1), :] = scale[15:16, :]
-            return carry
-
-        lax.fori_loop(0, 16, sweep, 0)
+            y0[x : x + 1, :] = value[0:1, :]
+            y1[x : x + 1, :] = value[1:2, :]
+            y14[x : x + 1, :] = value[14:15, :]
+            y15[x : x + 1, :] = value[15:16, :]
+            g0[x : x + 1, :] = scale[0:1, :]
+            g15[x : x + 1, :] = scale[15:16, :]
         nothing = jnp.zeros((1, 512), F32)
-
-        def residual(k, carry):
+        for k in range(4):
             total = jnp.zeros((16, 512), F32)
-            for q in range(4):
-                x = 4 * k + q
-                here = S[x + 1]
-                total = total + d[x] * (1.25 * F[x + 1] - here) + S[x] + S[x + 2]
+            for x in range(4 * k, 4 * k + 4):
+                here = s[x]
+                total = total + d[x] * (1.25 * f[x] - here)
                 total = total + beside_rows(here, nothing, nothing) + beside_z(here)
-            V[pl.ds(pl.multiple_of(16 * k, 16), 16), :] = total
-            return carry
-
-        lax.fori_loop(0, 4, residual, 0)
+                if x > 0:
+                    total = total + s[x - 1]
+                if x < 15:
+                    total = total + s[x + 1]
+            V[16 * k : 16 * k + 16, :] = total
         V[64:128, :] = absorb[...]
-        V[128:144, :] = S[1]
-        V[144:160, :] = S[16]
+        V[128:144, :] = s[0]
+        V[144:160, :] = s[15]
         V[160:176, :] = y0[...]
         V[176:192, :] = y15[...]
         out, src = iota((48, 192), 0), iota((48, 192), 1)
@@ -244,10 +248,8 @@
         faces = (out >= 32) & (src >= 128) & ((out - 32) // 4 == (src - 128) // 16) & ((src % 16) // 4 == cx)
         picked = dot((bulk | faces).astype(F32), V[...])
         block[...] = dot(picked, group_lanes(512))
-        near = jnp.where(x_even, 16, 1)
-        inner = jnp.where(x_even, 15, 2)
-        put(to_core, 0, S[near])
-        put(to_core, 64, S[inner])
+        put(to_core, 0, s[jnp.where(x_even, 15, 0)])
+        put(to_core, 64, s[jnp.where(x_even, 14, 1)])
         to_core[128:132, :] = jnp.where(x_even, block[36:40, :], block[32:36, :])
         to_core[132:136, :] = jnp.zeros((4, 128), F32)
         for at, (low, high) in enumerate(((y0, y15), (y1, y14), (g0, g15))):
@@ -306,7 +308,7 @@
         f, g, s, a_core, a_chip, a_row, a_odd, s_core, s_chip, s_row, s_odd = refs[:11]
         windows = refs[11 : 11 + ny]
         pressure, coarse = refs[11 + ny : 13 + ny]
-        every, res, diag, inv, one, two, sol, Pc, T, U, yl, yh, tl, th, ul, uh = refs[13 + ny :]
+        every, res, diag, inv, one, two, sol, Pc, T, U, yl, yh, tl, th, ul, uh, result, sems = refs[13 + ny :]
         x_at, y_at, x_even, y_even = where_am_i()
         for step, window in enumerate(windows):
             every[jnp.bitwise_xor(y_at, step)] = window[...]
@@ -348,9 +350,9 @@
             factor_next = 1.0 / (2.0 * aspect - factor)
             keep, gain = factor_next * factor, 2.0 * factor_next / half_range
 
-            def step(plane, carry, now=now, later=later, keep=keep, gain=gain):
+            lane = iota((16, 128), 1)
+            for plane in range(planes):
                 here = now[plane + 1]
-                lane = iota((16, 128), 1)
                 total = now[plane] + now[plane + 2]
                 total = total + pltpu.roll(here, 15, 0) + pltpu.roll(here, 1, 0)
                 total = total + jnp.where(lane == 127, 0.0, pltpu.roll(here, 127, 1))
@@ -360,9 +362,6 @@
                 direction = keep * here + gain * inv[plane] * residual
                 later[plane + 1] = direction
                 sol[plane + 1] = sol[plane + 1] + direction
-                return carry
-
-            lax.fori_loop(0, planes, step, 0)
             now, later = later, now
             factor = factor_next
         for plane in range(planes):
@@ -377,11 +376,8 @@
         T[0], T[1] = s_left2 + Pc[0], s_left + Pc[0]
         T[18], T[19] = s_right + Pc[5], s_right2 + Pc[5]
 
-        def third(x, carry):
+        for x in range(16):
             T[x + 2] = s[x] + Pc[x // 4 + 1]
-            return carry
-
-        lax.fori_loop(0, 16, third, 0)
         below, above = first_plane - 1, first_plane + 4
         y1_low, y1_high = halo_y(s_row, s_odd, 0, y_at, y_even)
         y2_low, y2_high = halo_y(s_row, s_odd, 64, y_at, y_even)
@@ -409,20 +405,17 @@
         def fourth_at(at, forcing, scale):
             here = T[at + 1]
             total = T[at] + T[at + 2] + beside_z(here)
-            total = total + beside_rows(here, tl[pl.ds(at + 7, 1), :], th[pl.ds(at + 7, 1), :])
+            total = total + beside_rows(here, tl[at + 7 : at + 8, :], th[at + 7 : at + 8, :])
             return 0.2 * here + forcing + scale * total
 
         U[0] = fourth_at(0, f_left, g_left)
         U[17] = fourth_at(17, f_right, g_right)
 
-        def fourth(x, carry):
+        for x in range(16):
             U[x + 1] = fourth_at(x + 1, f[x], g[x])
             here = T[x + 2]
-            yl[pl.ds(x, 1), :] = here[0:1, :]
-            yh[pl.ds(x, 1), :] = here[15:16, :]
-            return carry
-
-        lax.fori_loop(0, 16, fourth, 0)
+            yl[x : x + 1, :] = here[0:1, :]
+            yh[x : x + 1, :] = here[15:16, :]
         for ref, out, edge, far, forcing, scale in (
             (tl, ul, yl, outer["low"], f_low, g_low),
             (th, uh, yh, outer["high"], f_high, g_high),
@@ -431,14 +424,18 @@
             total = far + edge[...] + ref[7:23, :] + ref[9:25, :] + beside_z(here)
             out[...] = 0.2 * here + forcing + scale * total
 
-        def fifth(x, carry):
+        moves = []
+        for x in range(16):
             here = U[x + 1]
             total = U[x] + U[x + 2] + beside_z(here)
-            total = total + beside_rows(here, ul[pl.ds(x, 1), :], uh[pl.ds(x, 1), :])
-            pressure[x] = 0.2 * here + f[x] + g[x] * total
-            return carry
-
-        lax.fori_loop(0, 16, fifth, 0)
+            total = total + beside_rows(here, ul[x : x + 1, :], uh[x : x + 1, :])
+            result[x] = 0.2 * here + f[x] + g[x] * total
+            if x % 4 == 3:
+                part = pl.ds(x - 3, 4)
+                moves.append(pltpu.make_async_copy(result.at[part], pressure.at[part], sems.at[x // 4]))
+                moves[-1].start()
+        for move in moves:
+            move.wait()
 
     slab, field, long = (16, 512), (16, 16, 512), (18, 16, 512)
     core_pairs, chip_pairs = pairs_core(nx, ny), pairs_chip(nx, ny)
@@ -453,7 +450,10 @@
             set_up,
             [field, field, field, (64, 512), (128, 128), (128, 128), (64, 128), (64, 128)],
             source, reaction, boundary_kind, disk_id, disk_mask, thrust.reshape(1, -1),
-            scratch=[(8, 128), slab, slab],
+            in_specs=[HBM] * 6,
+            scratch=[field, field]
+            + [pltpu.VMEM(field, jnp.int32)] * 3
+            + [(1, thrust.shape[0]), slab, slab, pltpu.SemaphoreType.DMA((4, 5)), pltpu.SemaphoreType.DMA(())],
             name="set_up",
         )
         a_row, a_odd = swap(row, row_pairs[0]), swap(odd, odd_pairs)
@@ -462,7 +462,7 @@
             smooth,
             [field, (136, 128), (192, 128), (192, 128), (48, 128)],
             f, g, d, absorb, a_core, a_chip, a_row, a_odd,
-            scratch=[long, slab, slab, long, (192, 512), slab, slab, slab, slab, slab, slab],
+            scratch=[slab, slab, (192, 512), slab, slab, slab, slab, slab, slab],
             name="smooth",
         )
         s_core = swap(to_core, core_pairs)
@@ -480,7 +480,9 @@
             scratch=[(ny, 136, 128)]
             + [(planes, 16, 128)] * 3
             + [(planes + 2, 16, 128)] * 3
-            + [(6, 16, 512), (20, 16, 512), long, slab, slab, (32, 512), (32, 512), slab, slab],
+            + [(6, 16, 512), (20, 16, 512), long, slab, slab, (32, 512), (32, 512), slab, slab, field]
+            + [pltpu.SemaphoreType.DMA((4,))],
+            out_specs=[HBM, VMEM],
             name="finish",
         )
         return pressure, coarse

time: 42.6 us -> 39.3 us (0.923)
  Pallas kernels: 11.8 us -> 8.57 us
    pallas_call x6, Pallas kernels: 11.8 us -> 8.57 us  [call(): pl.pallas_call(kernel, out_shape=[jax.ShapeDtypeStruct(s, F32) for s in o...]
where the time goes in v2:
time: 39.3 us; the launch traced here: 38.9 us
  starting transfers between devices  14.2 us (36%)
  waiting for transfers between devices  9.64 us (25%)
  Pallas kernels  8.57 us (22%)
  local copies, waits for them, and re-layouts  5.85 us (15%)
  between operations  0.68 us (2%)
    ppermute x12, starting transfers between devices, swap(): return lax.ppermute(array, axes, pairs)  14.2 us
    ppermute x12, waiting for transfers between devices, swap(): return lax.ppermute(array, axes, pairs)  9.64 us
    pallas_call x6, Pallas kernels, call(): pl.pallas_call(kernel, out_shape=[jax.ShapeDtypeStruct(s, F32) for s in o...  8.57 us
    unnamed x12, local copies, waits for them, and re-layouts  5.85 us
  transfers between devices with their start and end apart: 12, of which 8 were waited for; matrix products, arithmetic and copies ran while one was open for 0% of the time, Pallas kernels for 0%

profile of v2, /device:TPU:0, one launch (start us, length us, event | category | flops | bytes accessed | tf_op | source)
XLA Modules:
  0.0 38.9 jit_solution(7147351429710423816)
XLA Ops:
  0.6 0.6 %copy-done.5 = f32[120]{0:T(128)S(1)} copy-done((f32[120]{0:T(128)S(1)}, f32[120]{0:T(128)}, u32[]{:S(2)}) %copy-start.5) | copy-done | bytes 504
  1.3 1.0 %copy-done = f32[16,16,512]{2,1,0:T(8,128)S(1)} copy-done((f32[16,16,512]{2,1,0:T(8,128)S(1)}, f32[16,16,512]{2,1,0:T(8,128)}, u32[]{:S(2)}) %copy-start) | copy-done | bytes 524312
  2.3 1.0 %copy-done.1 = f32[16,16,512]{2,1,0:T(8,128)S(1)} copy-done((f32[16,16,512]{2,1,0:T(8,128)S(1)}, f32[16,16,512]{2,1,0:T(8,128)}, u32[]{:S(2)}) %copy-start.1) | copy-done | bytes 524312
  3.4 1.0 %copy-done.2 = s32[16,16,512]{2,1,0:T(8,128)S(1)} copy-done((s32[16,16,512]{2,1,0:T(8,128)S(1)}, s32[16,16,512]{2,1,0:T(8,128)}, u32[]{:S(2)}) %copy-start.2) | copy-done | bytes 524312
  4.4 1.0 %copy-done.3 = s32[16,16,512]{2,1,0:T(8,128)S(1)} copy-done((s32[16,16,512]{2,1,0:T(8,128)S(1)}, s32[16,16,512]{2,1,0:T(8,128)}, u32[]{:S(2)}) %copy-start.3) | copy-done | bytes 524312
  5.5 1.0 %copy-done.4 = s32[16,16,512]{2,1,0:T(8,128)S(1)} copy-done((s32[16,16,512]{2,1,0:T(8,128)S(1)}, s32[16,16,512]{2,1,0:T(8,128)}, u32[]{:S(2)}) %copy-start.4) | copy-done | bytes 524312
  6.5 4.3 %set_up.1 = (f32[16,16,512]{2,1,0:T(8,128)S(1)}, f32[16,16,512]{2,1,0:T(8,128)S(1)}, f32[16,16,512]{2,1,0:T(8,128)S(1)}, f32[64,512]{1,0:T(8,128)S(1)}, f32[128,...) custom-call(f32[16,16,512]{2,1,0:T(8,128)S(1)} %copy-done, ...), custom_call_target="tpu_custom_call" | custom-call | tf_op jit(solution)/shard_map/set_up/pallas_call | solution.py:22
  10.8 0.5 %collective-permute-start = (f32[128,128]{1,0:T(8,128)S(1)}, f32[128,128]{1,0:T(8,128)S(1)}, u32[]{:S(2)}, u32[]{:S(2)}) collective-permute-start(f32[128,128]{1,0:T(8,128)S(1)} %get-tuple-element.23), channel_id=1, source_target_pairs={{0,4},{1,5},{2,6},{3,7},{4,0},{5,1},{6,2},{7,3},{8,12},{9,13},{10,... | collective-permute-start | bytes 196616 | tf_op jit(solution)/shard_map/ppermute | solution.py:446
  11.3 2.6 %collective-permute-start.1 = (f32[128,128]{1,0:T(8,128)S(1)}, f32[128,128]{1,0:T(8,128)S(1)}, u32[]{:S(2)}, u32[]{:S(2)}) collective-permute-start(f32[128,128]{1,0:T(8,128)S(1)} %get-tuple-element.24), channel_id=1, source_target_pairs={{0,1},{1,0},{2,3},{3,2},{4,8},{5,9},{6,10},{7,11},{8,4},{9,5},{10,... | collective-permute-start | bytes 196616 | tf_op jit(solution)/shard_map/ppermute | solution.py:446
  13.9 2.9 %collective-permute-start.3 = (f32[64,128]{1,0:T(8,128)S(1)}, f32[64,128]{1,0:T(8,128)S(1)}, u32[]{:S(2)}, u32[]{:S(2)}) collective-permute-start(f32[64,128]{1,0:T(8,128)S(1)} %get-tuple-element.26), channel_id=1, source_target_pairs={{0,3},{1,2},{2,1},{3,0},{4,7},{5,6},{6,5},{7,4},{8,11},{9,10},{10,... | collective-permute-start | bytes 98312 | tf_op jit(solution)/shard_map/ppermute | solution.py:446
  16.8 0.9 %collective-permute-done.2.row.refs_5_ = f32[64,128]{1,0:T(8,128)S(1)} collective-permute-done((f32[64,128]{1,0:T(8,128)S(1)}, f32[64,128]{1,0:T(8,128)S(1)}, u32[]{:S(2)}, u32[]{:S(2)}) %collective-permute-start.2) | collective-permute-done | bytes 32800 | tf_op jit(solution)/shard_map/ppermute | solution.py:446
  17.8 1.7 %collective-permute-done.3.odd.refs_6_ = f32[64,128]{1,0:T(8,128)S(1)} collective-permute-done((f32[64,128]{1,0:T(8,128)S(1)}, f32[64,128]{1,0:T(8,128)S(1)}, u32[]{:S(2)}, u32[]{:S(2)}) %collective-permute-start.3) | collective-permute-done | bytes 32800 | tf_op jit(solution)/shard_map/ppermute | solution.py:446
  19.4 1.3 %smooth.1 = (f32[16,16,512]{2,1,0:T(8,128)S(1)}, f32[136,128]{1,0:T(8,128)S(1)}, f32[192,128]{1,0:T(8,128)S(1)}, f32[192,128]{1,0:T(8,128)S(1)}, f32[48,128]{1,0:T(8,128)S(1)}) custom-call(f32[16,16,512]{2,1,0:T(8,128)S(1)} %get-tuple-element.19.f.refs_0_, f32[16,16,512]{2,1,0:T(8,128)S(1)} %get-tuple-element.20.g.refs_1_, ...), custom_call_target="tpu_custom_call" | custom-call | tf_op jit(solution)/shard_map/smooth/pallas_call | solution.py:22
  20.9 1.2 %collective-permute-done.4.core.s_core.refs_7_ = f32[136,128]{1,0:T(8,128)S(1)} collective-permute-done((f32[136,128]{1,0:T(8,128)S(1)}, f32[136,128]{1,0:T(8,128)S(1)}, u32[]{:S(2)}, u32[]{:S(2)}) %collective-permute-start.4) | collective-permute-done | bytes 69664 | tf_op jit(solution)/shard_map/ppermute | solution.py:446
  22.1 1.3 %collective-permute-start.5 = (f32[176,128]{1,0:T(8,128)S(1)}, f32[176,128]{1,0:T(8,128)S(1)}, u32[]{:S(2)}, u32[]{:S(2)}) collective-permute-start(f32[176,128]{1,0:T(8,128)S(1)} %get-tuple-element.30), channel_id=1, source_target_pairs={{0,1},{1,0},{2,3},{3,2},{4,8},{5,9},{6,10},{7,11},{8,4},{9,5},{10,... | collective-permute-start | bytes 270344 | tf_op jit(solution)/shard_map/ppermute | solution.py:446
  23.4 0.8 %collective-permute-start.6 = (f32[192,128]{1,0:T(8,128)S(1)}, f32[192,128]{1,0:T(8,128)S(1)}, u32[]{:S(2)}, u32[]{:S(2)}) collective-permute-start(f32[192,128]{1,0:T(8,128)S(1)} %get-tuple-element.31), channel_id=1, source_target_pairs={{0,1},{1,0},{2,3},{3,2},{4,5},{5,4},{6,7},{7,6},{8,9},{9,8},{10,11... | collective-permute-start | bytes 294920 | tf_op jit(solution)/shard_map/ppermute | solution.py:446
  24.2 2.2 %collective-permute-start.7 = (f32[192,128]{1,0:T(8,128)S(1)}, f32[192,128]{1,0:T(8,128)S(1)}, u32[]{:S(2)}, u32[]{:S(2)}) collective-permute-start(f32[192,128]{1,0:T(8,128)S(1)} %get-tuple-element.32), channel_id=1, source_target_pairs={{0,3},{1,2},{2,1},{3,0},{4,7},{5,6},{6,5},{7,4},{8,11},{9,10},{10,... | collective-permute-start | bytes 294920 | tf_op jit(solution)/shard_map/ppermute | solution.py:446
  26.4 0.5 %collective-permute-done.5.chip.refs_8_ = f32[176,128]{1,0:T(8,128)S(1)} collective-permute-done((f32[176,128]{1,0:T(8,128)S(1)}, f32[176,128]{1,0:T(8,128)S(1)}, u32[]{:S(2)}, u32[]{:S(2)}) %collective-permute-start.5) | collective-permute-done | bytes 90144 | tf_op jit(solution)/shard_map/ppermute | solution.py:446
  27.0 1.2 %collective-permute-done.8.core = f32[40,128]{1,0:T(8,128)S(1)} collective-permute-done((f32[40,128]{1,0:T(8,128)S(1)}, f32[40,128]{1,0:T(8,128)S(1)}, u32[]{:S(2)}, u32[]{:S(2)}) %collective-permute-start.8) | collective-permute-done | bytes 20512 | tf_op jit(solution)/shard_map/ppermute | solution.py:446
  28.2 3.0 %collective-permute-start.11 = (f32[136,128]{1,0:T(8,128)S(1)}, f32[136,128]{1,0:T(8,128)S(1)}, u32[]{:S(2)}, u32[]{:S(2)}) collective-permute-start(f32[136,128]{1,0:T(8,128)S(1)} %window.1.refs_11_), channel_id=1, source_target_pairs={{0,3},{1,2},{2,1},{3,0},{4,7},{5,6},{6,5},{7,4},{8,11},{9,10},{10,... | collective-permute-start | bytes 208904 | tf_op jit(solution)/shard_map/ppermute | solution.py:446
  31.2 0.5 %collective-permute-start.10 = (f32[136,128]{1,0:T(8,128)S(1)}, f32[136,128]{1,0:T(8,128)S(1)}, u32[]{:S(2)}, u32[]{:S(2)}) collective-permute-start(f32[136,128]{1,0:T(8,128)S(1)} %window.1.refs_11_), channel_id=1, source_target_pairs={{0,2},{1,3},{2,0},{3,1},{4,6},{5,7},{6,4},{7,5},{8,10},{9,11},{10,... | collective-permute-start | bytes 208904 | tf_op jit(solution)/shard_map/ppermute | solution.py:446
  31.9 1.9 %collective-permute-done.11.refs_14_ = f32[136,128]{1,0:T(8,128)S(1)} collective-permute-done((f32[136,128]{1,0:T(8,128)S(1)}, f32[136,128]{1,0:T(8,128)S(1)}, u32[]{:S(2)}, u32[]{:S(2)}) %collective-permute-start.11) | collective-permute-done | bytes 69664 | tf_op jit(solution)/shard_map/ppermute | solution.py:446
  33.8 1.8 %collective-permute-done.10.refs_13_ = f32[136,128]{1,0:T(8,128)S(1)} collective-permute-done((f32[136,128]{1,0:T(8,128)S(1)}, f32[136,128]{1,0:T(8,128)S(1)}, u32[]{:S(2)}, u32[]{:S(2)}) %collective-permute-start.10) | collective-permute-done | bytes 69664 | tf_op jit(solution)/shard_map/ppermute | solution.py:446
  36.0 2.9 %finish.1 = (f32[16,16,512]{2,1,0:T(8,128)}, f32[4,16,128]{2,1,0:T(8,128)}) custom-call(f32[16,16,512]{2,1,0:T(8,128)S(1)} %get-tuple-element.19.f.refs_0_, f32[16,16,512]{2,1,0:T(8,128)S(1)} %get-tuple-element.20.g.refs_1_, f32[16,16,512]{2,1,0:T(8,128)S(1)} %get-tuple-element.27.s.refs_2_, f32[128,128]{1,0:T(8,128)S(1)} %collective-permute-done.core.refs_3_, ...), custom_call_target="tpu_custom_call" | custom-call | tf_op jit(solution)/shard_map/finish/pallas_call | solution.py:22
  (18 shorter events, 1.0 us)
Async XLA Ops:
  0.6 0.7 %copy-start.5 = (f32[120]{0:T(128)S(1)}, f32[120]{0:T(128)}, u32[]{:S(2)}) copy-start(f32[120]{0:T(128)} %param.11) | copy-start | bytes 1444
  1.3 1.0 %copy-start = (f32[16,16,512]{2,1,0:T(8,128)S(1)}, f32[16,16,512]{2,1,0:T(8,128)}, u32[]{:S(2)}) copy-start(f32[16,16,512]{2,1,0:T(8,128)} %source_hbm.1) | copy-start | bytes 1572868
  2.3 1.0 %copy-start.1 = (f32[16,16,512]{2,1,0:T(8,128)S(1)}, f32[16,16,512]{2,1,0:T(8,128)}, u32[]{:S(2)}) copy-start(f32[16,16,512]{2,1,0:T(8,128)} %reaction_hbm.1) | copy-start | bytes 1572868
  3.4 1.0 %copy-start.2 = (s32[16,16,512]{2,1,0:T(8,128)S(1)}, s32[16,16,512]{2,1,0:T(8,128)}, u32[]{:S(2)}) copy-start(s32[16,16,512]{2,1,0:T(8,128)} %kind_hbm.1) | copy-start | bytes 1572868
  4.4 1.0 %copy-start.3 = (s32[16,16,512]{2,1,0:T(8,128)S(1)}, s32[16,16,512]{2,1,0:T(8,128)}, u32[]{:S(2)}) copy-start(s32[16,16,512]{2,1,0:T(8,128)} %id_hbm.1) | copy-start | bytes 1572868
  5.5 1.0 %copy-start.4 = (s32[16,16,512]{2,1,0:T(8,128)S(1)}, s32[16,16,512]{2,1,0:T(8,128)}, u32[]{:S(2)}) copy-start(s32[16,16,512]{2,1,0:T(8,128)} %mask_hbm.1) | copy-start | bytes 1572868
  10.8 8.7 %collective-permute-start = (f32[128,128]{1,0:T(8,128)S(1)}, f32[128,128]{1,0:T(8,128)S(1)}, u32[]{:S(2)}, u32[]{:S(2)}) collective-permute-start(f32[128,128]{1,0:T(8,128)S(1)} %get-tuple-element.23), channel_id=1, source_target_pairs={{0,4},{1,5},{2,6},{3,7},{4,0},{5,1},{6,2},{7,3},{8,12},{9,13},{10,... | collective-permute-start | bytes 196616 | tf_op jit(solution)/shard_map/ppermute | solution.py:446
  11.3 8.1 %collective-permute-start.1 = (f32[128,128]{1,0:T(8,128)S(1)}, f32[128,128]{1,0:T(8,128)S(1)}, u32[]{:S(2)}, u32[]{:S(2)}) collective-permute-start(f32[128,128]{1,0:T(8,128)S(1)} %get-tuple-element.24), channel_id=1, source_target_pairs={{0,1},{1,0},{2,3},{3,2},{4,8},{5,9},{6,10},{7,11},{8,4},{9,5},{10,... | collective-permute-start | bytes 196616 | tf_op jit(solution)/shard_map/ppermute | solution.py:446
  13.8 3.9 %collective-permute-start.2 = (f32[64,128]{1,0:T(8,128)S(1)}, f32[64,128]{1,0:T(8,128)S(1)}, u32[]{:S(2)}, u32[]{:S(2)}) collective-permute-start(f32[64,128]{1,0:T(8,128)S(1)} %get-tuple-element.25), channel_id=1, source_target_pairs={{0,1},{1,0},{2,3},{3,2},{4,5},{5,4},{6,7},{7,6},{8,9},{9,8},{10,11... | collective-permute-start | bytes 98312 | tf_op jit(solution)/shard_map/ppermute | solution.py:446
  13.9 5.5 %collective-permute-start.3 = (f32[64,128]{1,0:T(8,128)S(1)}, f32[64,128]{1,0:T(8,128)S(1)}, u32[]{:S(2)}, u32[]{:S(2)}) collective-permute-start(f32[64,128]{1,0:T(8,128)S(1)} %get-tuple-element.26), channel_id=1, source_target_pairs={{0,3},{1,2},{2,1},{3,0},{4,7},{5,6},{6,5},{7,4},{8,11},{9,10},{10,... | collective-permute-start | bytes 98312 | tf_op jit(solution)/shard_map/ppermute | solution.py:446
  20.8 1.3 %collective-permute-start.4 = (f32[136,128]{1,0:T(8,128)S(1)}, f32[136,128]{1,0:T(8,128)S(1)}, u32[]{:S(2)}, u32[]{:S(2)}) collective-permute-start(f32[136,128]{1,0:T(8,128)S(1)} %get-tuple-element.28), channel_id=1, source_target_pairs={{0,4},{1,5},{2,6},{3,7},{4,0},{5,1},{6,2},{7,3},{8,12},{9,13},{10,... | collective-permute-start | bytes 208904 | tf_op jit(solution)/shard_map/ppermute | solution.py:446
  22.1 4.8 %collective-permute-start.5 = (f32[176,128]{1,0:T(8,128)S(1)}, f32[176,128]{1,0:T(8,128)S(1)}, u32[]{:S(2)}, u32[]{:S(2)}) collective-permute-start(f32[176,128]{1,0:T(8,128)S(1)} %get-tuple-element.30), channel_id=1, source_target_pairs={{0,1},{1,0},{2,3},{3,2},{4,8},{5,9},{6,10},{7,11},{8,4},{9,5},{10,... | collective-permute-start | bytes 270344 | tf_op jit(solution)/shard_map/ppermute | solution.py:446
  23.4 8.4 %collective-permute-start.6 = (f32[192,128]{1,0:T(8,128)S(1)}, f32[192,128]{1,0:T(8,128)S(1)}, u32[]{:S(2)}, u32[]{:S(2)}) collective-permute-start(f32[192,128]{1,0:T(8,128)S(1)} %get-tuple-element.31), channel_id=1, source_target_pairs={{0,1},{1,0},{2,3},{3,2},{4,5},{5,4},{6,7},{7,6},{8,9},{9,8},{10,11... | collective-permute-start | bytes 294920 | tf_op jit(solution)/shard_map/ppermute | solution.py:446
  24.2 7.7 %collective-permute-start.7 = (f32[192,128]{1,0:T(8,128)S(1)}, f32[192,128]{1,0:T(8,128)S(1)}, u32[]{:S(2)}, u32[]{:S(2)}) collective-permute-start(f32[192,128]{1,0:T(8,128)S(1)} %get-tuple-element.32), channel_id=1, source_target_pairs={{0,3},{1,2},{2,1},{3,0},{4,7},{5,6},{6,5},{7,4},{8,11},{9,10},{10,... | collective-permute-start | bytes 294920 | tf_op jit(solution)/shard_map/ppermute | solution.py:446
  27.0 1.3 %collective-permute-start.8 = (f32[40,128]{1,0:T(8,128)S(1)}, f32[40,128]{1,0:T(8,128)S(1)}, u32[]{:S(2)}, u32[]{:S(2)}) collective-permute-start(f32[40,128]{1,0:T(8,128)S(1)} %get-tuple-element.34.full), channel_id=1, source_target_pairs={{0,4},{1,5},{2,6},{3,7},{4,0},{5,1},{6,2},{7,3},{8,12},{9,13},{10,... | collective-permute-start | bytes 61448 | tf_op jit(solution)/shard_map/ppermute | solution.py:446
  28.2 5.5 %collective-permute-start.11 = (f32[136,128]{1,0:T(8,128)S(1)}, f32[136,128]{1,0:T(8,128)S(1)}, u32[]{:S(2)}, u32[]{:S(2)}) collective-permute-start(f32[136,128]{1,0:T(8,128)S(1)} %window.1.refs_11_), channel_id=1, source_target_pairs={{0,3},{1,2},{2,1},{3,0},{4,7},{5,6},{6,5},{7,4},{8,11},{9,10},{10,... | collective-permute-start | bytes 208904 | tf_op jit(solution)/shard_map/ppermute | solution.py:446
  31.2 4.3 %collective-permute-start.10 = (f32[136,128]{1,0:T(8,128)S(1)}, f32[136,128]{1,0:T(8,128)S(1)}, u32[]{:S(2)}, u32[]{:S(2)}) collective-permute-start(f32[136,128]{1,0:T(8,128)S(1)} %window.1.refs_11_), channel_id=1, source_target_pairs={{0,2},{1,3},{2,0},{3,1},{4,6},{5,7},{6,4},{7,5},{8,10},{9,11},{10,... | collective-permute-start | bytes 208904 | tf_op jit(solution)/shard_map/ppermute | solution.py:446
  31.7 4.3 %collective-permute-start.9 = (f32[136,128]{1,0:T(8,128)S(1)}, f32[136,128]{1,0:T(8,128)S(1)}, u32[]{:S(2)}, u32[]{:S(2)}) collective-permute-start(f32[136,128]{1,0:T(8,128)S(1)} %window.1.refs_11_), channel_id=1, source_target_pairs={{0,1},{1,0},{2,3},{3,2},{4,5},{5,4},{6,7},{7,6},{8,9},{9,8},{10,11... | collective-permute-start | bytes 208904 | tf_op jit(solution)/shard_map/ppermute | solution.py:446

commit v3 on v2

--- a/solution.py
+++ b/solution.py
@@ -449,7 +449,10 @@
         f, g, d, absorb, core, chip, row, odd = call(
             set_up,
             [field, field, field, (64, 512), (128, 128), (128, 128), (64, 128), (64, 128)],
-            source, reaction, boundary_kind, disk_id, disk_mask, thrust.reshape(1, -1),
+            *(
+                pltpu.with_memory_space_constraint(array, pltpu.HBM)
+                for array in (source, reaction, boundary_kind, disk_id, disk_mask, thrust.reshape(1, -1))
+            ),
             in_specs=[HBM] * 6,
             scratch=[field, field]
             + [pltpu.VMEM(field, jnp.int32)] * 3

time: 39.3 us -> 31.4 us (0.80)
  local copies, waits for them, and re-layouts: 5.85 us -> 0 us
  Pallas kernels: 8.57 us -> 6.72 us
    unnamed x12 -> x0, local copies, waits for them, and re-layouts: 5.85 us -> none
    pallas_call x6, Pallas kernels: 8.57 us -> 6.72 us  [call(): pl.pallas_call(kernel, out_shape=[jax.ShapeDtypeStruct(s, F32) for s in o...]
where the time goes in v3:
time: 31.4 us; the launch traced here: 31.2 us
  starting transfers between devices  14.2 us (45%)
  waiting for transfers between devices  9.64 us (31%)
  Pallas kernels  6.72 us (21%)
  between operations  0.67 us (2%)
    ppermute x12, starting transfers between devices, swap(): return lax.ppermute(array, axes, pairs)  14.2 us
    ppermute x12, waiting for transfers between devices, swap(): return lax.ppermute(array, axes, pairs)  9.64 us
    pallas_call x6, Pallas kernels, call(): pl.pallas_call(kernel, out_shape=[jax.ShapeDtypeStruct(s, F32) for s in o...  6.72 us
  transfers between devices with their start and end apart: 12, of which 8 were waited for; matrix products, arithmetic and copies ran while one was open for 0% of the time, Pallas kernels for 0%

profile of v3, /device:TPU:0, one launch (start us, length us, event | category | flops | bytes accessed | tf_op | source)
XLA Modules:
  0.0 31.2 jit_solution(2053812545242952495)
XLA Ops:
  0.6 2.4 %set_up.1 = (f32[16,16,512]{2,1,0:T(8,128)S(1)}, f32[16,16,512]{2,1,0:T(8,128)S(1)}, f32[16,16,512]{2,1,0:T(8,128)S(1)}, f32[64,512]{1,0:T(8,128)S(1)}, f32[128,...) custom-call(f32[16,16,512]{2,1,0:T(8,128)} %source_hbm.1, ...), custom_call_target="tpu_custom_call" | custom-call | tf_op jit(solution)/shard_map/set_up/pallas_call | solution.py:22
  3.0 0.5 %collective-permute-start = (f32[128,128]{1,0:T(8,128)S(1)}, f32[128,128]{1,0:T(8,128)S(1)}, u32[]{:S(2)}, u32[]{:S(2)}) collective-permute-start(f32[128,128]{1,0:T(8,128)S(1)} %get-tuple-element.23), channel_id=1, source_target_pairs={{0,4},{1,5},{2,6},{3,7},{4,0},{5,1},{6,2},{7,3},{8,12},{9,13},{10,... | collective-permute-start | bytes 196616 | tf_op jit(solution)/shard_map/ppermute | solution.py:446
  3.5 2.6 %collective-permute-start.1 = (f32[128,128]{1,0:T(8,128)S(1)}, f32[128,128]{1,0:T(8,128)S(1)}, u32[]{:S(2)}, u32[]{:S(2)}) collective-permute-start(f32[128,128]{1,0:T(8,128)S(1)} %get-tuple-element.24), channel_id=1, source_target_pairs={{0,1},{1,0},{2,3},{3,2},{4,8},{5,9},{6,10},{7,11},{8,4},{9,5},{10,... | collective-permute-start | bytes 196616 | tf_op jit(solution)/shard_map/ppermute | solution.py:446
  6.1 0.1 collective-permute-start.2
  6.2 2.9 %collective-permute-start.3 = (f32[64,128]{1,0:T(8,128)S(1)}, f32[64,128]{1,0:T(8,128)S(1)}, u32[]{:S(2)}, u32[]{:S(2)}) collective-permute-start(f32[64,128]{1,0:T(8,128)S(1)} %get-tuple-element.26), channel_id=1, source_target_pairs={{0,3},{1,2},{2,1},{3,0},{4,7},{5,6},{6,5},{7,4},{8,11},{9,10},{10,... | collective-permute-start | bytes 98312 | tf_op jit(solution)/shard_map/ppermute | solution.py:446
  9.1 0.9 %collective-permute-done.2.row.refs_5_ = f32[64,128]{1,0:T(8,128)S(1)} collective-permute-done((f32[64,128]{1,0:T(8,128)S(1)}, f32[64,128]{1,0:T(8,128)S(1)}, u32[]{:S(2)}, u32[]{:S(2)}) %collective-permute-start.2) | collective-permute-done | bytes 32800 | tf_op jit(solution)/shard_map/ppermute | solution.py:446
  10.0 1.7 %collective-permute-done.3.odd.refs_6_ = f32[64,128]{1,0:T(8,128)S(1)} collective-permute-done((f32[64,128]{1,0:T(8,128)S(1)}, f32[64,128]{1,0:T(8,128)S(1)}, u32[]{:S(2)}, u32[]{:S(2)}) %collective-permute-start.3) | collective-permute-done | bytes 32800 | tf_op jit(solution)/shard_map/ppermute | solution.py:446
  11.7 1.4 %smooth.1 = (f32[16,16,512]{2,1,0:T(8,128)S(1)}, f32[136,128]{1,0:T(8,128)S(1)}, f32[192,128]{1,0:T(8,128)S(1)}, f32[192,128]{1,0:T(8,128)S(1)}, f32[48,128]{1,0:T(8,128)S(1)}) custom-call(f32[16,16,512]{2,1,0:T(8,128)S(1)} %get-tuple-element.19.f.refs_0_, f32[16,16,512]{2,1,0:T(8,128)S(1)} %get-tuple-element.20.g.refs_1_, ...), custom_call_target="tpu_custom_call" | custom-call | tf_op jit(solution)/shard_map/smooth/pallas_call | solution.py:22
  13.0 0.1 collective-permute-start.4
  13.2 1.2 %collective-permute-done.4.core.s_core.refs_7_ = f32[136,128]{1,0:T(8,128)S(1)} collective-permute-done((f32[136,128]{1,0:T(8,128)S(1)}, f32[136,128]{1,0:T(8,128)S(1)}, u32[]{:S(2)}, u32[]{:S(2)}) %collective-permute-start.4) | collective-permute-done | bytes 69664 | tf_op jit(solution)/shard_map/ppermute | solution.py:446
  14.4 1.3 %collective-permute-start.5 = (f32[176,128]{1,0:T(8,128)S(1)}, f32[176,128]{1,0:T(8,128)S(1)}, u32[]{:S(2)}, u32[]{:S(2)}) collective-permute-start(f32[176,128]{1,0:T(8,128)S(1)} %get-tuple-element.30), channel_id=1, source_target_pairs={{0,1},{1,0},{2,3},{3,2},{4,8},{5,9},{6,10},{7,11},{8,4},{9,5},{10,... | collective-permute-start | bytes 270344 | tf_op jit(solution)/shard_map/ppermute | solution.py:446
  15.7 0.8 %collective-permute-start.6 = (f32[192,128]{1,0:T(8,128)S(1)}, f32[192,128]{1,0:T(8,128)S(1)}, u32[]{:S(2)}, u32[]{:S(2)}) collective-permute-start(f32[192,128]{1,0:T(8,128)S(1)} %get-tuple-element.31), channel_id=1, source_target_pairs={{0,1},{1,0},{2,3},{3,2},{4,5},{5,4},{6,7},{7,6},{8,9},{9,8},{10,11... | collective-permute-start | bytes 294920 | tf_op jit(solution)/shard_map/ppermute | solution.py:446
  16.5 2.2 %collective-permute-start.7 = (f32[192,128]{1,0:T(8,128)S(1)}, f32[192,128]{1,0:T(8,128)S(1)}, u32[]{:S(2)}, u32[]{:S(2)}) collective-permute-start(f32[192,128]{1,0:T(8,128)S(1)} %get-tuple-element.32), channel_id=1, source_target_pairs={{0,3},{1,2},{2,1},{3,0},{4,7},{5,6},{6,5},{7,4},{8,11},{9,10},{10,... | collective-permute-start | bytes 294920 | tf_op jit(solution)/shard_map/ppermute | solution.py:446
  18.7 0.5 %collective-permute-done.5.chip.refs_8_ = f32[176,128]{1,0:T(8,128)S(1)} collective-permute-done((f32[176,128]{1,0:T(8,128)S(1)}, f32[176,128]{1,0:T(8,128)S(1)}, u32[]{:S(2)}, u32[]{:S(2)}) %collective-permute-start.5) | collective-permute-done | bytes 90144 | tf_op jit(solution)/shard_map/ppermute | solution.py:446
  19.3 0.1 collective-permute-start.8
  19.3 1.2 %collective-permute-done.8.core = f32[40,128]{1,0:T(8,128)S(1)} collective-permute-done((f32[40,128]{1,0:T(8,128)S(1)}, f32[40,128]{1,0:T(8,128)S(1)}, u32[]{:S(2)}, u32[]{:S(2)}) %collective-permute-start.8) | collective-permute-done | bytes 20512 | tf_op jit(solution)/shard_map/ppermute | solution.py:446
  20.5 3.0 %collective-permute-start.11 = (f32[136,128]{1,0:T(8,128)S(1)}, f32[136,128]{1,0:T(8,128)S(1)}, u32[]{:S(2)}, u32[]{:S(2)}) collective-permute-start(f32[136,128]{1,0:T(8,128)S(1)} %window.1.refs_11_), channel_id=1, source_target_pairs={{0,3},{1,2},{2,1},{3,0},{4,7},{5,6},{6,5},{7,4},{8,11},{9,10},{10,... | collective-permute-start | bytes 208904 | tf_op jit(solution)/shard_map/ppermute | solution.py:446
  23.5 0.5 %collective-permute-start.10 = (f32[136,128]{1,0:T(8,128)S(1)}, f32[136,128]{1,0:T(8,128)S(1)}, u32[]{:S(2)}, u32[]{:S(2)}) collective-permute-start(f32[136,128]{1,0:T(8,128)S(1)} %window.1.refs_11_), channel_id=1, source_target_pairs={{0,2},{1,3},{2,0},{3,1},{4,6},{5,7},{6,4},{7,5},{8,10},{9,11},{10,... | collective-permute-start | bytes 208904 | tf_op jit(solution)/shard_map/ppermute | solution.py:446
  24.0 0.2 collective-permute-start.9
  24.2 0.0 collective-permute-done.7.refs_10_
  24.2 1.9 %collective-permute-done.11.refs_14_ = f32[136,128]{1,0:T(8,128)S(1)} collective-permute-done((f32[136,128]{1,0:T(8,128)S(1)}, f32[136,128]{1,0:T(8,128)S(1)}, u32[]{:S(2)}, u32[]{:S(2)}) %collective-permute-start.11) | collective-permute-done | bytes 69664 | tf_op jit(solution)/shard_map/ppermute | solution.py:446
  26.1 1.8 %collective-permute-done.10.refs_13_ = f32[136,128]{1,0:T(8,128)S(1)} collective-permute-done((f32[136,128]{1,0:T(8,128)S(1)}, f32[136,128]{1,0:T(8,128)S(1)}, u32[]{:S(2)}, u32[]{:S(2)}) %collective-permute-start.10) | collective-permute-done | bytes 69664 | tf_op jit(solution)/shard_map/ppermute | solution.py:446
  27.8 0.5 %collective-permute-done.9.refs_12_ = f32[136,128]{1,0:T(8,128)S(1)} collective-permute-done((f32[136,128]{1,0:T(8,128)S(1)}, f32[136,128]{1,0:T(8,128)S(1)}, u32[]{:S(2)}, u32[]{:S(2)}) %collective-permute-start.9) | collective-permute-done | bytes 69664 | tf_op jit(solution)/shard_map/ppermute | solution.py:446
  28.3 2.9 %finish.1 = (f32[16,16,512]{2,1,0:T(8,128)}, f32[4,16,128]{2,1,0:T(8,128)}) custom-call(f32[16,16,512]{2,1,0:T(8,128)S(1)} %get-tuple-element.19.f.refs_0_, f32[16,16,512]{2,1,0:T(8,128)S(1)} %get-tuple-element.20.g.refs_1_, f32[16,16,512]{2,1,0:T(8,128)S(1)} %get-tuple-element.27.s.refs_2_, f32[128,128]{1,0:T(8,128)S(1)} %collective-permute-done.core.refs_3_, ...), custom_call_target="tpu_custom_call" | custom-call | tf_op jit(solution)/shard_map/finish/pallas_call | solution.py:22
  (6 shorter events, 0.1 us)
Async XLA Ops:
  3.0 8.7 %collective-permute-start = (f32[128,128]{1,0:T(8,128)S(1)}, f32[128,128]{1,0:T(8,128)S(1)}, u32[]{:S(2)}, u32[]{:S(2)}) collective-permute-start(f32[128,128]{1,0:T(8,128)S(1)} %get-tuple-element.23), channel_id=1, source_target_pairs={{0,4},{1,5},{2,6},{3,7},{4,0},{5,1},{6,2},{7,3},{8,12},{9,13},{10,... | collective-permute-start | bytes 196616 | tf_op jit(solution)/shard_map/ppermute | solution.py:446
  3.5 8.1 %collective-permute-start.1 = (f32[128,128]{1,0:T(8,128)S(1)}, f32[128,128]{1,0:T(8,128)S(1)}, u32[]{:S(2)}, u32[]{:S(2)}) collective-permute-start(f32[128,128]{1,0:T(8,128)S(1)} %get-tuple-element.24), channel_id=1, source_target_pairs={{0,1},{1,0},{2,3},{3,2},{4,8},{5,9},{6,10},{7,11},{8,4},{9,5},{10,... | collective-permute-start | bytes 196616 | tf_op jit(solution)/shard_map/ppermute | solution.py:446
  6.1 3.9 %collective-permute-start.2 = (f32[64,128]{1,0:T(8,128)S(1)}, f32[64,128]{1,0:T(8,128)S(1)}, u32[]{:S(2)}, u32[]{:S(2)}) collective-permute-start(f32[64,128]{1,0:T(8,128)S(1)} %get-tuple-element.25), channel_id=1, source_target_pairs={{0,1},{1,0},{2,3},{3,2},{4,5},{5,4},{6,7},{7,6},{8,9},{9,8},{10,11... | collective-permute-start | bytes 98312 | tf_op jit(solution)/shard_map/ppermute | solution.py:446
  6.2 5.5 %collective-permute-start.3 = (f32[64,128]{1,0:T(8,128)S(1)}, f32[64,128]{1,0:T(8,128)S(1)}, u32[]{:S(2)}, u32[]{:S(2)}) collective-permute-start(f32[64,128]{1,0:T(8,128)S(1)} %get-tuple-element.26), channel_id=1, source_target_pairs={{0,3},{1,2},{2,1},{3,0},{4,7},{5,6},{6,5},{7,4},{8,11},{9,10},{10,... | collective-permute-start | bytes 98312 | tf_op jit(solution)/shard_map/ppermute | solution.py:446
  13.0 1.3 %collective-permute-start.4 = (f32[136,128]{1,0:T(8,128)S(1)}, f32[136,128]{1,0:T(8,128)S(1)}, u32[]{:S(2)}, u32[]{:S(2)}) collective-permute-start(f32[136,128]{1,0:T(8,128)S(1)} %get-tuple-element.28), channel_id=1, source_target_pairs={{0,4},{1,5},{2,6},{3,7},{4,0},{5,1},{6,2},{7,3},{8,12},{9,13},{10,... | collective-permute-start | bytes 208904 | tf_op jit(solution)/shard_map/ppermute | solution.py:446
  14.4 4.8 %collective-permute-start.5 = (f32[176,128]{1,0:T(8,128)S(1)}, f32[176,128]{1,0:T(8,128)S(1)}, u32[]{:S(2)}, u32[]{:S(2)}) collective-permute-start(f32[176,128]{1,0:T(8,128)S(1)} %get-tuple-element.30), channel_id=1, source_target_pairs={{0,1},{1,0},{2,3},{3,2},{4,8},{5,9},{6,10},{7,11},{8,4},{9,5},{10,... | collective-permute-start | bytes 270344 | tf_op jit(solution)/shard_map/ppermute | solution.py:446
  15.7 8.4 %collective-permute-start.6 = (f32[192,128]{1,0:T(8,128)S(1)}, f32[192,128]{1,0:T(8,128)S(1)}, u32[]{:S(2)}, u32[]{:S(2)}) collective-permute-start(f32[192,128]{1,0:T(8,128)S(1)} %get-tuple-element.31), channel_id=1, source_target_pairs={{0,1},{1,0},{2,3},{3,2},{4,5},{5,4},{6,7},{7,6},{8,9},{9,8},{10,11... | collective-permute-start | bytes 294920 | tf_op jit(solution)/shard_map/ppermute | solution.py:446
  16.5 7.7 %collective-permute-start.7 = (f32[192,128]{1,0:T(8,128)S(1)}, f32[192,128]{1,0:T(8,128)S(1)}, u32[]{:S(2)}, u32[]{:S(2)}) collective-permute-start(f32[192,128]{1,0:T(8,128)S(1)} %get-tuple-element.32), channel_id=1, source_target_pairs={{0,3},{1,2},{2,1},{3,0},{4,7},{5,6},{6,5},{7,4},{8,11},{9,10},{10,... | collective-permute-start | bytes 294920 | tf_op jit(solution)/shard_map/ppermute | solution.py:446
  19.3 1.3 %collective-permute-start.8 = (f32[40,128]{1,0:T(8,128)S(1)}, f32[40,128]{1,0:T(8,128)S(1)}, u32[]{:S(2)}, u32[]{:S(2)}) collective-permute-start(f32[40,128]{1,0:T(8,128)S(1)} %get-tuple-element.34.full), channel_id=1, source_target_pairs={{0,4},{1,5},{2,6},{3,7},{4,0},{5,1},{6,2},{7,3},{8,12},{9,13},{10,... | collective-permute-start | bytes 61448 | tf_op jit(solution)/shard_map/ppermute | solution.py:446
  20.5 5.5 %collective-permute-start.11 = (f32[136,128]{1,0:T(8,128)S(1)}, f32[136,128]{1,0:T(8,128)S(1)}, u32[]{:S(2)}, u32[]{:S(2)}) collective-permute-start(f32[136,128]{1,0:T(8,128)S(1)} %window.1.refs_11_), channel_id=1, source_target_pairs={{0,3},{1,2},{2,1},{3,0},{4,7},{5,6},{6,5},{7,4},{8,11},{9,10},{10,... | collective-permute-start | bytes 208904 | tf_op jit(solution)/shard_map/ppermute | solution.py:446
  23.5 4.3 %collective-permute-start.10 = (f32[136,128]{1,0:T(8,128)S(1)}, f32[136,128]{1,0:T(8,128)S(1)}, u32[]{:S(2)}, u32[]{:S(2)}) collective-permute-start(f32[136,128]{1,0:T(8,128)S(1)} %window.1.refs_11_), channel_id=1, source_target_pairs={{0,2},{1,3},{2,0},{3,1},{4,6},{5,7},{6,4},{7,5},{8,10},{9,11},{10,... | collective-permute-start | bytes 208904 | tf_op jit(solution)/shard_map/ppermute | solution.py:446
  24.0 4.3 %collective-permute-start.9 = (f32[136,128]{1,0:T(8,128)S(1)}, f32[136,128]{1,0:T(8,128)S(1)}, u32[]{:S(2)}, u32[]{:S(2)}) collective-permute-start(f32[136,128]{1,0:T(8,128)S(1)} %window.1.refs_11_), channel_id=1, source_target_pairs={{0,1},{1,0},{2,3},{3,2},{4,5},{5,4},{6,7},{7,6},{8,9},{9,8},{10,11... | collective-permute-start | bytes 208904 | tf_op jit(solution)/shard_map/ppermute | solution.py:446

commit v4 on v2

--- a/solution.py
+++ b/solution.py
@@ -138,62 +138,69 @@
         x, y = lax.axis_index("gx"), lax.axis_index("gy")
         return x, y, x % 2 == 0, y % 2 == 0
 
-    def set_up(
-        source_hbm, reaction_hbm, kind_hbm, id_hbm, mask_hbm, thrust_hbm,
-        f, g, d, absorb, core, chip, row, odd,
-        source, reaction, kind, disk_id, disk_mask, table, y_low, y_high, sems, table_sem,
-    ):
+    def look_up(table, ids):
+        spare = jnp.zeros((1, 128 - table.shape[1]), F32)
+        row = jnp.broadcast_to(jnp.concatenate([table, spare], axis=1), (16, 128))
+        parts = [
+            jnp.take_along_axis(row, ids[:, 128 * j : 128 * (j + 1)], axis=1, mode="promise_in_bounds") for j in range(4)
+        ]
+        return jnp.concatenate(parts, axis=1)
+
+    def first_of(source, reaction, kinds, ids, mask, table):
+        a = reaction + jnp.where(kinds == 1, WALL_PENALTY, jnp.where(kinds == 2, INFLOW_PENALTY, 0.0))
+        diagonal = 6.0 + a
+        scale = OMEGA / diagonal
+        return (source + mask.astype(F32) * look_up(table, ids)) * scale, scale, diagonal, a
+
+    def faces(*refs):
+        inputs, thrust, messages, buffers, table, sems, table_sem = (
+            refs[:5], refs[5], refs[6:10], refs[10:15], refs[15], refs[16], refs[17]
+        )
+        core, chip, row, odd = messages
         _, _, x_even, y_even = where_am_i()
+        near, far = jnp.where(x_even, 15, 0), jnp.where(x_even, 0, 15)
+        moves = [pltpu.make_async_copy(thrust, table, table_sem)]
+        for i, (hbm, buffer) in enumerate(zip(inputs, buffers)):
+            for j, part in enumerate((hbm.at[:, 0, :], hbm.at[:, 15, :], hbm.at[far], hbm.at[near])):
+                moves.append(pltpu.make_async_copy(part, buffer.at[j], sems.at[i, j]))
+        for move in moves:
+            move.start()
+        for move in moves:
+            move.wait()
+        found = [first_of(*(buffer[j] for buffer in buffers), table[...])[:2] for j in range(4)]
+        (low, _), (high, _), (f_far, g_far), (f_near, g_near) = found
+        put(row, 0, jnp.where(y_even, high, low))
+        put(odd, 0, jnp.where(y_even, low, high))
+        put(chip, 0, f_far)
+        put(chip, 64, g_far)
+        put(core, 0, f_near)
+        put(core, 64, g_near)
+
+    def set_up(*refs):
+        inputs, thrust, (f, g, d, absorb) = refs[:5], refs[5], refs[6:10]
+        buffers, table, sems, table_sem = refs[10:15], refs[15], refs[16], refs[17]
         moves = []
-        arrays = (
-            (source_hbm, source), (reaction_hbm, reaction), (kind_hbm, kind), (id_hbm, disk_id), (mask_hbm, disk_mask)
-        )
-        table_move = pltpu.make_async_copy(thrust_hbm, table, table_sem)
+        table_move = pltpu.make_async_copy(thrust, table, table_sem)
         table_move.start()
         for k in range(4):
             part = pl.ds(4 * k, 4)
             moves.append(
-                [pltpu.make_async_copy(a.at[part], b.at[part], sems.at[k, i]) for i, (a, b) in enumerate(arrays)]
+                [
+                    pltpu.make_async_copy(a.at[part], b.at[part], sems.at[k, i])
+                    for i, (a, b) in enumerate(zip(inputs, buffers))
+                ]
             )
             for move in moves[k]:
                 move.start()
         table_move.wait()
-        spare = jnp.zeros((1, 128 - table.shape[1]), F32)
-        lookup = jnp.broadcast_to(jnp.concatenate([table[...], spare], axis=1), (16, 128))
-
         for k in range(4):
             for move in moves[k]:
                 move.wait()
             total = jnp.zeros((16, 512), F32)
             for x in range(4 * k, 4 * k + 4):
-                kinds = kind[x]
-                a = reaction[x] + jnp.where(kinds == 1, WALL_PENALTY, jnp.where(kinds == 2, INFLOW_PENALTY, 0.0))
+                f[x], g[x], d[x], a = first_of(*(buffer[x] for buffer in buffers), table[...])
                 total = total + a
-                diagonal = 6.0 + a
-                scale = OMEGA / diagonal
-                ids = disk_id[x]
-                picked = jnp.concatenate(
-                    [
-                        jnp.take_along_axis(lookup, ids[:, 128 * j : 128 * (j + 1)], axis=1, mode="promise_in_bounds")
-                        for j in range(4)
-                    ],
-                    axis=1,
-                )
-                first = (source[x] + disk_mask[x].astype(F32) * picked) * scale
-                f[x] = first
-                g[x] = scale
-                d[x] = diagonal
-                y_low[x : x + 1, :] = first[0:1, :]
-                y_high[x : x + 1, :] = first[15:16, :]
             absorb[16 * k : 16 * k + 16, :] = total
-        near, far = jnp.where(x_even, 15, 0), jnp.where(x_even, 0, 15)
-        put(core, 0, f[near])
-        put(core, 64, g[near])
-        put(chip, 0, f[far])
-        put(chip, 64, g[far])
-        low, high = y_low[...], y_high[...]
-        put(row, 0, jnp.where(y_even, high, low))
-        put(odd, 0, jnp.where(y_even, low, high))
 
     def halo_x(core, chip, row, x, x_even):
         a, b = get(core, row, 16, 512), get(chip, row, 16, 512)
@@ -446,18 +453,34 @@
         return lax.ppermute(array, axes, pairs)
 
     def local(source, reaction, boundary_kind, disk_id, disk_mask, thrust):
-        f, g, d, absorb, core, chip, row, odd = call(
-            set_up,
-            [field, field, field, (64, 512), (128, 128), (128, 128), (64, 128), (64, 128)],
-            source, reaction, boundary_kind, disk_id, disk_mask, thrust.reshape(1, -1),
+        inputs = [
+            pltpu.with_memory_space_constraint(array, pltpu.HBM)
+            for array in (source, reaction, boundary_kind, disk_id, disk_mask, thrust.reshape(1, -1))
+        ]
+
+        def staged(shape):
+            return (
+                [shape, shape]
+                + [pltpu.VMEM(shape, jnp.int32)] * 3
+                + [(1, thrust.shape[0]), pltpu.SemaphoreType.DMA((5, 5)), pltpu.SemaphoreType.DMA(())]
+            )
+
+        core, chip, row, odd = call(
+            faces,
+            [(128, 128), (128, 128), (64, 128), (64, 128)],
+            *inputs,
             in_specs=[HBM] * 6,
-            scratch=[field, field]
-            + [pltpu.VMEM(field, jnp.int32)] * 3
-            + [(1, thrust.shape[0]), slab, slab, pltpu.SemaphoreType.DMA((4, 5)), pltpu.SemaphoreType.DMA(())],
-            name="set_up",
+            scratch=staged((4, 16, 512)),
+            name="faces",
         )
-        a_row, a_odd = swap(row, row_pairs[0]), swap(odd, odd_pairs)
-        a_chip, a_core = swap(chip, chip_pairs), swap(core, core_pairs)
+        a_core, a_chip = swap(core, core_pairs), swap(chip, chip_pairs)
+        a_odd, a_row = swap(odd, odd_pairs), swap(row, row_pairs[0])
+        f, g, d, absorb = call(
+            set_up, [field, field, field, (64, 512)], *inputs, in_specs=[HBM] * 6, scratch=staged(field), name="set_up"
+        )
+        a_core, a_chip, a_odd, a_row, f, g, d, absorb = lax.optimization_barrier(
+            (a_core, a_chip, a_odd, a_row, f, g, d, absorb)
+        )
         s, to_core, to_row, to_odd, block = call(
             smooth,
             [field, (136, 128), (192, 128), (192, 128), (48, 128)],

time: 39.3 us -> 30.6 us (0.78)
  local copies, waits for them, and re-layouts: 5.85 us -> 0 us
  waiting for transfers between devices: 9.64 us -> 8.44 us
  starting transfers between devices: 14.2 us -> 13 us
    unnamed x12 -> x0, local copies, waits for them, and re-layouts: 5.85 us -> none
    ppermute x12, waiting for transfers between devices: 9.64 us -> 8.44 us  [swap(): return lax.ppermute(array, axes, pairs)]
    ppermute x12, starting transfers between devices: 14.2 us -> 13 us  [swap(): return lax.ppermute(array, axes, pairs)]
    pallas_call x6 -> x7, Pallas kernels: 8.57 us -> 8.22 us  [call(): pl.pallas_call(kernel, out_shape=[jax.ShapeDtypeStruct(s, F32) for s in o...]
  transfers between devices with their start and end apart: 12 -> 12, of which waited for: 8 -> 7; matrix products, arithmetic and copies ran while one was open for 0% -> 0% of each run, Pallas kernels for 0% -> 8%
where the time goes in v4:
time: 30.6 us; the launch traced here: 30.4 us
  starting transfers between devices  13 us (42%)
  waiting for transfers between devices  8.44 us (28%)
  Pallas kernels  8.22 us (27%)
  between operations  0.68 us (2%)
    ppermute x12, starting transfers between devices, swap(): return lax.ppermute(array, axes, pairs)  13 us
    ppermute x12, waiting for transfers between devices, swap(): return lax.ppermute(array, axes, pairs)  8.44 us
    pallas_call x7, Pallas kernels, call(): pl.pallas_call(kernel, out_shape=[jax.ShapeDtypeStruct(s, F32) for s in o...  8.22 us
  transfers between devices with their start and end apart: 12, of which 7 were waited for; matrix products, arithmetic and copies ran while one was open for 0% of the time, Pallas kernels for 8%

profile of v4, /device:TPU:0, one launch (start us, length us, event | category | flops | bytes accessed | tf_op | source)
XLA Modules:
  0.0 30.4 jit_solution(17779800513258425945)
XLA Ops:
  0.6 1.5 %faces.1 = (f32[128,128]{1,0:T(8,128)S(1)}, f32[128,128]{1,0:T(8,128)S(1)}, f32[64,128]{1,0:T(8,128)S(1)}, f32[64,128]{1,0:T(8,128)S(1)}) custom-call(f32[16,16,512]{2,1,0:T(8,128)} %refs_0_.3, f32[16,16,512]{2,1,0:T(8,128)} %refs_1_.3, s32[16,16,512]{2,1,0:T(8,128)} %refs_2_.3, s32[16,16,512]{2,1,0:T(8,128)} %refs_3_.3, s32[16,16,512]{2,1,0:T(8,128)} %refs_4_.3, ...), custom_call_target="tpu_custom_call" | custom-call | tf_op jit(solution)/shard_map/faces/pallas_call | solution.py:22
  2.1 0.5 %collective-permute-start = (f32[128,128]{1,0:T(8,128)S(1)}, f32[128,128]{1,0:T(8,128)S(1)}, u32[]{:S(2)}, u32[]{:S(2)}) collective-permute-start(f32[128,128]{1,0:T(8,128)S(1)} %get-tuple-element.27), channel_id=1, source_target_pairs={{0,4},{1,5},{2,6},{3,7},{4,0},{5,1},{6,2},{7,3},{8,12},{9,13},{10,... | collective-permute-start | bytes 196616 | tf_op jit(solution)/shard_map/ppermute | solution.py:453
  2.6 2.6 %collective-permute-start.1 = (f32[128,128]{1,0:T(8,128)S(1)}, f32[128,128]{1,0:T(8,128)S(1)}, u32[]{:S(2)}, u32[]{:S(2)}) collective-permute-start(f32[128,128]{1,0:T(8,128)S(1)} %get-tuple-element.28), channel_id=1, source_target_pairs={{0,1},{1,0},{2,3},{3,2},{4,8},{5,9},{6,10},{7,11},{8,4},{9,5},{10,... | collective-permute-start | bytes 196616 | tf_op jit(solution)/shard_map/ppermute | solution.py:453
  5.2 1.5 %collective-permute-start.2 = (f32[64,128]{1,0:T(8,128)S(1)}, f32[64,128]{1,0:T(8,128)S(1)}, u32[]{:S(2)}, u32[]{:S(2)}) collective-permute-start(f32[64,128]{1,0:T(8,128)S(1)} %get-tuple-element.29), channel_id=1, source_target_pairs={{0,3},{1,2},{2,1},{3,0},{4,7},{5,6},{6,5},{7,4},{8,11},{9,10},{10,... | collective-permute-start | bytes 98312 | tf_op jit(solution)/shard_map/ppermute | solution.py:453
  6.7 1.5 %collective-permute-start.3 = (f32[64,128]{1,0:T(8,128)S(1)}, f32[64,128]{1,0:T(8,128)S(1)}, u32[]{:S(2)}, u32[]{:S(2)}) collective-permute-start(f32[64,128]{1,0:T(8,128)S(1)} %get-tuple-element.30), channel_id=1, source_target_pairs={{0,1},{1,0},{2,3},{3,2},{4,5},{5,4},{6,7},{7,6},{8,9},{9,8},{10,11... | collective-permute-start | bytes 98312 | tf_op jit(solution)/shard_map/ppermute | solution.py:453
  8.2 2.4 %set_up.1 = (f32[16,16,512]{2,1,0:T(8,128)S(1)}, f32[16,16,512]{2,1,0:T(8,128)S(1)}, f32[16,16,512]{2,1,0:T(8,128)S(1)}, f32[64,512]{1,0:T(8,128)S(1)}) custom-call(f32[16,16,512]{2,1,0:T(8,128)} %refs_0_.3, f32[16,16,512]{2,1,0:T(8,128)} %refs_1_.3, s32[16,16,512]{2,1,0:T(8,128)} %refs_2_.3, s32[16,16,512]{2,1,0:T(8,128)} %refs_3_.3, ...), custom_call_target="tpu_custom_call" | custom-call | tf_op jit(solution)/shard_map/set_up/pallas_call | solution.py:22
  10.6 0.3 collective-permute-done.3.row.refs_5_
  10.9 1.4 %smooth.1 = (f32[16,16,512]{2,1,0:T(8,128)S(1)}, f32[136,128]{1,0:T(8,128)S(1)}, f32[192,128]{1,0:T(8,128)S(1)}, f32[192,128]{1,0:T(8,128)S(1)}, f32[48,128]{1,0:T(8,128)S(1)}) custom-call(f32[16,16,512]{2,1,0:T(8,128)S(1)} %get-tuple-element.35.f.refs_0_, f32[16,16,512]{2,1,0:T(8,128)S(1)} %get-tuple-element.36.g.refs_1_, ...), custom_call_target="tpu_custom_call" | custom-call | tf_op jit(solution)/shard_map/smooth/pallas_call | solution.py:22
  12.2 0.1 collective-permute-start.4
  12.3 1.2 %collective-permute-done.4.core.s_core.refs_7_ = f32[136,128]{1,0:T(8,128)S(1)} collective-permute-done((f32[136,128]{1,0:T(8,128)S(1)}, f32[136,128]{1,0:T(8,128)S(1)}, u32[]{:S(2)}, u32[]{:S(2)}) %collective-permute-start.4) | collective-permute-done | bytes 69664 | tf_op jit(solution)/shard_map/ppermute | solution.py:453
  13.6 1.3 %collective-permute-start.5 = (f32[176,128]{1,0:T(8,128)S(1)}, f32[176,128]{1,0:T(8,128)S(1)}, u32[]{:S(2)}, u32[]{:S(2)}) collective-permute-start(f32[176,128]{1,0:T(8,128)S(1)} %get-tuple-element.46), channel_id=1, source_target_pairs={{0,1},{1,0},{2,3},{3,2},{4,8},{5,9},{6,10},{7,11},{8,4},{9,5},{10,... | collective-permute-start | bytes 270344 | tf_op jit(solution)/shard_map/ppermute | solution.py:453
  14.9 0.8 %collective-permute-start.6 = (f32[192,128]{1,0:T(8,128)S(1)}, f32[192,128]{1,0:T(8,128)S(1)}, u32[]{:S(2)}, u32[]{:S(2)}) collective-permute-start(f32[192,128]{1,0:T(8,128)S(1)} %get-tuple-element.47), channel_id=1, source_target_pairs={{0,1},{1,0},{2,3},{3,2},{4,5},{5,4},{6,7},{7,6},{8,9},{9,8},{10,11... | collective-permute-start | bytes 294920 | tf_op jit(solution)/shard_map/ppermute | solution.py:453
  15.7 1.2 %collective-permute-start.7 = (f32[192,128]{1,0:T(8,128)S(1)}, f32[192,128]{1,0:T(8,128)S(1)}, u32[]{:S(2)}, u32[]{:S(2)}) collective-permute-start(f32[192,128]{1,0:T(8,128)S(1)} %get-tuple-element.48), channel_id=1, source_target_pairs={{0,3},{1,2},{2,1},{3,0},{4,7},{5,6},{6,5},{7,4},{8,11},{9,10},{10,... | collective-permute-start | bytes 294920 | tf_op jit(solution)/shard_map/ppermute | solution.py:453
  16.9 1.6 %collective-permute-done.5.chip.refs_8_ = f32[176,128]{1,0:T(8,128)S(1)} collective-permute-done((f32[176,128]{1,0:T(8,128)S(1)}, f32[176,128]{1,0:T(8,128)S(1)}, u32[]{:S(2)}, u32[]{:S(2)}) %collective-permute-start.5) | collective-permute-done | bytes 90144 | tf_op jit(solution)/shard_map/ppermute | solution.py:453
  18.5 0.1 collective-permute-start.8
  18.6 1.2 %collective-permute-done.8.core = f32[40,128]{1,0:T(8,128)S(1)} collective-permute-done((f32[40,128]{1,0:T(8,128)S(1)}, f32[40,128]{1,0:T(8,128)S(1)}, u32[]{:S(2)}, u32[]{:S(2)}) %collective-permute-start.8) | collective-permute-done | bytes 20512 | tf_op jit(solution)/shard_map/ppermute | solution.py:453
  19.8 1.7 %collective-permute-start.11 = (f32[136,128]{1,0:T(8,128)S(1)}, f32[136,128]{1,0:T(8,128)S(1)}, u32[]{:S(2)}, u32[]{:S(2)}) collective-permute-start(f32[136,128]{1,0:T(8,128)S(1)} %window.1.refs_11_), channel_id=1, source_target_pairs={{0,3},{1,2},{2,1},{3,0},{4,7},{5,6},{6,5},{7,4},{8,11},{9,10},{10,... | collective-permute-start | bytes 208904 | tf_op jit(solution)/shard_map/ppermute | solution.py:453
  21.4 1.7 %collective-permute-start.10 = (f32[136,128]{1,0:T(8,128)S(1)}, f32[136,128]{1,0:T(8,128)S(1)}, u32[]{:S(2)}, u32[]{:S(2)}) collective-permute-start(f32[136,128]{1,0:T(8,128)S(1)} %window.1.refs_11_), channel_id=1, source_target_pairs={{0,2},{1,3},{2,0},{3,1},{4,6},{5,7},{6,4},{7,5},{8,10},{9,11},{10,... | collective-permute-start | bytes 208904 | tf_op jit(solution)/shard_map/ppermute | solution.py:453
  23.1 0.2 collective-permute-start.9
  23.3 0.0 collective-permute-done.6.refs_9_
  23.3 1.8 %collective-permute-done.11.refs_14_ = f32[136,128]{1,0:T(8,128)S(1)} collective-permute-done((f32[136,128]{1,0:T(8,128)S(1)}, f32[136,128]{1,0:T(8,128)S(1)}, u32[]{:S(2)}, u32[]{:S(2)}) %collective-permute-start.11) | collective-permute-done | bytes 69664 | tf_op jit(solution)/shard_map/ppermute | solution.py:453
  25.1 1.4 %collective-permute-done.10.refs_13_ = f32[136,128]{1,0:T(8,128)S(1)} collective-permute-done((f32[136,128]{1,0:T(8,128)S(1)}, f32[136,128]{1,0:T(8,128)S(1)}, u32[]{:S(2)}, u32[]{:S(2)}) %collective-permute-start.10) | collective-permute-done | bytes 69664 | tf_op jit(solution)/shard_map/ppermute | solution.py:453
  26.5 1.0 %collective-permute-done.9.refs_12_ = f32[136,128]{1,0:T(8,128)S(1)} collective-permute-done((f32[136,128]{1,0:T(8,128)S(1)}, f32[136,128]{1,0:T(8,128)S(1)}, u32[]{:S(2)}, u32[]{:S(2)}) %collective-permute-start.9) | collective-permute-done | bytes 69664 | tf_op jit(solution)/shard_map/ppermute | solution.py:453
  27.4 2.9 %finish.1 = (f32[16,16,512]{2,1,0:T(8,128)}, f32[4,16,128]{2,1,0:T(8,128)}) custom-call(f32[16,16,512]{2,1,0:T(8,128)S(1)} %get-tuple-element.35.f.refs_0_, f32[16,16,512]{2,1,0:T(8,128)S(1)} %get-tuple-element.36.g.refs_1_, f32[16,16,512]{2,1,0:T(8,128)S(1)} %get-tuple-element.43.s.refs_2_, f32[128,128]{1,0:T(8,128)S(1)} %collective-permute-done.core.refs_3_, ...), custom_call_target="tpu_custom_call" | custom-call | tf_op jit(solution)/shard_map/finish/pallas_call | solution.py:22
  (7 shorter events, 0.1 us)
Async XLA Ops:
  2.1 8.7 %collective-permute-start = (f32[128,128]{1,0:T(8,128)S(1)}, f32[128,128]{1,0:T(8,128)S(1)}, u32[]{:S(2)}, u32[]{:S(2)}) collective-permute-start(f32[128,128]{1,0:T(8,128)S(1)} %get-tuple-element.27), channel_id=1, source_target_pairs={{0,4},{1,5},{2,6},{3,7},{4,0},{5,1},{6,2},{7,3},{8,12},{9,13},{10,... | collective-permute-start | bytes 196616 | tf_op jit(solution)/shard_map/ppermute | solution.py:453
  2.6 8.2 %collective-permute-start.1 = (f32[128,128]{1,0:T(8,128)S(1)}, f32[128,128]{1,0:T(8,128)S(1)}, u32[]{:S(2)}, u32[]{:S(2)}) collective-permute-start(f32[128,128]{1,0:T(8,128)S(1)} %get-tuple-element.28), channel_id=1, source_target_pairs={{0,1},{1,0},{2,3},{3,2},{4,8},{5,9},{6,10},{7,11},{8,4},{9,5},{10,... | collective-permute-start | bytes 196616 | tf_op jit(solution)/shard_map/ppermute | solution.py:453
  5.2 5.4 %collective-permute-start.2 = (f32[64,128]{1,0:T(8,128)S(1)}, f32[64,128]{1,0:T(8,128)S(1)}, u32[]{:S(2)}, u32[]{:S(2)}) collective-permute-start(f32[64,128]{1,0:T(8,128)S(1)} %get-tuple-element.29), channel_id=1, source_target_pairs={{0,3},{1,2},{2,1},{3,0},{4,7},{5,6},{6,5},{7,4},{8,11},{9,10},{10,... | collective-permute-start | bytes 98312 | tf_op jit(solution)/shard_map/ppermute | solution.py:453
  6.7 4.2 %collective-permute-start.3 = (f32[64,128]{1,0:T(8,128)S(1)}, f32[64,128]{1,0:T(8,128)S(1)}, u32[]{:S(2)}, u32[]{:S(2)}) collective-permute-start(f32[64,128]{1,0:T(8,128)S(1)} %get-tuple-element.30), channel_id=1, source_target_pairs={{0,1},{1,0},{2,3},{3,2},{4,5},{5,4},{6,7},{7,6},{8,9},{9,8},{10,11... | collective-permute-start | bytes 98312 | tf_op jit(solution)/shard_map/ppermute | solution.py:453
  12.2 1.3 %collective-permute-start.4 = (f32[136,128]{1,0:T(8,128)S(1)}, f32[136,128]{1,0:T(8,128)S(1)}, u32[]{:S(2)}, u32[]{:S(2)}) collective-permute-start(f32[136,128]{1,0:T(8,128)S(1)} %get-tuple-element.44), channel_id=1, source_target_pairs={{0,4},{1,5},{2,6},{3,7},{4,0},{5,1},{6,2},{7,3},{8,12},{9,13},{10,... | collective-permute-start | bytes 208904 | tf_op jit(solution)/shard_map/ppermute | solution.py:453
  13.6 4.9 %collective-permute-start.5 = (f32[176,128]{1,0:T(8,128)S(1)}, f32[176,128]{1,0:T(8,128)S(1)}, u32[]{:S(2)}, u32[]{:S(2)}) collective-permute-start(f32[176,128]{1,0:T(8,128)S(1)} %get-tuple-element.46), channel_id=1, source_target_pairs={{0,1},{1,0},{2,3},{3,2},{4,8},{5,9},{6,10},{7,11},{8,4},{9,5},{10,... | collective-permute-start | bytes 270344 | tf_op jit(solution)/shard_map/ppermute | solution.py:453
  14.9 8.4 %collective-permute-start.6 = (f32[192,128]{1,0:T(8,128)S(1)}, f32[192,128]{1,0:T(8,128)S(1)}, u32[]{:S(2)}, u32[]{:S(2)}) collective-permute-start(f32[192,128]{1,0:T(8,128)S(1)} %get-tuple-element.47), channel_id=1, source_target_pairs={{0,1},{1,0},{2,3},{3,2},{4,5},{5,4},{6,7},{7,6},{8,9},{9,8},{10,11... | collective-permute-start | bytes 294920 | tf_op jit(solution)/shard_map/ppermute | solution.py:453
  15.7 7.6 %collective-permute-start.7 = (f32[192,128]{1,0:T(8,128)S(1)}, f32[192,128]{1,0:T(8,128)S(1)}, u32[]{:S(2)}, u32[]{:S(2)}) collective-permute-start(f32[192,128]{1,0:T(8,128)S(1)} %get-tuple-element.48), channel_id=1, source_target_pairs={{0,3},{1,2},{2,1},{3,0},{4,7},{5,6},{6,5},{7,4},{8,11},{9,10},{10,... | collective-permute-start | bytes 294920 | tf_op jit(solution)/shard_map/ppermute | solution.py:453
  18.5 1.3 %collective-permute-start.8 = (f32[40,128]{1,0:T(8,128)S(1)}, f32[40,128]{1,0:T(8,128)S(1)}, u32[]{:S(2)}, u32[]{:S(2)}) collective-permute-start(f32[40,128]{1,0:T(8,128)S(1)} %get-tuple-element.50.full), channel_id=1, source_target_pairs={{0,4},{1,5},{2,6},{3,7},{4,0},{5,1},{6,2},{7,3},{8,12},{9,13},{10,... | collective-permute-start | bytes 61448 | tf_op jit(solution)/shard_map/ppermute | solution.py:453
  19.8 5.3 %collective-permute-start.11 = (f32[136,128]{1,0:T(8,128)S(1)}, f32[136,128]{1,0:T(8,128)S(1)}, u32[]{:S(2)}, u32[]{:S(2)}) collective-permute-start(f32[136,128]{1,0:T(8,128)S(1)} %window.1.refs_11_), channel_id=1, source_target_pairs={{0,3},{1,2},{2,1},{3,0},{4,7},{5,6},{6,5},{7,4},{8,11},{9,10},{10,... | collective-permute-start | bytes 208904 | tf_op jit(solution)/shard_map/ppermute | solution.py:453
  21.4 5.0 %collective-permute-start.10 = (f32[136,128]{1,0:T(8,128)S(1)}, f32[136,128]{1,0:T(8,128)S(1)}, u32[]{:S(2)}, u32[]{:S(2)}) collective-permute-start(f32[136,128]{1,0:T(8,128)S(1)} %window.1.refs_11_), channel_id=1, source_target_pairs={{0,2},{1,3},{2,0},{3,1},{4,6},{5,7},{6,4},{7,5},{8,10},{9,11},{10,... | collective-permute-start | bytes 208904 | tf_op jit(solution)/shard_map/ppermute | solution.py:453
  23.1 4.3 %collective-permute-start.9 = (f32[136,128]{1,0:T(8,128)S(1)}, f32[136,128]{1,0:T(8,128)S(1)}, u32[]{:S(2)}, u32[]{:S(2)}) collective-permute-start(f32[136,128]{1,0:T(8,128)S(1)} %window.1.refs_11_), channel_id=1, source_target_pairs={{0,1},{1,0},{2,3},{3,2},{4,5},{5,4},{6,7},{7,6},{8,9},{9,8},{10,11... | collective-permute-start | bytes 208904 | tf_op jit(solution)/shard_map/ppermute | solution.py:453

commit v5 on v4

--- a/solution.py
+++ b/solution.py
@@ -79,12 +79,30 @@
     return above + below
 
 
-def beside_rows(slab, low, high):
-    rows = slab.shape[0]
-    row = iota(slab.shape, 0)
-    above = jnp.where(row == rows - 1, jnp.broadcast_to(high, slab.shape), pltpu.roll(slab, rows - 1, 0))
-    below = jnp.where(row == 0, jnp.broadcast_to(low, slab.shape), pltpu.roll(slab, 1, 0))
-    return above + below
+def beside(slab, low=None, high=None):
+    rows, depth = slab.shape
+    tiles, columns = rows // 8, depth // 128
+    lane, row = iota((8, 128), 1), iota((8, 128), 0)
+    piece = [[slab[8 * t : 8 * t + 8, 128 * j : 128 * j + 128] for j in range(columns)] for t in range(tiles)]
+    left = [[pltpu.roll(p, 127, 1) for p in line] for line in piece]
+    right = [[pltpu.roll(p, 1, 1) for p in line] for line in piece]
+    up = [[pltpu.roll(p, 7, 0) for p in line] for line in piece]
+    down = [[pltpu.roll(p, 1, 0) for p in line] for line in piece]
+
+    def outer(line, j):
+        return 0.0 if line is None else jnp.broadcast_to(line[:, 128 * j : 128 * j + 128], (8, 128))
+
+    lines = []
+    for t in range(tiles):
+        parts = []
+        for j in range(columns):
+            above = jnp.where(lane == 127, left[t][j + 1] if j + 1 < columns else 0.0, left[t][j])
+            below = jnp.where(lane == 0, right[t][j - 1] if j > 0 else 0.0, right[t][j])
+            after = jnp.where(row == 7, up[t + 1][j] if t + 1 < tiles else outer(high, j), up[t][j])
+            before = jnp.where(row == 0, down[t - 1][j] if t > 0 else outer(low, j), down[t][j])
+            parts.append((above + below) + (after + before))
+        lines.append(jnp.concatenate(parts, axis=1))
+    return jnp.concatenate(lines, axis=0)
 
 
 def dot(left, right):
@@ -176,29 +194,11 @@
         put(core, 0, f_near)
         put(core, 64, g_near)
 
-    def set_up(*refs):
-        inputs, thrust, (f, g, d, absorb) = refs[:5], refs[5], refs[6:10]
-        buffers, table, sems, table_sem = refs[10:15], refs[15], refs[16], refs[17]
-        moves = []
-        table_move = pltpu.make_async_copy(thrust, table, table_sem)
-        table_move.start()
+    def set_up(source, reaction, kind, disk_id, disk_mask, table, f, g, d, absorb):
         for k in range(4):
-            part = pl.ds(4 * k, 4)
-            moves.append(
-                [
-                    pltpu.make_async_copy(a.at[part], b.at[part], sems.at[k, i])
-                    for i, (a, b) in enumerate(zip(inputs, buffers))
-                ]
-            )
-            for move in moves[k]:
-                move.start()
-        table_move.wait()
-        for k in range(4):
-            for move in moves[k]:
-                move.wait()
             total = jnp.zeros((16, 512), F32)
             for x in range(4 * k, 4 * k + 4):
-                f[x], g[x], d[x], a = first_of(*(buffer[x] for buffer in buffers), table[...])
+                f[x], g[x], d[x], a = first_of(source[x], reaction[x], kind[x], disk_id[x], disk_mask[x], table[...])
                 total = total + a
             absorb[16 * k : 16 * k + 16, :] = total
 
@@ -222,7 +222,7 @@
             here = f[x]
             scale = g[x]
             total = (f[x - 1] if x > 0 else left) + (f[x + 1] if x < 15 else right)
-            total = total + beside_rows(here, lo[x : x + 1, :], hi[x : x + 1, :]) + beside_z(here)
+            total = total + beside(here, lo[x : x + 1, :], hi[x : x + 1, :])
             value = 1.2 * here + scale * total
             s[x] = value
             y0[x : x + 1, :] = value[0:1, :]
@@ -231,13 +231,12 @@
             y15[x : x + 1, :] = value[15:16, :]
             g0[x : x + 1, :] = scale[0:1, :]
             g15[x : x + 1, :] = scale[15:16, :]
-        nothing = jnp.zeros((1, 512), F32)
         for k in range(4):
             total = jnp.zeros((16, 512), F32)
             for x in range(4 * k, 4 * k + 4):
                 here = s[x]
                 total = total + d[x] * (1.25 * f[x] - here)
-                total = total + beside_rows(here, nothing, nothing) + beside_z(here)
+                total = total + beside(here)
                 if x > 0:
                     total = total + s[x - 1]
                 if x < 15:
@@ -315,7 +314,7 @@
         f, g, s, a_core, a_chip, a_row, a_odd, s_core, s_chip, s_row, s_odd = refs[:11]
         windows = refs[11 : 11 + ny]
         pressure, coarse = refs[11 + ny : 13 + ny]
-        every, res, diag, inv, one, two, sol, Pc, T, U, yl, yh, tl, th, ul, uh, result, sems = refs[13 + ny :]
+        every, res, diag, inv, one, two, sol, Pc, T, U, yl, yh, tl, th, ul, uh, result, slab_out, sems = refs[13 + ny :]
         x_at, y_at, x_even, y_even = where_am_i()
         for step, window in enumerate(windows):
             every[jnp.bitwise_xor(y_at, step)] = window[...]
@@ -373,7 +372,9 @@
             factor = factor_next
         for plane in range(planes):
             for cx in range(4):
-                coarse[cx, plane : plane + 1, :] = sol[plane + 1, 4 + cx : 5 + cx, :]
+                slab_out[cx, plane : plane + 1, :] = sol[plane + 1, 4 + cx : 5 + cx, :]
+        moves = [pltpu.make_async_copy(slab_out, coarse, sems.at[8])]
+        moves[0].start()
 
         first_plane = 4 * y_at + 1
         for at in range(6):
@@ -411,8 +412,7 @@
 
         def fourth_at(at, forcing, scale):
             here = T[at + 1]
-            total = T[at] + T[at + 2] + beside_z(here)
-            total = total + beside_rows(here, tl[at + 7 : at + 8, :], th[at + 7 : at + 8, :])
+            total = T[at] + T[at + 2] + beside(here, tl[at + 7 : at + 8, :], th[at + 7 : at + 8, :])
             return 0.2 * here + forcing + scale * total
 
         U[0] = fourth_at(0, f_left, g_left)
@@ -431,15 +431,13 @@
             total = far + edge[...] + ref[7:23, :] + ref[9:25, :] + beside_z(here)
             out[...] = 0.2 * here + forcing + scale * total
 
-        moves = []
         for x in range(16):
             here = U[x + 1]
-            total = U[x] + U[x + 2] + beside_z(here)
-            total = total + beside_rows(here, ul[x : x + 1, :], uh[x : x + 1, :])
+            total = U[x] + U[x + 2] + beside(here, ul[x : x + 1, :], uh[x : x + 1, :])
             result[x] = 0.2 * here + f[x] + g[x] * total
-            if x % 4 == 3:
-                part = pl.ds(x - 3, 4)
-                moves.append(pltpu.make_async_copy(result.at[part], pressure.at[part], sems.at[x // 4]))
+            if x % 2 == 1:
+                part = pl.ds(x - 1, 2)
+                moves.append(pltpu.make_async_copy(result.at[part], pressure.at[part], sems.at[x // 2]))
                 moves[-1].start()
         for move in moves:
             move.wait()
@@ -453,31 +451,21 @@
         return lax.ppermute(array, axes, pairs)
 
     def local(source, reaction, boundary_kind, disk_id, disk_mask, thrust):
-        inputs = [
-            pltpu.with_memory_space_constraint(array, pltpu.HBM)
-            for array in (source, reaction, boundary_kind, disk_id, disk_mask, thrust.reshape(1, -1))
-        ]
-
-        def staged(shape):
-            return (
-                [shape, shape]
-                + [pltpu.VMEM(shape, jnp.int32)] * 3
-                + [(1, thrust.shape[0]), pltpu.SemaphoreType.DMA((5, 5)), pltpu.SemaphoreType.DMA(())]
-            )
-
+        inputs = (source, reaction, boundary_kind, disk_id, disk_mask, thrust.reshape(1, -1))
+        some = (4, 16, 512)
         core, chip, row, odd = call(
             faces,
             [(128, 128), (128, 128), (64, 128), (64, 128)],
-            *inputs,
+            *(pltpu.with_memory_space_constraint(array, pltpu.HBM) for array in inputs),
             in_specs=[HBM] * 6,
-            scratch=staged((4, 16, 512)),
+            scratch=[some, some]
+            + [pltpu.VMEM(some, jnp.int32)] * 3
+            + [(1, thrust.shape[0]), pltpu.SemaphoreType.DMA((5, 4)), pltpu.SemaphoreType.DMA(())],
             name="faces",
         )
         a_core, a_chip = swap(core, core_pairs), swap(chip, chip_pairs)
         a_odd, a_row = swap(odd, odd_pairs), swap(row, row_pairs[0])
-        f, g, d, absorb = call(
-            set_up, [field, field, field, (64, 512)], *inputs, in_specs=[HBM] * 6, scratch=staged(field), name="set_up"
-        )
+        f, g, d, absorb = call(set_up, [field, field, field, (64, 512)], *inputs, name="set_up")
         a_core, a_chip, a_odd, a_row, f, g, d, absorb = lax.optimization_barrier(
             (a_core, a_chip, a_odd, a_row, f, g, d, absorb)
         )
@@ -504,8 +492,8 @@
             + [(planes, 16, 128)] * 3
             + [(planes + 2, 16, 128)] * 3
             + [(6, 16, 512), (20, 16, 512), long, slab, slab, (32, 512), (32, 512), slab, slab, field]
-            + [pltpu.SemaphoreType.DMA((4,))],
-            out_specs=[HBM, VMEM],
+            + [(4, planes, 128), pltpu.SemaphoreType.DMA((9,))],
+            out_specs=[HBM, HBM],
             name="finish",
         )
         return pressure, coarse

time: 30.6 us -> 30.1 us (0.984)
  Pallas kernels: 8.22 us -> 5.79 us
  waiting for transfers between devices: 8.44 us -> 10.4 us
    pallas_call x7, Pallas kernels: 8.22 us -> 5.79 us  [call(): pl.pallas_call(kernel, out_shape=[jax.ShapeDtypeStruct(s, F32) for s in o...]
    ppermute x12, waiting for transfers between devices: 8.44 us -> 10.4 us  [swap(): return lax.ppermute(array, axes, pairs)]
  transfers between devices with their start and end apart: 12 -> 12, of which waited for: 7 -> 8; matrix products, arithmetic and copies ran while one was open for 0% -> 0% of each run, Pallas kernels for 8% -> 2%
where the time goes in v5:
time: 30.1 us; the launch traced here: 29.9 us
  starting transfers between devices  13 us (43%)
  waiting for transfers between devices  10.4 us (35%)
  Pallas kernels  5.79 us (19%)
  between operations  0.73 us (2%)
    ppermute x12, starting transfers between devices, swap(): return lax.ppermute(array, axes, pairs)  13 us
    ppermute x12, waiting for transfers between devices, swap(): return lax.ppermute(array, axes, pairs)  10.4 us
    pallas_call x7, Pallas kernels, call(): pl.pallas_call(kernel, out_shape=[jax.ShapeDtypeStruct(s, F32) for s in o...  5.79 us
  transfers between devices with their start and end apart: 12, of which 8 were waited for; matrix products, arithmetic and copies ran while one was open for 0% of the time, Pallas kernels for 2%

profile of v5, /device:TPU:0, one launch (start us, length us, event | category | flops | bytes accessed | tf_op | source)
XLA Modules:
  0.0 29.9 jit_solution(1083428397375446370)
XLA Ops:
  0.7 1.6 %faces.1 = (f32[128,128]{1,0:T(8,128)S(1)}, f32[128,128]{1,0:T(8,128)S(1)}, f32[64,128]{1,0:T(8,128)S(1)}, f32[64,128]{1,0:T(8,128)S(1)}) custom-call(f32[16,16,512]{2,1,0:T(8,128)} %source.1, f32[16,16,512]{2,1,0:T(8,128)} %reaction.1, s32[16,16,512]{2,1,0:T(8,128)} %kind.1, s32[16,16,512]{2,1,0:T(8,128)} %disk_id.1, s32[16,16,512]{2,1,0:T(8,128)} %disk_mask.1, ...), custom_call_target="tpu_custom_call" | custom-call | tf_op jit(solution)/shard_map/faces/pallas_call | solution.py:22
  2.3 0.5 %collective-permute-start = (f32[128,128]{1,0:T(8,128)S(1)}, f32[128,128]{1,0:T(8,128)S(1)}, u32[]{:S(2)}, u32[]{:S(2)}) collective-permute-start(f32[128,128]{1,0:T(8,128)S(1)} %get-tuple-element.27), channel_id=1, source_target_pairs={{0,4},{1,5},{2,6},{3,7},{4,0},{5,1},{6,2},{7,3},{8,12},{9,13},{10,... | collective-permute-start | bytes 196616 | tf_op jit(solution)/shard_map/ppermute | solution.py:451
  2.8 2.6 %collective-permute-start.1 = (f32[128,128]{1,0:T(8,128)S(1)}, f32[128,128]{1,0:T(8,128)S(1)}, u32[]{:S(2)}, u32[]{:S(2)}) collective-permute-start(f32[128,128]{1,0:T(8,128)S(1)} %get-tuple-element.28), channel_id=1, source_target_pairs={{0,1},{1,0},{2,3},{3,2},{4,8},{5,9},{6,10},{7,11},{8,4},{9,5},{10,... | collective-permute-start | bytes 196616 | tf_op jit(solution)/shard_map/ppermute | solution.py:451
  5.4 1.5 %collective-permute-start.2 = (f32[64,128]{1,0:T(8,128)S(1)}, f32[64,128]{1,0:T(8,128)S(1)}, u32[]{:S(2)}, u32[]{:S(2)}) collective-permute-start(f32[64,128]{1,0:T(8,128)S(1)} %get-tuple-element.29), channel_id=1, source_target_pairs={{0,3},{1,2},{2,1},{3,0},{4,7},{5,6},{6,5},{7,4},{8,11},{9,10},{10,... | collective-permute-start | bytes 98312 | tf_op jit(solution)/shard_map/ppermute | solution.py:451
  6.9 1.5 %collective-permute-start.3 = (f32[64,128]{1,0:T(8,128)S(1)}, f32[64,128]{1,0:T(8,128)S(1)}, u32[]{:S(2)}, u32[]{:S(2)}) collective-permute-start(f32[64,128]{1,0:T(8,128)S(1)} %get-tuple-element.30), channel_id=1, source_target_pairs={{0,1},{1,0},{2,3},{3,2},{4,5},{5,4},{6,7},{7,6},{8,9},{9,8},{10,11... | collective-permute-start | bytes 98312 | tf_op jit(solution)/shard_map/ppermute | solution.py:451
  8.4 0.5 %set_up.1 = (f32[16,16,512]{2,1,0:T(8,128)S(1)}, f32[16,16,512]{2,1,0:T(8,128)S(1)}, f32[16,16,512]{2,1,0:T(8,128)S(1)}, f32[64,512]{1,0:T(8,128)S(1)}) custom-call(f32[16,16,512]{2,1,0:T(8,128)S(1)} %copy-done, f32[16,16,512]{2,1,0:T(8,128)S(1)} %copy-done.1, s32[16,16,512]{2,1,0:T(8,128)S(1)} %copy-done.2, s32[16,16,512]{2,1,0:T(8,128)S(1)} %copy-done.3, ...), custom_call_target="tpu_custom_call" | custom-call | tf_op jit(solution)/shard_map/set_up/pallas_call | solution.py:22
  8.8 1.3 %collective-permute-done.2.odd.refs_6_ = f32[64,128]{1,0:T(8,128)S(1)} collective-permute-done((f32[64,128]{1,0:T(8,128)S(1)}, f32[64,128]{1,0:T(8,128)S(1)}, u32[]{:S(2)}, u32[]{:S(2)}) %collective-permute-start.2) | collective-permute-done | bytes 32800 | tf_op jit(solution)/shard_map/ppermute | solution.py:451
  10.2 0.8 %collective-permute-done.3.row.refs_5_ = f32[64,128]{1,0:T(8,128)S(1)} collective-permute-done((f32[64,128]{1,0:T(8,128)S(1)}, f32[64,128]{1,0:T(8,128)S(1)}, u32[]{:S(2)}, u32[]{:S(2)}) %collective-permute-start.3) | collective-permute-done | bytes 32800 | tf_op jit(solution)/shard_map/ppermute | solution.py:451
  11.0 1.4 %smooth.1 = (f32[16,16,512]{2,1,0:T(8,128)S(1)}, f32[136,128]{1,0:T(8,128)S(1)}, f32[192,128]{1,0:T(8,128)S(1)}, f32[192,128]{1,0:T(8,128)S(1)}, f32[48,128]{1,0:T(8,128)S(1)}) custom-call(f32[16,16,512]{2,1,0:T(8,128)S(1)} %get-tuple-element.35.f.refs_0_, f32[16,16,512]{2,1,0:T(8,128)S(1)} %get-tuple-element.36.g.refs_1_, ...), custom_call_target="tpu_custom_call" | custom-call | tf_op jit(solution)/shard_map/smooth/pallas_call | solution.py:22
  12.5 0.1 collective-permute-start.4
  12.5 1.2 %collective-permute-done.4.core.s_core.refs_7_ = f32[136,128]{1,0:T(8,128)S(1)} collective-permute-done((f32[136,128]{1,0:T(8,128)S(1)}, f32[136,128]{1,0:T(8,128)S(1)}, u32[]{:S(2)}, u32[]{:S(2)}) %collective-permute-start.4) | collective-permute-done | bytes 69664 | tf_op jit(solution)/shard_map/ppermute | solution.py:451
  13.8 1.3 %collective-permute-start.5 = (f32[176,128]{1,0:T(8,128)S(1)}, f32[176,128]{1,0:T(8,128)S(1)}, u32[]{:S(2)}, u32[]{:S(2)}) collective-permute-start(f32[176,128]{1,0:T(8,128)S(1)} %get-tuple-element.46), channel_id=1, source_target_pairs={{0,1},{1,0},{2,3},{3,2},{4,8},{5,9},{6,10},{7,11},{8,4},{9,5},{10,... | collective-permute-start | bytes 270344 | tf_op jit(solution)/shard_map/ppermute | solution.py:451
  15.1 0.8 %collective-permute-start.6 = (f32[192,128]{1,0:T(8,128)S(1)}, f32[192,128]{1,0:T(8,128)S(1)}, u32[]{:S(2)}, u32[]{:S(2)}) collective-permute-start(f32[192,128]{1,0:T(8,128)S(1)} %get-tuple-element.47), channel_id=1, source_target_pairs={{0,1},{1,0},{2,3},{3,2},{4,5},{5,4},{6,7},{7,6},{8,9},{9,8},{10,11... | collective-permute-start | bytes 294920 | tf_op jit(solution)/shard_map/ppermute | solution.py:451
  15.9 1.2 %collective-permute-start.7 = (f32[192,128]{1,0:T(8,128)S(1)}, f32[192,128]{1,0:T(8,128)S(1)}, u32[]{:S(2)}, u32[]{:S(2)}) collective-permute-start(f32[192,128]{1,0:T(8,128)S(1)} %get-tuple-element.48), channel_id=1, source_target_pairs={{0,3},{1,2},{2,1},{3,0},{4,7},{5,6},{6,5},{7,4},{8,11},{9,10},{10,... | collective-permute-start | bytes 294920 | tf_op jit(solution)/shard_map/ppermute | solution.py:451
  17.1 1.6 %collective-permute-done.5.chip.refs_8_ = f32[176,128]{1,0:T(8,128)S(1)} collective-permute-done((f32[176,128]{1,0:T(8,128)S(1)}, f32[176,128]{1,0:T(8,128)S(1)}, u32[]{:S(2)}, u32[]{:S(2)}) %collective-permute-start.5) | collective-permute-done | bytes 90144 | tf_op jit(solution)/shard_map/ppermute | solution.py:451
  18.7 0.1 collective-permute-start.8
  18.8 1.2 %collective-permute-done.8.core = f32[40,128]{1,0:T(8,128)S(1)} collective-permute-done((f32[40,128]{1,0:T(8,128)S(1)}, f32[40,128]{1,0:T(8,128)S(1)}, u32[]{:S(2)}, u32[]{:S(2)}) %collective-permute-start.8) | collective-permute-done | bytes 20512 | tf_op jit(solution)/shard_map/ppermute | solution.py:451
  20.0 1.7 %collective-permute-start.11 = (f32[136,128]{1,0:T(8,128)S(1)}, f32[136,128]{1,0:T(8,128)S(1)}, u32[]{:S(2)}, u32[]{:S(2)}) collective-permute-start(f32[136,128]{1,0:T(8,128)S(1)} %window.1.refs_11_), channel_id=1, source_target_pairs={{0,3},{1,2},{2,1},{3,0},{4,7},{5,6},{6,5},{7,4},{8,11},{9,10},{10,... | collective-permute-start | bytes 208904 | tf_op jit(solution)/shard_map/ppermute | solution.py:451
  21.6 1.7 %collective-permute-start.10 = (f32[136,128]{1,0:T(8,128)S(1)}, f32[136,128]{1,0:T(8,128)S(1)}, u32[]{:S(2)}, u32[]{:S(2)}) collective-permute-start(f32[136,128]{1,0:T(8,128)S(1)} %window.1.refs_11_), channel_id=1, source_target_pairs={{0,2},{1,3},{2,0},{3,1},{4,6},{5,7},{6,4},{7,5},{8,10},{9,11},{10,... | collective-permute-start | bytes 208904 | tf_op jit(solution)/shard_map/ppermute | solution.py:451
  23.4 0.2 collective-permute-start.9
  23.5 1.8 %collective-permute-done.11.refs_14_ = f32[136,128]{1,0:T(8,128)S(1)} collective-permute-done((f32[136,128]{1,0:T(8,128)S(1)}, f32[136,128]{1,0:T(8,128)S(1)}, u32[]{:S(2)}, u32[]{:S(2)}) %collective-permute-start.11) | collective-permute-done | bytes 69664 | tf_op jit(solution)/shard_map/ppermute | solution.py:451
  25.3 1.4 %collective-permute-done.10.refs_13_ = f32[136,128]{1,0:T(8,128)S(1)} collective-permute-done((f32[136,128]{1,0:T(8,128)S(1)}, f32[136,128]{1,0:T(8,128)S(1)}, u32[]{:S(2)}, u32[]{:S(2)}) %collective-permute-start.10) | collective-permute-done | bytes 69664 | tf_op jit(solution)/shard_map/ppermute | solution.py:451
  26.7 1.0 %collective-permute-done.9.refs_12_ = f32[136,128]{1,0:T(8,128)S(1)} collective-permute-done((f32[136,128]{1,0:T(8,128)S(1)}, f32[136,128]{1,0:T(8,128)S(1)}, u32[]{:S(2)}, u32[]{:S(2)}) %collective-permute-start.9) | collective-permute-done | bytes 69664 | tf_op jit(solution)/shard_map/ppermute | solution.py:451
  27.7 2.3 %finish.1 = (f32[16,16,512]{2,1,0:T(8,128)}, f32[4,16,128]{2,1,0:T(8,128)}) custom-call(f32[16,16,512]{2,1,0:T(8,128)S(1)} %get-tuple-element.35.f.refs_0_, f32[16,16,512]{2,1,0:T(8,128)S(1)} %get-tuple-element.36.g.refs_1_, f32[16,16,512]{2,1,0:T(8,128)S(1)} %get-tuple-element.43.s.refs_2_, f32[128,128]{1,0:T(8,128)S(1)} %collective-permute-done.core.refs_3_, ...), custom_call_target="tpu_custom_call" | custom-call | tf_op jit(solution)/shard_map/finish/pallas_call | solution.py:22
  (19 shorter events, 0.1 us)
Async XLA Ops:
  0.6 7.7 %copy-start = (f32[16,16,512]{2,1,0:T(8,128)S(1)}, f32[16,16,512]{2,1,0:T(8,128)}, u32[]{:S(2)}) copy-start(f32[16,16,512]{2,1,0:T(8,128)} %source.1) | copy-start | bytes 1572868
  0.6 7.7 %copy-start.1 = (f32[16,16,512]{2,1,0:T(8,128)S(1)}, f32[16,16,512]{2,1,0:T(8,128)}, u32[]{:S(2)}) copy-start(f32[16,16,512]{2,1,0:T(8,128)} %reaction.1) | copy-start | bytes 1572868
  0.7 7.7 %copy-start.2 = (s32[16,16,512]{2,1,0:T(8,128)S(1)}, s32[16,16,512]{2,1,0:T(8,128)}, u32[]{:S(2)}) copy-start(s32[16,16,512]{2,1,0:T(8,128)} %kind.1) | copy-start | bytes 1572868
  0.7 7.7 %copy-start.3 = (s32[16,16,512]{2,1,0:T(8,128)S(1)}, s32[16,16,512]{2,1,0:T(8,128)}, u32[]{:S(2)}) copy-start(s32[16,16,512]{2,1,0:T(8,128)} %disk_id.1) | copy-start | bytes 1572868
  0.7 7.7 %copy-start.4 = (s32[16,16,512]{2,1,0:T(8,128)S(1)}, s32[16,16,512]{2,1,0:T(8,128)}, u32[]{:S(2)}) copy-start(s32[16,16,512]{2,1,0:T(8,128)} %disk_mask.1) | copy-start | bytes 1572868
  2.3 8.8 %collective-permute-start = (f32[128,128]{1,0:T(8,128)S(1)}, f32[128,128]{1,0:T(8,128)S(1)}, u32[]{:S(2)}, u32[]{:S(2)}) collective-permute-start(f32[128,128]{1,0:T(8,128)S(1)} %get-tuple-element.27), channel_id=1, source_target_pairs={{0,4},{1,5},{2,6},{3,7},{4,0},{5,1},{6,2},{7,3},{8,12},{9,13},{10,... | collective-permute-start | bytes 196616 | tf_op jit(solution)/shard_map/ppermute | solution.py:451
  2.8 8.2 %collective-permute-start.1 = (f32[128,128]{1,0:T(8,128)S(1)}, f32[128,128]{1,0:T(8,128)S(1)}, u32[]{:S(2)}, u32[]{:S(2)}) collective-permute-start(f32[128,128]{1,0:T(8,128)S(1)} %get-tuple-element.28), channel_id=1, source_target_pairs={{0,1},{1,0},{2,3},{3,2},{4,8},{5,9},{6,10},{7,11},{8,4},{9,5},{10,... | collective-permute-start | bytes 196616 | tf_op jit(solution)/shard_map/ppermute | solution.py:451
  5.4 3.0 %copy-start.5 = (f32[120]{0:T(128)S(1)}, f32[120]{0:T(128)}, u32[]{:S(2)}) copy-start(f32[120]{0:T(128)} %param.11) | copy-start | bytes 1444
  5.4 4.8 %collective-permute-start.2 = (f32[64,128]{1,0:T(8,128)S(1)}, f32[64,128]{1,0:T(8,128)S(1)}, u32[]{:S(2)}, u32[]{:S(2)}) collective-permute-start(f32[64,128]{1,0:T(8,128)S(1)} %get-tuple-element.29), channel_id=1, source_target_pairs={{0,3},{1,2},{2,1},{3,0},{4,7},{5,6},{6,5},{7,4},{8,11},{9,10},{10,... | collective-permute-start | bytes 98312 | tf_op jit(solution)/shard_map/ppermute | solution.py:451
  6.9 4.2 %collective-permute-start.3 = (f32[64,128]{1,0:T(8,128)S(1)}, f32[64,128]{1,0:T(8,128)S(1)}, u32[]{:S(2)}, u32[]{:S(2)}) collective-permute-start(f32[64,128]{1,0:T(8,128)S(1)} %get-tuple-element.30), channel_id=1, source_target_pairs={{0,1},{1,0},{2,3},{3,2},{4,5},{5,4},{6,7},{7,6},{8,9},{9,8},{10,11... | collective-permute-start | bytes 98312 | tf_op jit(solution)/shard_map/ppermute | solution.py:451
  12.5 1.3 %collective-permute-start.4 = (f32[136,128]{1,0:T(8,128)S(1)}, f32[136,128]{1,0:T(8,128)S(1)}, u32[]{:S(2)}, u32[]{:S(2)}) collective-permute-start(f32[136,128]{1,0:T(8,128)S(1)} %get-tuple-element.44), channel_id=1, source_target_pairs={{0,4},{1,5},{2,6},{3,7},{4,0},{5,1},{6,2},{7,3},{8,12},{9,13},{10,... | collective-permute-start | bytes 208904 | tf_op jit(solution)/shard_map/ppermute | solution.py:451
  13.8 4.9 %collective-permute-start.5 = (f32[176,128]{1,0:T(8,128)S(1)}, f32[176,128]{1,0:T(8,128)S(1)}, u32[]{:S(2)}, u32[]{:S(2)}) collective-permute-start(f32[176,128]{1,0:T(8,128)S(1)} %get-tuple-element.46), channel_id=1, source_target_pairs={{0,1},{1,0},{2,3},{3,2},{4,8},{5,9},{6,10},{7,11},{8,4},{9,5},{10,... | collective-permute-start | bytes 270344 | tf_op jit(solution)/shard_map/ppermute | solution.py:451
  15.1 8.4 %collective-permute-start.6 = (f32[192,128]{1,0:T(8,128)S(1)}, f32[192,128]{1,0:T(8,128)S(1)}, u32[]{:S(2)}, u32[]{:S(2)}) collective-permute-start(f32[192,128]{1,0:T(8,128)S(1)} %get-tuple-element.47), channel_id=1, source_target_pairs={{0,1},{1,0},{2,3},{3,2},{4,5},{5,4},{6,7},{7,6},{8,9},{9,8},{10,11... | collective-permute-start | bytes 294920 | tf_op jit(solution)/shard_map/ppermute | solution.py:451
  15.9 7.6 %collective-permute-start.7 = (f32[192,128]{1,0:T(8,128)S(1)}, f32[192,128]{1,0:T(8,128)S(1)}, u32[]{:S(2)}, u32[]{:S(2)}) collective-permute-start(f32[192,128]{1,0:T(8,128)S(1)} %get-tuple-element.48), channel_id=1, source_target_pairs={{0,3},{1,2},{2,1},{3,0},{4,7},{5,6},{6,5},{7,4},{8,11},{9,10},{10,... | collective-permute-start | bytes 294920 | tf_op jit(solution)/shard_map/ppermute | solution.py:451
  18.7 1.3 %collective-permute-start.8 = (f32[40,128]{1,0:T(8,128)S(1)}, f32[40,128]{1,0:T(8,128)S(1)}, u32[]{:S(2)}, u32[]{:S(2)}) collective-permute-start(f32[40,128]{1,0:T(8,128)S(1)} %get-tuple-element.50.full), channel_id=1, source_target_pairs={{0,4},{1,5},{2,6},{3,7},{4,0},{5,1},{6,2},{7,3},{8,12},{9,13},{10,... | collective-permute-start | bytes 61448 | tf_op jit(solution)/shard_map/ppermute | solution.py:451
  20.0 5.3 %collective-permute-start.11 = (f32[136,128]{1,0:T(8,128)S(1)}, f32[136,128]{1,0:T(8,128)S(1)}, u32[]{:S(2)}, u32[]{:S(2)}) collective-permute-start(f32[136,128]{1,0:T(8,128)S(1)} %window.1.refs_11_), channel_id=1, source_target_pairs={{0,3},{1,2},{2,1},{3,0},{4,7},{5,6},{6,5},{7,4},{8,11},{9,10},{10,... | collective-permute-start | bytes 208904 | tf_op jit(solution)/shard_map/ppermute | solution.py:451
  21.6 5.0 %collective-permute-start.10 = (f32[136,128]{1,0:T(8,128)S(1)}, f32[136,128]{1,0:T(8,128)S(1)}, u32[]{:S(2)}, u32[]{:S(2)}) collective-permute-start(f32[136,128]{1,0:T(8,128)S(1)} %window.1.refs_11_), channel_id=1, source_target_pairs={{0,2},{1,3},{2,0},{3,1},{4,6},{5,7},{6,4},{7,5},{8,10},{9,11},{10,... | collective-permute-start | bytes 208904 | tf_op jit(solution)/shard_map/ppermute | solution.py:451
  23.4 4.3 %collective-permute-start.9 = (f32[136,128]{1,0:T(8,128)S(1)}, f32[136,128]{1,0:T(8,128)S(1)}, u32[]{:S(2)}, u32[]{:S(2)}) collective-permute-start(f32[136,128]{1,0:T(8,128)S(1)} %window.1.refs_11_), channel_id=1, source_target_pairs={{0,1},{1,0},{2,3},{3,2},{4,5},{5,4},{6,7},{7,6},{8,9},{9,8},{10,11... | collective-permute-start | bytes 208904 | tf_op jit(solution)/shard_map/ppermute | solution.py:451

commit v6 on v5

--- a/solution.py
+++ b/solution.py
@@ -185,14 +185,11 @@
             move.start()
         for move in moves:
             move.wait()
-        found = [first_of(*(buffer[j] for buffer in buffers), table[...])[:2] for j in range(4)]
-        (low, _), (high, _), (f_far, g_far), (f_near, g_near) = found
+        low, high, f_far, f_near = (first_of(*(buffer[j] for buffer in buffers), table[...])[0] for j in range(4))
         put(row, 0, jnp.where(y_even, high, low))
         put(odd, 0, jnp.where(y_even, low, high))
         put(chip, 0, f_far)
-        put(chip, 64, g_far)
         put(core, 0, f_near)
-        put(core, 64, g_near)
 
     def set_up(source, reaction, kind, disk_id, disk_mask, table, f, g, d, absorb):
         for k in range(4):
@@ -256,42 +253,44 @@
         block[...] = dot(picked, group_lanes(512))
         put(to_core, 0, s[jnp.where(x_even, 15, 0)])
         put(to_core, 64, s[jnp.where(x_even, 14, 1)])
-        to_core[128:132, :] = jnp.where(x_even, block[36:40, :], block[32:36, :])
-        to_core[132:136, :] = jnp.zeros((4, 128), F32)
+        put(to_core, 128, g[jnp.where(x_even, 15, 0)])
+        to_core[192:196, :] = jnp.where(x_even, block[36:40, :], block[32:36, :])
+        to_core[196:200, :] = jnp.zeros((4, 128), F32)
         for at, (low, high) in enumerate(((y0, y15), (y1, y14), (g0, g15))):
             a, b = low[...], high[...]
             put(to_row, 64 * at, jnp.where(y_even, b, a))
             put(to_odd, 64 * at, jnp.where(y_even, a, b))
 
-    def to_chip_kernel(block, core, s, mine, to_chip):
+    def to_chip_kernel(block, core, s, g, mine, to_chip):
         _, _, x_even, _ = where_am_i()
         mine[...] = jnp.concatenate([block[0:32, :], block[40:48, :]], axis=0)
-        face = core[128:136, :]
+        face = core[192:200, :]
         for cy in range(4):
             line = face[cy : cy + 1, :]
             mine[8 * cy : 8 * cy + 1, :] = block[8 * cy : 8 * cy + 1, :] + jnp.where(x_even, 0.0, line)
             mine[8 * cy + 3 : 8 * cy + 4, :] = block[8 * cy + 3 : 8 * cy + 4, :] + jnp.where(x_even, line, 0.0)
         put(to_chip, 0, s[jnp.where(x_even, 0, 15)])
         put(to_chip, 64, s[jnp.where(x_even, 1, 14)])
-        to_chip[128:168, :] = mine[...]
-        to_chip[168:172, :] = jnp.where(x_even, block[32:36, :], block[36:40, :])
-        to_chip[172:176, :] = jnp.zeros((4, 128), F32)
+        put(to_chip, 128, g[jnp.where(x_even, 0, 15)])
+        to_chip[192:232, :] = mine[...]
+        to_chip[232:236, :] = jnp.where(x_even, block[32:36, :], block[36:40, :])
+        to_chip[236:240, :] = jnp.zeros((4, 128), F32)
 
     def from_chip_kernel(mine, block, chip, full, beyond):
         x_at, _, x_even, _ = where_am_i()
         has = jnp.where(x_even, x_at > 0, x_at < nx - 1)
         full[...] = mine[...]
-        beyond[...] = chip[128:168, :]
+        beyond[...] = chip[192:232, :]
         mine_face = jnp.where(x_even, block[32:36, :], block[36:40, :])
-        face = chip[168:176, :]
+        face = chip[232:240, :]
         for cy in range(4):
             line = jnp.where(has, face[cy : cy + 1, :], 0.0)
             own = mine_face[cy : cy + 1, :]
             a, b = 8 * cy, 8 * cy + 3
             full[a : a + 1, :] = mine[a : a + 1, :] + jnp.where(x_even, line, 0.0)
             full[b : b + 1, :] = mine[b : b + 1, :] + jnp.where(x_even, 0.0, line)
-            beyond[a : a + 1, :] = chip[128 + a : 129 + a, :] + jnp.where(x_even, 0.0, own)
-            beyond[b : b + 1, :] = chip[128 + b : 129 + b, :] + jnp.where(x_even, own, 0.0)
+            beyond[a : a + 1, :] = chip[192 + a : 193 + a, :] + jnp.where(x_even, 0.0, own)
+            beyond[b : b + 1, :] = chip[192 + b : 193 + b, :] + jnp.where(x_even, own, 0.0)
 
     def window_kernel(full, beyond, core, chip, s_core, s, window):
         x_at, _, x_even, _ = where_am_i()
@@ -408,7 +407,7 @@
                 ref[at : at + 1, :] = corner + spread_lanes(sol[plane, cx : cx + 1, :])
 
         f_left, f_right = halo_x(a_core, a_chip, 0, x_at, x_even)
-        g_left, g_right = halo_x(a_core, a_chip, 64, x_at, x_even)
+        g_left, g_right = halo_x(s_core, s_chip, 128, x_at, x_even)
 
         def fourth_at(at, forcing, scale):
             here = T[at + 1]
@@ -455,7 +454,7 @@
         some = (4, 16, 512)
         core, chip, row, odd = call(
             faces,
-            [(128, 128), (128, 128), (64, 128), (64, 128)],
+            [(64, 128)] * 4,
             *(pltpu.with_memory_space_constraint(array, pltpu.HBM) for array in inputs),
             in_specs=[HBM] * 6,
             scratch=[some, some]
@@ -466,19 +465,19 @@
         a_core, a_chip = swap(core, core_pairs), swap(chip, chip_pairs)
         a_odd, a_row = swap(odd, odd_pairs), swap(row, row_pairs[0])
         f, g, d, absorb = call(set_up, [field, field, field, (64, 512)], *inputs, name="set_up")
-        a_core, a_chip, a_odd, a_row, f, g, d, absorb = lax.optimization_barrier(
-            (a_core, a_chip, a_odd, a_row, f, g, d, absorb)
+        a_odd, a_row, a_chip, a_core, f, g, d, absorb = lax.optimization_barrier(
+            (a_odd, a_row, a_chip, a_core, f, g, d, absorb)
         )
         s, to_core, to_row, to_odd, block = call(
             smooth,
-            [field, (136, 128), (192, 128), (192, 128), (48, 128)],
+            [field, (200, 128), (192, 128), (192, 128), (48, 128)],
             f, g, d, absorb, a_core, a_chip, a_row, a_odd,
             scratch=[slab, slab, (192, 512), slab, slab, slab, slab, slab, slab],
             name="smooth",
         )
         s_core = swap(to_core, core_pairs)
         s_row, s_odd = swap(to_row, row_pairs[0]), swap(to_odd, odd_pairs)
-        mine, to_chip = call(to_chip_kernel, [(40, 128), (176, 128)], block, s_core, s, name="to_chip")
+        mine, to_chip = call(to_chip_kernel, [(40, 128), (240, 128)], block, s_core, s, g, name="to_chip")
         s_chip = swap(to_chip, chip_pairs)
         full, beyond = call(from_chip_kernel, [(40, 128), (40, 128)], mine, block, s_chip, name="from_chip")
         c_core = swap(full, core_pairs)

time: 30.1 us -> 30.7 us (1.020)
  starting transfers between devices: 13 us -> 13.4 us
    ppermute x12, starting transfers between devices: 13 us -> 13.4 us  [swap(): return lax.ppermute(array, axes, pairs)]
where the time goes in v6:
time: 30.7 us; the launch traced here: 30.5 us
  starting transfers between devices  13.4 us (44%)
  waiting for transfers between devices  10.6 us (35%)
  Pallas kernels  5.78 us (19%)
  between operations  0.75 us (2%)
    ppermute x12, starting transfers between devices, swap(): return lax.ppermute(array, axes, pairs)  13.4 us
    ppermute x12, waiting for transfers between devices, swap(): return lax.ppermute(array, axes, pairs)  10.6 us
    pallas_call x7, Pallas kernels, call(): pl.pallas_call(kernel, out_shape=[jax.ShapeDtypeStruct(s, F32) for s in o...  5.78 us
  transfers between devices with their start and end apart: 12, of which 8 were waited for; matrix products, arithmetic and copies ran while one was open for 0% of the time, Pallas kernels for 2%

profile of v6, /device:TPU:0, one launch (start us, length us, event | category | flops | bytes accessed | tf_op | source)
XLA Modules:
  0.0 30.5 jit_solution(7469147174772918961)
XLA Ops:
  0.7 1.6 %faces.1 = (f32[64,128]{1,0:T(8,128)S(1)}, f32[64,128]{1,0:T(8,128)S(1)}, f32[64,128]{1,0:T(8,128)S(1)}, f32[64,128]{1,0:T(8,128)S(1)}) custom-call(f32[16,16,512]{2,1,0:T(8,128)} %source.1, f32[16,16,512]{2,1,0:T(8,128)} %reaction.1, s32[16,16,512]{2,1,0:T(8,128)} %kind.1, s32[16,16,512]{2,1,0:T(8,128)} %disk_id.1, s32[16,16,512]{2,1,0:T(8,128)} %disk_mask.1, ...), custom_call_target="tpu_custom_call" | custom-call | tf_op jit(solution)/shard_map/faces/pallas_call | solution.py:22
  2.3 4.0 %collective-permute-start = (f32[64,128]{1,0:T(8,128)S(1)}, f32[64,128]{1,0:T(8,128)S(1)}, u32[]{:S(2)}, u32[]{:S(2)}) collective-permute-start(f32[64,128]{1,0:T(8,128)S(1)} %get-tuple-element.27), channel_id=1, source_target_pairs={{0,3},{1,2},{2,1},{3,0},{4,7},{5,6},{6,5},{7,4},{8,11},{9,10},{10,... | collective-permute-start | bytes 98312 | tf_op jit(solution)/shard_map/ppermute | solution.py:450
  6.2 0.5 %collective-permute-start.1 = (f32[64,128]{1,0:T(8,128)S(1)}, f32[64,128]{1,0:T(8,128)S(1)}, u32[]{:S(2)}, u32[]{:S(2)}) collective-permute-start(f32[64,128]{1,0:T(8,128)S(1)} %get-tuple-element.28), channel_id=1, source_target_pairs={{0,1},{1,0},{2,3},{3,2},{4,5},{5,4},{6,7},{7,6},{8,9},{9,8},{10,11... | collective-permute-start | bytes 98312 | tf_op jit(solution)/shard_map/ppermute | solution.py:450
  6.8 1.5 %collective-permute-start.2 = (f32[64,128]{1,0:T(8,128)S(1)}, f32[64,128]{1,0:T(8,128)S(1)}, u32[]{:S(2)}, u32[]{:S(2)}) collective-permute-start(f32[64,128]{1,0:T(8,128)S(1)} %get-tuple-element.29), channel_id=1, source_target_pairs={{0,1},{1,0},{2,3},{3,2},{4,8},{5,9},{6,10},{7,11},{8,4},{9,5},{10,... | collective-permute-start | bytes 98312 | tf_op jit(solution)/shard_map/ppermute | solution.py:450
  8.3 0.2 collective-permute-start.3
  8.5 0.5 %set_up.1 = (f32[16,16,512]{2,1,0:T(8,128)S(1)}, f32[16,16,512]{2,1,0:T(8,128)S(1)}, f32[16,16,512]{2,1,0:T(8,128)S(1)}, f32[64,512]{1,0:T(8,128)S(1)}) custom-call(f32[16,16,512]{2,1,0:T(8,128)S(1)} %copy-done, f32[16,16,512]{2,1,0:T(8,128)S(1)} %copy-done.1, s32[16,16,512]{2,1,0:T(8,128)S(1)} %copy-done.2, s32[16,16,512]{2,1,0:T(8,128)S(1)} %copy-done.3, ...), custom_call_target="tpu_custom_call" | custom-call | tf_op jit(solution)/shard_map/set_up/pallas_call | solution.py:22
  9.0 1.2 %collective-permute-done.1.row.refs_5_ = f32[64,128]{1,0:T(8,128)S(1)} collective-permute-done((f32[64,128]{1,0:T(8,128)S(1)}, f32[64,128]{1,0:T(8,128)S(1)}, u32[]{:S(2)}, u32[]{:S(2)}) %collective-permute-start.1) | collective-permute-done | bytes 32800 | tf_op jit(solution)/shard_map/ppermute | solution.py:450
  10.2 0.5 %collective-permute-done.2.chip.refs_4_ = f32[64,128]{1,0:T(8,128)S(1)} collective-permute-done((f32[64,128]{1,0:T(8,128)S(1)}, f32[64,128]{1,0:T(8,128)S(1)}, u32[]{:S(2)}, u32[]{:S(2)}) %collective-permute-start.2) | collective-permute-done | bytes 32800 | tf_op jit(solution)/shard_map/ppermute | solution.py:450
  10.7 1.4 %smooth.1 = (f32[16,16,512]{2,1,0:T(8,128)S(1)}, f32[200,128]{1,0:T(8,128)S(1)}, f32[192,128]{1,0:T(8,128)S(1)}, f32[192,128]{1,0:T(8,128)S(1)}, f32[48,128]{1,0:T(8,128)S(1)}) custom-call(f32[16,16,512]{2,1,0:T(8,128)S(1)} %get-tuple-element.35.f.refs_0_, f32[16,16,512]{2,1,0:T(8,128)S(1)} %get-tuple-element.36.g.refs_1_, ...), custom_call_target="tpu_custom_call" | custom-call | tf_op jit(solution)/shard_map/smooth/pallas_call | solution.py:22
  12.1 0.1 collective-permute-start.4
  12.2 1.3 %collective-permute-done.4.core.s_core.refs_7_ = f32[200,128]{1,0:T(8,128)S(1)} collective-permute-done((f32[200,128]{1,0:T(8,128)S(1)}, f32[200,128]{1,0:T(8,128)S(1)}, u32[]{:S(2)}, u32[]{:S(2)}) %collective-permute-start.4) | collective-permute-done | bytes 102432 | tf_op jit(solution)/shard_map/ppermute | solution.py:450
  13.5 1.6 %collective-permute-start.5 = (f32[240,128]{1,0:T(8,128)S(1)}, f32[240,128]{1,0:T(8,128)S(1)}, u32[]{:S(2)}, u32[]{:S(2)}) collective-permute-start(f32[240,128]{1,0:T(8,128)S(1)} %get-tuple-element.46), channel_id=1, source_target_pairs={{0,1},{1,0},{2,3},{3,2},{4,8},{5,9},{6,10},{7,11},{8,4},{9,5},{10,... | collective-permute-start | bytes 368648 | tf_op jit(solution)/shard_map/ppermute | solution.py:450
  15.0 0.5 %collective-permute-start.6 = (f32[192,128]{1,0:T(8,128)S(1)}, f32[192,128]{1,0:T(8,128)S(1)}, u32[]{:S(2)}, u32[]{:S(2)}) collective-permute-start(f32[192,128]{1,0:T(8,128)S(1)} %get-tuple-element.47), channel_id=1, source_target_pairs={{0,1},{1,0},{2,3},{3,2},{4,5},{5,4},{6,7},{7,6},{8,9},{9,8},{10,11... | collective-permute-start | bytes 294920 | tf_op jit(solution)/shard_map/ppermute | solution.py:450
  15.6 1.4 %collective-permute-start.7 = (f32[192,128]{1,0:T(8,128)S(1)}, f32[192,128]{1,0:T(8,128)S(1)}, u32[]{:S(2)}, u32[]{:S(2)}) collective-permute-start(f32[192,128]{1,0:T(8,128)S(1)} %get-tuple-element.48), channel_id=1, source_target_pairs={{0,3},{1,2},{2,1},{3,0},{4,7},{5,6},{6,5},{7,4},{8,11},{9,10},{10,... | collective-permute-start | bytes 294920 | tf_op jit(solution)/shard_map/ppermute | solution.py:450
  17.0 2.5 %collective-permute-done.5.chip.refs_8_ = f32[240,128]{1,0:T(8,128)S(1)} collective-permute-done((f32[240,128]{1,0:T(8,128)S(1)}, f32[240,128]{1,0:T(8,128)S(1)}, u32[]{:S(2)}, u32[]{:S(2)}) %collective-permute-start.5) | collective-permute-done | bytes 122912 | tf_op jit(solution)/shard_map/ppermute | solution.py:450
  19.6 0.1 collective-permute-start.8
  19.7 1.2 %collective-permute-done.8.core = f32[40,128]{1,0:T(8,128)S(1)} collective-permute-done((f32[40,128]{1,0:T(8,128)S(1)}, f32[40,128]{1,0:T(8,128)S(1)}, u32[]{:S(2)}, u32[]{:S(2)}) %collective-permute-start.8) | collective-permute-done | bytes 20512 | tf_op jit(solution)/shard_map/ppermute | solution.py:450
  20.9 1.5 %collective-permute-start.11 = (f32[136,128]{1,0:T(8,128)S(1)}, f32[136,128]{1,0:T(8,128)S(1)}, u32[]{:S(2)}, u32[]{:S(2)}) collective-permute-start(f32[136,128]{1,0:T(8,128)S(1)} %window.1.refs_11_), channel_id=1, source_target_pairs={{0,3},{1,2},{2,1},{3,0},{4,7},{5,6},{6,5},{7,4},{8,11},{9,10},{10,... | collective-permute-start | bytes 208904 | tf_op jit(solution)/shard_map/ppermute | solution.py:450
  22.4 1.5 %collective-permute-start.10 = (f32[136,128]{1,0:T(8,128)S(1)}, f32[136,128]{1,0:T(8,128)S(1)}, u32[]{:S(2)}, u32[]{:S(2)}) collective-permute-start(f32[136,128]{1,0:T(8,128)S(1)} %window.1.refs_11_), channel_id=1, source_target_pairs={{0,2},{1,3},{2,0},{3,1},{4,6},{5,7},{6,4},{7,5},{8,10},{9,11},{10,... | collective-permute-start | bytes 208904 | tf_op jit(solution)/shard_map/ppermute | solution.py:450
  23.9 0.5 %collective-permute-start.9 = (f32[136,128]{1,0:T(8,128)S(1)}, f32[136,128]{1,0:T(8,128)S(1)}, u32[]{:S(2)}, u32[]{:S(2)}) collective-permute-start(f32[136,128]{1,0:T(8,128)S(1)} %window.1.refs_11_), channel_id=1, source_target_pairs={{0,1},{1,0},{2,3},{3,2},{4,5},{5,4},{6,7},{7,6},{8,9},{9,8},{10,11... | collective-permute-start | bytes 208904 | tf_op jit(solution)/shard_map/ppermute | solution.py:450
  24.4 1.8 %collective-permute-done.11.refs_14_ = f32[136,128]{1,0:T(8,128)S(1)} collective-permute-done((f32[136,128]{1,0:T(8,128)S(1)}, f32[136,128]{1,0:T(8,128)S(1)}, u32[]{:S(2)}, u32[]{:S(2)}) %collective-permute-start.11) | collective-permute-done | bytes 69664 | tf_op jit(solution)/shard_map/ppermute | solution.py:450
  26.3 1.3 %collective-permute-done.10.refs_13_ = f32[136,128]{1,0:T(8,128)S(1)} collective-permute-done((f32[136,128]{1,0:T(8,128)S(1)}, f32[136,128]{1,0:T(8,128)S(1)}, u32[]{:S(2)}, u32[]{:S(2)}) %collective-permute-start.10) | collective-permute-done | bytes 69664 | tf_op jit(solution)/shard_map/ppermute | solution.py:450
  27.6 0.7 %collective-permute-done.9.refs_12_ = f32[136,128]{1,0:T(8,128)S(1)} collective-permute-done((f32[136,128]{1,0:T(8,128)S(1)}, f32[136,128]{1,0:T(8,128)S(1)}, u32[]{:S(2)}, u32[]{:S(2)}) %collective-permute-start.9) | collective-permute-done | bytes 69664 | tf_op jit(solution)/shard_map/ppermute | solution.py:450
  28.2 2.3 %finish.1 = (f32[16,16,512]{2,1,0:T(8,128)}, f32[4,16,128]{2,1,0:T(8,128)}) custom-call(f32[16,16,512]{2,1,0:T(8,128)S(1)} %get-tuple-element.35.f.refs_0_, f32[16,16,512]{2,1,0:T(8,128)S(1)} %get-tuple-element.36.g.refs_1_, f32[16,16,512]{2,1,0:T(8,128)S(1)} %get-tuple-element.43.s.refs_2_, f32[64,128]{1,0:T(8,128)S(1)} %collective-permute-done.3.core.refs_3_, ...), custom_call_target="tpu_custom_call" | custom-call | tf_op jit(solution)/shard_map/finish/pallas_call | solution.py:22
  (19 shorter events, 0.1 us)
Async XLA Ops:
  0.6 7.8 %copy-start = (f32[16,16,512]{2,1,0:T(8,128)S(1)}, f32[16,16,512]{2,1,0:T(8,128)}, u32[]{:S(2)}) copy-start(f32[16,16,512]{2,1,0:T(8,128)} %source.1) | copy-start | bytes 1572868
  0.6 7.8 %copy-start.1 = (f32[16,16,512]{2,1,0:T(8,128)S(1)}, f32[16,16,512]{2,1,0:T(8,128)}, u32[]{:S(2)}) copy-start(f32[16,16,512]{2,1,0:T(8,128)} %reaction.1) | copy-start | bytes 1572868
  0.7 7.8 %copy-start.2 = (s32[16,16,512]{2,1,0:T(8,128)S(1)}, s32[16,16,512]{2,1,0:T(8,128)}, u32[]{:S(2)}) copy-start(s32[16,16,512]{2,1,0:T(8,128)} %kind.1) | copy-start | bytes 1572868
  0.7 7.8 %copy-start.3 = (s32[16,16,512]{2,1,0:T(8,128)S(1)}, s32[16,16,512]{2,1,0:T(8,128)}, u32[]{:S(2)}) copy-start(s32[16,16,512]{2,1,0:T(8,128)} %disk_id.1) | copy-start | bytes 1572868
  0.7 7.8 %copy-start.4 = (s32[16,16,512]{2,1,0:T(8,128)S(1)}, s32[16,16,512]{2,1,0:T(8,128)}, u32[]{:S(2)}) copy-start(s32[16,16,512]{2,1,0:T(8,128)} %disk_mask.1) | copy-start | bytes 1572868
  2.3 6.7 %collective-permute-start = (f32[64,128]{1,0:T(8,128)S(1)}, f32[64,128]{1,0:T(8,128)S(1)}, u32[]{:S(2)}, u32[]{:S(2)}) collective-permute-start(f32[64,128]{1,0:T(8,128)S(1)} %get-tuple-element.27), channel_id=1, source_target_pairs={{0,3},{1,2},{2,1},{3,0},{4,7},{5,6},{6,5},{7,4},{8,11},{9,10},{10,... | collective-permute-start | bytes 98312 | tf_op jit(solution)/shard_map/ppermute | solution.py:450
  6.2 3.9 %collective-permute-start.1 = (f32[64,128]{1,0:T(8,128)S(1)}, f32[64,128]{1,0:T(8,128)S(1)}, u32[]{:S(2)}, u32[]{:S(2)}) collective-permute-start(f32[64,128]{1,0:T(8,128)S(1)} %get-tuple-element.28), channel_id=1, source_target_pairs={{0,1},{1,0},{2,3},{3,2},{4,5},{5,4},{6,7},{7,6},{8,9},{9,8},{10,11... | collective-permute-start | bytes 98312 | tf_op jit(solution)/shard_map/ppermute | solution.py:450
  6.8 1.7 %copy-start.5 = (f32[120]{0:T(128)S(1)}, f32[120]{0:T(128)}, u32[]{:S(2)}) copy-start(f32[120]{0:T(128)} %param.11) | copy-start | bytes 1444
  6.8 3.9 %collective-permute-start.2 = (f32[64,128]{1,0:T(8,128)S(1)}, f32[64,128]{1,0:T(8,128)S(1)}, u32[]{:S(2)}, u32[]{:S(2)}) collective-permute-start(f32[64,128]{1,0:T(8,128)S(1)} %get-tuple-element.29), channel_id=1, source_target_pairs={{0,1},{1,0},{2,3},{3,2},{4,8},{5,9},{6,10},{7,11},{8,4},{9,5},{10,... | collective-permute-start | bytes 98312 | tf_op jit(solution)/shard_map/ppermute | solution.py:450
  8.3 2.4 %collective-permute-start.3 = (f32[64,128]{1,0:T(8,128)S(1)}, f32[64,128]{1,0:T(8,128)S(1)}, u32[]{:S(2)}, u32[]{:S(2)}) collective-permute-start(f32[64,128]{1,0:T(8,128)S(1)} %get-tuple-element.30), channel_id=1, source_target_pairs={{0,4},{1,5},{2,6},{3,7},{4,0},{5,1},{6,2},{7,3},{8,12},{9,13},{10,... | collective-permute-start | bytes 98312 | tf_op jit(solution)/shard_map/ppermute | solution.py:450
  12.1 1.4 %collective-permute-start.4 = (f32[200,128]{1,0:T(8,128)S(1)}, f32[200,128]{1,0:T(8,128)S(1)}, u32[]{:S(2)}, u32[]{:S(2)}) collective-permute-start(f32[200,128]{1,0:T(8,128)S(1)} %get-tuple-element.44), channel_id=1, source_target_pairs={{0,4},{1,5},{2,6},{3,7},{4,0},{5,1},{6,2},{7,3},{8,12},{9,13},{10,... | collective-permute-start | bytes 307208 | tf_op jit(solution)/shard_map/ppermute | solution.py:450
  13.5 6.1 %collective-permute-start.5 = (f32[240,128]{1,0:T(8,128)S(1)}, f32[240,128]{1,0:T(8,128)S(1)}, u32[]{:S(2)}, u32[]{:S(2)}) collective-permute-start(f32[240,128]{1,0:T(8,128)S(1)} %get-tuple-element.46), channel_id=1, source_target_pairs={{0,1},{1,0},{2,3},{3,2},{4,8},{5,9},{6,10},{7,11},{8,4},{9,5},{10,... | collective-permute-start | bytes 368648 | tf_op jit(solution)/shard_map/ppermute | solution.py:450
  15.0 9.4 %collective-permute-start.6 = (f32[192,128]{1,0:T(8,128)S(1)}, f32[192,128]{1,0:T(8,128)S(1)}, u32[]{:S(2)}, u32[]{:S(2)}) collective-permute-start(f32[192,128]{1,0:T(8,128)S(1)} %get-tuple-element.47), channel_id=1, source_target_pairs={{0,1},{1,0},{2,3},{3,2},{4,5},{5,4},{6,7},{7,6},{8,9},{9,8},{10,11... | collective-permute-start | bytes 294920 | tf_op jit(solution)/shard_map/ppermute | solution.py:450
  15.6 8.8 %collective-permute-start.7 = (f32[192,128]{1,0:T(8,128)S(1)}, f32[192,128]{1,0:T(8,128)S(1)}, u32[]{:S(2)}, u32[]{:S(2)}) collective-permute-start(f32[192,128]{1,0:T(8,128)S(1)} %get-tuple-element.48), channel_id=1, source_target_pairs={{0,3},{1,2},{2,1},{3,0},{4,7},{5,6},{6,5},{7,4},{8,11},{9,10},{10,... | collective-permute-start | bytes 294920 | tf_op jit(solution)/shard_map/ppermute | solution.py:450
  19.6 1.3 %collective-permute-start.8 = (f32[40,128]{1,0:T(8,128)S(1)}, f32[40,128]{1,0:T(8,128)S(1)}, u32[]{:S(2)}, u32[]{:S(2)}) collective-permute-start(f32[40,128]{1,0:T(8,128)S(1)} %get-tuple-element.50.full), channel_id=1, source_target_pairs={{0,4},{1,5},{2,6},{3,7},{4,0},{5,1},{6,2},{7,3},{8,12},{9,13},{10,... | collective-permute-start | bytes 61448 | tf_op jit(solution)/shard_map/ppermute | solution.py:450
  20.9 5.4 %collective-permute-start.11 = (f32[136,128]{1,0:T(8,128)S(1)}, f32[136,128]{1,0:T(8,128)S(1)}, u32[]{:S(2)}, u32[]{:S(2)}) collective-permute-start(f32[136,128]{1,0:T(8,128)S(1)} %window.1.refs_11_), channel_id=1, source_target_pairs={{0,3},{1,2},{2,1},{3,0},{4,7},{5,6},{6,5},{7,4},{8,11},{9,10},{10,... | collective-permute-start | bytes 208904 | tf_op jit(solution)/shard_map/ppermute | solution.py:450
  22.4 5.2 %collective-permute-start.10 = (f32[136,128]{1,0:T(8,128)S(1)}, f32[136,128]{1,0:T(8,128)S(1)}, u32[]{:S(2)}, u32[]{:S(2)}) collective-permute-start(f32[136,128]{1,0:T(8,128)S(1)} %window.1.refs_11_), channel_id=1, source_target_pairs={{0,2},{1,3},{2,0},{3,1},{4,6},{5,7},{6,4},{7,5},{8,10},{9,11},{10,... | collective-permute-start | bytes 208904 | tf_op jit(solution)/shard_map/ppermute | solution.py:450
  23.9 4.3 %collective-permute-start.9 = (f32[136,128]{1,0:T(8,128)S(1)}, f32[136,128]{1,0:T(8,128)S(1)}, u32[]{:S(2)}, u32[]{:S(2)}) collective-permute-start(f32[136,128]{1,0:T(8,128)S(1)} %window.1.refs_11_), channel_id=1, source_target_pairs={{0,1},{1,0},{2,3},{3,2},{4,5},{5,4},{6,7},{7,6},{8,9},{9,8},{10,11... | collective-permute-start | bytes 208904 | tf_op jit(solution)/shard_map/ppermute | solution.py:450

commit v7 on v6

--- a/solution.py
+++ b/solution.py
@@ -39,7 +39,7 @@
     for x in range(nx):
         for y in range(ny):
             if x in (0, nx - 1):
-                found.append((x * ny + y, x * ny + (y ^ 1)))
+                found.append((x * ny + y, x * ny + (y ^ (ny // 2))))
             else:
                 found.append((x * ny + y, (x + 1 if x % 2 else x - 1) * ny + y))
     return found

time: 30.7 us -> 29.5 us (0.961)
  waiting for transfers between devices: 10.6 us -> 9.36 us
    ppermute x12, waiting for transfers between devices: 10.6 us -> 9.36 us  [swap(): return lax.ppermute(array, axes, pairs)]
where the time goes in v7:
time: 29.5 us; the launch traced here: 29.3 us
  starting transfers between devices  13.4 us (45%)
  waiting for transfers between devices  9.36 us (32%)
  Pallas kernels  5.78 us (20%)
  between operations  0.75 us (3%)
    ppermute x12, starting transfers between devices, swap(): return lax.ppermute(array, axes, pairs)  13.4 us
    ppermute x12, waiting for transfers between devices, swap(): return lax.ppermute(array, axes, pairs)  9.36 us
    pallas_call x7, Pallas kernels, call(): pl.pallas_call(kernel, out_shape=[jax.ShapeDtypeStruct(s, F32) for s in o...  5.78 us
  transfers between devices with their start and end apart: 12, of which 8 were waited for; matrix products, arithmetic and copies ran while one was open for 0% of the time, Pallas kernels for 2%

profile of v7, /device:TPU:0, one launch (start us, length us, event | category | flops | bytes accessed | tf_op | source)
XLA Modules:
  0.0 29.3 jit_solution(726730057332800321)
XLA Ops:
  0.7 1.6 %faces.1 = (f32[64,128]{1,0:T(8,128)S(1)}, f32[64,128]{1,0:T(8,128)S(1)}, f32[64,128]{1,0:T(8,128)S(1)}, f32[64,128]{1,0:T(8,128)S(1)}) custom-call(f32[16,16,512]{2,1,0:T(8,128)} %source.1, f32[16,16,512]{2,1,0:T(8,128)} %reaction.1, s32[16,16,512]{2,1,0:T(8,128)} %kind.1, s32[16,16,512]{2,1,0:T(8,128)} %disk_id.1, s32[16,16,512]{2,1,0:T(8,128)} %disk_mask.1, ...), custom_call_target="tpu_custom_call" | custom-call | tf_op jit(solution)/shard_map/faces/pallas_call | solution.py:22
  2.3 4.0 %collective-permute-start = (f32[64,128]{1,0:T(8,128)S(1)}, f32[64,128]{1,0:T(8,128)S(1)}, u32[]{:S(2)}, u32[]{:S(2)}) collective-permute-start(f32[64,128]{1,0:T(8,128)S(1)} %get-tuple-element.27), channel_id=1, source_target_pairs={{0,3},{1,2},{2,1},{3,0},{4,7},{5,6},{6,5},{7,4},{8,11},{9,10},{10,... | collective-permute-start | bytes 98312 | tf_op jit(solution)/shard_map/ppermute | solution.py:450
  6.2 0.5 %collective-permute-start.1 = (f32[64,128]{1,0:T(8,128)S(1)}, f32[64,128]{1,0:T(8,128)S(1)}, u32[]{:S(2)}, u32[]{:S(2)}) collective-permute-start(f32[64,128]{1,0:T(8,128)S(1)} %get-tuple-element.28), channel_id=1, source_target_pairs={{0,1},{1,0},{2,3},{3,2},{4,5},{5,4},{6,7},{7,6},{8,9},{9,8},{10,11... | collective-permute-start | bytes 98312 | tf_op jit(solution)/shard_map/ppermute | solution.py:450
  6.8 0.1 collective-permute-start.2
  6.9 1.6 %collective-permute-start.3 = (f32[64,128]{1,0:T(8,128)S(1)}, f32[64,128]{1,0:T(8,128)S(1)}, u32[]{:S(2)}, u32[]{:S(2)}) collective-permute-start(f32[64,128]{1,0:T(8,128)S(1)} %get-tuple-element.30), channel_id=1, source_target_pairs={{0,4},{1,5},{2,6},{3,7},{4,0},{5,1},{6,2},{7,3},{8,12},{9,13},{10,... | collective-permute-start | bytes 98312 | tf_op jit(solution)/shard_map/ppermute | solution.py:450
  8.5 0.5 %set_up.1 = (f32[16,16,512]{2,1,0:T(8,128)S(1)}, f32[16,16,512]{2,1,0:T(8,128)S(1)}, f32[16,16,512]{2,1,0:T(8,128)S(1)}, f32[64,512]{1,0:T(8,128)S(1)}) custom-call(f32[16,16,512]{2,1,0:T(8,128)S(1)} %copy-done, f32[16,16,512]{2,1,0:T(8,128)S(1)} %copy-done.1, s32[16,16,512]{2,1,0:T(8,128)S(1)} %copy-done.2, s32[16,16,512]{2,1,0:T(8,128)S(1)} %copy-done.3, ...), custom_call_target="tpu_custom_call" | custom-call | tf_op jit(solution)/shard_map/set_up/pallas_call | solution.py:22
  9.0 1.2 %collective-permute-done.1.row.refs_5_ = f32[64,128]{1,0:T(8,128)S(1)} collective-permute-done((f32[64,128]{1,0:T(8,128)S(1)}, f32[64,128]{1,0:T(8,128)S(1)}, u32[]{:S(2)}, u32[]{:S(2)}) %collective-permute-start.1) | collective-permute-done | bytes 32800 | tf_op jit(solution)/shard_map/ppermute | solution.py:450
  10.2 0.5 %collective-permute-done.2.chip.refs_4_ = f32[64,128]{1,0:T(8,128)S(1)} collective-permute-done((f32[64,128]{1,0:T(8,128)S(1)}, f32[64,128]{1,0:T(8,128)S(1)}, u32[]{:S(2)}, u32[]{:S(2)}) %collective-permute-start.2) | collective-permute-done | bytes 32800 | tf_op jit(solution)/shard_map/ppermute | solution.py:450
  10.7 1.4 %smooth.1 = (f32[16,16,512]{2,1,0:T(8,128)S(1)}, f32[200,128]{1,0:T(8,128)S(1)}, f32[192,128]{1,0:T(8,128)S(1)}, f32[192,128]{1,0:T(8,128)S(1)}, f32[48,128]{1,0:T(8,128)S(1)}) custom-call(f32[16,16,512]{2,1,0:T(8,128)S(1)} %get-tuple-element.35.f.refs_0_, f32[16,16,512]{2,1,0:T(8,128)S(1)} %get-tuple-element.36.g.refs_1_, ...), custom_call_target="tpu_custom_call" | custom-call | tf_op jit(solution)/shard_map/smooth/pallas_call | solution.py:22
  12.1 0.1 collective-permute-start.4
  12.2 1.3 %collective-permute-done.4.core.s_core.refs_7_ = f32[200,128]{1,0:T(8,128)S(1)} collective-permute-done((f32[200,128]{1,0:T(8,128)S(1)}, f32[200,128]{1,0:T(8,128)S(1)}, u32[]{:S(2)}, u32[]{:S(2)}) %collective-permute-start.4) | collective-permute-done | bytes 102432 | tf_op jit(solution)/shard_map/ppermute | solution.py:450
  13.5 0.2 collective-permute-start.5
  13.7 1.9 %collective-permute-start.6 = (f32[192,128]{1,0:T(8,128)S(1)}, f32[192,128]{1,0:T(8,128)S(1)}, u32[]{:S(2)}, u32[]{:S(2)}) collective-permute-start(f32[192,128]{1,0:T(8,128)S(1)} %get-tuple-element.47), channel_id=1, source_target_pairs={{0,1},{1,0},{2,3},{3,2},{4,5},{5,4},{6,7},{7,6},{8,9},{9,8},{10,11... | collective-permute-start | bytes 294920 | tf_op jit(solution)/shard_map/ppermute | solution.py:450
  15.6 1.5 %collective-permute-start.7 = (f32[192,128]{1,0:T(8,128)S(1)}, f32[192,128]{1,0:T(8,128)S(1)}, u32[]{:S(2)}, u32[]{:S(2)}) collective-permute-start(f32[192,128]{1,0:T(8,128)S(1)} %get-tuple-element.48), channel_id=1, source_target_pairs={{0,3},{1,2},{2,1},{3,0},{4,7},{5,6},{6,5},{7,4},{8,11},{9,10},{10,... | collective-permute-start | bytes 294920 | tf_op jit(solution)/shard_map/ppermute | solution.py:450
  17.0 1.4 %collective-permute-done.5.chip.refs_8_ = f32[240,128]{1,0:T(8,128)S(1)} collective-permute-done((f32[240,128]{1,0:T(8,128)S(1)}, f32[240,128]{1,0:T(8,128)S(1)}, u32[]{:S(2)}, u32[]{:S(2)}) %collective-permute-start.5) | collective-permute-done | bytes 122912 | tf_op jit(solution)/shard_map/ppermute | solution.py:450
  18.5 0.1 collective-permute-start.8
  18.5 1.2 %collective-permute-done.8.core = f32[40,128]{1,0:T(8,128)S(1)} collective-permute-done((f32[40,128]{1,0:T(8,128)S(1)}, f32[40,128]{1,0:T(8,128)S(1)}, u32[]{:S(2)}, u32[]{:S(2)}) %collective-permute-start.8) | collective-permute-done | bytes 20512 | tf_op jit(solution)/shard_map/ppermute | solution.py:450
  19.7 1.5 %collective-permute-start.11 = (f32[136,128]{1,0:T(8,128)S(1)}, f32[136,128]{1,0:T(8,128)S(1)}, u32[]{:S(2)}, u32[]{:S(2)}) collective-permute-start(f32[136,128]{1,0:T(8,128)S(1)} %window.1.refs_11_), channel_id=1, source_target_pairs={{0,3},{1,2},{2,1},{3,0},{4,7},{5,6},{6,5},{7,4},{8,11},{9,10},{10,... | collective-permute-start | bytes 208904 | tf_op jit(solution)/shard_map/ppermute | solution.py:450
  21.2 1.5 %collective-permute-start.10 = (f32[136,128]{1,0:T(8,128)S(1)}, f32[136,128]{1,0:T(8,128)S(1)}, u32[]{:S(2)}, u32[]{:S(2)}) collective-permute-start(f32[136,128]{1,0:T(8,128)S(1)} %window.1.refs_11_), channel_id=1, source_target_pairs={{0,2},{1,3},{2,0},{3,1},{4,6},{5,7},{6,4},{7,5},{8,10},{9,11},{10,... | collective-permute-start | bytes 208904 | tf_op jit(solution)/shard_map/ppermute | solution.py:450
  22.8 0.5 %collective-permute-start.9 = (f32[136,128]{1,0:T(8,128)S(1)}, f32[136,128]{1,0:T(8,128)S(1)}, u32[]{:S(2)}, u32[]{:S(2)}) collective-permute-start(f32[136,128]{1,0:T(8,128)S(1)} %window.1.refs_11_), channel_id=1, source_target_pairs={{0,1},{1,0},{2,3},{3,2},{4,5},{5,4},{6,7},{7,6},{8,9},{9,8},{10,11... | collective-permute-start | bytes 208904 | tf_op jit(solution)/shard_map/ppermute | solution.py:450
  23.3 1.9 %collective-permute-done.11.refs_14_ = f32[136,128]{1,0:T(8,128)S(1)} collective-permute-done((f32[136,128]{1,0:T(8,128)S(1)}, f32[136,128]{1,0:T(8,128)S(1)}, u32[]{:S(2)}, u32[]{:S(2)}) %collective-permute-start.11) | collective-permute-done | bytes 69664 | tf_op jit(solution)/shard_map/ppermute | solution.py:450
  25.2 1.3 %collective-permute-done.10.refs_13_ = f32[136,128]{1,0:T(8,128)S(1)} collective-permute-done((f32[136,128]{1,0:T(8,128)S(1)}, f32[136,128]{1,0:T(8,128)S(1)}, u32[]{:S(2)}, u32[]{:S(2)}) %collective-permute-start.10) | collective-permute-done | bytes 69664 | tf_op jit(solution)/shard_map/ppermute | solution.py:450
  26.4 0.6 %collective-permute-done.9.refs_12_ = f32[136,128]{1,0:T(8,128)S(1)} collective-permute-done((f32[136,128]{1,0:T(8,128)S(1)}, f32[136,128]{1,0:T(8,128)S(1)}, u32[]{:S(2)}, u32[]{:S(2)}) %collective-permute-start.9) | collective-permute-done | bytes 69664 | tf_op jit(solution)/shard_map/ppermute | solution.py:450
  27.1 2.3 %finish.1 = (f32[16,16,512]{2,1,0:T(8,128)}, f32[4,16,128]{2,1,0:T(8,128)}) custom-call(f32[16,16,512]{2,1,0:T(8,128)S(1)} %get-tuple-element.35.f.refs_0_, f32[16,16,512]{2,1,0:T(8,128)S(1)} %get-tuple-element.36.g.refs_1_, f32[16,16,512]{2,1,0:T(8,128)S(1)} %get-tuple-element.43.s.refs_2_, f32[64,128]{1,0:T(8,128)S(1)} %collective-permute-done.3.core.refs_3_, ...), custom_call_target="tpu_custom_call" | custom-call | tf_op jit(solution)/shard_map/finish/pallas_call | solution.py:22
  (19 shorter events, 0.1 us)
Async XLA Ops:
  0.6 7.8 %copy-start = (f32[16,16,512]{2,1,0:T(8,128)S(1)}, f32[16,16,512]{2,1,0:T(8,128)}, u32[]{:S(2)}) copy-start(f32[16,16,512]{2,1,0:T(8,128)} %source.1) | copy-start | bytes 1572868
  0.6 7.8 %copy-start.1 = (f32[16,16,512]{2,1,0:T(8,128)S(1)}, f32[16,16,512]{2,1,0:T(8,128)}, u32[]{:S(2)}) copy-start(f32[16,16,512]{2,1,0:T(8,128)} %reaction.1) | copy-start | bytes 1572868
  0.7 7.8 %copy-start.2 = (s32[16,16,512]{2,1,0:T(8,128)S(1)}, s32[16,16,512]{2,1,0:T(8,128)}, u32[]{:S(2)}) copy-start(s32[16,16,512]{2,1,0:T(8,128)} %kind.1) | copy-start | bytes 1572868
  0.7 7.8 %copy-start.3 = (s32[16,16,512]{2,1,0:T(8,128)S(1)}, s32[16,16,512]{2,1,0:T(8,128)}, u32[]{:S(2)}) copy-start(s32[16,16,512]{2,1,0:T(8,128)} %disk_id.1) | copy-start | bytes 1572868
  0.7 7.8 %copy-start.4 = (s32[16,16,512]{2,1,0:T(8,128)S(1)}, s32[16,16,512]{2,1,0:T(8,128)}, u32[]{:S(2)}) copy-start(s32[16,16,512]{2,1,0:T(8,128)} %disk_mask.1) | copy-start | bytes 1572868
  2.3 6.7 %collective-permute-start = (f32[64,128]{1,0:T(8,128)S(1)}, f32[64,128]{1,0:T(8,128)S(1)}, u32[]{:S(2)}, u32[]{:S(2)}) collective-permute-start(f32[64,128]{1,0:T(8,128)S(1)} %get-tuple-element.27), channel_id=1, source_target_pairs={{0,3},{1,2},{2,1},{3,0},{4,7},{5,6},{6,5},{7,4},{8,11},{9,10},{10,... | collective-permute-start | bytes 98312 | tf_op jit(solution)/shard_map/ppermute | solution.py:450
  6.2 3.9 %collective-permute-start.1 = (f32[64,128]{1,0:T(8,128)S(1)}, f32[64,128]{1,0:T(8,128)S(1)}, u32[]{:S(2)}, u32[]{:S(2)}) collective-permute-start(f32[64,128]{1,0:T(8,128)S(1)} %get-tuple-element.28), channel_id=1, source_target_pairs={{0,1},{1,0},{2,3},{3,2},{4,5},{5,4},{6,7},{7,6},{8,9},{9,8},{10,11... | collective-permute-start | bytes 98312 | tf_op jit(solution)/shard_map/ppermute | solution.py:450
  6.8 1.7 %copy-start.5 = (f32[120]{0:T(128)S(1)}, f32[120]{0:T(128)}, u32[]{:S(2)}) copy-start(f32[120]{0:T(128)} %param.11) | copy-start | bytes 1444
  6.8 3.9 %collective-permute-start.2 = (f32[64,128]{1,0:T(8,128)S(1)}, f32[64,128]{1,0:T(8,128)S(1)}, u32[]{:S(2)}, u32[]{:S(2)}) collective-permute-start(f32[64,128]{1,0:T(8,128)S(1)} %get-tuple-element.29), channel_id=1, source_target_pairs={{0,2},{1,3},{2,0},{3,1},{4,8},{5,9},{6,10},{7,11},{8,4},{9,5},{10,... | collective-permute-start | bytes 98312 | tf_op jit(solution)/shard_map/ppermute | solution.py:450
  6.9 3.8 %collective-permute-start.3 = (f32[64,128]{1,0:T(8,128)S(1)}, f32[64,128]{1,0:T(8,128)S(1)}, u32[]{:S(2)}, u32[]{:S(2)}) collective-permute-start(f32[64,128]{1,0:T(8,128)S(1)} %get-tuple-element.30), channel_id=1, source_target_pairs={{0,4},{1,5},{2,6},{3,7},{4,0},{5,1},{6,2},{7,3},{8,12},{9,13},{10,... | collective-permute-start | bytes 98312 | tf_op jit(solution)/shard_map/ppermute | solution.py:450
  12.1 1.4 %collective-permute-start.4 = (f32[200,128]{1,0:T(8,128)S(1)}, f32[200,128]{1,0:T(8,128)S(1)}, u32[]{:S(2)}, u32[]{:S(2)}) collective-permute-start(f32[200,128]{1,0:T(8,128)S(1)} %get-tuple-element.44), channel_id=1, source_target_pairs={{0,4},{1,5},{2,6},{3,7},{4,0},{5,1},{6,2},{7,3},{8,12},{9,13},{10,... | collective-permute-start | bytes 307208 | tf_op jit(solution)/shard_map/ppermute | solution.py:450
  13.5 4.9 %collective-permute-start.5 = (f32[240,128]{1,0:T(8,128)S(1)}, f32[240,128]{1,0:T(8,128)S(1)}, u32[]{:S(2)}, u32[]{:S(2)}) collective-permute-start(f32[240,128]{1,0:T(8,128)S(1)} %get-tuple-element.46), channel_id=1, source_target_pairs={{0,2},{1,3},{2,0},{3,1},{4,8},{5,9},{6,10},{7,11},{8,4},{9,5},{10,... | collective-permute-start | bytes 368648 | tf_op jit(solution)/shard_map/ppermute | solution.py:450
  13.7 9.6 %collective-permute-start.6 = (f32[192,128]{1,0:T(8,128)S(1)}, f32[192,128]{1,0:T(8,128)S(1)}, u32[]{:S(2)}, u32[]{:S(2)}) collective-permute-start(f32[192,128]{1,0:T(8,128)S(1)} %get-tuple-element.47), channel_id=1, source_target_pairs={{0,1},{1,0},{2,3},{3,2},{4,5},{5,4},{6,7},{7,6},{8,9},{9,8},{10,11... | collective-permute-start | bytes 294920 | tf_op jit(solution)/shard_map/ppermute | solution.py:450
  15.6 7.7 %collective-permute-start.7 = (f32[192,128]{1,0:T(8,128)S(1)}, f32[192,128]{1,0:T(8,128)S(1)}, u32[]{:S(2)}, u32[]{:S(2)}) collective-permute-start(f32[192,128]{1,0:T(8,128)S(1)} %get-tuple-element.48), channel_id=1, source_target_pairs={{0,3},{1,2},{2,1},{3,0},{4,7},{5,6},{6,5},{7,4},{8,11},{9,10},{10,... | collective-permute-start | bytes 294920 | tf_op jit(solution)/shard_map/ppermute | solution.py:450
  18.5 1.3 %collective-permute-start.8 = (f32[40,128]{1,0:T(8,128)S(1)}, f32[40,128]{1,0:T(8,128)S(1)}, u32[]{:S(2)}, u32[]{:S(2)}) collective-permute-start(f32[40,128]{1,0:T(8,128)S(1)} %get-tuple-element.50.full), channel_id=1, source_target_pairs={{0,4},{1,5},{2,6},{3,7},{4,0},{5,1},{6,2},{7,3},{8,12},{9,13},{10,... | collective-permute-start | bytes 61448 | tf_op jit(solution)/shard_map/ppermute | solution.py:450
  19.7 5.4 %collective-permute-start.11 = (f32[136,128]{1,0:T(8,128)S(1)}, f32[136,128]{1,0:T(8,128)S(1)}, u32[]{:S(2)}, u32[]{:S(2)}) collective-permute-start(f32[136,128]{1,0:T(8,128)S(1)} %window.1.refs_11_), channel_id=1, source_target_pairs={{0,3},{1,2},{2,1},{3,0},{4,7},{5,6},{6,5},{7,4},{8,11},{9,10},{10,... | collective-permute-start | bytes 208904 | tf_op jit(solution)/shard_map/ppermute | solution.py:450
  21.2 5.2 %collective-permute-start.10 = (f32[136,128]{1,0:T(8,128)S(1)}, f32[136,128]{1,0:T(8,128)S(1)}, u32[]{:S(2)}, u32[]{:S(2)}) collective-permute-start(f32[136,128]{1,0:T(8,128)S(1)} %window.1.refs_11_), channel_id=1, source_target_pairs={{0,2},{1,3},{2,0},{3,1},{4,6},{5,7},{6,4},{7,5},{8,10},{9,11},{10,... | collective-permute-start | bytes 208904 | tf_op jit(solution)/shard_map/ppermute | solution.py:450
  22.8 4.3 %collective-permute-start.9 = (f32[136,128]{1,0:T(8,128)S(1)}, f32[136,128]{1,0:T(8,128)S(1)}, u32[]{:S(2)}, u32[]{:S(2)}) collective-permute-start(f32[136,128]{1,0:T(8,128)S(1)} %window.1.refs_11_), channel_id=1, source_target_pairs={{0,1},{1,0},{2,3},{3,2},{4,5},{5,4},{6,7},{7,6},{8,9},{9,8},{10,11... | collective-permute-start | bytes 208904 | tf_op jit(solution)/shard_map/ppermute | solution.py:450

commit v8 on v7

--- a/solution.py
+++ b/solution.py
@@ -211,7 +211,7 @@
         high = jnp.where(y < ny - 1, jnp.where(y_even, a, b), 0.0)
         return low, high
 
-    def smooth(f, g, d, absorb, core, chip, row, odd, s, to_core, to_row, to_odd, block, lo, hi, V, y0, y1, y14, y15, g0, g15):
+    def smooth(f, g, core, chip, row, odd, s, to_core, y_faces, x_faces, y_more, lo, hi, y0, y1, y14, y15, g0, g15):
         x_at, y_at, x_even, y_even = where_am_i()
         left, right = halo_x(core, chip, 0, x_at, x_even)
         lo[...], hi[...] = halo_y(row, odd, 0, y_at, y_even)
@@ -228,6 +228,21 @@
             y15[x : x + 1, :] = value[15:16, :]
             g0[x : x + 1, :] = scale[0:1, :]
             g15[x : x + 1, :] = scale[15:16, :]
+        y_faces[0:16, :] = y0[...]
+        y_faces[16:32, :] = y15[...]
+        out, src = iota((8, 32), 0), iota((8, 32), 1)
+        pick = ((out // 4 == src // 16) & (out % 4 == (src % 16) // 4)).astype(F32)
+        sides = jnp.concatenate([s[0], s[15]], axis=0)
+        x_faces[...] = dot(dot(pick, sides), group_lanes(512))
+        put(to_core, 0, s[jnp.where(x_even, 15, 0)])
+        put(to_core, 64, s[jnp.where(x_even, 14, 1)])
+        put(to_core, 128, g[jnp.where(x_even, 15, 0)])
+        to_core[192:196, :] = jnp.where(x_even, x_faces[4:8, :], x_faces[0:4, :])
+        to_core[196:200, :] = jnp.zeros((4, 128), F32)
+        for at, ref in enumerate((y1, y14, g0, g15)):
+            y_more[16 * at : 16 * at + 16, :] = ref[...]
+
+    def restrict(f, d, absorb, s, y_faces, block, V):
         for k in range(4):
             total = jnp.zeros((16, 512), F32)
             for x in range(4 * k, 4 * k + 4):
@@ -240,48 +255,41 @@
                     total = total + s[x + 1]
             V[16 * k : 16 * k + 16, :] = total
         V[64:128, :] = absorb[...]
-        V[128:144, :] = s[0]
-        V[144:160, :] = s[15]
-        V[160:176, :] = y0[...]
-        V[176:192, :] = y15[...]
-        out, src = iota((48, 192), 0), iota((48, 192), 1)
+        V[128:160, :] = y_faces[...]
+        out, src = iota((40, 160), 0), iota((40, 160), 1)
         cx, cy = out % 4, out // 8
         in_bulk = (out < 32) & (src < 128) & (src // 64 == (out // 4) % 2)
         bulk = in_bulk & ((src % 64) // 16 == cx) & ((src % 16) // 4 == cy)
-        faces = (out >= 32) & (src >= 128) & ((out - 32) // 4 == (src - 128) // 16) & ((src % 16) // 4 == cx)
-        picked = dot((bulk | faces).astype(F32), V[...])
+        faces_too = (out >= 32) & (src >= 128) & ((out - 32) // 4 == (src - 128) // 16) & ((src % 16) // 4 == cx)
+        picked = dot((bulk | faces_too).astype(F32), V[...])
         block[...] = dot(picked, group_lanes(512))
-        put(to_core, 0, s[jnp.where(x_even, 15, 0)])
-        put(to_core, 64, s[jnp.where(x_even, 14, 1)])
-        put(to_core, 128, g[jnp.where(x_even, 15, 0)])
-        to_core[192:196, :] = jnp.where(x_even, block[36:40, :], block[32:36, :])
-        to_core[196:200, :] = jnp.zeros((4, 128), F32)
-        for at, (low, high) in enumerate(((y0, y15), (y1, y14), (g0, g15))):
-            a, b = low[...], high[...]
-            put(to_row, 64 * at, jnp.where(y_even, b, a))
-            put(to_odd, 64 * at, jnp.where(y_even, a, b))
-
-    def to_chip_kernel(block, core, s, g, mine, to_chip):
-        _, _, x_even, _ = where_am_i()
-        mine[...] = jnp.concatenate([block[0:32, :], block[40:48, :]], axis=0)
+
+    def to_chip_kernel(block, x_faces, core, s, g, y_faces, y_more, mine, to_chip, to_row, to_odd):
+        _, _, x_even, y_even = where_am_i()
+        mine[...] = block[...]
         face = core[192:200, :]
         for cy in range(4):
             line = face[cy : cy + 1, :]
-            mine[8 * cy : 8 * cy + 1, :] = block[8 * cy : 8 * cy + 1, :] + jnp.where(x_even, 0.0, line)
-            mine[8 * cy + 3 : 8 * cy + 4, :] = block[8 * cy + 3 : 8 * cy + 4, :] + jnp.where(x_even, line, 0.0)
+            a, b = 8 * cy, 8 * cy + 3
+            mine[a : a + 1, :] = block[a : a + 1, :] + jnp.where(x_even, 0.0, line)
+            mine[b : b + 1, :] = block[b : b + 1, :] + jnp.where(x_even, line, 0.0)
         put(to_chip, 0, s[jnp.where(x_even, 0, 15)])
         put(to_chip, 64, s[jnp.where(x_even, 1, 14)])
         put(to_chip, 128, g[jnp.where(x_even, 0, 15)])
         to_chip[192:232, :] = mine[...]
-        to_chip[232:236, :] = jnp.where(x_even, block[32:36, :], block[36:40, :])
+        to_chip[232:236, :] = jnp.where(x_even, x_faces[0:4, :], x_faces[4:8, :])
         to_chip[236:240, :] = jnp.zeros((4, 128), F32)
-
-    def from_chip_kernel(mine, block, chip, full, beyond):
+        for at, (ref, base) in enumerate(((y_faces, 0), (y_more, 0), (y_more, 32))):
+            a, b = ref[base : base + 16, :], ref[base + 16 : base + 32, :]
+            put(to_row, 64 * at, jnp.where(y_even, b, a))
+            put(to_odd, 64 * at, jnp.where(y_even, a, b))
+
+    def from_chip_kernel(mine, x_faces, chip, full, beyond):
         x_at, _, x_even, _ = where_am_i()
         has = jnp.where(x_even, x_at > 0, x_at < nx - 1)
         full[...] = mine[...]
         beyond[...] = chip[192:232, :]
-        mine_face = jnp.where(x_even, block[32:36, :], block[36:40, :])
+        mine_face = jnp.where(x_even, x_faces[0:4, :], x_faces[4:8, :])
         face = chip[232:240, :]
         for cy in range(4):
             line = jnp.where(has, face[cy : cy + 1, :], 0.0)
@@ -292,7 +300,7 @@
             beyond[a : a + 1, :] = chip[192 + a : 193 + a, :] + jnp.where(x_even, 0.0, own)
             beyond[b : b + 1, :] = chip[192 + b : 193 + b, :] + jnp.where(x_even, own, 0.0)
 
-    def window_kernel(full, beyond, core, chip, s_core, s, window):
+    def window_kernel(full, beyond, core, chip, s_core, window):
         x_at, _, x_even, _ = where_am_i()
         mid = full[...]
         a, b = core[...], beyond[...]
@@ -303,9 +311,11 @@
                 window[24 * cy + 12 + 4 * at : 24 * cy + 16 + 4 * at, :] = block[8 * cy + 4 : 8 * cy + 8, :]
             window[96 + 4 * at : 100 + 4 * at, :] = block[32:36, :]
             window[108 + 4 * at : 112 + 4 * at, :] = block[36:40, :]
-        low, high = halo_x(s_core, chip, 0, x_at, x_even)
-        for at, line in enumerate((low[0:1, :], low[15:16, :], high[0:1, :], high[15:16, :])):
-            put(window, 120 + 4 * at, line)
+        for at, line in enumerate((0, 15)):
+            near = jnp.concatenate([s_core[16 * j + line : 16 * j + line + 1, :] for j in range(4)], axis=0)
+            far = jnp.concatenate([chip[16 * j + line : 16 * j + line + 1, :] for j in range(4)], axis=0)
+            window[120 + 4 * at : 124 + 4 * at, :] = jnp.where(x_at > 0, jnp.where(x_even, far, near), 0.0)
+            window[128 + 4 * at : 132 + 4 * at, :] = jnp.where(x_at < nx - 1, jnp.where(x_even, near, far), 0.0)
 
     planes = 4 * ny
 
@@ -468,20 +478,26 @@
         a_odd, a_row, a_chip, a_core, f, g, d, absorb = lax.optimization_barrier(
             (a_odd, a_row, a_chip, a_core, f, g, d, absorb)
         )
-        s, to_core, to_row, to_odd, block = call(
+        s, to_core, y_faces, x_faces, y_more = call(
             smooth,
-            [field, (200, 128), (192, 128), (192, 128), (48, 128)],
-            f, g, d, absorb, a_core, a_chip, a_row, a_odd,
-            scratch=[slab, slab, (192, 512), slab, slab, slab, slab, slab, slab],
+            [field, (200, 128), (32, 512), (8, 128), (64, 512)],
+            f, g, a_core, a_chip, a_row, a_odd,
+            scratch=[slab] * 8,
             name="smooth",
         )
         s_core = swap(to_core, core_pairs)
+        (block,) = call(restrict, [(40, 128)], f, d, absorb, s, y_faces, scratch=[(160, 512)], name="restrict")
+        mine, to_chip, to_row, to_odd = call(
+            to_chip_kernel,
+            [(40, 128), (240, 128), (192, 128), (192, 128)],
+            block, x_faces, s_core, s, g, y_faces, y_more,
+            name="to_chip",
+        )
+        s_chip = swap(to_chip, chip_pairs)
         s_row, s_odd = swap(to_row, row_pairs[0]), swap(to_odd, odd_pairs)
-        mine, to_chip = call(to_chip_kernel, [(40, 128), (240, 128)], block, s_core, s, g, name="to_chip")
-        s_chip = swap(to_chip, chip_pairs)
-        full, beyond = call(from_chip_kernel, [(40, 128), (40, 128)], mine, block, s_chip, name="from_chip")
+        full, beyond = call(from_chip_kernel, [(40, 128), (40, 128)], mine, x_faces, s_chip, name="from_chip")
         c_core = swap(full, core_pairs)
-        (window,) = call(window_kernel, [(136, 128)], full, beyond, c_core, s_chip, s_core, s, name="window")
+        (window,) = call(window_kernel, [(136, 128)], full, beyond, c_core, s_chip, s_core, name="window")
         windows = [window] + [swap(window, pairs) for pairs in row_pairs]
         pressure, coarse = call(
             finish,

time: 29.5 us -> 28.8 us (0.976)
  waiting for transfers between devices: 9.36 us -> 8.5 us
    ppermute x12, waiting for transfers between devices: 9.36 us -> 8.5 us  [swap(): return lax.ppermute(array, axes, pairs)]
    pallas_call x7 -> x8, Pallas kernels: 5.78 us -> 5.93 us  [call(): pl.pallas_call(kernel, out_shape=[jax.ShapeDtypeStruct(s, F32) for s in o...]
  transfers between devices with their start and end apart: 12 -> 12, of which waited for: 8 -> 8; matrix products, arithmetic and copies ran while one was open for 0% -> 0% of each run, Pallas kernels for 2% -> 5%
where the time goes in v8:
time: 28.8 us; the launch traced here: 28.6 us
  starting transfers between devices  13.4 us (47%)
  waiting for transfers between devices  8.5 us (30%)
  Pallas kernels  5.93 us (21%)
  between operations  0.76 us (3%)
    ppermute x12, starting transfers between devices, swap(): return lax.ppermute(array, axes, pairs)  13.4 us
    ppermute x12, waiting for transfers between devices, swap(): return lax.ppermute(array, axes, pairs)  8.5 us
    pallas_call x8, Pallas kernels, call(): pl.pallas_call(kernel, out_shape=[jax.ShapeDtypeStruct(s, F32) for s in o...  5.93 us
  transfers between devices with their start and end apart: 12, of which 8 were waited for; matrix products, arithmetic and copies ran while one was open for 0% of the time, Pallas kernels for 5%

profile of v8, /device:TPU:0, one launch (start us, length us, event | category | flops | bytes accessed | tf_op | source)
XLA Modules:
  0.0 28.6 jit_solution(8637109782728195244)
XLA Ops:
  0.7 1.6 %faces.1 = (f32[64,128]{1,0:T(8,128)S(1)}, f32[64,128]{1,0:T(8,128)S(1)}, f32[64,128]{1,0:T(8,128)S(1)}, f32[64,128]{1,0:T(8,128)S(1)}) custom-call(f32[16,16,512]{2,1,0:T(8,128)} %source.1, f32[16,16,512]{2,1,0:T(8,128)} %reaction.1, s32[16,16,512]{2,1,0:T(8,128)} %kind.1, s32[16,16,512]{2,1,0:T(8,128)} %disk_id.1, s32[16,16,512]{2,1,0:T(8,128)} %disk_mask.1, ...), custom_call_target="tpu_custom_call" | custom-call | tf_op jit(solution)/shard_map/faces/pallas_call | solution.py:22
  2.3 4.0 %collective-permute-start = (f32[64,128]{1,0:T(8,128)S(1)}, f32[64,128]{1,0:T(8,128)S(1)}, u32[]{:S(2)}, u32[]{:S(2)}) collective-permute-start(f32[64,128]{1,0:T(8,128)S(1)} %get-tuple-element.29), channel_id=1, source_target_pairs={{0,3},{1,2},{2,1},{3,0},{4,7},{5,6},{6,5},{7,4},{8,11},{9,10},{10,... | collective-permute-start | bytes 98312 | tf_op jit(solution)/shard_map/ppermute | solution.py:460
  6.2 0.5 %collective-permute-start.1 = (f32[64,128]{1,0:T(8,128)S(1)}, f32[64,128]{1,0:T(8,128)S(1)}, u32[]{:S(2)}, u32[]{:S(2)}) collective-permute-start(f32[64,128]{1,0:T(8,128)S(1)} %get-tuple-element.30), channel_id=1, source_target_pairs={{0,1},{1,0},{2,3},{3,2},{4,5},{5,4},{6,7},{7,6},{8,9},{9,8},{10,11... | collective-permute-start | bytes 98312 | tf_op jit(solution)/shard_map/ppermute | solution.py:460
  6.8 0.1 collective-permute-start.2
  6.9 1.6 %collective-permute-start.3 = (f32[64,128]{1,0:T(8,128)S(1)}, f32[64,128]{1,0:T(8,128)S(1)}, u32[]{:S(2)}, u32[]{:S(2)}) collective-permute-start(f32[64,128]{1,0:T(8,128)S(1)} %get-tuple-element.32), channel_id=1, source_target_pairs={{0,4},{1,5},{2,6},{3,7},{4,0},{5,1},{6,2},{7,3},{8,12},{9,13},{10,... | collective-permute-start | bytes 98312 | tf_op jit(solution)/shard_map/ppermute | solution.py:460
  8.5 0.5 %set_up.1 = (f32[16,16,512]{2,1,0:T(8,128)S(1)}, f32[16,16,512]{2,1,0:T(8,128)S(1)}, f32[16,16,512]{2,1,0:T(8,128)S(1)}, f32[64,512]{1,0:T(8,128)S(1)}) custom-call(f32[16,16,512]{2,1,0:T(8,128)S(1)} %copy-done, f32[16,16,512]{2,1,0:T(8,128)S(1)} %copy-done.1, s32[16,16,512]{2,1,0:T(8,128)S(1)} %copy-done.2, s32[16,16,512]{2,1,0:T(8,128)S(1)} %copy-done.3, ...), custom_call_target="tpu_custom_call" | custom-call | tf_op jit(solution)/shard_map/set_up/pallas_call | solution.py:22
  9.0 1.2 %collective-permute-done.1.row.refs_5_ = f32[64,128]{1,0:T(8,128)S(1)} collective-permute-done((f32[64,128]{1,0:T(8,128)S(1)}, f32[64,128]{1,0:T(8,128)S(1)}, u32[]{:S(2)}, u32[]{:S(2)}) %collective-permute-start.1) | collective-permute-done | bytes 32800 | tf_op jit(solution)/shard_map/ppermute | solution.py:460
  10.2 0.5 %collective-permute-done.2.chip.refs_4_ = f32[64,128]{1,0:T(8,128)S(1)} collective-permute-done((f32[64,128]{1,0:T(8,128)S(1)}, f32[64,128]{1,0:T(8,128)S(1)}, u32[]{:S(2)}, u32[]{:S(2)}) %collective-permute-start.2) | collective-permute-done | bytes 32800 | tf_op jit(solution)/shard_map/ppermute | solution.py:460
  10.7 0.7 %smooth.1 = (f32[16,16,512]{2,1,0:T(8,128)S(1)}, f32[200,128]{1,0:T(8,128)S(1)}, f32[32,512]{1,0:T(8,128)S(1)}, f32[8,128]{1,0:T(8,128)S(1)}, f32[64,512]{1,0:T(8,128)S(1)}) custom-call(f32[16,16,512]{2,1,0:T(8,128)S(1)} %get-tuple-element.37.f.refs_0_, f32[16,16,512]{2,1,0:T(8,128)S(1)} %get-tuple-element.38.g.refs_1_, ...), custom_call_target="tpu_custom_call" | custom-call | tf_op jit(solution)/shard_map/smooth/pallas_call | solution.py:22
  11.4 0.9 %restrict.1.block = f32[40,128]{1,0:T(8,128)S(1)} custom-call(f32[16,16,512]{2,1,0:T(8,128)S(1)} %get-tuple-element.37.f.refs_0_, f32[16,16,512]{2,1,0:T(8,128)S(1)} %get-tuple-element.45.d, f32[64,512]{1,0:T(8,128)S(1)} %get-tuple-element.46.absorb, f32[16,16,512]{2,1,0:T(8,128)S(1)} %get-tuple-element.43.s.refs_2_, f32[32,512]{1,0:T(8,128)S(1)} %get-tuple-element.47.y_faces), custom_call_target="tpu_custom_call" | custom-call | tf_op jit(solution)/shard_map/restrict/pallas_call | solution.py:22
  12.3 0.4 %collective-permute-done.4.core.s_core.refs_7_ = f32[200,128]{1,0:T(8,128)S(1)} collective-permute-done((f32[200,128]{1,0:T(8,128)S(1)}, f32[200,128]{1,0:T(8,128)S(1)}, u32[]{:S(2)}, u32[]{:S(2)}) %collective-permute-start.4) | collective-permute-done | bytes 102432 | tf_op jit(solution)/shard_map/ppermute | solution.py:460
  12.8 0.2 collective-permute-start.5
  12.9 1.9 %collective-permute-start.6 = (f32[192,128]{1,0:T(8,128)S(1)}, f32[192,128]{1,0:T(8,128)S(1)}, u32[]{:S(2)}, u32[]{:S(2)}) collective-permute-start(f32[192,128]{1,0:T(8,128)S(1)} %get-tuple-element.51), channel_id=1, source_target_pairs={{0,1},{1,0},{2,3},{3,2},{4,5},{5,4},{6,7},{7,6},{8,9},{9,8},{10,11... | collective-permute-start | bytes 294920 | tf_op jit(solution)/shard_map/ppermute | solution.py:460
  14.8 1.5 %collective-permute-start.7 = (f32[192,128]{1,0:T(8,128)S(1)}, f32[192,128]{1,0:T(8,128)S(1)}, u32[]{:S(2)}, u32[]{:S(2)}) collective-permute-start(f32[192,128]{1,0:T(8,128)S(1)} %get-tuple-element.52), channel_id=1, source_target_pairs={{0,3},{1,2},{2,1},{3,0},{4,7},{5,6},{6,5},{7,4},{8,11},{9,10},{10,... | collective-permute-start | bytes 294920 | tf_op jit(solution)/shard_map/ppermute | solution.py:460
  16.3 1.4 %collective-permute-done.5.chip.refs_8_ = f32[240,128]{1,0:T(8,128)S(1)} collective-permute-done((f32[240,128]{1,0:T(8,128)S(1)}, f32[240,128]{1,0:T(8,128)S(1)}, u32[]{:S(2)}, u32[]{:S(2)}) %collective-permute-start.5) | collective-permute-done | bytes 122912 | tf_op jit(solution)/shard_map/ppermute | solution.py:460
  17.7 0.1 collective-permute-start.8
  17.8 1.2 %collective-permute-done.8.core = f32[40,128]{1,0:T(8,128)S(1)} collective-permute-done((f32[40,128]{1,0:T(8,128)S(1)}, f32[40,128]{1,0:T(8,128)S(1)}, u32[]{:S(2)}, u32[]{:S(2)}) %collective-permute-start.8) | collective-permute-done | bytes 20512 | tf_op jit(solution)/shard_map/ppermute | solution.py:460
  19.0 1.5 %collective-permute-start.11 = (f32[136,128]{1,0:T(8,128)S(1)}, f32[136,128]{1,0:T(8,128)S(1)}, u32[]{:S(2)}, u32[]{:S(2)}) collective-permute-start(f32[136,128]{1,0:T(8,128)S(1)} %window.1.refs_11_), channel_id=1, source_target_pairs={{0,3},{1,2},{2,1},{3,0},{4,7},{5,6},{6,5},{7,4},{8,11},{9,10},{10,... | collective-permute-start | bytes 208904 | tf_op jit(solution)/shard_map/ppermute | solution.py:460
  20.5 1.5 %collective-permute-start.10 = (f32[136,128]{1,0:T(8,128)S(1)}, f32[136,128]{1,0:T(8,128)S(1)}, u32[]{:S(2)}, u32[]{:S(2)}) collective-permute-start(f32[136,128]{1,0:T(8,128)S(1)} %window.1.refs_11_), channel_id=1, source_target_pairs={{0,2},{1,3},{2,0},{3,1},{4,6},{5,7},{6,4},{7,5},{8,10},{9,11},{10,... | collective-permute-start | bytes 208904 | tf_op jit(solution)/shard_map/ppermute | solution.py:460
  22.0 0.5 %collective-permute-start.9 = (f32[136,128]{1,0:T(8,128)S(1)}, f32[136,128]{1,0:T(8,128)S(1)}, u32[]{:S(2)}, u32[]{:S(2)}) collective-permute-start(f32[136,128]{1,0:T(8,128)S(1)} %window.1.refs_11_), channel_id=1, source_target_pairs={{0,1},{1,0},{2,3},{3,2},{4,5},{5,4},{6,7},{7,6},{8,9},{9,8},{10,11... | collective-permute-start | bytes 208904 | tf_op jit(solution)/shard_map/ppermute | solution.py:460
  22.6 1.9 %collective-permute-done.11.refs_14_ = f32[136,128]{1,0:T(8,128)S(1)} collective-permute-done((f32[136,128]{1,0:T(8,128)S(1)}, f32[136,128]{1,0:T(8,128)S(1)}, u32[]{:S(2)}, u32[]{:S(2)}) %collective-permute-start.11) | collective-permute-done | bytes 69664 | tf_op jit(solution)/shard_map/ppermute | solution.py:460
  24.4 1.3 %collective-permute-done.10.refs_13_ = f32[136,128]{1,0:T(8,128)S(1)} collective-permute-done((f32[136,128]{1,0:T(8,128)S(1)}, f32[136,128]{1,0:T(8,128)S(1)}, u32[]{:S(2)}, u32[]{:S(2)}) %collective-permute-start.10) | collective-permute-done | bytes 69664 | tf_op jit(solution)/shard_map/ppermute | solution.py:460
  25.7 0.6 %collective-permute-done.9.refs_12_ = f32[136,128]{1,0:T(8,128)S(1)} collective-permute-done((f32[136,128]{1,0:T(8,128)S(1)}, f32[136,128]{1,0:T(8,128)S(1)}, u32[]{:S(2)}, u32[]{:S(2)}) %collective-permute-start.9) | collective-permute-done | bytes 69664 | tf_op jit(solution)/shard_map/ppermute | solution.py:460
  26.3 2.3 %finish.1 = (f32[16,16,512]{2,1,0:T(8,128)}, f32[4,16,128]{2,1,0:T(8,128)}) custom-call(f32[16,16,512]{2,1,0:T(8,128)S(1)} %get-tuple-element.37.f.refs_0_, f32[16,16,512]{2,1,0:T(8,128)S(1)} %get-tuple-element.38.g.refs_1_, f32[16,16,512]{2,1,0:T(8,128)S(1)} %get-tuple-element.43.s.refs_2_, f32[64,128]{1,0:T(8,128)S(1)} %collective-permute-done.3.core.refs_3_, ...), custom_call_target="tpu_custom_call" | custom-call | tf_op jit(solution)/shard_map/finish/pallas_call | solution.py:22
  (20 shorter events, 0.2 us)
Async XLA Ops:
  0.6 7.8 %copy-start = (f32[16,16,512]{2,1,0:T(8,128)S(1)}, f32[16,16,512]{2,1,0:T(8,128)}, u32[]{:S(2)}) copy-start(f32[16,16,512]{2,1,0:T(8,128)} %source.1) | copy-start | bytes 1572868
  0.6 7.8 %copy-start.1 = (f32[16,16,512]{2,1,0:T(8,128)S(1)}, f32[16,16,512]{2,1,0:T(8,128)}, u32[]{:S(2)}) copy-start(f32[16,16,512]{2,1,0:T(8,128)} %reaction.1) | copy-start | bytes 1572868
  0.7 7.8 %copy-start.2 = (s32[16,16,512]{2,1,0:T(8,128)S(1)}, s32[16,16,512]{2,1,0:T(8,128)}, u32[]{:S(2)}) copy-start(s32[16,16,512]{2,1,0:T(8,128)} %kind.1) | copy-start | bytes 1572868
  0.7 7.8 %copy-start.3 = (s32[16,16,512]{2,1,0:T(8,128)S(1)}, s32[16,16,512]{2,1,0:T(8,128)}, u32[]{:S(2)}) copy-start(s32[16,16,512]{2,1,0:T(8,128)} %disk_id.1) | copy-start | bytes 1572868
  0.7 7.8 %copy-start.4 = (s32[16,16,512]{2,1,0:T(8,128)S(1)}, s32[16,16,512]{2,1,0:T(8,128)}, u32[]{:S(2)}) copy-start(s32[16,16,512]{2,1,0:T(8,128)} %disk_mask.1) | copy-start | bytes 1572868
  2.3 6.7 %collective-permute-start = (f32[64,128]{1,0:T(8,128)S(1)}, f32[64,128]{1,0:T(8,128)S(1)}, u32[]{:S(2)}, u32[]{:S(2)}) collective-permute-start(f32[64,128]{1,0:T(8,128)S(1)} %get-tuple-element.29), channel_id=1, source_target_pairs={{0,3},{1,2},{2,1},{3,0},{4,7},{5,6},{6,5},{7,4},{8,11},{9,10},{10,... | collective-permute-start | bytes 98312 | tf_op jit(solution)/shard_map/ppermute | solution.py:460
  6.2 3.9 %collective-permute-start.1 = (f32[64,128]{1,0:T(8,128)S(1)}, f32[64,128]{1,0:T(8,128)S(1)}, u32[]{:S(2)}, u32[]{:S(2)}) collective-permute-start(f32[64,128]{1,0:T(8,128)S(1)} %get-tuple-element.30), channel_id=1, source_target_pairs={{0,1},{1,0},{2,3},{3,2},{4,5},{5,4},{6,7},{7,6},{8,9},{9,8},{10,11... | collective-permute-start | bytes 98312 | tf_op jit(solution)/shard_map/ppermute | solution.py:460
  6.8 1.7 %copy-start.5 = (f32[120]{0:T(128)S(1)}, f32[120]{0:T(128)}, u32[]{:S(2)}) copy-start(f32[120]{0:T(128)} %param.11) | copy-start | bytes 1444
  6.8 3.9 %collective-permute-start.2 = (f32[64,128]{1,0:T(8,128)S(1)}, f32[64,128]{1,0:T(8,128)S(1)}, u32[]{:S(2)}, u32[]{:S(2)}) collective-permute-start(f32[64,128]{1,0:T(8,128)S(1)} %get-tuple-element.31), channel_id=1, source_target_pairs={{0,2},{1,3},{2,0},{3,1},{4,8},{5,9},{6,10},{7,11},{8,4},{9,5},{10,... | collective-permute-start | bytes 98312 | tf_op jit(solution)/shard_map/ppermute | solution.py:460
  6.9 3.8 %collective-permute-start.3 = (f32[64,128]{1,0:T(8,128)S(1)}, f32[64,128]{1,0:T(8,128)S(1)}, u32[]{:S(2)}, u32[]{:S(2)}) collective-permute-start(f32[64,128]{1,0:T(8,128)S(1)} %get-tuple-element.32), channel_id=1, source_target_pairs={{0,4},{1,5},{2,6},{3,7},{4,0},{5,1},{6,2},{7,3},{8,12},{9,13},{10,... | collective-permute-start | bytes 98312 | tf_op jit(solution)/shard_map/ppermute | solution.py:460
  11.4 1.3 %collective-permute-start.4 = (f32[200,128]{1,0:T(8,128)S(1)}, f32[200,128]{1,0:T(8,128)S(1)}, u32[]{:S(2)}, u32[]{:S(2)}) collective-permute-start(f32[200,128]{1,0:T(8,128)S(1)} %get-tuple-element.44), channel_id=1, source_target_pairs={{0,4},{1,5},{2,6},{3,7},{4,0},{5,1},{6,2},{7,3},{8,12},{9,13},{10,... | collective-permute-start | bytes 307208 | tf_op jit(solution)/shard_map/ppermute | solution.py:460
  12.8 4.9 %collective-permute-start.5 = (f32[240,128]{1,0:T(8,128)S(1)}, f32[240,128]{1,0:T(8,128)S(1)}, u32[]{:S(2)}, u32[]{:S(2)}) collective-permute-start(f32[240,128]{1,0:T(8,128)S(1)} %get-tuple-element.50), channel_id=1, source_target_pairs={{0,2},{1,3},{2,0},{3,1},{4,8},{5,9},{6,10},{7,11},{8,4},{9,5},{10,... | collective-permute-start | bytes 368648 | tf_op jit(solution)/shard_map/ppermute | solution.py:460
  12.9 9.6 %collective-permute-start.6 = (f32[192,128]{1,0:T(8,128)S(1)}, f32[192,128]{1,0:T(8,128)S(1)}, u32[]{:S(2)}, u32[]{:S(2)}) collective-permute-start(f32[192,128]{1,0:T(8,128)S(1)} %get-tuple-element.51), channel_id=1, source_target_pairs={{0,1},{1,0},{2,3},{3,2},{4,5},{5,4},{6,7},{7,6},{8,9},{9,8},{10,11... | collective-permute-start | bytes 294920 | tf_op jit(solution)/shard_map/ppermute | solution.py:460
  14.8 7.7 %collective-permute-start.7 = (f32[192,128]{1,0:T(8,128)S(1)}, f32[192,128]{1,0:T(8,128)S(1)}, u32[]{:S(2)}, u32[]{:S(2)}) collective-permute-start(f32[192,128]{1,0:T(8,128)S(1)} %get-tuple-element.52), channel_id=1, source_target_pairs={{0,3},{1,2},{2,1},{3,0},{4,7},{5,6},{6,5},{7,4},{8,11},{9,10},{10,... | collective-permute-start | bytes 294920 | tf_op jit(solution)/shard_map/ppermute | solution.py:460
  17.7 1.3 %collective-permute-start.8 = (f32[40,128]{1,0:T(8,128)S(1)}, f32[40,128]{1,0:T(8,128)S(1)}, u32[]{:S(2)}, u32[]{:S(2)}) collective-permute-start(f32[40,128]{1,0:T(8,128)S(1)} %get-tuple-element.54.full), channel_id=1, source_target_pairs={{0,4},{1,5},{2,6},{3,7},{4,0},{5,1},{6,2},{7,3},{8,12},{9,13},{10,... | collective-permute-start | bytes 61448 | tf_op jit(solution)/shard_map/ppermute | solution.py:460
  19.0 5.4 %collective-permute-start.11 = (f32[136,128]{1,0:T(8,128)S(1)}, f32[136,128]{1,0:T(8,128)S(1)}, u32[]{:S(2)}, u32[]{:S(2)}) collective-permute-start(f32[136,128]{1,0:T(8,128)S(1)} %window.1.refs_11_), channel_id=1, source_target_pairs={{0,3},{1,2},{2,1},{3,0},{4,7},{5,6},{6,5},{7,4},{8,11},{9,10},{10,... | collective-permute-start | bytes 208904 | tf_op jit(solution)/shard_map/ppermute | solution.py:460
  20.5 5.2 %collective-permute-start.10 = (f32[136,128]{1,0:T(8,128)S(1)}, f32[136,128]{1,0:T(8,128)S(1)}, u32[]{:S(2)}, u32[]{:S(2)}) collective-permute-start(f32[136,128]{1,0:T(8,128)S(1)} %window.1.refs_11_), channel_id=1, source_target_pairs={{0,2},{1,3},{2,0},{3,1},{4,6},{5,7},{6,4},{7,5},{8,10},{9,11},{10,... | collective-permute-start | bytes 208904 | tf_op jit(solution)/shard_map/ppermute | solution.py:460
  22.0 4.3 %collective-permute-start.9 = (f32[136,128]{1,0:T(8,128)S(1)}, f32[136,128]{1,0:T(8,128)S(1)}, u32[]{:S(2)}, u32[]{:S(2)}) collective-permute-start(f32[136,128]{1,0:T(8,128)S(1)} %window.1.refs_11_), channel_id=1, source_target_pairs={{0,1},{1,0},{2,3},{3,2},{4,5},{5,4},{6,7},{7,6},{8,9},{9,8},{10,11... | collective-permute-start | bytes 208904 | tf_op jit(solution)/shard_map/ppermute | solution.py:460

commit v9 on v8

--- a/solution.py
+++ b/solution.py
@@ -185,19 +185,26 @@
             move.start()
         for move in moves:
             move.wait()
-        low, high, f_far, f_near = (first_of(*(buffer[j] for buffer in buffers), table[...])[0] for j in range(4))
+        (low, g_low), (high, g_high), (f_far, _), (f_near, _) = (
+            first_of(*(buffer[j] for buffer in buffers), table[...])[:2] for j in range(4)
+        )
         put(row, 0, jnp.where(y_even, high, low))
+        put(row, 64, jnp.where(y_even, g_high, g_low))
         put(odd, 0, jnp.where(y_even, low, high))
+        put(odd, 64, jnp.where(y_even, g_low, g_high))
         put(chip, 0, f_far)
         put(core, 0, f_near)
 
-    def set_up(source, reaction, kind, disk_id, disk_mask, table, f, g, d, absorb):
+    def set_up(source, reaction, kind, disk_id, disk_mask, table, f, g, d, absorb, V):
         for k in range(4):
             total = jnp.zeros((16, 512), F32)
             for x in range(4 * k, 4 * k + 4):
                 f[x], g[x], d[x], a = first_of(source[x], reaction[x], kind[x], disk_id[x], disk_mask[x], table[...])
                 total = total + a
-            absorb[16 * k : 16 * k + 16, :] = total
+            V[16 * k : 16 * k + 16, :] = total
+        out, src = iota((16, 64), 0), iota((16, 64), 1)
+        pick = ((src // 16 == out % 4) & ((src % 16) // 4 == out // 4)).astype(F32)
+        absorb[...] = dot(dot(pick, V[...]), group_lanes(512))
 
     def halo_x(core, chip, row, x, x_even):
         a, b = get(core, row, 16, 512), get(chip, row, 16, 512)
@@ -211,7 +218,7 @@
         high = jnp.where(y < ny - 1, jnp.where(y_even, a, b), 0.0)
         return low, high
 
-    def smooth(f, g, core, chip, row, odd, s, to_core, y_faces, x_faces, y_more, lo, hi, y0, y1, y14, y15, g0, g15):
+    def smooth(f, g, absorb, core, chip, row, odd, s, to_core, sums, y_faces, y_more, lo, hi, y0, y1, y14, y15):
         x_at, y_at, x_even, y_even = where_am_i()
         left, right = halo_x(core, chip, 0, x_at, x_even)
         lo[...], hi[...] = halo_y(row, odd, 0, y_at, y_even)
@@ -226,23 +233,23 @@
             y1[x : x + 1, :] = value[1:2, :]
             y14[x : x + 1, :] = value[14:15, :]
             y15[x : x + 1, :] = value[15:16, :]
-            g0[x : x + 1, :] = scale[0:1, :]
-            g15[x : x + 1, :] = scale[15:16, :]
         y_faces[0:16, :] = y0[...]
         y_faces[16:32, :] = y15[...]
-        out, src = iota((8, 32), 0), iota((8, 32), 1)
+        out, src = iota((16, 64), 0), iota((16, 64), 1)
         pick = ((out // 4 == src // 16) & (out % 4 == (src % 16) // 4)).astype(F32)
-        sides = jnp.concatenate([s[0], s[15]], axis=0)
-        x_faces[...] = dot(dot(pick, sides), group_lanes(512))
+        sides = jnp.concatenate([s[0], s[15], y0[...], y15[...]], axis=0)
+        sums[...] = dot(dot(pick, sides), group_lanes(512))
         put(to_core, 0, s[jnp.where(x_even, 15, 0)])
         put(to_core, 64, s[jnp.where(x_even, 14, 1)])
         put(to_core, 128, g[jnp.where(x_even, 15, 0)])
-        to_core[192:196, :] = jnp.where(x_even, x_faces[4:8, :], x_faces[0:4, :])
+        to_core[192:196, :] = jnp.where(x_even, sums[4:8, :], sums[0:4, :])
         to_core[196:200, :] = jnp.zeros((4, 128), F32)
-        for at, ref in enumerate((y1, y14, g0, g15)):
+        to_core[200:208, :] = sums[8:16, :]
+        to_core[208:224, :] = absorb[...]
+        for at, ref in enumerate((y1, y14)):
             y_more[16 * at : 16 * at + 16, :] = ref[...]
 
-    def restrict(f, d, absorb, s, y_faces, block, V):
+    def restrict(f, d, absorb, s, sums, block, V):
         for k in range(4):
             total = jnp.zeros((16, 512), F32)
             for x in range(4 * k, 4 * k + 4):
@@ -254,17 +261,15 @@
                 if x < 15:
                     total = total + s[x + 1]
             V[16 * k : 16 * k + 16, :] = total
-        V[64:128, :] = absorb[...]
-        V[128:160, :] = y_faces[...]
-        out, src = iota((40, 160), 0), iota((40, 160), 1)
-        cx, cy = out % 4, out // 8
-        in_bulk = (out < 32) & (src < 128) & (src // 64 == (out // 4) % 2)
-        bulk = in_bulk & ((src % 64) // 16 == cx) & ((src % 16) // 4 == cy)
-        faces_too = (out >= 32) & (src >= 128) & ((out - 32) // 4 == (src - 128) // 16) & ((src % 16) // 4 == cx)
-        picked = dot((bulk | faces_too).astype(F32), V[...])
-        block[...] = dot(picked, group_lanes(512))
-
-    def to_chip_kernel(block, x_faces, core, s, g, y_faces, y_more, mine, to_chip, to_row, to_odd):
+        out, src = iota((16, 64), 0), iota((16, 64), 1)
+        pick = ((src // 16 == out % 4) & ((src % 16) // 4 == out // 4)).astype(F32)
+        found = dot(dot(pick, V[...]), group_lanes(512))
+        for cy in range(4):
+            block[8 * cy : 8 * cy + 4, :] = found[4 * cy : 4 * cy + 4, :]
+            block[8 * cy + 4 : 8 * cy + 8, :] = absorb[4 * cy : 4 * cy + 4, :]
+        block[32:40, :] = sums[8:16, :]
+
+    def to_chip_kernel(block, sums, absorb, core, s, g, y_faces, y_more, mine, to_chip, to_row, to_odd):
         _, _, x_even, y_even = where_am_i()
         mine[...] = block[...]
         face = core[192:200, :]
@@ -277,19 +282,32 @@
         put(to_chip, 64, s[jnp.where(x_even, 1, 14)])
         put(to_chip, 128, g[jnp.where(x_even, 0, 15)])
         to_chip[192:232, :] = mine[...]
-        to_chip[232:236, :] = jnp.where(x_even, x_faces[0:4, :], x_faces[4:8, :])
+        to_chip[232:236, :] = jnp.where(x_even, sums[0:4, :], sums[4:8, :])
         to_chip[236:240, :] = jnp.zeros((4, 128), F32)
-        for at, (ref, base) in enumerate(((y_faces, 0), (y_more, 0), (y_more, 32))):
-            a, b = ref[base : base + 16, :], ref[base + 16 : base + 32, :]
+        for at, ref in enumerate((y_faces, y_more)):
+            a, b = ref[0:16, :], ref[16:32, :]
             put(to_row, 64 * at, jnp.where(y_even, b, a))
             put(to_odd, 64 * at, jnp.where(y_even, a, b))
-
-    def from_chip_kernel(mine, x_faces, chip, full, beyond):
+        first_line, last_line = (
+            jnp.concatenate([core[16 * j + line : 16 * j + line + 1, :] for j in range(4)], axis=0) for line in (0, 15)
+        )
+        for ref, corner in (
+            (to_row, jnp.where(y_even, last_line, first_line)),
+            (to_odd, jnp.where(y_even, first_line, last_line)),
+        ):
+            ref[128:144, :] = absorb[...]
+            ref[144:160, :] = core[208:224, :]
+            ref[160:168, :] = sums[8:16, :]
+            ref[168:176, :] = core[200:208, :]
+            ref[176:180, :] = corner
+            ref[180:192, :] = jnp.zeros((12, 128), F32)
+
+    def from_chip_kernel(mine, sums, chip, full, beyond):
         x_at, _, x_even, _ = where_am_i()
         has = jnp.where(x_even, x_at > 0, x_at < nx - 1)
         full[...] = mine[...]
         beyond[...] = chip[192:232, :]
-        mine_face = jnp.where(x_even, x_faces[0:4, :], x_faces[4:8, :])
+        mine_face = jnp.where(x_even, sums[0:4, :], sums[4:8, :])
         face = chip[232:240, :]
         for cy in range(4):
             line = jnp.where(has, face[cy : cy + 1, :], 0.0)
@@ -300,7 +318,7 @@
             beyond[a : a + 1, :] = chip[192 + a : 193 + a, :] + jnp.where(x_even, 0.0, own)
             beyond[b : b + 1, :] = chip[192 + b : 193 + b, :] + jnp.where(x_even, own, 0.0)
 
-    def window_kernel(full, beyond, core, chip, s_core, window):
+    def window_kernel(full, beyond, core, chip, s_core, window, short):
         x_at, _, x_even, _ = where_am_i()
         mid = full[...]
         a, b = core[...], beyond[...]
@@ -316,8 +334,15 @@
             far = jnp.concatenate([chip[16 * j + line : 16 * j + line + 1, :] for j in range(4)], axis=0)
             window[120 + 4 * at : 124 + 4 * at, :] = jnp.where(x_at > 0, jnp.where(x_even, far, near), 0.0)
             window[128 + 4 * at : 132 + 4 * at, :] = jnp.where(x_at < nx - 1, jnp.where(x_even, near, far), 0.0)
+            short[72 + 4 * at : 76 + 4 * at, :] = far
+        for cy in range(4):
+            for at, block in enumerate((left, mid, right)):
+                short[12 * cy + 4 * at : 12 * cy + 4 * at + 4, :] = block[8 * cy : 8 * cy + 4, :]
+            short[48 + 4 * cy : 52 + 4 * cy, :] = beyond[8 * cy + 4 : 8 * cy + 8, :]
+        short[64:72, :] = beyond[32:40, :]
 
     planes = 4 * ny
+    short_steps = (1, 3) if ny == 4 else (1,)
 
     def finish(*refs):
         f, g, s, a_core, a_chip, a_row, a_odd, s_core, s_chip, s_row, s_odd = refs[:11]
@@ -326,7 +351,31 @@
         every, res, diag, inv, one, two, sol, Pc, T, U, yl, yh, tl, th, ul, uh, result, slab_out, sems = refs[13 + ny :]
         x_at, y_at, x_even, y_even = where_am_i()
         for step, window in enumerate(windows):
-            every[jnp.bitwise_xor(y_at, step)] = window[...]
+            there = jnp.bitwise_xor(y_at, step)
+            if step not in short_steps:
+                every[there] = window[...]
+                continue
+            faces_of = s_row if step == 1 else s_odd
+
+            def three(at, own, core, chip):
+                every[there, at : at + 4, :] = jnp.where(x_even, chip, core)
+                if own is not None:
+                    every[there, at + 4 : at + 8, :] = own
+                every[there, at + 8 : at + 12, :] = jnp.where(x_even, core, chip)
+
+            for cy in range(4):
+                at = 4 * cy
+                every[there, 24 * cy : 24 * cy + 12, :] = window[12 * cy : 12 * cy + 12, :]
+                three(
+                    24 * cy + 12, faces_of[128 + at : 132 + at, :], faces_of[144 + at : 148 + at, :],
+                    window[48 + at : 52 + at, :],
+                )
+            for at in (0, 4):
+                three(
+                    96 + 3 * at, faces_of[160 + at : 164 + at, :], faces_of[168 + at : 172 + at, :],
+                    window[64 + at : 68 + at, :],
+                )
+                three(120 + at, None, faces_of[176:180, :], window[72 + at : 76 + at, :])
 
         row = iota((16, 128), 0)
         valid = ((row >= 4) | (x_at > 0)) & ((row < 8) | (x_at < nx - 1)) & (row < 12)
@@ -398,7 +447,7 @@
         below, above = first_plane - 1, first_plane + 4
         y1_low, y1_high = halo_y(s_row, s_odd, 0, y_at, y_even)
         y2_low, y2_high = halo_y(s_row, s_odd, 64, y_at, y_even)
-        g_low, g_high = halo_y(s_row, s_odd, 128, y_at, y_even)
+        g_low, g_high = halo_y(a_row, a_odd, 64, y_at, y_even)
         f_low, f_high = halo_y(a_row, a_odd, 0, y_at, y_even)
         before, after = jnp.maximum(y_at - 1, 0), jnp.minimum(y_at + 1, ny - 1)
         outer = {}
@@ -464,7 +513,7 @@
         some = (4, 16, 512)
         core, chip, row, odd = call(
             faces,
-            [(64, 128)] * 4,
+            [(64, 128), (64, 128), (128, 128), (128, 128)],
             *(pltpu.with_memory_space_constraint(array, pltpu.HBM) for array in inputs),
             in_specs=[HBM] * 6,
             scratch=[some, some]
@@ -474,31 +523,37 @@
         )
         a_core, a_chip = swap(core, core_pairs), swap(chip, chip_pairs)
         a_odd, a_row = swap(odd, odd_pairs), swap(row, row_pairs[0])
-        f, g, d, absorb = call(set_up, [field, field, field, (64, 512)], *inputs, name="set_up")
+        f, g, d, absorb = call(
+            set_up, [field, field, field, (16, 128)], *inputs, scratch=[(64, 512)], name="set_up"
+        )
         a_odd, a_row, a_chip, a_core, f, g, d, absorb = lax.optimization_barrier(
             (a_odd, a_row, a_chip, a_core, f, g, d, absorb)
         )
-        s, to_core, y_faces, x_faces, y_more = call(
+        s, to_core, sums, y_faces, y_more = call(
             smooth,
-            [field, (200, 128), (32, 512), (8, 128), (64, 512)],
-            f, g, a_core, a_chip, a_row, a_odd,
-            scratch=[slab] * 8,
+            [field, (224, 128), (16, 128), (32, 512), (32, 512)],
+            f, g, absorb, a_core, a_chip, a_row, a_odd,
+            scratch=[slab] * 6,
             name="smooth",
         )
         s_core = swap(to_core, core_pairs)
-        (block,) = call(restrict, [(40, 128)], f, d, absorb, s, y_faces, scratch=[(160, 512)], name="restrict")
+        (block,) = call(restrict, [(40, 128)], f, d, absorb, s, sums, scratch=[(64, 512)], name="restrict")
         mine, to_chip, to_row, to_odd = call(
             to_chip_kernel,
             [(40, 128), (240, 128), (192, 128), (192, 128)],
-            block, x_faces, s_core, s, g, y_faces, y_more,
+            block, sums, absorb, s_core, s, g, y_faces, y_more,
             name="to_chip",
         )
         s_chip = swap(to_chip, chip_pairs)
         s_row, s_odd = swap(to_row, row_pairs[0]), swap(to_odd, odd_pairs)
-        full, beyond = call(from_chip_kernel, [(40, 128), (40, 128)], mine, x_faces, s_chip, name="from_chip")
+        full, beyond = call(from_chip_kernel, [(40, 128), (40, 128)], mine, sums, s_chip, name="from_chip")
         c_core = swap(full, core_pairs)
-        (window,) = call(window_kernel, [(136, 128)], full, beyond, c_core, s_chip, s_core, name="window")
-        windows = [window] + [swap(window, pairs) for pairs in row_pairs]
+        window, short = call(
+            window_kernel, [(136, 128), (80, 128)], full, beyond, c_core, s_chip, s_core, name="window"
+        )
+        windows = [window] + [
+            swap(short if step in short_steps else window, row_pairs[step - 1]) for step in range(1, ny)
+        ]
         pressure, coarse = call(
             finish,
             [field, (4, planes, 128)],

time: 28.8 us -> 28.7 us (level)
  transfers between devices with their start and end apart: 12 -> 12, of which waited for: 8 -> 6; matrix products, arithmetic and copies ran while one was open for 0% -> 0% of each run, Pallas kernels for 5% -> 4%
where the time goes in v9:
time: 28.7 us; the launch traced here: 28.5 us
  starting transfers between devices  13.4 us (47%)
  waiting for transfers between devices  8.3 us (29%)
  Pallas kernels  6.03 us (21%)
  between operations  0.75 us (3%)
    ppermute x12, starting transfers between devices, swap(): return lax.ppermute(array, axes, pairs)  13.4 us
    ppermute x12, waiting for transfers between devices, swap(): return lax.ppermute(array, axes, pairs)  8.3 us
    pallas_call x8, Pallas kernels, call(): pl.pallas_call(kernel, out_shape=[jax.ShapeDtypeStruct(s, F32) for s in o...  6.03 us
  transfers between devices with their start and end apart: 12, of which 6 were waited for; matrix products, arithmetic and copies ran while one was open for 0% of the time, Pallas kernels for 4%

profile of v9, /device:TPU:0, one launch (start us, length us, event | category | flops | bytes accessed | tf_op | source)
XLA Modules:
  0.0 28.5 jit_solution(7967726305863988783)
XLA Ops:
  0.7 1.6 %faces.1 = (f32[64,128]{1,0:T(8,128)S(1)}, f32[64,128]{1,0:T(8,128)S(1)}, f32[128,128]{1,0:T(8,128)S(1)}, f32[128,128]{1,0:T(8,128)S(1)}) custom-call(f32[16,16,512]{2,1,0:T(8,128)} %source.1, f32[16,16,512]{2,1,0:T(8,128)} %reaction.1, s32[16,16,512]{2,1,0:T(8,128)} %kind.1, s32[16,16,512]{2,1,0:T(8,128)} %disk_id.1, s32[16,16,512]{2,1,0:T(8,128)} %disk_mask.1, ...), custom_call_target="tpu_custom_call" | custom-call | tf_op jit(solution)/shard_map/faces/pallas_call | solution.py:22
  2.3 4.0 %collective-permute-start = (f32[128,128]{1,0:T(8,128)S(1)}, f32[128,128]{1,0:T(8,128)S(1)}, u32[]{:S(2)}, u32[]{:S(2)}) collective-permute-start(f32[128,128]{1,0:T(8,128)S(1)} %get-tuple-element.31), channel_id=1, source_target_pairs={{0,3},{1,2},{2,1},{3,0},{4,7},{5,6},{6,5},{7,4},{8,11},{9,10},{10,... | collective-permute-start | bytes 196616 | tf_op jit(solution)/shard_map/ppermute | solution.py:509
  6.2 0.5 %collective-permute-start.1 = (f32[128,128]{1,0:T(8,128)S(1)}, f32[128,128]{1,0:T(8,128)S(1)}, u32[]{:S(2)}, u32[]{:S(2)}) collective-permute-start(f32[128,128]{1,0:T(8,128)S(1)} %get-tuple-element.32), channel_id=1, source_target_pairs={{0,1},{1,0},{2,3},{3,2},{4,5},{5,4},{6,7},{7,6},{8,9},{9,8},{10,11... | collective-permute-start | bytes 196616 | tf_op jit(solution)/shard_map/ppermute | solution.py:509
  6.8 0.1 collective-permute-start.2
  6.9 1.6 %collective-permute-start.3 = (f32[64,128]{1,0:T(8,128)S(1)}, f32[64,128]{1,0:T(8,128)S(1)}, u32[]{:S(2)}, u32[]{:S(2)}) collective-permute-start(f32[64,128]{1,0:T(8,128)S(1)} %get-tuple-element.34), channel_id=1, source_target_pairs={{0,4},{1,5},{2,6},{3,7},{4,0},{5,1},{6,2},{7,3},{8,12},{9,13},{10,... | collective-permute-start | bytes 98312 | tf_op jit(solution)/shard_map/ppermute | solution.py:509
  8.5 0.5 %set_up.1 = (f32[16,16,512]{2,1,0:T(8,128)S(1)}, f32[16,16,512]{2,1,0:T(8,128)S(1)}, f32[16,16,512]{2,1,0:T(8,128)S(1)}, f32[16,128]{1,0:T(8,128)S(1)}) custom-call(f32[16,16,512]{2,1,0:T(8,128)S(1)} %copy-done, f32[16,16,512]{2,1,0:T(8,128)S(1)} %copy-done.1, s32[16,16,512]{2,1,0:T(8,128)S(1)} %copy-done.2, s32[16,16,512]{2,1,0:T(8,128)S(1)} %copy-done.3, ...), custom_call_target="tpu_custom_call" | custom-call | tf_op jit(solution)/shard_map/set_up/pallas_call | solution.py:22
  9.0 1.6 %collective-permute-done.2.chip.refs_4_ = f32[64,128]{1,0:T(8,128)S(1)} collective-permute-done((f32[64,128]{1,0:T(8,128)S(1)}, f32[64,128]{1,0:T(8,128)S(1)}, u32[]{:S(2)}, u32[]{:S(2)}) %collective-permute-start.2) | collective-permute-done | bytes 32800 | tf_op jit(solution)/shard_map/ppermute | solution.py:509
  10.7 0.0 collective-permute-done.3.core.refs_3_
  10.7 0.8 %smooth.1 = (f32[16,16,512]{2,1,0:T(8,128)S(1)}, f32[224,128]{1,0:T(8,128)S(1)}, f32[16,128]{1,0:T(8,128)S(1)}, f32[32,512]{1,0:T(8,128)S(1)}, f32[32,512]{1,0:T(8,128)S(1)}) custom-call(f32[16,16,512]{2,1,0:T(8,128)S(1)} %get-tuple-element.39.f.refs_0_, f32[16,16,512]{2,1,0:T(8,128)S(1)} %get-tuple-element.40.g.refs_1_, ...), custom_call_target="tpu_custom_call" | custom-call | tf_op jit(solution)/shard_map/smooth/pallas_call | solution.py:22
  11.6 0.1 collective-permute-start.4
  11.6 0.7 %restrict.1.block = f32[40,128]{1,0:T(8,128)S(1)} custom-call(f32[16,16,512]{2,1,0:T(8,128)S(1)} %get-tuple-element.39.f.refs_0_, f32[16,16,512]{2,1,0:T(8,128)S(1)} %get-tuple-element.48.d, f32[16,128]{1,0:T(8,128)S(1)} %get-tuple-element.41.absorb, f32[16,16,512]{2,1,0:T(8,128)S(1)} %get-tuple-element.46.s.refs_2_, f32[16,128]{1,0:T(8,128)S(1)} %get-tuple-element.49.sums), custom_call_target="tpu_custom_call" | custom-call | tf_op jit(solution)/shard_map/restrict/pallas_call | solution.py:22
  12.3 0.6 %collective-permute-done.4.core.s_core.refs_7_ = f32[224,128]{1,0:T(8,128)S(1)} collective-permute-done((f32[224,128]{1,0:T(8,128)S(1)}, f32[224,128]{1,0:T(8,128)S(1)}, u32[]{:S(2)}, u32[]{:S(2)}) %collective-permute-start.4) | collective-permute-done | bytes 114720 | tf_op jit(solution)/shard_map/ppermute | solution.py:509
  13.0 0.5 %collective-permute-start.5 = (f32[240,128]{1,0:T(8,128)S(1)}, f32[240,128]{1,0:T(8,128)S(1)}, u32[]{:S(2)}, u32[]{:S(2)}) collective-permute-start(f32[240,128]{1,0:T(8,128)S(1)} %get-tuple-element.52), channel_id=1, source_target_pairs={{0,2},{1,3},{2,0},{3,1},{4,8},{5,9},{6,10},{7,11},{8,4},{9,5},{10,... | collective-permute-start | bytes 368648 | tf_op jit(solution)/shard_map/ppermute | solution.py:509
  13.5 1.6 %collective-permute-start.6 = (f32[192,128]{1,0:T(8,128)S(1)}, f32[192,128]{1,0:T(8,128)S(1)}, u32[]{:S(2)}, u32[]{:S(2)}) collective-permute-start(f32[192,128]{1,0:T(8,128)S(1)} %get-tuple-element.53), channel_id=1, source_target_pairs={{0,1},{1,0},{2,3},{3,2},{4,5},{5,4},{6,7},{7,6},{8,9},{9,8},{10,11... | collective-permute-start | bytes 294920 | tf_op jit(solution)/shard_map/ppermute | solution.py:509
  15.0 1.5 %collective-permute-start.7 = (f32[192,128]{1,0:T(8,128)S(1)}, f32[192,128]{1,0:T(8,128)S(1)}, u32[]{:S(2)}, u32[]{:S(2)}) collective-permute-start(f32[192,128]{1,0:T(8,128)S(1)} %get-tuple-element.54), channel_id=1, source_target_pairs={{0,3},{1,2},{2,1},{3,0},{4,7},{5,6},{6,5},{7,4},{8,11},{9,10},{10,... | collective-permute-start | bytes 294920 | tf_op jit(solution)/shard_map/ppermute | solution.py:509
  16.5 1.4 %collective-permute-done.5.chip.refs_8_ = f32[240,128]{1,0:T(8,128)S(1)} collective-permute-done((f32[240,128]{1,0:T(8,128)S(1)}, f32[240,128]{1,0:T(8,128)S(1)}, u32[]{:S(2)}, u32[]{:S(2)}) %collective-permute-start.5) | collective-permute-done | bytes 122912 | tf_op jit(solution)/shard_map/ppermute | solution.py:509
  17.9 0.1 collective-permute-start.8
  18.0 1.2 %collective-permute-done.8.core = f32[40,128]{1,0:T(8,128)S(1)} collective-permute-done((f32[40,128]{1,0:T(8,128)S(1)}, f32[40,128]{1,0:T(8,128)S(1)}, u32[]{:S(2)}, u32[]{:S(2)}) %collective-permute-start.8) | collective-permute-done | bytes 20512 | tf_op jit(solution)/shard_map/ppermute | solution.py:509
  19.2 0.5 %collective-permute-start.10 = (f32[136,128]{1,0:T(8,128)S(1)}, f32[136,128]{1,0:T(8,128)S(1)}, u32[]{:S(2)}, u32[]{:S(2)}) collective-permute-start(f32[136,128]{1,0:T(8,128)S(1)} %get-tuple-element.58.refs_11_), channel_id=1, source_target_pairs={{0,2},{1,3},{2,0},{3,1},{4,6},{5,7},{6,4},{7,5},{8,10},{9,11},{10,... | collective-permute-start | bytes 208904 | tf_op jit(solution)/shard_map/ppermute | solution.py:509
  19.7 2.5 %collective-permute-start.11 = (f32[80,128]{1,0:T(8,128)S(1)}, f32[80,128]{1,0:T(8,128)S(1)}, u32[]{:S(2)}, u32[]{:S(2)}) collective-permute-start(f32[80,128]{1,0:T(8,128)S(1)} %get-tuple-element.59), channel_id=1, source_target_pairs={{0,3},{1,2},{2,1},{3,0},{4,7},{5,6},{6,5},{7,4},{8,11},{9,10},{10,... | collective-permute-start | bytes 122888 | tf_op jit(solution)/shard_map/ppermute | solution.py:509
  22.2 0.5 %collective-permute-start.9 = (f32[80,128]{1,0:T(8,128)S(1)}, f32[80,128]{1,0:T(8,128)S(1)}, u32[]{:S(2)}, u32[]{:S(2)}) collective-permute-start(f32[80,128]{1,0:T(8,128)S(1)} %get-tuple-element.59), channel_id=1, source_target_pairs={{0,1},{1,0},{2,3},{3,2},{4,5},{5,4},{6,7},{7,6},{8,9},{9,8},{10,11... | collective-permute-start | bytes 122888 | tf_op jit(solution)/shard_map/ppermute | solution.py:509
  22.8 2.1 %collective-permute-done.11.refs_14_ = f32[80,128]{1,0:T(8,128)S(1)} collective-permute-done((f32[80,128]{1,0:T(8,128)S(1)}, f32[80,128]{1,0:T(8,128)S(1)}, u32[]{:S(2)}, u32[]{:S(2)}) %collective-permute-start.11) | collective-permute-done | bytes 40992 | tf_op jit(solution)/shard_map/ppermute | solution.py:509
  24.9 1.4 %collective-permute-done.9.refs_12_ = f32[80,128]{1,0:T(8,128)S(1)} collective-permute-done((f32[80,128]{1,0:T(8,128)S(1)}, f32[80,128]{1,0:T(8,128)S(1)}, u32[]{:S(2)}, u32[]{:S(2)}) %collective-permute-start.9) | collective-permute-done | bytes 40992 | tf_op jit(solution)/shard_map/ppermute | solution.py:509
  26.3 2.3 %finish.1 = (f32[16,16,512]{2,1,0:T(8,128)}, f32[4,16,128]{2,1,0:T(8,128)}) custom-call(f32[16,16,512]{2,1,0:T(8,128)S(1)} %get-tuple-element.39.f.refs_0_, f32[16,16,512]{2,1,0:T(8,128)S(1)} %get-tuple-element.40.g.refs_1_, f32[16,16,512]{2,1,0:T(8,128)S(1)} %get-tuple-element.46.s.refs_2_, f32[64,128]{1,0:T(8,128)S(1)} %collective-permute-done.3.core.refs_3_, ...), custom_call_target="tpu_custom_call" | custom-call | tf_op jit(solution)/shard_map/finish/pallas_call | solution.py:22
  (20 shorter events, 0.1 us)
Async XLA Ops:
  0.6 7.8 %copy-start = (f32[16,16,512]{2,1,0:T(8,128)S(1)}, f32[16,16,512]{2,1,0:T(8,128)}, u32[]{:S(2)}) copy-start(f32[16,16,512]{2,1,0:T(8,128)} %source.1) | copy-start | bytes 1572868
  0.6 7.8 %copy-start.1 = (f32[16,16,512]{2,1,0:T(8,128)S(1)}, f32[16,16,512]{2,1,0:T(8,128)}, u32[]{:S(2)}) copy-start(f32[16,16,512]{2,1,0:T(8,128)} %reaction.1) | copy-start | bytes 1572868
  0.7 7.8 %copy-start.2 = (s32[16,16,512]{2,1,0:T(8,128)S(1)}, s32[16,16,512]{2,1,0:T(8,128)}, u32[]{:S(2)}) copy-start(s32[16,16,512]{2,1,0:T(8,128)} %kind.1) | copy-start | bytes 1572868
  0.7 7.8 %copy-start.3 = (s32[16,16,512]{2,1,0:T(8,128)S(1)}, s32[16,16,512]{2,1,0:T(8,128)}, u32[]{:S(2)}) copy-start(s32[16,16,512]{2,1,0:T(8,128)} %disk_id.1) | copy-start | bytes 1572868
  0.7 7.8 %copy-start.4 = (s32[16,16,512]{2,1,0:T(8,128)S(1)}, s32[16,16,512]{2,1,0:T(8,128)}, u32[]{:S(2)}) copy-start(s32[16,16,512]{2,1,0:T(8,128)} %disk_mask.1) | copy-start | bytes 1572868
  2.3 8.4 %collective-permute-start = (f32[128,128]{1,0:T(8,128)S(1)}, f32[128,128]{1,0:T(8,128)S(1)}, u32[]{:S(2)}, u32[]{:S(2)}) collective-permute-start(f32[128,128]{1,0:T(8,128)S(1)} %get-tuple-element.31), channel_id=1, source_target_pairs={{0,3},{1,2},{2,1},{3,0},{4,7},{5,6},{6,5},{7,4},{8,11},{9,10},{10,... | collective-permute-start | bytes 196616 | tf_op jit(solution)/shard_map/ppermute | solution.py:509
  6.2 4.5 %collective-permute-start.1 = (f32[128,128]{1,0:T(8,128)S(1)}, f32[128,128]{1,0:T(8,128)S(1)}, u32[]{:S(2)}, u32[]{:S(2)}) collective-permute-start(f32[128,128]{1,0:T(8,128)S(1)} %get-tuple-element.32), channel_id=1, source_target_pairs={{0,1},{1,0},{2,3},{3,2},{4,5},{5,4},{6,7},{7,6},{8,9},{9,8},{10,11... | collective-permute-start | bytes 196616 | tf_op jit(solution)/shard_map/ppermute | solution.py:509
  6.8 1.7 %copy-start.5 = (f32[120]{0:T(128)S(1)}, f32[120]{0:T(128)}, u32[]{:S(2)}) copy-start(f32[120]{0:T(128)} %param.11) | copy-start | bytes 1444
  6.8 3.9 %collective-permute-start.2 = (f32[64,128]{1,0:T(8,128)S(1)}, f32[64,128]{1,0:T(8,128)S(1)}, u32[]{:S(2)}, u32[]{:S(2)}) collective-permute-start(f32[64,128]{1,0:T(8,128)S(1)} %get-tuple-element.33), channel_id=1, source_target_pairs={{0,2},{1,3},{2,0},{3,1},{4,8},{5,9},{6,10},{7,11},{8,4},{9,5},{10,... | collective-permute-start | bytes 98312 | tf_op jit(solution)/shard_map/ppermute | solution.py:509
  6.9 3.8 %collective-permute-start.3 = (f32[64,128]{1,0:T(8,128)S(1)}, f32[64,128]{1,0:T(8,128)S(1)}, u32[]{:S(2)}, u32[]{:S(2)}) collective-permute-start(f32[64,128]{1,0:T(8,128)S(1)} %get-tuple-element.34), channel_id=1, source_target_pairs={{0,4},{1,5},{2,6},{3,7},{4,0},{5,1},{6,2},{7,3},{8,12},{9,13},{10,... | collective-permute-start | bytes 98312 | tf_op jit(solution)/shard_map/ppermute | solution.py:509
  11.6 1.4 %collective-permute-start.4 = (f32[224,128]{1,0:T(8,128)S(1)}, f32[224,128]{1,0:T(8,128)S(1)}, u32[]{:S(2)}, u32[]{:S(2)}) collective-permute-start(f32[224,128]{1,0:T(8,128)S(1)} %get-tuple-element.47), channel_id=1, source_target_pairs={{0,4},{1,5},{2,6},{3,7},{4,0},{5,1},{6,2},{7,3},{8,12},{9,13},{10,... | collective-permute-start | bytes 344072 | tf_op jit(solution)/shard_map/ppermute | solution.py:509
  13.0 4.9 %collective-permute-start.5 = (f32[240,128]{1,0:T(8,128)S(1)}, f32[240,128]{1,0:T(8,128)S(1)}, u32[]{:S(2)}, u32[]{:S(2)}) collective-permute-start(f32[240,128]{1,0:T(8,128)S(1)} %get-tuple-element.52), channel_id=1, source_target_pairs={{0,2},{1,3},{2,0},{3,1},{4,8},{5,9},{6,10},{7,11},{8,4},{9,5},{10,... | collective-permute-start | bytes 368648 | tf_op jit(solution)/shard_map/ppermute | solution.py:509
  13.5 9.3 %collective-permute-start.6 = (f32[192,128]{1,0:T(8,128)S(1)}, f32[192,128]{1,0:T(8,128)S(1)}, u32[]{:S(2)}, u32[]{:S(2)}) collective-permute-start(f32[192,128]{1,0:T(8,128)S(1)} %get-tuple-element.53), channel_id=1, source_target_pairs={{0,1},{1,0},{2,3},{3,2},{4,5},{5,4},{6,7},{7,6},{8,9},{9,8},{10,11... | collective-permute-start | bytes 294920 | tf_op jit(solution)/shard_map/ppermute | solution.py:509
  15.0 7.7 %collective-permute-start.7 = (f32[192,128]{1,0:T(8,128)S(1)}, f32[192,128]{1,0:T(8,128)S(1)}, u32[]{:S(2)}, u32[]{:S(2)}) collective-permute-start(f32[192,128]{1,0:T(8,128)S(1)} %get-tuple-element.54), channel_id=1, source_target_pairs={{0,3},{1,2},{2,1},{3,0},{4,7},{5,6},{6,5},{7,4},{8,11},{9,10},{10,... | collective-permute-start | bytes 294920 | tf_op jit(solution)/shard_map/ppermute | solution.py:509
  17.9 1.3 %collective-permute-start.8 = (f32[40,128]{1,0:T(8,128)S(1)}, f32[40,128]{1,0:T(8,128)S(1)}, u32[]{:S(2)}, u32[]{:S(2)}) collective-permute-start(f32[40,128]{1,0:T(8,128)S(1)} %get-tuple-element.56.full), channel_id=1, source_target_pairs={{0,4},{1,5},{2,6},{3,7},{4,0},{5,1},{6,2},{7,3},{8,12},{9,13},{10,... | collective-permute-start | bytes 61448 | tf_op jit(solution)/shard_map/ppermute | solution.py:509
  19.2 7.0 %collective-permute-start.10 = (f32[136,128]{1,0:T(8,128)S(1)}, f32[136,128]{1,0:T(8,128)S(1)}, u32[]{:S(2)}, u32[]{:S(2)}) collective-permute-start(f32[136,128]{1,0:T(8,128)S(1)} %get-tuple-element.58.refs_11_), channel_id=1, source_target_pairs={{0,2},{1,3},{2,0},{3,1},{4,6},{5,7},{6,4},{7,5},{8,10},{9,11},{10,... | collective-permute-start | bytes 208904 | tf_op jit(solution)/shard_map/ppermute | solution.py:509
  19.7 5.1 %collective-permute-start.11 = (f32[80,128]{1,0:T(8,128)S(1)}, f32[80,128]{1,0:T(8,128)S(1)}, u32[]{:S(2)}, u32[]{:S(2)}) collective-permute-start(f32[80,128]{1,0:T(8,128)S(1)} %get-tuple-element.59), channel_id=1, source_target_pairs={{0,3},{1,2},{2,1},{3,0},{4,7},{5,6},{6,5},{7,4},{8,11},{9,10},{10,... | collective-permute-start | bytes 122888 | tf_op jit(solution)/shard_map/ppermute | solution.py:509
  22.2 4.0 %collective-permute-start.9 = (f32[80,128]{1,0:T(8,128)S(1)}, f32[80,128]{1,0:T(8,128)S(1)}, u32[]{:S(2)}, u32[]{:S(2)}) collective-permute-start(f32[80,128]{1,0:T(8,128)S(1)} %get-tuple-element.59), channel_id=1, source_target_pairs={{0,1},{1,0},{2,3},{3,2},{4,5},{5,4},{6,7},{7,6},{8,9},{9,8},{10,11... | collective-permute-start | bytes 122888 | tf_op jit(solution)/shard_map/ppermute | solution.py:509

commit v10 on v9

--- a/solution.py
+++ b/solution.py
@@ -344,11 +344,33 @@
     planes = 4 * ny
     short_steps = (1, 3) if ny == 4 else (1,)
 
+    def prepare(f, g, s, a_core, a_chip, a_row, a_odd, s_core, s_chip, s_row, s_odd, u, u_low, u_high, g_x, g_y, edge):
+        x_at, y_at, x_even, y_even = where_am_i()
+        s_left, s_right = halo_x(s_core, s_chip, 0, x_at, x_even)
+        s_left2, s_right2 = halo_x(s_core, s_chip, 64, x_at, x_even)
+        f_left, f_right = halo_x(a_core, a_chip, 0, x_at, x_even)
+        g_x[0], g_x[1] = halo_x(s_core, s_chip, 128, x_at, x_even)
+        y1 = halo_y(s_row, s_odd, 0, y_at, y_even)
+        y2 = halo_y(s_row, s_odd, 64, y_at, y_even)
+        f_y = halo_y(a_row, a_odd, 0, y_at, y_even)
+        g_y[0], g_y[1] = halo_y(a_row, a_odd, 64, y_at, y_even)
+        u[0] = 0.2 * s_left + f_left + g_x[0] * (s_left2 + s[0] + beside(s_left))
+        u[17] = 0.2 * s_right + f_right + g_x[1] * (s_right2 + s[15] + beside(s_right))
+        for x in range(16):
+            here = s[x]
+            total = (s[x - 1] if x > 0 else s_left) + (s[x + 1] if x < 15 else s_right)
+            total = total + beside(here, y1[0][x : x + 1, :], y1[1][x : x + 1, :])
+            u[x + 1] = 0.2 * here + f[x] + g[x] * total
+            edge[0, x : x + 1, :] = here[0:1, :]
+            edge[1, x : x + 1, :] = here[15:16, :]
+        for at, out in enumerate((u_low, u_high)):
+            out[...] = 0.2 * y1[at] + f_y[at] + g_y[at] * (y2[at] + edge[at] + beside(y1[at]))
+
     def finish(*refs):
-        f, g, s, a_core, a_chip, a_row, a_odd, s_core, s_chip, s_row, s_odd = refs[:11]
-        windows = refs[11 : 11 + ny]
-        pressure, coarse = refs[11 + ny : 13 + ny]
-        every, res, diag, inv, one, two, sol, Pc, T, U, yl, yh, tl, th, ul, uh, result, slab_out, sems = refs[13 + ny :]
+        f, g, u, u_low, u_high, g_x, g_y, s_row, s_odd = refs[:9]
+        windows = refs[9 : 9 + ny]
+        pressure, coarse = refs[9 + ny : 11 + ny]
+        every, res, diag, inv, one, two, sol, C, U, ul, uh, result, slab_out, sems = refs[11 + ny :]
         x_at, y_at, x_even, y_even = where_am_i()
         for step, window in enumerate(windows):
             there = jnp.bitwise_xor(y_at, step)
@@ -435,59 +457,46 @@
         moves[0].start()
 
         first_plane = 4 * y_at + 1
+        below, above = first_plane - 1, first_plane + 4
         for at in range(6):
-            Pc[at] = spread_lanes(spread_planes(sol, first_plane, 3 + at))
-        s_left, s_right = halo_x(s_core, s_chip, 0, x_at, x_even)
-        s_left2, s_right2 = halo_x(s_core, s_chip, 64, x_at, x_even)
-        T[0], T[1] = s_left2 + Pc[0], s_left + Pc[0]
-        T[18], T[19] = s_right + Pc[5], s_right2 + Pc[5]
-
-        for x in range(16):
-            T[x + 2] = s[x] + Pc[x // 4 + 1]
-        below, above = first_plane - 1, first_plane + 4
-        y1_low, y1_high = halo_y(s_row, s_odd, 0, y_at, y_even)
-        y2_low, y2_high = halo_y(s_row, s_odd, 64, y_at, y_even)
-        g_low, g_high = halo_y(a_row, a_odd, 64, y_at, y_even)
-        f_low, f_high = halo_y(a_row, a_odd, 0, y_at, y_even)
+            C[at] = spread_lanes(spread_planes(sol, first_plane, 3 + at))
+        outside = [[spread_lanes(sol[plane, 3 + at : 4 + at, :]) for at in range(6)] for plane in (below, above)]
         before, after = jnp.maximum(y_at - 1, 0), jnp.minimum(y_at + 1, ny - 1)
-        outer = {}
-        for name, ref, plane, s1, s2, who, inside, line in (
-            ("low", tl, below, y1_low, y2_low, before, y_at > 0, 1),
-            ("high", th, above, y1_high, y2_high, after, y_at < ny - 1, 0),
-        ):
-            spread = spread_lanes(spread_rows(sol, plane, 4))
-            ref[8:24, :] = s1 + spread
-            outer[name] = s2 + spread
-            for at, cx, base, there in ((7, 3, 0, x_at > 0), (24, 8, 2, x_at < nx - 1)):
+        corners = []
+        for who, inside, line in ((before, y_at > 0, 1), (after, y_at < ny - 1, 0)):
+            for base, there in ((0, x_at > 0), (2, x_at < nx - 1)):
                 corner = jnp.concatenate(
                     [every[who, pl.ds(120 + 4 * (base + line) + j, 1), :] for j in range(4)], axis=1
                 )
-                corner = jnp.where(inside & there, corner, 0.0)
-                ref[at : at + 1, :] = corner + spread_lanes(sol[plane, cx : cx + 1, :])
-
-        f_left, f_right = halo_x(a_core, a_chip, 0, x_at, x_even)
-        g_left, g_right = halo_x(s_core, s_chip, 128, x_at, x_even)
-
-        def fourth_at(at, forcing, scale):
-            here = T[at + 1]
-            total = T[at] + T[at + 2] + beside(here, tl[at + 7 : at + 8, :], th[at + 7 : at + 8, :])
-            return 0.2 * here + forcing + scale * total
-
-        U[0] = fourth_at(0, f_left, g_left)
-        U[17] = fourth_at(17, f_right, g_right)
-
-        for x in range(16):
-            U[x + 1] = fourth_at(x + 1, f[x], g[x])
-            here = T[x + 2]
-            yl[x : x + 1, :] = here[0:1, :]
-            yh[x : x + 1, :] = here[15:16, :]
-        for ref, out, edge, far, forcing, scale in (
-            (tl, ul, yl, outer["low"], f_low, g_low),
-            (th, uh, yh, outer["high"], f_high, g_high),
+                corners.append(jnp.where(inside & there, corner, 0.0))
+        edge_row = iota((16, 512), 0)
+
+        def ends(first, last):
+            first, last = (jnp.broadcast_to(line, (16, 512)) for line in (first, last))
+            return jnp.where(edge_row == 0, first, jnp.where(edge_row == 15, last, 0.0))
+
+        for at in range(6):
+            here = C[at]
+            around = beside(here, outside[0][at], outside[1][at])
+            fifth_of = 0.2 * here
+            if at == 0:
+                U[0] = u[0] + fifth_of + g_x[0] * (around + here + C[1] + ends(corners[0], corners[2]))
+            elif at == 5:
+                U[17] = u[17] + fifth_of + g_x[1] * (around + here + C[4] + ends(corners[1], corners[3]))
+            else:
+                inner = around + 2.0 * here
+                sides = [around + here + C[at - 1], inner, inner, around + here + C[at + 1]]
+                for q in range(4):
+                    x = 4 * (at - 1) + q
+                    U[x + 1] = u[x + 1] + fifth_of + g[x] * sides[q]
+        for at, (part, out, plane, inside) in enumerate(
+            ((u_low, ul, below, first_plane), (u_high, uh, above, first_plane + 3))
         ):
-            here = ref[8:24, :]
-            total = far + edge[...] + ref[7:23, :] + ref[9:25, :] + beside_z(here)
-            out[...] = 0.2 * here + forcing + scale * total
+            beyond = spread_lanes(spread_rows(sol, plane, 4))
+            edge = spread_lanes(spread_rows(sol, inside, 4))
+            around = beside(beyond, outside[at][0], outside[at][5])
+            total = beyond + edge + around + ends(corners[2 * at], corners[2 * at + 1])
+            out[...] = part[...] + 0.2 * beyond + g_y[at] * total
 
         for x in range(16):
             here = U[x + 1]
@@ -554,15 +563,21 @@
         windows = [window] + [
             swap(short if step in short_steps else window, row_pairs[step - 1]) for step in range(1, ny)
         ]
+        prepared = call(
+            prepare,
+            [long, slab, slab, (2, 16, 512), (2, 16, 512)],
+            f, g, s, a_core, a_chip, a_row, a_odd, s_core, s_chip, s_row, s_odd,
+            scratch=[(2, 16, 512)],
+            name="prepare",
+        )
         pressure, coarse = call(
             finish,
             [field, (4, planes, 128)],
-            f, g, s, a_core, a_chip, a_row, a_odd, s_core, s_chip, s_row, s_odd, *windows,
+            f, g, *prepared, s_row, s_odd, *windows,
             scratch=[(ny, 136, 128)]
             + [(planes, 16, 128)] * 3
             + [(planes + 2, 16, 128)] * 3
-            + [(6, 16, 512), (20, 16, 512), long, slab, slab, (32, 512), (32, 512), slab, slab, field]
-            + [(4, planes, 128), pltpu.SemaphoreType.DMA((9,))],
+            + [(6, 16, 512), long, slab, slab, field, (4, planes, 128), pltpu.SemaphoreType.DMA((9,))],
             out_specs=[HBM, HBM],
             name="finish",
         )

time: 28.7 us -> 28.5 us (level)
  waiting for transfers between devices: 8.3 us -> 7.68 us
  Pallas kernels: 6.03 us -> 6.46 us
    ppermute x12, waiting for transfers between devices: 8.3 us -> 7.68 us  [swap(): return lax.ppermute(array, axes, pairs)]
    pallas_call x8 -> x9, Pallas kernels: 6.03 us -> 6.46 us  [call(): pl.pallas_call(kernel, out_shape=[jax.ShapeDtypeStruct(s, F32) for s in o...]
  transfers between devices with their start and end apart: 12 -> 12, of which waited for: 6 -> 6; matrix products, arithmetic and copies ran while one was open for 0% -> 0% of each run, Pallas kernels for 4% -> 6%
where the time goes in v10:
time: 28.5 us; the launch traced here: 28.4 us
  starting transfers between devices  13.4 us (47%)
  waiting for transfers between devices  7.68 us (27%)
  Pallas kernels  6.46 us (23%)
  between operations  0.76 us (3%)
    ppermute x12, starting transfers between devices, swap(): return lax.ppermute(array, axes, pairs)  13.4 us
    ppermute x12, waiting for transfers between devices, swap(): return lax.ppermute(array, axes, pairs)  7.68 us
    pallas_call x9, Pallas kernels, call(): pl.pallas_call(kernel, out_shape=[jax.ShapeDtypeStruct(s, F32) for s in o...  6.46 us
  transfers between devices with their start and end apart: 12, of which 6 were waited for; matrix products, arithmetic and copies ran while one was open for 0% of the time, Pallas kernels for 6%

profile of v10, /device:TPU:0, one launch (start us, length us, event | category | flops | bytes accessed | tf_op | source)
XLA Modules:
  0.0 28.4 jit_solution(15858170931183601455)
XLA Ops:
  0.7 1.6 %faces.1 = (f32[64,128]{1,0:T(8,128)S(1)}, f32[64,128]{1,0:T(8,128)S(1)}, f32[128,128]{1,0:T(8,128)S(1)}, f32[128,128]{1,0:T(8,128)S(1)}) custom-call(f32[16,16,512]{2,1,0:T(8,128)} %source.1, f32[16,16,512]{2,1,0:T(8,128)} %reaction.1, s32[16,16,512]{2,1,0:T(8,128)} %kind.1, s32[16,16,512]{2,1,0:T(8,128)} %disk_id.1, s32[16,16,512]{2,1,0:T(8,128)} %disk_mask.1, ...), custom_call_target="tpu_custom_call" | custom-call | tf_op jit(solution)/shard_map/faces/pallas_call | solution.py:22
  2.3 4.0 %collective-permute-start = (f32[128,128]{1,0:T(8,128)S(1)}, f32[128,128]{1,0:T(8,128)S(1)}, u32[]{:S(2)}, u32[]{:S(2)}) collective-permute-start(f32[128,128]{1,0:T(8,128)S(1)} %get-tuple-element.36), channel_id=1, source_target_pairs={{0,3},{1,2},{2,1},{3,0},{4,7},{5,6},{6,5},{7,4},{8,11},{9,10},{10,... | collective-permute-start | bytes 196616 | tf_op jit(solution)/shard_map/ppermute | solution.py:518
  6.2 0.5 %collective-permute-start.1 = (f32[128,128]{1,0:T(8,128)S(1)}, f32[128,128]{1,0:T(8,128)S(1)}, u32[]{:S(2)}, u32[]{:S(2)}) collective-permute-start(f32[128,128]{1,0:T(8,128)S(1)} %get-tuple-element.37), channel_id=1, source_target_pairs={{0,1},{1,0},{2,3},{3,2},{4,5},{5,4},{6,7},{7,6},{8,9},{9,8},{10,11... | collective-permute-start | bytes 196616 | tf_op jit(solution)/shard_map/ppermute | solution.py:518
  6.8 0.1 collective-permute-start.2
  6.9 1.6 %collective-permute-start.3 = (f32[64,128]{1,0:T(8,128)S(1)}, f32[64,128]{1,0:T(8,128)S(1)}, u32[]{:S(2)}, u32[]{:S(2)}) collective-permute-start(f32[64,128]{1,0:T(8,128)S(1)} %get-tuple-element.39), channel_id=1, source_target_pairs={{0,4},{1,5},{2,6},{3,7},{4,0},{5,1},{6,2},{7,3},{8,12},{9,13},{10,... | collective-permute-start | bytes 98312 | tf_op jit(solution)/shard_map/ppermute | solution.py:518
  8.5 0.5 %set_up.1 = (f32[16,16,512]{2,1,0:T(8,128)S(1)}, f32[16,16,512]{2,1,0:T(8,128)S(1)}, f32[16,16,512]{2,1,0:T(8,128)S(1)}, f32[16,128]{1,0:T(8,128)S(1)}) custom-call(f32[16,16,512]{2,1,0:T(8,128)S(1)} %copy-done, f32[16,16,512]{2,1,0:T(8,128)S(1)} %copy-done.1, s32[16,16,512]{2,1,0:T(8,128)S(1)} %copy-done.2, s32[16,16,512]{2,1,0:T(8,128)S(1)} %copy-done.3, ...), custom_call_target="tpu_custom_call" | custom-call | tf_op jit(solution)/shard_map/set_up/pallas_call | solution.py:22
  9.0 1.7 %collective-permute-done.2.chip.a_chip = f32[64,128]{1,0:T(8,128)S(1)} collective-permute-done((f32[64,128]{1,0:T(8,128)S(1)}, f32[64,128]{1,0:T(8,128)S(1)}, u32[]{:S(2)}, u32[]{:S(2)}) %collective-permute-start.2) | collective-permute-done | bytes 32800 | tf_op jit(solution)/shard_map/ppermute | solution.py:518
  10.7 0.8 %smooth.1 = (f32[16,16,512]{2,1,0:T(8,128)S(1)}, f32[224,128]{1,0:T(8,128)S(1)}, f32[16,128]{1,0:T(8,128)S(1)}, f32[32,512]{1,0:T(8,128)S(1)}, f32[32,512]{1,0:T(8,128)S(1)}) custom-call(f32[16,16,512]{2,1,0:T(8,128)S(1)} %get-tuple-element.44.f.refs_0_, f32[16,16,512]{2,1,0:T(8,128)S(1)} %get-tuple-element.45.g.refs_1_, ...), custom_call_target="tpu_custom_call" | custom-call | tf_op jit(solution)/shard_map/smooth/pallas_call | solution.py:22
  11.5 0.1 collective-permute-start.4
  11.6 0.7 %restrict.1.block = f32[40,128]{1,0:T(8,128)S(1)} custom-call(f32[16,16,512]{2,1,0:T(8,128)S(1)} %get-tuple-element.44.f.refs_0_, f32[16,16,512]{2,1,0:T(8,128)S(1)} %get-tuple-element.53.d, f32[16,128]{1,0:T(8,128)S(1)} %get-tuple-element.46.absorb, f32[16,16,512]{2,1,0:T(8,128)S(1)} %get-tuple-element.51.s, f32[16,128]{1,0:T(8,128)S(1)} %get-tuple-element.54.sums), custom_call_target="tpu_custom_call" | custom-call | tf_op jit(solution)/shard_map/restrict/pallas_call | solution.py:22
  12.3 0.6 %collective-permute-done.4.core.s_core = f32[224,128]{1,0:T(8,128)S(1)} collective-permute-done((f32[224,128]{1,0:T(8,128)S(1)}, f32[224,128]{1,0:T(8,128)S(1)}, u32[]{:S(2)}, u32[]{:S(2)}) %collective-permute-start.4) | collective-permute-done | bytes 114720 | tf_op jit(solution)/shard_map/ppermute | solution.py:518
  13.0 0.5 %collective-permute-start.5 = (f32[240,128]{1,0:T(8,128)S(1)}, f32[240,128]{1,0:T(8,128)S(1)}, u32[]{:S(2)}, u32[]{:S(2)}) collective-permute-start(f32[240,128]{1,0:T(8,128)S(1)} %get-tuple-element.57), channel_id=1, source_target_pairs={{0,2},{1,3},{2,0},{3,1},{4,8},{5,9},{6,10},{7,11},{8,4},{9,5},{10,... | collective-permute-start | bytes 368648 | tf_op jit(solution)/shard_map/ppermute | solution.py:518
  13.5 1.6 %collective-permute-start.6 = (f32[192,128]{1,0:T(8,128)S(1)}, f32[192,128]{1,0:T(8,128)S(1)}, u32[]{:S(2)}, u32[]{:S(2)}) collective-permute-start(f32[192,128]{1,0:T(8,128)S(1)} %get-tuple-element.58), channel_id=1, source_target_pairs={{0,1},{1,0},{2,3},{3,2},{4,5},{5,4},{6,7},{7,6},{8,9},{9,8},{10,11... | collective-permute-start | bytes 294920 | tf_op jit(solution)/shard_map/ppermute | solution.py:518
  15.0 1.5 %collective-permute-start.7 = (f32[192,128]{1,0:T(8,128)S(1)}, f32[192,128]{1,0:T(8,128)S(1)}, u32[]{:S(2)}, u32[]{:S(2)}) collective-permute-start(f32[192,128]{1,0:T(8,128)S(1)} %get-tuple-element.59), channel_id=1, source_target_pairs={{0,3},{1,2},{2,1},{3,0},{4,7},{5,6},{6,5},{7,4},{8,11},{9,10},{10,... | collective-permute-start | bytes 294920 | tf_op jit(solution)/shard_map/ppermute | solution.py:518
  16.5 1.4 %collective-permute-done.5.s_chip.chip = f32[240,128]{1,0:T(8,128)S(1)} collective-permute-done((f32[240,128]{1,0:T(8,128)S(1)}, f32[240,128]{1,0:T(8,128)S(1)}, u32[]{:S(2)}, u32[]{:S(2)}) %collective-permute-start.5) | collective-permute-done | bytes 122912 | tf_op jit(solution)/shard_map/ppermute | solution.py:518
  17.9 0.1 collective-permute-start.8
  18.0 1.2 %collective-permute-done.8.core = f32[40,128]{1,0:T(8,128)S(1)} collective-permute-done((f32[40,128]{1,0:T(8,128)S(1)}, f32[40,128]{1,0:T(8,128)S(1)}, u32[]{:S(2)}, u32[]{:S(2)}) %collective-permute-start.8) | collective-permute-done | bytes 20512 | tf_op jit(solution)/shard_map/ppermute | solution.py:518
  19.2 0.5 %collective-permute-start.10 = (f32[136,128]{1,0:T(8,128)S(1)}, f32[136,128]{1,0:T(8,128)S(1)}, u32[]{:S(2)}, u32[]{:S(2)}) collective-permute-start(f32[136,128]{1,0:T(8,128)S(1)} %get-tuple-element.68.refs_9_), channel_id=1, source_target_pairs={{0,2},{1,3},{2,0},{3,1},{4,6},{5,7},{6,4},{7,5},{8,10},{9,11},{10,... | collective-permute-start | bytes 208904 | tf_op jit(solution)/shard_map/ppermute | solution.py:518
  19.7 1.6 %collective-permute-start.9 = (f32[80,128]{1,0:T(8,128)S(1)}, f32[80,128]{1,0:T(8,128)S(1)}, u32[]{:S(2)}, u32[]{:S(2)}) collective-permute-start(f32[80,128]{1,0:T(8,128)S(1)} %get-tuple-element.69), channel_id=1, source_target_pairs={{0,1},{1,0},{2,3},{3,2},{4,5},{5,4},{6,7},{7,6},{8,9},{9,8},{10,11... | collective-permute-start | bytes 122888 | tf_op jit(solution)/shard_map/ppermute | solution.py:518
  21.3 1.5 %collective-permute-start.11 = (f32[80,128]{1,0:T(8,128)S(1)}, f32[80,128]{1,0:T(8,128)S(1)}, u32[]{:S(2)}, u32[]{:S(2)}) collective-permute-start(f32[80,128]{1,0:T(8,128)S(1)} %get-tuple-element.69), channel_id=1, source_target_pairs={{0,3},{1,2},{2,1},{3,0},{4,7},{5,6},{6,5},{7,4},{8,11},{9,10},{10,... | collective-permute-start | bytes 122888 | tf_op jit(solution)/shard_map/ppermute | solution.py:518
  22.8 0.5 %prepare.1 = (f32[18,16,512]{2,1,0:T(8,128)S(1)}, f32[16,512]{1,0:T(8,128)S(1)}, f32[16,512]{1,0:T(8,128)S(1)}, f32[2,16,512]{2,1,0:T(8,128)S(1)}, f32[2,16,512]{2,1,0:T(8,128)S(1)}) custom-call(f32[16,16,512]{2,1,0:T(8,128)S(1)} %get-tuple-element.44.f.refs_0_, f32[16,16,512]{2,1,0:T(8,128)S(1)} %get-tuple-element.45.g.refs_1_, ...), custom_call_target="tpu_custom_call" | custom-call | tf_op jit(solution)/shard_map/prepare/pallas_call | solution.py:22
  23.3 0.4 %collective-permute-done.9.refs_10_ = f32[80,128]{1,0:T(8,128)S(1)} collective-permute-done((f32[80,128]{1,0:T(8,128)S(1)}, f32[80,128]{1,0:T(8,128)S(1)}, u32[]{:S(2)}, u32[]{:S(2)}) %collective-permute-start.9) | collective-permute-done | bytes 40992 | tf_op jit(solution)/shard_map/ppermute | solution.py:518
  23.7 2.5 %collective-permute-done.11.refs_12_ = f32[80,128]{1,0:T(8,128)S(1)} collective-permute-done((f32[80,128]{1,0:T(8,128)S(1)}, f32[80,128]{1,0:T(8,128)S(1)}, u32[]{:S(2)}, u32[]{:S(2)}) %collective-permute-start.11) | collective-permute-done | bytes 40992 | tf_op jit(solution)/shard_map/ppermute | solution.py:518
  26.2 2.2 %finish.1 = (f32[16,16,512]{2,1,0:T(8,128)}, f32[4,16,128]{2,1,0:T(8,128)}) custom-call(f32[16,16,512]{2,1,0:T(8,128)S(1)} %get-tuple-element.44.f.refs_0_, f32[16,16,512]{2,1,0:T(8,128)S(1)} %get-tuple-element.45.g.refs_1_, f32[18,16,512]{2,1,0:T(8,128)S(1)} %get-tuple-element.60.refs_2_, f32[16,512]{1,0:T(8,128)S(1)} %get-tuple-element.61.refs_3_, ...), custom_call_target="tpu_custom_call" | custom-call | tf_op jit(solution)/shard_map/finish/pallas_call | solution.py:22
  (21 shorter events, 0.1 us)
Async XLA Ops:
  0.6 7.8 %copy-start = (f32[16,16,512]{2,1,0:T(8,128)S(1)}, f32[16,16,512]{2,1,0:T(8,128)}, u32[]{:S(2)}) copy-start(f32[16,16,512]{2,1,0:T(8,128)} %source.1) | copy-start | bytes 1572868
  0.6 7.8 %copy-start.1 = (f32[16,16,512]{2,1,0:T(8,128)S(1)}, f32[16,16,512]{2,1,0:T(8,128)}, u32[]{:S(2)}) copy-start(f32[16,16,512]{2,1,0:T(8,128)} %reaction.1) | copy-start | bytes 1572868
  0.7 7.8 %copy-start.2 = (s32[16,16,512]{2,1,0:T(8,128)S(1)}, s32[16,16,512]{2,1,0:T(8,128)}, u32[]{:S(2)}) copy-start(s32[16,16,512]{2,1,0:T(8,128)} %kind.1) | copy-start | bytes 1572868
  0.7 7.8 %copy-start.3 = (s32[16,16,512]{2,1,0:T(8,128)S(1)}, s32[16,16,512]{2,1,0:T(8,128)}, u32[]{:S(2)}) copy-start(s32[16,16,512]{2,1,0:T(8,128)} %disk_id.1) | copy-start | bytes 1572868
  0.7 7.8 %copy-start.4 = (s32[16,16,512]{2,1,0:T(8,128)S(1)}, s32[16,16,512]{2,1,0:T(8,128)}, u32[]{:S(2)}) copy-start(s32[16,16,512]{2,1,0:T(8,128)} %disk_mask.1) | copy-start | bytes 1572868
  2.3 8.4 %collective-permute-start = (f32[128,128]{1,0:T(8,128)S(1)}, f32[128,128]{1,0:T(8,128)S(1)}, u32[]{:S(2)}, u32[]{:S(2)}) collective-permute-start(f32[128,128]{1,0:T(8,128)S(1)} %get-tuple-element.36), channel_id=1, source_target_pairs={{0,3},{1,2},{2,1},{3,0},{4,7},{5,6},{6,5},{7,4},{8,11},{9,10},{10,... | collective-permute-start | bytes 196616 | tf_op jit(solution)/shard_map/ppermute | solution.py:518
  6.2 4.5 %collective-permute-start.1 = (f32[128,128]{1,0:T(8,128)S(1)}, f32[128,128]{1,0:T(8,128)S(1)}, u32[]{:S(2)}, u32[]{:S(2)}) collective-permute-start(f32[128,128]{1,0:T(8,128)S(1)} %get-tuple-element.37), channel_id=1, source_target_pairs={{0,1},{1,0},{2,3},{3,2},{4,5},{5,4},{6,7},{7,6},{8,9},{9,8},{10,11... | collective-permute-start | bytes 196616 | tf_op jit(solution)/shard_map/ppermute | solution.py:518
  6.8 1.7 %copy-start.5 = (f32[120]{0:T(128)S(1)}, f32[120]{0:T(128)}, u32[]{:S(2)}) copy-start(f32[120]{0:T(128)} %param.11) | copy-start | bytes 1444
  6.8 3.9 %collective-permute-start.2 = (f32[64,128]{1,0:T(8,128)S(1)}, f32[64,128]{1,0:T(8,128)S(1)}, u32[]{:S(2)}, u32[]{:S(2)}) collective-permute-start(f32[64,128]{1,0:T(8,128)S(1)} %get-tuple-element.38), channel_id=1, source_target_pairs={{0,2},{1,3},{2,0},{3,1},{4,8},{5,9},{6,10},{7,11},{8,4},{9,5},{10,... | collective-permute-start | bytes 98312 | tf_op jit(solution)/shard_map/ppermute | solution.py:518
  6.9 3.8 %collective-permute-start.3 = (f32[64,128]{1,0:T(8,128)S(1)}, f32[64,128]{1,0:T(8,128)S(1)}, u32[]{:S(2)}, u32[]{:S(2)}) collective-permute-start(f32[64,128]{1,0:T(8,128)S(1)} %get-tuple-element.39), channel_id=1, source_target_pairs={{0,4},{1,5},{2,6},{3,7},{4,0},{5,1},{6,2},{7,3},{8,12},{9,13},{10,... | collective-permute-start | bytes 98312 | tf_op jit(solution)/shard_map/ppermute | solution.py:518
  11.5 1.4 %collective-permute-start.4 = (f32[224,128]{1,0:T(8,128)S(1)}, f32[224,128]{1,0:T(8,128)S(1)}, u32[]{:S(2)}, u32[]{:S(2)}) collective-permute-start(f32[224,128]{1,0:T(8,128)S(1)} %get-tuple-element.52), channel_id=1, source_target_pairs={{0,4},{1,5},{2,6},{3,7},{4,0},{5,1},{6,2},{7,3},{8,12},{9,13},{10,... | collective-permute-start | bytes 344072 | tf_op jit(solution)/shard_map/ppermute | solution.py:518
  13.0 4.9 %collective-permute-start.5 = (f32[240,128]{1,0:T(8,128)S(1)}, f32[240,128]{1,0:T(8,128)S(1)}, u32[]{:S(2)}, u32[]{:S(2)}) collective-permute-start(f32[240,128]{1,0:T(8,128)S(1)} %get-tuple-element.57), channel_id=1, source_target_pairs={{0,2},{1,3},{2,0},{3,1},{4,8},{5,9},{6,10},{7,11},{8,4},{9,5},{10,... | collective-permute-start | bytes 368648 | tf_op jit(solution)/shard_map/ppermute | solution.py:518
  13.5 9.3 %collective-permute-start.6 = (f32[192,128]{1,0:T(8,128)S(1)}, f32[192,128]{1,0:T(8,128)S(1)}, u32[]{:S(2)}, u32[]{:S(2)}) collective-permute-start(f32[192,128]{1,0:T(8,128)S(1)} %get-tuple-element.58), channel_id=1, source_target_pairs={{0,1},{1,0},{2,3},{3,2},{4,5},{5,4},{6,7},{7,6},{8,9},{9,8},{10,11... | collective-permute-start | bytes 294920 | tf_op jit(solution)/shard_map/ppermute | solution.py:518
  15.0 7.7 %collective-permute-start.7 = (f32[192,128]{1,0:T(8,128)S(1)}, f32[192,128]{1,0:T(8,128)S(1)}, u32[]{:S(2)}, u32[]{:S(2)}) collective-permute-start(f32[192,128]{1,0:T(8,128)S(1)} %get-tuple-element.59), channel_id=1, source_target_pairs={{0,3},{1,2},{2,1},{3,0},{4,7},{5,6},{6,5},{7,4},{8,11},{9,10},{10,... | collective-permute-start | bytes 294920 | tf_op jit(solution)/shard_map/ppermute | solution.py:518
  17.9 1.3 %collective-permute-start.8 = (f32[40,128]{1,0:T(8,128)S(1)}, f32[40,128]{1,0:T(8,128)S(1)}, u32[]{:S(2)}, u32[]{:S(2)}) collective-permute-start(f32[40,128]{1,0:T(8,128)S(1)} %get-tuple-element.66.full), channel_id=1, source_target_pairs={{0,4},{1,5},{2,6},{3,7},{4,0},{5,1},{6,2},{7,3},{8,12},{9,13},{10,... | collective-permute-start | bytes 61448 | tf_op jit(solution)/shard_map/ppermute | solution.py:518
  19.2 7.0 %collective-permute-start.10 = (f32[136,128]{1,0:T(8,128)S(1)}, f32[136,128]{1,0:T(8,128)S(1)}, u32[]{:S(2)}, u32[]{:S(2)}) collective-permute-start(f32[136,128]{1,0:T(8,128)S(1)} %get-tuple-element.68.refs_9_), channel_id=1, source_target_pairs={{0,2},{1,3},{2,0},{3,1},{4,6},{5,7},{6,4},{7,5},{8,10},{9,11},{10,... | collective-permute-start | bytes 208904 | tf_op jit(solution)/shard_map/ppermute | solution.py:518
  19.7 4.0 %collective-permute-start.9 = (f32[80,128]{1,0:T(8,128)S(1)}, f32[80,128]{1,0:T(8,128)S(1)}, u32[]{:S(2)}, u32[]{:S(2)}) collective-permute-start(f32[80,128]{1,0:T(8,128)S(1)} %get-tuple-element.69), channel_id=1, source_target_pairs={{0,1},{1,0},{2,3},{3,2},{4,5},{5,4},{6,7},{7,6},{8,9},{9,8},{10,11... | collective-permute-start | bytes 122888 | tf_op jit(solution)/shard_map/ppermute | solution.py:518
  21.3 4.9 %collective-permute-start.11 = (f32[80,128]{1,0:T(8,128)S(1)}, f32[80,128]{1,0:T(8,128)S(1)}, u32[]{:S(2)}, u32[]{:S(2)}) collective-permute-start(f32[80,128]{1,0:T(8,128)S(1)} %get-tuple-element.69), channel_id=1, source_target_pairs={{0,3},{1,2},{2,1},{3,0},{4,7},{5,6},{6,5},{7,4},{8,11},{9,10},{10,... | collective-permute-start | bytes 122888 | tf_op jit(solution)/shard_map/ppermute | solution.py:518

commit v11 on v10

--- a/solution.py
+++ b/solution.py
@@ -16,6 +16,8 @@
 
 
 HBM = pl.BlockSpec(memory_space=pltpu.HBM)
+MORE = 152
+FACES = 192
 
 
 def call(kernel, outs, *args, scratch=(), name=None, in_specs=None, out_specs=None):
@@ -206,8 +208,8 @@
         pick = ((src // 16 == out % 4) & ((src % 16) // 4 == out // 4)).astype(F32)
         absorb[...] = dot(dot(pick, V[...]), group_lanes(512))
 
-    def halo_x(core, chip, row, x, x_even):
-        a, b = get(core, row, 16, 512), get(chip, row, 16, 512)
+    def halo_x(core, chip, row, x, x_even, chip_row=None):
+        a, b = get(core, row, 16, 512), get(chip, row if chip_row is None else chip_row, 16, 512)
         left = jnp.where(x > 0, jnp.where(x_even, b, a), 0.0)
         right = jnp.where(x < nx - 1, jnp.where(x_even, a, b), 0.0)
         return left, right
@@ -279,11 +281,9 @@
             mine[a : a + 1, :] = block[a : a + 1, :] + jnp.where(x_even, 0.0, line)
             mine[b : b + 1, :] = block[b : b + 1, :] + jnp.where(x_even, line, 0.0)
         put(to_chip, 0, s[jnp.where(x_even, 0, 15)])
-        put(to_chip, 64, s[jnp.where(x_even, 1, 14)])
-        put(to_chip, 128, g[jnp.where(x_even, 0, 15)])
-        to_chip[192:232, :] = mine[...]
-        to_chip[232:236, :] = jnp.where(x_even, sums[0:4, :], sums[4:8, :])
-        to_chip[236:240, :] = jnp.zeros((4, 128), F32)
+        to_chip[64:104, :] = mine[...]
+        to_chip[104:108, :] = jnp.where(x_even, sums[0:4, :], sums[4:8, :])
+        to_chip[108:112, :] = jnp.zeros((4, 128), F32)
         for at, ref in enumerate((y_faces, y_more)):
             a, b = ref[0:16, :], ref[16:32, :]
             put(to_row, 64 * at, jnp.where(y_even, b, a))
@@ -300,23 +300,26 @@
             ref[160:168, :] = sums[8:16, :]
             ref[168:176, :] = core[200:208, :]
             ref[176:180, :] = corner
-            ref[180:192, :] = jnp.zeros((12, 128), F32)
-
-    def from_chip_kernel(mine, sums, chip, full, beyond):
+            ref[180:FACES, :] = jnp.zeros((FACES - 180, 128), F32)
+
+    def from_chip_kernel(mine, sums, chip, s, g, full, beyond, more):
         x_at, _, x_even, _ = where_am_i()
         has = jnp.where(x_even, x_at > 0, x_at < nx - 1)
         full[...] = mine[...]
-        beyond[...] = chip[192:232, :]
+        beyond[...] = chip[64:104, :]
         mine_face = jnp.where(x_even, sums[0:4, :], sums[4:8, :])
-        face = chip[232:240, :]
+        face = chip[104:112, :]
         for cy in range(4):
             line = jnp.where(has, face[cy : cy + 1, :], 0.0)
             own = mine_face[cy : cy + 1, :]
             a, b = 8 * cy, 8 * cy + 3
             full[a : a + 1, :] = mine[a : a + 1, :] + jnp.where(x_even, line, 0.0)
             full[b : b + 1, :] = mine[b : b + 1, :] + jnp.where(x_even, 0.0, line)
-            beyond[a : a + 1, :] = chip[192 + a : 193 + a, :] + jnp.where(x_even, 0.0, own)
-            beyond[b : b + 1, :] = chip[192 + b : 193 + b, :] + jnp.where(x_even, own, 0.0)
+            beyond[a : a + 1, :] = chip[64 + a : 65 + a, :] + jnp.where(x_even, 0.0, own)
+            beyond[b : b + 1, :] = chip[64 + b : 65 + b, :] + jnp.where(x_even, own, 0.0)
+        put(more, 0, s[jnp.where(x_even, 1, 14)])
+        put(more, 64, g[jnp.where(x_even, 0, 15)])
+        more[128:MORE, :] = jnp.zeros((MORE - 128, 128), F32)
 
     def window_kernel(full, beyond, core, chip, s_core, window, short):
         x_at, _, x_even, _ = where_am_i()
@@ -344,12 +347,12 @@
     planes = 4 * ny
     short_steps = (1, 3) if ny == 4 else (1,)
 
-    def prepare(f, g, s, a_core, a_chip, a_row, a_odd, s_core, s_chip, s_row, s_odd, u, u_low, u_high, g_x, g_y, edge):
+    def prepare(f, g, s, a_core, a_chip, a_row, a_odd, s_core, s_chip, s_more, s_row, s_odd, u, u_low, u_high, g_x, g_y, edge):
         x_at, y_at, x_even, y_even = where_am_i()
         s_left, s_right = halo_x(s_core, s_chip, 0, x_at, x_even)
-        s_left2, s_right2 = halo_x(s_core, s_chip, 64, x_at, x_even)
+        s_left2, s_right2 = halo_x(s_core, s_more, 64, x_at, x_even, 0)
         f_left, f_right = halo_x(a_core, a_chip, 0, x_at, x_even)
-        g_x[0], g_x[1] = halo_x(s_core, s_chip, 128, x_at, x_even)
+        g_x[0], g_x[1] = halo_x(s_core, s_more, 128, x_at, x_even, 64)
         y1 = halo_y(s_row, s_odd, 0, y_at, y_even)
         y2 = halo_y(s_row, s_odd, 64, y_at, y_even)
         f_y = halo_y(a_row, a_odd, 0, y_at, y_even)
@@ -549,14 +552,16 @@
         (block,) = call(restrict, [(40, 128)], f, d, absorb, s, sums, scratch=[(64, 512)], name="restrict")
         mine, to_chip, to_row, to_odd = call(
             to_chip_kernel,
-            [(40, 128), (240, 128), (192, 128), (192, 128)],
+            [(40, 128), (112, 128), (FACES, 128), (FACES, 128)],
             block, sums, absorb, s_core, s, g, y_faces, y_more,
             name="to_chip",
         )
         s_chip = swap(to_chip, chip_pairs)
         s_row, s_odd = swap(to_row, row_pairs[0]), swap(to_odd, odd_pairs)
-        full, beyond = call(from_chip_kernel, [(40, 128), (40, 128)], mine, sums, s_chip, name="from_chip")
-        c_core = swap(full, core_pairs)
+        full, beyond, more = call(
+            from_chip_kernel, [(40, 128), (40, 128), (MORE, 128)], mine, sums, s_chip, s, g, name="from_chip"
+        )
+        c_core, s_more = swap(full, core_pairs), swap(more, chip_pairs)
         window, short = call(
             window_kernel, [(136, 128), (80, 128)], full, beyond, c_core, s_chip, s_core, name="window"
         )
@@ -566,7 +571,7 @@
         prepared = call(
             prepare,
             [long, slab, slab, (2, 16, 512), (2, 16, 512)],
-            f, g, s, a_core, a_chip, a_row, a_odd, s_core, s_chip, s_row, s_odd,
+            f, g, s, a_core, a_chip, a_row, a_odd, s_core, s_chip, s_more, s_row, s_odd,
             scratch=[(2, 16, 512)],
             name="prepare",
         )

time: 28.5 us -> 28.2 us (0.989)
  waiting for transfers between devices: 7.68 us -> 6.89 us
  starting transfers between devices: 13.4 us -> 13.9 us
    ppermute x12 -> x13, waiting for transfers between devices: 7.68 us -> 6.89 us  [swap(): return lax.ppermute(array, axes, pairs)]
    ppermute x12 -> x13, starting transfers between devices: 13.4 us -> 13.9 us  [swap(): return lax.ppermute(array, axes, pairs)]
  transfers between devices with their start and end apart: 12 -> 13, of which waited for: 6 -> 6; matrix products, arithmetic and copies ran while one was open for 0% -> 0% of each run, Pallas kernels for 6% -> 7%
where the time goes in v11:
time: 28.2 us; the launch traced here: 28.1 us
  starting transfers between devices  13.9 us (49%)
  waiting for transfers between devices  6.89 us (24%)
  Pallas kernels  6.47 us (23%)
  between operations  0.76 us (3%)
    ppermute x13, starting transfers between devices, swap(): return lax.ppermute(array, axes, pairs)  13.9 us
    ppermute x13, waiting for transfers between devices, swap(): return lax.ppermute(array, axes, pairs)  6.89 us
    pallas_call x9, Pallas kernels, call(): pl.pallas_call(kernel, out_shape=[jax.ShapeDtypeStruct(s, F32) for s in o...  6.47 us
  transfers between devices with their start and end apart: 13, of which 6 were waited for; matrix products, arithmetic and copies ran while one was open for 0% of the time, Pallas kernels for 7%

profile of v11, /device:TPU:0, one launch (start us, length us, event | category | flops | bytes accessed | tf_op | source)
XLA Modules:
  0.0 28.1 jit_solution(1949052539352115495)
XLA Ops:
  0.7 1.6 %faces.1 = (f32[64,128]{1,0:T(8,128)S(1)}, f32[64,128]{1,0:T(8,128)S(1)}, f32[128,128]{1,0:T(8,128)S(1)}, f32[128,128]{1,0:T(8,128)S(1)}) custom-call(f32[16,16,512]{2,1,0:T(8,128)} %source.1, f32[16,16,512]{2,1,0:T(8,128)} %reaction.1, s32[16,16,512]{2,1,0:T(8,128)} %kind.1, s32[16,16,512]{2,1,0:T(8,128)} %disk_id.1, s32[16,16,512]{2,1,0:T(8,128)} %disk_mask.1, ...), custom_call_target="tpu_custom_call" | custom-call | tf_op jit(solution)/shard_map/faces/pallas_call | solution.py:24
  2.3 4.0 %collective-permute-start = (f32[128,128]{1,0:T(8,128)S(1)}, f32[128,128]{1,0:T(8,128)S(1)}, u32[]{:S(2)}, u32[]{:S(2)}) collective-permute-start(f32[128,128]{1,0:T(8,128)S(1)} %get-tuple-element.37), channel_id=1, source_target_pairs={{0,3},{1,2},{2,1},{3,0},{4,7},{5,6},{6,5},{7,4},{8,11},{9,10},{10,... | collective-permute-start | bytes 196616 | tf_op jit(solution)/shard_map/ppermute | solution.py:521
  6.2 0.5 %collective-permute-start.1 = (f32[128,128]{1,0:T(8,128)S(1)}, f32[128,128]{1,0:T(8,128)S(1)}, u32[]{:S(2)}, u32[]{:S(2)}) collective-permute-start(f32[128,128]{1,0:T(8,128)S(1)} %get-tuple-element.38), channel_id=1, source_target_pairs={{0,1},{1,0},{2,3},{3,2},{4,5},{5,4},{6,7},{7,6},{8,9},{9,8},{10,11... | collective-permute-start | bytes 196616 | tf_op jit(solution)/shard_map/ppermute | solution.py:521
  6.8 0.1 collective-permute-start.2
  6.9 1.6 %collective-permute-start.3 = (f32[64,128]{1,0:T(8,128)S(1)}, f32[64,128]{1,0:T(8,128)S(1)}, u32[]{:S(2)}, u32[]{:S(2)}) collective-permute-start(f32[64,128]{1,0:T(8,128)S(1)} %get-tuple-element.40), channel_id=1, source_target_pairs={{0,4},{1,5},{2,6},{3,7},{4,0},{5,1},{6,2},{7,3},{8,12},{9,13},{10,... | collective-permute-start | bytes 98312 | tf_op jit(solution)/shard_map/ppermute | solution.py:521
  8.5 0.5 %set_up.1 = (f32[16,16,512]{2,1,0:T(8,128)S(1)}, f32[16,16,512]{2,1,0:T(8,128)S(1)}, f32[16,16,512]{2,1,0:T(8,128)S(1)}, f32[16,128]{1,0:T(8,128)S(1)}) custom-call(f32[16,16,512]{2,1,0:T(8,128)S(1)} %copy-done, f32[16,16,512]{2,1,0:T(8,128)S(1)} %copy-done.1, s32[16,16,512]{2,1,0:T(8,128)S(1)} %copy-done.2, s32[16,16,512]{2,1,0:T(8,128)S(1)} %copy-done.3, ...), custom_call_target="tpu_custom_call" | custom-call | tf_op jit(solution)/shard_map/set_up/pallas_call | solution.py:24
  9.0 1.6 %collective-permute-done.2.chip.a_chip = f32[64,128]{1,0:T(8,128)S(1)} collective-permute-done((f32[64,128]{1,0:T(8,128)S(1)}, f32[64,128]{1,0:T(8,128)S(1)}, u32[]{:S(2)}, u32[]{:S(2)}) %collective-permute-start.2) | collective-permute-done | bytes 32800 | tf_op jit(solution)/shard_map/ppermute | solution.py:521
  10.7 0.8 %smooth.1 = (f32[16,16,512]{2,1,0:T(8,128)S(1)}, f32[224,128]{1,0:T(8,128)S(1)}, f32[16,128]{1,0:T(8,128)S(1)}, f32[32,512]{1,0:T(8,128)S(1)}, f32[32,512]{1,0:T(8,128)S(1)}) custom-call(f32[16,16,512]{2,1,0:T(8,128)S(1)} %get-tuple-element.45.f.refs_0_, f32[16,16,512]{2,1,0:T(8,128)S(1)} %get-tuple-element.46.g.refs_1_, ...), custom_call_target="tpu_custom_call" | custom-call | tf_op jit(solution)/shard_map/smooth/pallas_call | solution.py:24
  11.5 0.1 collective-permute-start.4
  11.6 0.7 %restrict.1.block = f32[40,128]{1,0:T(8,128)S(1)} custom-call(f32[16,16,512]{2,1,0:T(8,128)S(1)} %get-tuple-element.45.f.refs_0_, f32[16,16,512]{2,1,0:T(8,128)S(1)} %get-tuple-element.54.d, f32[16,128]{1,0:T(8,128)S(1)} %get-tuple-element.47.absorb, f32[16,16,512]{2,1,0:T(8,128)S(1)} %get-tuple-element.52.s, f32[16,128]{1,0:T(8,128)S(1)} %get-tuple-element.55.sums), custom_call_target="tpu_custom_call" | custom-call | tf_op jit(solution)/shard_map/restrict/pallas_call | solution.py:24
  12.3 0.6 %collective-permute-done.4.core.s_core = f32[224,128]{1,0:T(8,128)S(1)} collective-permute-done((f32[224,128]{1,0:T(8,128)S(1)}, f32[224,128]{1,0:T(8,128)S(1)}, u32[]{:S(2)}, u32[]{:S(2)}) %collective-permute-start.4) | collective-permute-done | bytes 114720 | tf_op jit(solution)/shard_map/ppermute | solution.py:521
  13.0 0.5 %collective-permute-start.5 = (f32[112,128]{1,0:T(8,128)S(1)}, f32[112,128]{1,0:T(8,128)S(1)}, u32[]{:S(2)}, u32[]{:S(2)}) collective-permute-start(f32[112,128]{1,0:T(8,128)S(1)} %get-tuple-element.58), channel_id=1, source_target_pairs={{0,2},{1,3},{2,0},{3,1},{4,8},{5,9},{6,10},{7,11},{8,4},{9,5},{10,... | collective-permute-start | bytes 172040 | tf_op jit(solution)/shard_map/ppermute | solution.py:521
  13.5 1.6 %collective-permute-start.7 = (f32[192,128]{1,0:T(8,128)S(1)}, f32[192,128]{1,0:T(8,128)S(1)}, u32[]{:S(2)}, u32[]{:S(2)}) collective-permute-start(f32[192,128]{1,0:T(8,128)S(1)} %get-tuple-element.61), channel_id=1, source_target_pairs={{0,1},{1,0},{2,3},{3,2},{4,5},{5,4},{6,7},{7,6},{8,9},{9,8},{10,11... | collective-permute-start | bytes 294920 | tf_op jit(solution)/shard_map/ppermute | solution.py:521
  15.0 1.5 %collective-permute-start.8 = (f32[192,128]{1,0:T(8,128)S(1)}, f32[192,128]{1,0:T(8,128)S(1)}, u32[]{:S(2)}, u32[]{:S(2)}) collective-permute-start(f32[192,128]{1,0:T(8,128)S(1)} %get-tuple-element.62), channel_id=1, source_target_pairs={{0,3},{1,2},{2,1},{3,0},{4,7},{5,6},{6,5},{7,4},{8,11},{9,10},{10,... | collective-permute-start | bytes 294920 | tf_op jit(solution)/shard_map/ppermute | solution.py:521
  16.5 0.7 %collective-permute-done.5.chip.s_chip = f32[112,128]{1,0:T(8,128)S(1)} collective-permute-done((f32[112,128]{1,0:T(8,128)S(1)}, f32[112,128]{1,0:T(8,128)S(1)}, u32[]{:S(2)}, u32[]{:S(2)}) %collective-permute-start.5) | collective-permute-done | bytes 57376 | tf_op jit(solution)/shard_map/ppermute | solution.py:521
  17.3 0.5 %collective-permute-start.6 = (f32[152,128]{1,0:T(8,128)S(1)}, f32[152,128]{1,0:T(8,128)S(1)}, u32[]{:S(2)}, u32[]{:S(2)}) collective-permute-start(f32[152,128]{1,0:T(8,128)S(1)} %get-tuple-element.60), channel_id=1, source_target_pairs={{0,2},{1,3},{2,0},{3,1},{4,8},{5,9},{6,10},{7,11},{8,4},{9,5},{10,... | collective-permute-start | bytes 233480 | tf_op jit(solution)/shard_map/ppermute | solution.py:521
  17.8 0.7 %collective-permute-done.9.core = f32[40,128]{1,0:T(8,128)S(1)} collective-permute-done((f32[40,128]{1,0:T(8,128)S(1)}, f32[40,128]{1,0:T(8,128)S(1)}, u32[]{:S(2)}, u32[]{:S(2)}) %collective-permute-start.9) | collective-permute-done | bytes 20512 | tf_op jit(solution)/shard_map/ppermute | solution.py:521
  18.5 1.0 %collective-permute-start.11 = (f32[136,128]{1,0:T(8,128)S(1)}, f32[136,128]{1,0:T(8,128)S(1)}, u32[]{:S(2)}, u32[]{:S(2)}) collective-permute-start(f32[136,128]{1,0:T(8,128)S(1)} %get-tuple-element.70.refs_9_), channel_id=1, source_target_pairs={{0,2},{1,3},{2,0},{3,1},{4,6},{5,7},{6,4},{7,5},{8,10},{9,11},{10,... | collective-permute-start | bytes 208904 | tf_op jit(solution)/shard_map/ppermute | solution.py:521
  19.5 1.5 %collective-permute-start.10 = (f32[80,128]{1,0:T(8,128)S(1)}, f32[80,128]{1,0:T(8,128)S(1)}, u32[]{:S(2)}, u32[]{:S(2)}) collective-permute-start(f32[80,128]{1,0:T(8,128)S(1)} %get-tuple-element.71), channel_id=1, source_target_pairs={{0,1},{1,0},{2,3},{3,2},{4,5},{5,4},{6,7},{7,6},{8,9},{9,8},{10,11... | collective-permute-start | bytes 122888 | tf_op jit(solution)/shard_map/ppermute | solution.py:521
  21.0 1.1 %collective-permute-start.12 = (f32[80,128]{1,0:T(8,128)S(1)}, f32[80,128]{1,0:T(8,128)S(1)}, u32[]{:S(2)}, u32[]{:S(2)}) collective-permute-start(f32[80,128]{1,0:T(8,128)S(1)} %get-tuple-element.71), channel_id=1, source_target_pairs={{0,3},{1,2},{2,1},{3,0},{4,7},{5,6},{6,5},{7,4},{8,11},{9,10},{10,... | collective-permute-start | bytes 122888 | tf_op jit(solution)/shard_map/ppermute | solution.py:521
  22.1 0.9 %collective-permute-done.6.s_more = f32[152,128]{1,0:T(8,128)S(1)} collective-permute-done((f32[152,128]{1,0:T(8,128)S(1)}, f32[152,128]{1,0:T(8,128)S(1)}, u32[]{:S(2)}, u32[]{:S(2)}) %collective-permute-start.6) | collective-permute-done | bytes 77856 | tf_op jit(solution)/shard_map/ppermute | solution.py:521
  22.9 0.6 %prepare.1 = (f32[18,16,512]{2,1,0:T(8,128)S(1)}, f32[16,512]{1,0:T(8,128)S(1)}, f32[16,512]{1,0:T(8,128)S(1)}, f32[2,16,512]{2,1,0:T(8,128)S(1)}, f32[2,16,512]{2,1,0:T(8,128)S(1)}) custom-call(f32[16,16,512]{2,1,0:T(8,128)S(1)} %get-tuple-element.45.f.refs_0_, f32[16,16,512]{2,1,0:T(8,128)S(1)} %get-tuple-element.46.g.refs_1_, ...), custom_call_target="tpu_custom_call" | custom-call | tf_op jit(solution)/shard_map/prepare/pallas_call | solution.py:24
  23.5 2.4 %collective-permute-done.12.refs_12_ = f32[80,128]{1,0:T(8,128)S(1)} collective-permute-done((f32[80,128]{1,0:T(8,128)S(1)}, f32[80,128]{1,0:T(8,128)S(1)}, u32[]{:S(2)}, u32[]{:S(2)}) %collective-permute-start.12) | collective-permute-done | bytes 40992 | tf_op jit(solution)/shard_map/ppermute | solution.py:521
  25.9 2.2 %finish.1 = (f32[16,16,512]{2,1,0:T(8,128)}, f32[4,16,128]{2,1,0:T(8,128)}) custom-call(f32[16,16,512]{2,1,0:T(8,128)S(1)} %get-tuple-element.45.f.refs_0_, f32[16,16,512]{2,1,0:T(8,128)S(1)} %get-tuple-element.46.g.refs_1_, f32[18,16,512]{2,1,0:T(8,128)S(1)} %get-tuple-element.63.refs_2_, f32[16,512]{1,0:T(8,128)S(1)} %get-tuple-element.64.refs_3_, ...), custom_call_target="tpu_custom_call" | custom-call | tf_op jit(solution)/shard_map/finish/pallas_call | solution.py:24
  (23 shorter events, 0.2 us)
Async XLA Ops:
  0.6 7.8 %copy-start = (f32[16,16,512]{2,1,0:T(8,128)S(1)}, f32[16,16,512]{2,1,0:T(8,128)}, u32[]{:S(2)}) copy-start(f32[16,16,512]{2,1,0:T(8,128)} %source.1) | copy-start | bytes 1572868
  0.6 7.8 %copy-start.1 = (f32[16,16,512]{2,1,0:T(8,128)S(1)}, f32[16,16,512]{2,1,0:T(8,128)}, u32[]{:S(2)}) copy-start(f32[16,16,512]{2,1,0:T(8,128)} %reaction.1) | copy-start | bytes 1572868
  0.7 7.8 %copy-start.2 = (s32[16,16,512]{2,1,0:T(8,128)S(1)}, s32[16,16,512]{2,1,0:T(8,128)}, u32[]{:S(2)}) copy-start(s32[16,16,512]{2,1,0:T(8,128)} %kind.1) | copy-start | bytes 1572868
  0.7 7.8 %copy-start.3 = (s32[16,16,512]{2,1,0:T(8,128)S(1)}, s32[16,16,512]{2,1,0:T(8,128)}, u32[]{:S(2)}) copy-start(s32[16,16,512]{2,1,0:T(8,128)} %disk_id.1) | copy-start | bytes 1572868
  0.7 7.8 %copy-start.4 = (s32[16,16,512]{2,1,0:T(8,128)S(1)}, s32[16,16,512]{2,1,0:T(8,128)}, u32[]{:S(2)}) copy-start(s32[16,16,512]{2,1,0:T(8,128)} %disk_mask.1) | copy-start | bytes 1572868
  2.3 8.4 %collective-permute-start = (f32[128,128]{1,0:T(8,128)S(1)}, f32[128,128]{1,0:T(8,128)S(1)}, u32[]{:S(2)}, u32[]{:S(2)}) collective-permute-start(f32[128,128]{1,0:T(8,128)S(1)} %get-tuple-element.37), channel_id=1, source_target_pairs={{0,3},{1,2},{2,1},{3,0},{4,7},{5,6},{6,5},{7,4},{8,11},{9,10},{10,... | collective-permute-start | bytes 196616 | tf_op jit(solution)/shard_map/ppermute | solution.py:521
  6.2 4.5 %collective-permute-start.1 = (f32[128,128]{1,0:T(8,128)S(1)}, f32[128,128]{1,0:T(8,128)S(1)}, u32[]{:S(2)}, u32[]{:S(2)}) collective-permute-start(f32[128,128]{1,0:T(8,128)S(1)} %get-tuple-element.38), channel_id=1, source_target_pairs={{0,1},{1,0},{2,3},{3,2},{4,5},{5,4},{6,7},{7,6},{8,9},{9,8},{10,11... | collective-permute-start | bytes 196616 | tf_op jit(solution)/shard_map/ppermute | solution.py:521
  6.8 1.7 %copy-start.5 = (f32[120]{0:T(128)S(1)}, f32[120]{0:T(128)}, u32[]{:S(2)}) copy-start(f32[120]{0:T(128)} %param.11) | copy-start | bytes 1444
  6.8 3.9 %collective-permute-start.2 = (f32[64,128]{1,0:T(8,128)S(1)}, f32[64,128]{1,0:T(8,128)S(1)}, u32[]{:S(2)}, u32[]{:S(2)}) collective-permute-start(f32[64,128]{1,0:T(8,128)S(1)} %get-tuple-element.39), channel_id=1, source_target_pairs={{0,2},{1,3},{2,0},{3,1},{4,8},{5,9},{6,10},{7,11},{8,4},{9,5},{10,... | collective-permute-start | bytes 98312 | tf_op jit(solution)/shard_map/ppermute | solution.py:521
  6.9 3.8 %collective-permute-start.3 = (f32[64,128]{1,0:T(8,128)S(1)}, f32[64,128]{1,0:T(8,128)S(1)}, u32[]{:S(2)}, u32[]{:S(2)}) collective-permute-start(f32[64,128]{1,0:T(8,128)S(1)} %get-tuple-element.40), channel_id=1, source_target_pairs={{0,4},{1,5},{2,6},{3,7},{4,0},{5,1},{6,2},{7,3},{8,12},{9,13},{10,... | collective-permute-start | bytes 98312 | tf_op jit(solution)/shard_map/ppermute | solution.py:521
  11.5 1.4 %collective-permute-start.4 = (f32[224,128]{1,0:T(8,128)S(1)}, f32[224,128]{1,0:T(8,128)S(1)}, u32[]{:S(2)}, u32[]{:S(2)}) collective-permute-start(f32[224,128]{1,0:T(8,128)S(1)} %get-tuple-element.53), channel_id=1, source_target_pairs={{0,4},{1,5},{2,6},{3,7},{4,0},{5,1},{6,2},{7,3},{8,12},{9,13},{10,... | collective-permute-start | bytes 344072 | tf_op jit(solution)/shard_map/ppermute | solution.py:521
  13.0 4.2 %collective-permute-start.5 = (f32[112,128]{1,0:T(8,128)S(1)}, f32[112,128]{1,0:T(8,128)S(1)}, u32[]{:S(2)}, u32[]{:S(2)}) collective-permute-start(f32[112,128]{1,0:T(8,128)S(1)} %get-tuple-element.58), channel_id=1, source_target_pairs={{0,2},{1,3},{2,0},{3,1},{4,8},{5,9},{6,10},{7,11},{8,4},{9,5},{10,... | collective-permute-start | bytes 172040 | tf_op jit(solution)/shard_map/ppermute | solution.py:521
  13.5 7.5 %collective-permute-start.7 = (f32[192,128]{1,0:T(8,128)S(1)}, f32[192,128]{1,0:T(8,128)S(1)}, u32[]{:S(2)}, u32[]{:S(2)}) collective-permute-start(f32[192,128]{1,0:T(8,128)S(1)} %get-tuple-element.61), channel_id=1, source_target_pairs={{0,1},{1,0},{2,3},{3,2},{4,5},{5,4},{6,7},{7,6},{8,9},{9,8},{10,11... | collective-permute-start | bytes 294920 | tf_op jit(solution)/shard_map/ppermute | solution.py:521
  15.0 7.1 %collective-permute-start.8 = (f32[192,128]{1,0:T(8,128)S(1)}, f32[192,128]{1,0:T(8,128)S(1)}, u32[]{:S(2)}, u32[]{:S(2)}) collective-permute-start(f32[192,128]{1,0:T(8,128)S(1)} %get-tuple-element.62), channel_id=1, source_target_pairs={{0,3},{1,2},{2,1},{3,0},{4,7},{5,6},{6,5},{7,4},{8,11},{9,10},{10,... | collective-permute-start | bytes 294920 | tf_op jit(solution)/shard_map/ppermute | solution.py:521
  17.2 1.3 %collective-permute-start.9 = (f32[40,128]{1,0:T(8,128)S(1)}, f32[40,128]{1,0:T(8,128)S(1)}, u32[]{:S(2)}, u32[]{:S(2)}) collective-permute-start(f32[40,128]{1,0:T(8,128)S(1)} %get-tuple-element.68.full), channel_id=1, source_target_pairs={{0,4},{1,5},{2,6},{3,7},{4,0},{5,1},{6,2},{7,3},{8,12},{9,13},{10,... | collective-permute-start | bytes 61448 | tf_op jit(solution)/shard_map/ppermute | solution.py:521
  17.3 5.6 %collective-permute-start.6 = (f32[152,128]{1,0:T(8,128)S(1)}, f32[152,128]{1,0:T(8,128)S(1)}, u32[]{:S(2)}, u32[]{:S(2)}) collective-permute-start(f32[152,128]{1,0:T(8,128)S(1)} %get-tuple-element.60), channel_id=1, source_target_pairs={{0,2},{1,3},{2,0},{3,1},{4,8},{5,9},{6,10},{7,11},{8,4},{9,5},{10,... | collective-permute-start | bytes 233480 | tf_op jit(solution)/shard_map/ppermute | solution.py:521
  18.5 7.4 %collective-permute-start.11 = (f32[136,128]{1,0:T(8,128)S(1)}, f32[136,128]{1,0:T(8,128)S(1)}, u32[]{:S(2)}, u32[]{:S(2)}) collective-permute-start(f32[136,128]{1,0:T(8,128)S(1)} %get-tuple-element.70.refs_9_), channel_id=1, source_target_pairs={{0,2},{1,3},{2,0},{3,1},{4,6},{5,7},{6,4},{7,5},{8,10},{9,11},{10,... | collective-permute-start | bytes 208904 | tf_op jit(solution)/shard_map/ppermute | solution.py:521
  19.5 4.0 %collective-permute-start.10 = (f32[80,128]{1,0:T(8,128)S(1)}, f32[80,128]{1,0:T(8,128)S(1)}, u32[]{:S(2)}, u32[]{:S(2)}) collective-permute-start(f32[80,128]{1,0:T(8,128)S(1)} %get-tuple-element.71), channel_id=1, source_target_pairs={{0,1},{1,0},{2,3},{3,2},{4,5},{5,4},{6,7},{7,6},{8,9},{9,8},{10,11... | collective-permute-start | bytes 122888 | tf_op jit(solution)/shard_map/ppermute | solution.py:521
  21.0 4.9 %collective-permute-start.12 = (f32[80,128]{1,0:T(8,128)S(1)}, f32[80,128]{1,0:T(8,128)S(1)}, u32[]{:S(2)}, u32[]{:S(2)}) collective-permute-start(f32[80,128]{1,0:T(8,128)S(1)} %get-tuple-element.71), channel_id=1, source_target_pairs={{0,3},{1,2},{2,1},{3,0},{4,7},{5,6},{6,5},{7,4},{8,11},{9,10},{10,... | collective-permute-start | bytes 122888 | tf_op jit(solution)/shard_map/ppermute | solution.py:521

commit v12 on v11

--- a/solution.py
+++ b/solution.py
@@ -105,6 +105,13 @@
             parts.append((above + below) + (after + before))
         lines.append(jnp.concatenate(parts, axis=1))
     return jnp.concatenate(lines, axis=0)
+
+
+def outer_rows(low, high):
+    row = iota((8, 512), 0)
+    first = jnp.where(row == 0, jnp.broadcast_to(low, row.shape), 0.0)
+    last = jnp.where(row == 7, jnp.broadcast_to(high, row.shape), 0.0)
+    return jnp.concatenate([first, last], axis=0)
 
 
 def dot(left, right):
@@ -197,7 +204,7 @@
         put(chip, 0, f_far)
         put(core, 0, f_near)
 
-    def set_up(source, reaction, kind, disk_id, disk_mask, table, f, g, d, absorb, V):
+    def set_up(source, reaction, kind, disk_id, disk_mask, table, f, g, d, absorb, inner, V):
         for k in range(4):
             total = jnp.zeros((16, 512), F32)
             for x in range(4 * k, 4 * k + 4):
@@ -207,6 +214,13 @@
         out, src = iota((16, 64), 0), iota((16, 64), 1)
         pick = ((src // 16 == out % 4) & ((src % 16) // 4 == out // 4)).astype(F32)
         absorb[...] = dot(dot(pick, V[...]), group_lanes(512))
+        for x in range(16):
+            total = beside(f[x])
+            if x > 0:
+                total = total + f[x - 1]
+            if x < 15:
+                total = total + f[x + 1]
+            inner[x] = 1.2 * f[x] + g[x] * total
 
     def halo_x(core, chip, row, x, x_even, chip_row=None):
         a, b = get(core, row, 16, 512), get(chip, row if chip_row is None else chip_row, 16, 512)
@@ -220,16 +234,17 @@
         high = jnp.where(y < ny - 1, jnp.where(y_even, a, b), 0.0)
         return low, high
 
-    def smooth(f, g, absorb, core, chip, row, odd, s, to_core, sums, y_faces, y_more, lo, hi, y0, y1, y14, y15):
+    def smooth(inner, g, absorb, core, chip, row, odd, s, to_core, sums, y_faces, y_more, lo, hi, y0, y1, y14, y15):
         x_at, y_at, x_even, y_even = where_am_i()
         left, right = halo_x(core, chip, 0, x_at, x_even)
         lo[...], hi[...] = halo_y(row, odd, 0, y_at, y_even)
         for x in range(16):
-            here = f[x]
-            scale = g[x]
-            total = (f[x - 1] if x > 0 else left) + (f[x + 1] if x < 15 else right)
-            total = total + beside(here, lo[x : x + 1, :], hi[x : x + 1, :])
-            value = 1.2 * here + scale * total
+            total = outer_rows(lo[x : x + 1, :], hi[x : x + 1, :])
+            if x == 0:
+                total = total + left
+            if x == 15:
+                total = total + right
+            value = inner[x] + g[x] * total
             s[x] = value
             y0[x : x + 1, :] = value[0:1, :]
             y1[x : x + 1, :] = value[1:2, :]
@@ -535,16 +550,16 @@
         )
         a_core, a_chip = swap(core, core_pairs), swap(chip, chip_pairs)
         a_odd, a_row = swap(odd, odd_pairs), swap(row, row_pairs[0])
-        f, g, d, absorb = call(
-            set_up, [field, field, field, (16, 128)], *inputs, scratch=[(64, 512)], name="set_up"
-        )
-        a_odd, a_row, a_chip, a_core, f, g, d, absorb = lax.optimization_barrier(
-            (a_odd, a_row, a_chip, a_core, f, g, d, absorb)
+        f, g, d, absorb, inner = call(
+            set_up, [field, field, field, (16, 128), field], *inputs, scratch=[(64, 512)], name="set_up"
+        )
+        a_odd, a_row, a_chip, a_core, f, g, d, absorb, inner = lax.optimization_barrier(
+            (a_odd, a_row, a_chip, a_core, f, g, d, absorb, inner)
         )
         s, to_core, sums, y_faces, y_more = call(
             smooth,
             [field, (224, 128), (16, 128), (32, 512), (32, 512)],
-            f, g, absorb, a_core, a_chip, a_row, a_odd,
+            inner, g, absorb, a_core, a_chip, a_row, a_odd,
             scratch=[slab] * 6,
             name="smooth",
         )

time: 28.2 us -> 28 us (level)
  transfers between devices with their start and end apart: 13 -> 13, of which waited for: 6 -> 6; matrix products, arithmetic and copies ran while one was open for 0% -> 0% of each run, Pallas kernels for 7% -> 8%
where the time goes in v12:
time: 28 us; the launch traced here: 27.8 us
  starting transfers between devices  13.9 us (50%)
  waiting for transfers between devices  6.64 us (24%)
  Pallas kernels  6.45 us (23%)
  between operations  0.77 us (3%)
    ppermute x13, starting transfers between devices, swap(): return lax.ppermute(array, axes, pairs)  13.9 us
    ppermute x13, waiting for transfers between devices, swap(): return lax.ppermute(array, axes, pairs)  6.64 us
    pallas_call x9, Pallas kernels, call(): pl.pallas_call(kernel, out_shape=[jax.ShapeDtypeStruct(s, F32) for s in o...  6.45 us
  transfers between devices with their start and end apart: 13, of which 6 were waited for; matrix products, arithmetic and copies ran while one was open for 0% of the time, Pallas kernels for 8%

profile of v12, /device:TPU:0, one launch (start us, length us, event | category | flops | bytes accessed | tf_op | source)
XLA Modules:
  0.0 27.8 jit_solution(7992432526191136109)
XLA Ops:
  0.7 1.6 %faces.1 = (f32[64,128]{1,0:T(8,128)S(1)}, f32[64,128]{1,0:T(8,128)S(1)}, f32[128,128]{1,0:T(8,128)S(1)}, f32[128,128]{1,0:T(8,128)S(1)}) custom-call(f32[16,16,512]{2,1,0:T(8,128)} %source.1, f32[16,16,512]{2,1,0:T(8,128)} %reaction.1, s32[16,16,512]{2,1,0:T(8,128)} %kind.1, s32[16,16,512]{2,1,0:T(8,128)} %disk_id.1, s32[16,16,512]{2,1,0:T(8,128)} %disk_mask.1, ...), custom_call_target="tpu_custom_call" | custom-call | tf_op jit(solution)/shard_map/faces/pallas_call | solution.py:24
  2.3 4.0 %collective-permute-start = (f32[128,128]{1,0:T(8,128)S(1)}, f32[128,128]{1,0:T(8,128)S(1)}, u32[]{:S(2)}, u32[]{:S(2)}) collective-permute-start(f32[128,128]{1,0:T(8,128)S(1)} %get-tuple-element.39), channel_id=1, source_target_pairs={{0,3},{1,2},{2,1},{3,0},{4,7},{5,6},{6,5},{7,4},{8,11},{9,10},{10,... | collective-permute-start | bytes 196616 | tf_op jit(solution)/shard_map/ppermute | solution.py:536
  6.2 0.5 %collective-permute-start.1 = (f32[128,128]{1,0:T(8,128)S(1)}, f32[128,128]{1,0:T(8,128)S(1)}, u32[]{:S(2)}, u32[]{:S(2)}) collective-permute-start(f32[128,128]{1,0:T(8,128)S(1)} %get-tuple-element.40), channel_id=1, source_target_pairs={{0,1},{1,0},{2,3},{3,2},{4,5},{5,4},{6,7},{7,6},{8,9},{9,8},{10,11... | collective-permute-start | bytes 196616 | tf_op jit(solution)/shard_map/ppermute | solution.py:536
  6.8 0.1 collective-permute-start.2
  6.9 1.6 %collective-permute-start.3 = (f32[64,128]{1,0:T(8,128)S(1)}, f32[64,128]{1,0:T(8,128)S(1)}, u32[]{:S(2)}, u32[]{:S(2)}) collective-permute-start(f32[64,128]{1,0:T(8,128)S(1)} %get-tuple-element.42), channel_id=1, source_target_pairs={{0,4},{1,5},{2,6},{3,7},{4,0},{5,1},{6,2},{7,3},{8,12},{9,13},{10,... | collective-permute-start | bytes 98312 | tf_op jit(solution)/shard_map/ppermute | solution.py:536
  8.5 0.8 %set_up.1 = (f32[16,16,512]{2,1,0:T(8,128)S(1)}, f32[16,16,512]{2,1,0:T(8,128)S(1)}, f32[16,16,512]{2,1,0:T(8,128)S(1)}, f32[16,128]{1,0:T(8,128)S(1)}, f32[16,16,512]{2,1,0:T(8,128)S(1)}) custom-call(f32[16,16,512]{2,1,0:T(8,128)S(1)} %copy-done, f32[16,16,512]{2,1,0:T(8,128)S(1)} %copy-done.1, s32[16,16,512]{2,1,0:T(8,128)S(1)} %copy-done.2, ...), custom_call_target="tpu_custom_call" | custom-call | tf_op jit(solution)/shard_map/set_up/pallas_call | solution.py:24
  9.3 1.4 %collective-permute-done.2.chip.a_chip = f32[64,128]{1,0:T(8,128)S(1)} collective-permute-done((f32[64,128]{1,0:T(8,128)S(1)}, f32[64,128]{1,0:T(8,128)S(1)}, u32[]{:S(2)}, u32[]{:S(2)}) %collective-permute-start.2) | collective-permute-done | bytes 32800 | tf_op jit(solution)/shard_map/ppermute | solution.py:536
  10.7 0.6 %smooth.1 = (f32[16,16,512]{2,1,0:T(8,128)S(1)}, f32[224,128]{1,0:T(8,128)S(1)}, f32[16,128]{1,0:T(8,128)S(1)}, f32[32,512]{1,0:T(8,128)S(1)}, f32[32,512]{1,0:T(8,128)S(1)}) custom-call(f32[16,16,512]{2,1,0:T(8,128)S(1)} %get-tuple-element.50.inner, f32[16,16,512]{2,1,0:T(8,128)S(1)} %get-tuple-element.49.g.refs_1_, ...), custom_call_target="tpu_custom_call" | custom-call | tf_op jit(solution)/shard_map/smooth/pallas_call | solution.py:24
  11.3 0.1 collective-permute-start.4
  11.3 0.7 %restrict.1.block = f32[40,128]{1,0:T(8,128)S(1)} custom-call(f32[16,16,512]{2,1,0:T(8,128)S(1)} %get-tuple-element.48.f.refs_0_, f32[16,16,512]{2,1,0:T(8,128)S(1)} %get-tuple-element.58.d, f32[16,128]{1,0:T(8,128)S(1)} %get-tuple-element.51.absorb, f32[16,16,512]{2,1,0:T(8,128)S(1)} %get-tuple-element.56.s, f32[16,128]{1,0:T(8,128)S(1)} %get-tuple-element.59.sums), custom_call_target="tpu_custom_call" | custom-call | tf_op jit(solution)/shard_map/restrict/pallas_call | solution.py:24
  12.1 0.6 %collective-permute-done.4.core.s_core = f32[224,128]{1,0:T(8,128)S(1)} collective-permute-done((f32[224,128]{1,0:T(8,128)S(1)}, f32[224,128]{1,0:T(8,128)S(1)}, u32[]{:S(2)}, u32[]{:S(2)}) %collective-permute-start.4) | collective-permute-done | bytes 114720 | tf_op jit(solution)/shard_map/ppermute | solution.py:536
  12.7 0.5 %collective-permute-start.5 = (f32[112,128]{1,0:T(8,128)S(1)}, f32[112,128]{1,0:T(8,128)S(1)}, u32[]{:S(2)}, u32[]{:S(2)}) collective-permute-start(f32[112,128]{1,0:T(8,128)S(1)} %get-tuple-element.62), channel_id=1, source_target_pairs={{0,2},{1,3},{2,0},{3,1},{4,8},{5,9},{6,10},{7,11},{8,4},{9,5},{10,... | collective-permute-start | bytes 172040 | tf_op jit(solution)/shard_map/ppermute | solution.py:536
  13.2 1.6 %collective-permute-start.7 = (f32[192,128]{1,0:T(8,128)S(1)}, f32[192,128]{1,0:T(8,128)S(1)}, u32[]{:S(2)}, u32[]{:S(2)}) collective-permute-start(f32[192,128]{1,0:T(8,128)S(1)} %get-tuple-element.65), channel_id=1, source_target_pairs={{0,1},{1,0},{2,3},{3,2},{4,5},{5,4},{6,7},{7,6},{8,9},{9,8},{10,11... | collective-permute-start | bytes 294920 | tf_op jit(solution)/shard_map/ppermute | solution.py:536
  14.8 1.5 %collective-permute-start.8 = (f32[192,128]{1,0:T(8,128)S(1)}, f32[192,128]{1,0:T(8,128)S(1)}, u32[]{:S(2)}, u32[]{:S(2)}) collective-permute-start(f32[192,128]{1,0:T(8,128)S(1)} %get-tuple-element.66), channel_id=1, source_target_pairs={{0,3},{1,2},{2,1},{3,0},{4,7},{5,6},{6,5},{7,4},{8,11},{9,10},{10,... | collective-permute-start | bytes 294920 | tf_op jit(solution)/shard_map/ppermute | solution.py:536
  16.2 0.7 %collective-permute-done.5.chip.s_chip = f32[112,128]{1,0:T(8,128)S(1)} collective-permute-done((f32[112,128]{1,0:T(8,128)S(1)}, f32[112,128]{1,0:T(8,128)S(1)}, u32[]{:S(2)}, u32[]{:S(2)}) %collective-permute-start.5) | collective-permute-done | bytes 57376 | tf_op jit(solution)/shard_map/ppermute | solution.py:536
  17.1 0.5 %collective-permute-start.6 = (f32[152,128]{1,0:T(8,128)S(1)}, f32[152,128]{1,0:T(8,128)S(1)}, u32[]{:S(2)}, u32[]{:S(2)}) collective-permute-start(f32[152,128]{1,0:T(8,128)S(1)} %get-tuple-element.64), channel_id=1, source_target_pairs={{0,2},{1,3},{2,0},{3,1},{4,8},{5,9},{6,10},{7,11},{8,4},{9,5},{10,... | collective-permute-start | bytes 233480 | tf_op jit(solution)/shard_map/ppermute | solution.py:536
  17.6 0.7 %collective-permute-done.9.core = f32[40,128]{1,0:T(8,128)S(1)} collective-permute-done((f32[40,128]{1,0:T(8,128)S(1)}, f32[40,128]{1,0:T(8,128)S(1)}, u32[]{:S(2)}, u32[]{:S(2)}) %collective-permute-start.9) | collective-permute-done | bytes 20512 | tf_op jit(solution)/shard_map/ppermute | solution.py:536
  18.3 1.0 %collective-permute-start.11 = (f32[136,128]{1,0:T(8,128)S(1)}, f32[136,128]{1,0:T(8,128)S(1)}, u32[]{:S(2)}, u32[]{:S(2)}) collective-permute-start(f32[136,128]{1,0:T(8,128)S(1)} %get-tuple-element.74.refs_9_), channel_id=1, source_target_pairs={{0,2},{1,3},{2,0},{3,1},{4,6},{5,7},{6,4},{7,5},{8,10},{9,11},{10,... | collective-permute-start | bytes 208904 | tf_op jit(solution)/shard_map/ppermute | solution.py:536
  19.2 1.5 %collective-permute-start.10 = (f32[80,128]{1,0:T(8,128)S(1)}, f32[80,128]{1,0:T(8,128)S(1)}, u32[]{:S(2)}, u32[]{:S(2)}) collective-permute-start(f32[80,128]{1,0:T(8,128)S(1)} %get-tuple-element.75), channel_id=1, source_target_pairs={{0,1},{1,0},{2,3},{3,2},{4,5},{5,4},{6,7},{7,6},{8,9},{9,8},{10,11... | collective-permute-start | bytes 122888 | tf_op jit(solution)/shard_map/ppermute | solution.py:536
  20.7 1.1 %collective-permute-start.12 = (f32[80,128]{1,0:T(8,128)S(1)}, f32[80,128]{1,0:T(8,128)S(1)}, u32[]{:S(2)}, u32[]{:S(2)}) collective-permute-start(f32[80,128]{1,0:T(8,128)S(1)} %get-tuple-element.75), channel_id=1, source_target_pairs={{0,3},{1,2},{2,1},{3,0},{4,7},{5,6},{6,5},{7,4},{8,11},{9,10},{10,... | collective-permute-start | bytes 122888 | tf_op jit(solution)/shard_map/ppermute | solution.py:536
  21.8 0.9 %collective-permute-done.6.s_more = f32[152,128]{1,0:T(8,128)S(1)} collective-permute-done((f32[152,128]{1,0:T(8,128)S(1)}, f32[152,128]{1,0:T(8,128)S(1)}, u32[]{:S(2)}, u32[]{:S(2)}) %collective-permute-start.6) | collective-permute-done | bytes 77856 | tf_op jit(solution)/shard_map/ppermute | solution.py:536
  22.7 0.5 %prepare.1 = (f32[18,16,512]{2,1,0:T(8,128)S(1)}, f32[16,512]{1,0:T(8,128)S(1)}, f32[16,512]{1,0:T(8,128)S(1)}, f32[2,16,512]{2,1,0:T(8,128)S(1)}, f32[2,16,512]{2,1,0:T(8,128)S(1)}) custom-call(f32[16,16,512]{2,1,0:T(8,128)S(1)} %get-tuple-element.48.f.refs_0_, f32[16,16,512]{2,1,0:T(8,128)S(1)} %get-tuple-element.49.g.refs_1_, ...), custom_call_target="tpu_custom_call" | custom-call | tf_op jit(solution)/shard_map/prepare/pallas_call | solution.py:24
  23.2 2.4 %collective-permute-done.12.refs_12_ = f32[80,128]{1,0:T(8,128)S(1)} collective-permute-done((f32[80,128]{1,0:T(8,128)S(1)}, f32[80,128]{1,0:T(8,128)S(1)}, u32[]{:S(2)}, u32[]{:S(2)}) %collective-permute-start.12) | collective-permute-done | bytes 40992 | tf_op jit(solution)/shard_map/ppermute | solution.py:536
  25.6 2.2 %finish.1 = (f32[16,16,512]{2,1,0:T(8,128)}, f32[4,16,128]{2,1,0:T(8,128)}) custom-call(f32[16,16,512]{2,1,0:T(8,128)S(1)} %get-tuple-element.48.f.refs_0_, f32[16,16,512]{2,1,0:T(8,128)S(1)} %get-tuple-element.49.g.refs_1_, f32[18,16,512]{2,1,0:T(8,128)S(1)} %get-tuple-element.67.refs_2_, f32[16,512]{1,0:T(8,128)S(1)} %get-tuple-element.68.refs_3_, ...), custom_call_target="tpu_custom_call" | custom-call | tf_op jit(solution)/shard_map/finish/pallas_call | solution.py:24
  (23 shorter events, 0.2 us)
Async XLA Ops:
  0.6 7.8 %copy-start = (f32[16,16,512]{2,1,0:T(8,128)S(1)}, f32[16,16,512]{2,1,0:T(8,128)}, u32[]{:S(2)}) copy-start(f32[16,16,512]{2,1,0:T(8,128)} %source.1) | copy-start | bytes 1572868
  0.6 7.8 %copy-start.1 = (f32[16,16,512]{2,1,0:T(8,128)S(1)}, f32[16,16,512]{2,1,0:T(8,128)}, u32[]{:S(2)}) copy-start(f32[16,16,512]{2,1,0:T(8,128)} %reaction.1) | copy-start | bytes 1572868
  0.7 7.8 %copy-start.2 = (s32[16,16,512]{2,1,0:T(8,128)S(1)}, s32[16,16,512]{2,1,0:T(8,128)}, u32[]{:S(2)}) copy-start(s32[16,16,512]{2,1,0:T(8,128)} %kind.1) | copy-start | bytes 1572868
  0.7 7.8 %copy-start.3 = (s32[16,16,512]{2,1,0:T(8,128)S(1)}, s32[16,16,512]{2,1,0:T(8,128)}, u32[]{:S(2)}) copy-start(s32[16,16,512]{2,1,0:T(8,128)} %disk_id.1) | copy-start | bytes 1572868
  0.7 7.8 %copy-start.4 = (s32[16,16,512]{2,1,0:T(8,128)S(1)}, s32[16,16,512]{2,1,0:T(8,128)}, u32[]{:S(2)}) copy-start(s32[16,16,512]{2,1,0:T(8,128)} %disk_mask.1) | copy-start | bytes 1572868
  2.3 8.4 %collective-permute-start = (f32[128,128]{1,0:T(8,128)S(1)}, f32[128,128]{1,0:T(8,128)S(1)}, u32[]{:S(2)}, u32[]{:S(2)}) collective-permute-start(f32[128,128]{1,0:T(8,128)S(1)} %get-tuple-element.39), channel_id=1, source_target_pairs={{0,3},{1,2},{2,1},{3,0},{4,7},{5,6},{6,5},{7,4},{8,11},{9,10},{10,... | collective-permute-start | bytes 196616 | tf_op jit(solution)/shard_map/ppermute | solution.py:536
  6.2 4.5 %collective-permute-start.1 = (f32[128,128]{1,0:T(8,128)S(1)}, f32[128,128]{1,0:T(8,128)S(1)}, u32[]{:S(2)}, u32[]{:S(2)}) collective-permute-start(f32[128,128]{1,0:T(8,128)S(1)} %get-tuple-element.40), channel_id=1, source_target_pairs={{0,1},{1,0},{2,3},{3,2},{4,5},{5,4},{6,7},{7,6},{8,9},{9,8},{10,11... | collective-permute-start | bytes 196616 | tf_op jit(solution)/shard_map/ppermute | solution.py:536
  6.8 1.7 %copy-start.5 = (f32[120]{0:T(128)S(1)}, f32[120]{0:T(128)}, u32[]{:S(2)}) copy-start(f32[120]{0:T(128)} %param.11) | copy-start | bytes 1444
  6.8 3.9 %collective-permute-start.2 = (f32[64,128]{1,0:T(8,128)S(1)}, f32[64,128]{1,0:T(8,128)S(1)}, u32[]{:S(2)}, u32[]{:S(2)}) collective-permute-start(f32[64,128]{1,0:T(8,128)S(1)} %get-tuple-element.41), channel_id=1, source_target_pairs={{0,2},{1,3},{2,0},{3,1},{4,8},{5,9},{6,10},{7,11},{8,4},{9,5},{10,... | collective-permute-start | bytes 98312 | tf_op jit(solution)/shard_map/ppermute | solution.py:536
  6.9 3.8 %collective-permute-start.3 = (f32[64,128]{1,0:T(8,128)S(1)}, f32[64,128]{1,0:T(8,128)S(1)}, u32[]{:S(2)}, u32[]{:S(2)}) collective-permute-start(f32[64,128]{1,0:T(8,128)S(1)} %get-tuple-element.42), channel_id=1, source_target_pairs={{0,4},{1,5},{2,6},{3,7},{4,0},{5,1},{6,2},{7,3},{8,12},{9,13},{10,... | collective-permute-start | bytes 98312 | tf_op jit(solution)/shard_map/ppermute | solution.py:536
  11.3 1.4 %collective-permute-start.4 = (f32[224,128]{1,0:T(8,128)S(1)}, f32[224,128]{1,0:T(8,128)S(1)}, u32[]{:S(2)}, u32[]{:S(2)}) collective-permute-start(f32[224,128]{1,0:T(8,128)S(1)} %get-tuple-element.57), channel_id=1, source_target_pairs={{0,4},{1,5},{2,6},{3,7},{4,0},{5,1},{6,2},{7,3},{8,12},{9,13},{10,... | collective-permute-start | bytes 344072 | tf_op jit(solution)/shard_map/ppermute | solution.py:536
  12.7 4.2 %collective-permute-start.5 = (f32[112,128]{1,0:T(8,128)S(1)}, f32[112,128]{1,0:T(8,128)S(1)}, u32[]{:S(2)}, u32[]{:S(2)}) collective-permute-start(f32[112,128]{1,0:T(8,128)S(1)} %get-tuple-element.62), channel_id=1, source_target_pairs={{0,2},{1,3},{2,0},{3,1},{4,8},{5,9},{6,10},{7,11},{8,4},{9,5},{10,... | collective-permute-start | bytes 172040 | tf_op jit(solution)/shard_map/ppermute | solution.py:536
  13.2 7.5 %collective-permute-start.7 = (f32[192,128]{1,0:T(8,128)S(1)}, f32[192,128]{1,0:T(8,128)S(1)}, u32[]{:S(2)}, u32[]{:S(2)}) collective-permute-start(f32[192,128]{1,0:T(8,128)S(1)} %get-tuple-element.65), channel_id=1, source_target_pairs={{0,1},{1,0},{2,3},{3,2},{4,5},{5,4},{6,7},{7,6},{8,9},{9,8},{10,11... | collective-permute-start | bytes 294920 | tf_op jit(solution)/shard_map/ppermute | solution.py:536
  14.8 7.1 %collective-permute-start.8 = (f32[192,128]{1,0:T(8,128)S(1)}, f32[192,128]{1,0:T(8,128)S(1)}, u32[]{:S(2)}, u32[]{:S(2)}) collective-permute-start(f32[192,128]{1,0:T(8,128)S(1)} %get-tuple-element.66), channel_id=1, source_target_pairs={{0,3},{1,2},{2,1},{3,0},{4,7},{5,6},{6,5},{7,4},{8,11},{9,10},{10,... | collective-permute-start | bytes 294920 | tf_op jit(solution)/shard_map/ppermute | solution.py:536
  17.0 1.3 %collective-permute-start.9 = (f32[40,128]{1,0:T(8,128)S(1)}, f32[40,128]{1,0:T(8,128)S(1)}, u32[]{:S(2)}, u32[]{:S(2)}) collective-permute-start(f32[40,128]{1,0:T(8,128)S(1)} %get-tuple-element.72.full), channel_id=1, source_target_pairs={{0,4},{1,5},{2,6},{3,7},{4,0},{5,1},{6,2},{7,3},{8,12},{9,13},{10,... | collective-permute-start | bytes 61448 | tf_op jit(solution)/shard_map/ppermute | solution.py:536
  17.1 5.6 %collective-permute-start.6 = (f32[152,128]{1,0:T(8,128)S(1)}, f32[152,128]{1,0:T(8,128)S(1)}, u32[]{:S(2)}, u32[]{:S(2)}) collective-permute-start(f32[152,128]{1,0:T(8,128)S(1)} %get-tuple-element.64), channel_id=1, source_target_pairs={{0,2},{1,3},{2,0},{3,1},{4,8},{5,9},{6,10},{7,11},{8,4},{9,5},{10,... | collective-permute-start | bytes 233480 | tf_op jit(solution)/shard_map/ppermute | solution.py:536
  18.3 7.4 %collective-permute-start.11 = (f32[136,128]{1,0:T(8,128)S(1)}, f32[136,128]{1,0:T(8,128)S(1)}, u32[]{:S(2)}, u32[]{:S(2)}) collective-permute-start(f32[136,128]{1,0:T(8,128)S(1)} %get-tuple-element.74.refs_9_), channel_id=1, source_target_pairs={{0,2},{1,3},{2,0},{3,1},{4,6},{5,7},{6,4},{7,5},{8,10},{9,11},{10,... | collective-permute-start | bytes 208904 | tf_op jit(solution)/shard_map/ppermute | solution.py:536
  19.2 4.0 %collective-permute-start.10 = (f32[80,128]{1,0:T(8,128)S(1)}, f32[80,128]{1,0:T(8,128)S(1)}, u32[]{:S(2)}, u32[]{:S(2)}) collective-permute-start(f32[80,128]{1,0:T(8,128)S(1)} %get-tuple-element.75), channel_id=1, source_target_pairs={{0,1},{1,0},{2,3},{3,2},{4,5},{5,4},{6,7},{7,6},{8,9},{9,8},{10,11... | collective-permute-start | bytes 122888 | tf_op jit(solution)/shard_map/ppermute | solution.py:536
  20.7 4.9 %collective-permute-start.12 = (f32[80,128]{1,0:T(8,128)S(1)}, f32[80,128]{1,0:T(8,128)S(1)}, u32[]{:S(2)}, u32[]{:S(2)}) collective-permute-start(f32[80,128]{1,0:T(8,128)S(1)} %get-tuple-element.75), channel_id=1, source_target_pairs={{0,3},{1,2},{2,1},{3,0},{4,7},{5,6},{6,5},{7,4},{8,11},{9,10},{10,... | collective-permute-start | bytes 122888 | tf_op jit(solution)/shard_map/ppermute | solution.py:536

commit v13 on v12

--- a/solution.py
+++ b/solution.py
@@ -204,7 +204,7 @@
         put(chip, 0, f_far)
         put(core, 0, f_near)
 
-    def set_up(source, reaction, kind, disk_id, disk_mask, table, f, g, d, absorb, inner, V):
+    def set_up(source, reaction, kind, disk_id, disk_mask, table, f, g, d, absorb, inner, rows, V):
         for k in range(4):
             total = jnp.zeros((16, 512), F32)
             for x in range(4 * k, 4 * k + 4):
@@ -220,7 +220,10 @@
                 total = total + f[x - 1]
             if x < 15:
                 total = total + f[x + 1]
-            inner[x] = 1.2 * f[x] + g[x] * total
+            value = 1.2 * f[x] + g[x] * total
+            inner[x] = value
+            for at, part in enumerate((value[0:1, :], value[15:16, :], g[x, 0:1, :], g[x, 15:16, :])):
+                rows[at, x : x + 1, :] = part
 
     def halo_x(core, chip, row, x, x_even, chip_row=None):
         a, b = get(core, row, 16, 512), get(chip, row if chip_row is None else chip_row, 16, 512)
@@ -234,7 +237,33 @@
         high = jnp.where(y < ny - 1, jnp.where(y_even, a, b), 0.0)
         return low, high
 
-    def smooth(inner, g, absorb, core, chip, row, odd, s, to_core, sums, y_faces, y_more, lo, hi, y0, y1, y14, y15):
+    def early(inner, g, rows, absorb, core, chip, row, odd, to_core, sums, y_faces, lo, hi):
+        x_at, y_at, x_even, y_even = where_am_i()
+        left, right = halo_x(core, chip, 0, x_at, x_even)
+        lo[...], hi[...] = halo_y(row, odd, 0, y_at, y_even)
+
+        def second_at(x, outer=0.0):
+            return inner[x] + g[x] * (outer_rows(lo[pl.ds(x, 1), :], hi[pl.ds(x, 1), :]) + outer)
+
+        s_first, s_last = second_at(0, left), second_at(15, right)
+        row_of = iota((16, 512), 0)
+        for at, (outer, line) in enumerate(((lo, slice(0, 1)), (hi, slice(15, 16)))):
+            first, last = (jnp.broadcast_to(side[line, :], (16, 512)) for side in (left, right))
+            more = jnp.where(row_of == 0, first, jnp.where(row_of == 15, last, 0.0))
+            y_faces[16 * at : 16 * at + 16, :] = rows[at] + rows[2 + at] * (outer[...] + more)
+        out, src = iota((16, 64), 0), iota((16, 64), 1)
+        pick = ((out // 4 == src // 16) & (out % 4 == (src % 16) // 4)).astype(F32)
+        sides = jnp.concatenate([s_first, s_last, y_faces[...]], axis=0)
+        sums[...] = dot(dot(pick, sides), group_lanes(512))
+        put(to_core, 0, jnp.where(x_even, s_last, s_first))
+        put(to_core, 64, second_at(jnp.where(x_even, 14, 1)))
+        put(to_core, 128, g[jnp.where(x_even, 15, 0)])
+        to_core[192:196, :] = jnp.where(x_even, sums[4:8, :], sums[0:4, :])
+        to_core[196:200, :] = jnp.zeros((4, 128), F32)
+        to_core[200:208, :] = sums[8:16, :]
+        to_core[208:224, :] = absorb[...]
+
+    def restrict(f, g, d, absorb, inner, sums, core, chip, row, odd, s, block, y_more, lo, hi, V):
         x_at, y_at, x_even, y_even = where_am_i()
         left, right = halo_x(core, chip, 0, x_at, x_even)
         lo[...], hi[...] = halo_y(row, odd, 0, y_at, y_even)
@@ -246,27 +275,8 @@
                 total = total + right
             value = inner[x] + g[x] * total
             s[x] = value
-            y0[x : x + 1, :] = value[0:1, :]
-            y1[x : x + 1, :] = value[1:2, :]
-            y14[x : x + 1, :] = value[14:15, :]
-            y15[x : x + 1, :] = value[15:16, :]
-        y_faces[0:16, :] = y0[...]
-        y_faces[16:32, :] = y15[...]
-        out, src = iota((16, 64), 0), iota((16, 64), 1)
-        pick = ((out // 4 == src // 16) & (out % 4 == (src % 16) // 4)).astype(F32)
-        sides = jnp.concatenate([s[0], s[15], y0[...], y15[...]], axis=0)
-        sums[...] = dot(dot(pick, sides), group_lanes(512))
-        put(to_core, 0, s[jnp.where(x_even, 15, 0)])
-        put(to_core, 64, s[jnp.where(x_even, 14, 1)])
-        put(to_core, 128, g[jnp.where(x_even, 15, 0)])
-        to_core[192:196, :] = jnp.where(x_even, sums[4:8, :], sums[0:4, :])
-        to_core[196:200, :] = jnp.zeros((4, 128), F32)
-        to_core[200:208, :] = sums[8:16, :]
-        to_core[208:224, :] = absorb[...]
-        for at, ref in enumerate((y1, y14)):
-            y_more[16 * at : 16 * at + 16, :] = ref[...]
-
-    def restrict(f, d, absorb, s, sums, block, V):
+            y_more[x : x + 1, :] = value[1:2, :]
+            y_more[16 + x : 17 + x, :] = value[14:15, :]
         for k in range(4):
             total = jnp.zeros((16, 512), F32)
             for x in range(4 * k, 4 * k + 4):
@@ -550,21 +560,27 @@
         )
         a_core, a_chip = swap(core, core_pairs), swap(chip, chip_pairs)
         a_odd, a_row = swap(odd, odd_pairs), swap(row, row_pairs[0])
-        f, g, d, absorb, inner = call(
-            set_up, [field, field, field, (16, 128), field], *inputs, scratch=[(64, 512)], name="set_up"
-        )
-        a_odd, a_row, a_chip, a_core, f, g, d, absorb, inner = lax.optimization_barrier(
-            (a_odd, a_row, a_chip, a_core, f, g, d, absorb, inner)
-        )
-        s, to_core, sums, y_faces, y_more = call(
-            smooth,
-            [field, (224, 128), (16, 128), (32, 512), (32, 512)],
-            inner, g, absorb, a_core, a_chip, a_row, a_odd,
-            scratch=[slab] * 6,
-            name="smooth",
+        f, g, d, absorb, inner, rows = call(
+            set_up, [field, field, field, (16, 128), field, (4, 16, 512)], *inputs, scratch=[(64, 512)], name="set_up"
+        )
+        a_odd, a_row, a_chip, a_core, f, g, d, absorb, inner, rows = lax.optimization_barrier(
+            (a_odd, a_row, a_chip, a_core, f, g, d, absorb, inner, rows)
+        )
+        to_core, sums, y_faces = call(
+            early,
+            [(224, 128), (16, 128), (32, 512)],
+            inner, g, rows, absorb, a_core, a_chip, a_row, a_odd,
+            scratch=[slab] * 2,
+            name="early",
         )
         s_core = swap(to_core, core_pairs)
-        (block,) = call(restrict, [(40, 128)], f, d, absorb, s, sums, scratch=[(64, 512)], name="restrict")
+        s, block, y_more = call(
+            restrict,
+            [field, (40, 128), (32, 512)],
+            f, g, d, absorb, inner, sums, a_core, a_chip, a_row, a_odd,
+            scratch=[slab, slab, (64, 512)],
+            name="restrict",
+        )
         mine, to_chip, to_row, to_odd = call(
             to_chip_kernel,
             [(40, 128), (112, 128), (FACES, 128), (FACES, 128)],

time: 28 us -> 27.8 us (level)
  no operation moved by 1% of the time
where the time goes in v13:
time: 27.8 us; the launch traced here: 27.7 us
  starting transfers between devices  13.9 us (50%)
  waiting for transfers between devices  6.49 us (23%)
  Pallas kernels  6.47 us (23%)
  between operations  0.77 us (3%)
    ppermute x13, starting transfers between devices, swap(): return lax.ppermute(array, axes, pairs)  13.9 us
    ppermute x13, waiting for transfers between devices, swap(): return lax.ppermute(array, axes, pairs)  6.49 us
    pallas_call x9, Pallas kernels, call(): pl.pallas_call(kernel, out_shape=[jax.ShapeDtypeStruct(s, F32) for s in o...  6.47 us
  transfers between devices with their start and end apart: 13, of which 6 were waited for; matrix products, arithmetic and copies ran while one was open for 0% of the time, Pallas kernels for 8%

profile of v13, /device:TPU:0, one launch (start us, length us, event | category | flops | bytes accessed | tf_op | source)
XLA Modules:
  0.0 27.7 jit_solution(14389861766525565546)
XLA Ops:
  0.7 1.6 %faces.1 = (f32[64,128]{1,0:T(8,128)S(1)}, f32[64,128]{1,0:T(8,128)S(1)}, f32[128,128]{1,0:T(8,128)S(1)}, f32[128,128]{1,0:T(8,128)S(1)}) custom-call(f32[16,16,512]{2,1,0:T(8,128)} %source.1, f32[16,16,512]{2,1,0:T(8,128)} %reaction.1, s32[16,16,512]{2,1,0:T(8,128)} %kind.1, s32[16,16,512]{2,1,0:T(8,128)} %disk_id.1, s32[16,16,512]{2,1,0:T(8,128)} %disk_mask.1, ...), custom_call_target="tpu_custom_call" | custom-call | tf_op jit(solution)/shard_map/faces/pallas_call | solution.py:24
  2.3 4.0 %collective-permute-start = (f32[128,128]{1,0:T(8,128)S(1)}, f32[128,128]{1,0:T(8,128)S(1)}, u32[]{:S(2)}, u32[]{:S(2)}) collective-permute-start(f32[128,128]{1,0:T(8,128)S(1)} %get-tuple-element.42), channel_id=1, source_target_pairs={{0,3},{1,2},{2,1},{3,0},{4,7},{5,6},{6,5},{7,4},{8,11},{9,10},{10,... | collective-permute-start | bytes 196616 | tf_op jit(solution)/shard_map/ppermute | solution.py:546
  6.2 0.5 %collective-permute-start.1 = (f32[128,128]{1,0:T(8,128)S(1)}, f32[128,128]{1,0:T(8,128)S(1)}, u32[]{:S(2)}, u32[]{:S(2)}) collective-permute-start(f32[128,128]{1,0:T(8,128)S(1)} %get-tuple-element.43), channel_id=1, source_target_pairs={{0,1},{1,0},{2,3},{3,2},{4,5},{5,4},{6,7},{7,6},{8,9},{9,8},{10,11... | collective-permute-start | bytes 196616 | tf_op jit(solution)/shard_map/ppermute | solution.py:546
  6.8 0.1 collective-permute-start.2
  6.9 1.6 %collective-permute-start.3 = (f32[64,128]{1,0:T(8,128)S(1)}, f32[64,128]{1,0:T(8,128)S(1)}, u32[]{:S(2)}, u32[]{:S(2)}) collective-permute-start(f32[64,128]{1,0:T(8,128)S(1)} %get-tuple-element.45), channel_id=1, source_target_pairs={{0,4},{1,5},{2,6},{3,7},{4,0},{5,1},{6,2},{7,3},{8,12},{9,13},{10,... | collective-permute-start | bytes 98312 | tf_op jit(solution)/shard_map/ppermute | solution.py:546
  8.5 0.9 %set_up.1 = (f32[16,16,512]{2,1,0:T(8,128)S(1)}, f32[16,16,512]{2,1,0:T(8,128)S(1)}, f32[16,16,512]{2,1,0:T(8,128)S(1)}, f32[16,128]{1,0:T(8,128)S(1)}, f32[16,1...) custom-call(f32[16,16,512]{2,1,0:T(8,128)S(1)} %copy-done, f32[16,16,512]{2,1,0:T(8,128)S(1)} %copy-done.1, ...), custom_call_target="tpu_custom_call" | custom-call | tf_op jit(solution)/shard_map/set_up/pallas_call | solution.py:24
  9.4 1.3 %collective-permute-done.2.chip.a_chip = f32[64,128]{1,0:T(8,128)S(1)} collective-permute-done((f32[64,128]{1,0:T(8,128)S(1)}, f32[64,128]{1,0:T(8,128)S(1)}, u32[]{:S(2)}, u32[]{:S(2)}) %collective-permute-start.2) | collective-permute-done | bytes 32800 | tf_op jit(solution)/shard_map/ppermute | solution.py:546
  10.7 0.4 %early.1 = (f32[224,128]{1,0:T(8,128)S(1)}, f32[16,128]{1,0:T(8,128)S(1)}, f32[32,512]{1,0:T(8,128)S(1)}) custom-call(f32[16,16,512]{2,1,0:T(8,128)S(1)} %get-tuple-element.56.inner, f32[16,16,512]{2,1,0:T(8,128)S(1)} %get-tuple-element.53.g.refs_1_, f32[4,16,512]{2,1,0:T(8,128)S(1)} %get-tuple-element.57.rows, f32[16,128]{1,0:T(8,128)S(1)} %get-tuple-element.55.absorb, ...), custom_call_target="tpu_custom_call" | custom-call | tf_op jit(solution)/shard_map/early/pallas_call | solution.py:24
  11.2 0.8 %restrict.1 = (f32[16,16,512]{2,1,0:T(8,128)S(1)}, f32[40,128]{1,0:T(8,128)S(1)}, f32[32,512]{1,0:T(8,128)S(1)}) custom-call(f32[16,16,512]{2,1,0:T(8,128)S(1)} %get-tuple-element.52.f.refs_0_, f32[16,16,512]{2,1,0:T(8,128)S(1)} %get-tuple-element.53.g.refs_1_, f32[16,16,512]{2,1,0:T(8,128)S(1)} %get-tuple-element.54.d, ...), custom_call_target="tpu_custom_call" | custom-call | tf_op jit(solution)/shard_map/restrict/pallas_call | solution.py:24
  12.0 0.5 %collective-permute-done.4.core.s_core = f32[224,128]{1,0:T(8,128)S(1)} collective-permute-done((f32[224,128]{1,0:T(8,128)S(1)}, f32[224,128]{1,0:T(8,128)S(1)}, u32[]{:S(2)}, u32[]{:S(2)}) %collective-permute-start.4) | collective-permute-done | bytes 114720 | tf_op jit(solution)/shard_map/ppermute | solution.py:546
  12.6 0.5 %collective-permute-start.5 = (f32[112,128]{1,0:T(8,128)S(1)}, f32[112,128]{1,0:T(8,128)S(1)}, u32[]{:S(2)}, u32[]{:S(2)}) collective-permute-start(f32[112,128]{1,0:T(8,128)S(1)} %get-tuple-element.68), channel_id=1, source_target_pairs={{0,2},{1,3},{2,0},{3,1},{4,8},{5,9},{6,10},{7,11},{8,4},{9,5},{10,... | collective-permute-start | bytes 172040 | tf_op jit(solution)/shard_map/ppermute | solution.py:546
  13.1 1.6 %collective-permute-start.7 = (f32[192,128]{1,0:T(8,128)S(1)}, f32[192,128]{1,0:T(8,128)S(1)}, u32[]{:S(2)}, u32[]{:S(2)}) collective-permute-start(f32[192,128]{1,0:T(8,128)S(1)} %get-tuple-element.71), channel_id=1, source_target_pairs={{0,1},{1,0},{2,3},{3,2},{4,5},{5,4},{6,7},{7,6},{8,9},{9,8},{10,11... | collective-permute-start | bytes 294920 | tf_op jit(solution)/shard_map/ppermute | solution.py:546
  14.6 1.5 %collective-permute-start.8 = (f32[192,128]{1,0:T(8,128)S(1)}, f32[192,128]{1,0:T(8,128)S(1)}, u32[]{:S(2)}, u32[]{:S(2)}) collective-permute-start(f32[192,128]{1,0:T(8,128)S(1)} %get-tuple-element.72), channel_id=1, source_target_pairs={{0,3},{1,2},{2,1},{3,0},{4,7},{5,6},{6,5},{7,4},{8,11},{9,10},{10,... | collective-permute-start | bytes 294920 | tf_op jit(solution)/shard_map/ppermute | solution.py:546
  16.1 0.7 %collective-permute-done.5.chip.s_chip = f32[112,128]{1,0:T(8,128)S(1)} collective-permute-done((f32[112,128]{1,0:T(8,128)S(1)}, f32[112,128]{1,0:T(8,128)S(1)}, u32[]{:S(2)}, u32[]{:S(2)}) %collective-permute-start.5) | collective-permute-done | bytes 57376 | tf_op jit(solution)/shard_map/ppermute | solution.py:546
  16.8 0.1 collective-permute-start.9
  16.9 0.5 %collective-permute-start.6 = (f32[152,128]{1,0:T(8,128)S(1)}, f32[152,128]{1,0:T(8,128)S(1)}, u32[]{:S(2)}, u32[]{:S(2)}) collective-permute-start(f32[152,128]{1,0:T(8,128)S(1)} %get-tuple-element.70), channel_id=1, source_target_pairs={{0,2},{1,3},{2,0},{3,1},{4,8},{5,9},{6,10},{7,11},{8,4},{9,5},{10,... | collective-permute-start | bytes 233480 | tf_op jit(solution)/shard_map/ppermute | solution.py:546
  17.4 0.7 %collective-permute-done.9.core = f32[40,128]{1,0:T(8,128)S(1)} collective-permute-done((f32[40,128]{1,0:T(8,128)S(1)}, f32[40,128]{1,0:T(8,128)S(1)}, u32[]{:S(2)}, u32[]{:S(2)}) %collective-permute-start.9) | collective-permute-done | bytes 20512 | tf_op jit(solution)/shard_map/ppermute | solution.py:546
  18.1 1.0 %collective-permute-start.11 = (f32[136,128]{1,0:T(8,128)S(1)}, f32[136,128]{1,0:T(8,128)S(1)}, u32[]{:S(2)}, u32[]{:S(2)}) collective-permute-start(f32[136,128]{1,0:T(8,128)S(1)} %get-tuple-element.80.refs_9_), channel_id=1, source_target_pairs={{0,2},{1,3},{2,0},{3,1},{4,6},{5,7},{6,4},{7,5},{8,10},{9,11},{10,... | collective-permute-start | bytes 208904 | tf_op jit(solution)/shard_map/ppermute | solution.py:546
  19.1 1.5 %collective-permute-start.10 = (f32[80,128]{1,0:T(8,128)S(1)}, f32[80,128]{1,0:T(8,128)S(1)}, u32[]{:S(2)}, u32[]{:S(2)}) collective-permute-start(f32[80,128]{1,0:T(8,128)S(1)} %get-tuple-element.81), channel_id=1, source_target_pairs={{0,1},{1,0},{2,3},{3,2},{4,5},{5,4},{6,7},{7,6},{8,9},{9,8},{10,11... | collective-permute-start | bytes 122888 | tf_op jit(solution)/shard_map/ppermute | solution.py:546
  20.6 1.1 %collective-permute-start.12 = (f32[80,128]{1,0:T(8,128)S(1)}, f32[80,128]{1,0:T(8,128)S(1)}, u32[]{:S(2)}, u32[]{:S(2)}) collective-permute-start(f32[80,128]{1,0:T(8,128)S(1)} %get-tuple-element.81), channel_id=1, source_target_pairs={{0,3},{1,2},{2,1},{3,0},{4,7},{5,6},{6,5},{7,4},{8,11},{9,10},{10,... | collective-permute-start | bytes 122888 | tf_op jit(solution)/shard_map/ppermute | solution.py:546
  21.7 0.9 %collective-permute-done.6.s_more = f32[152,128]{1,0:T(8,128)S(1)} collective-permute-done((f32[152,128]{1,0:T(8,128)S(1)}, f32[152,128]{1,0:T(8,128)S(1)}, u32[]{:S(2)}, u32[]{:S(2)}) %collective-permute-start.6) | collective-permute-done | bytes 77856 | tf_op jit(solution)/shard_map/ppermute | solution.py:546
  22.5 0.5 %prepare.1 = (f32[18,16,512]{2,1,0:T(8,128)S(1)}, f32[16,512]{1,0:T(8,128)S(1)}, f32[16,512]{1,0:T(8,128)S(1)}, f32[2,16,512]{2,1,0:T(8,128)S(1)}, f32[2,16,512]{2,1,0:T(8,128)S(1)}) custom-call(f32[16,16,512]{2,1,0:T(8,128)S(1)} %get-tuple-element.52.f.refs_0_, f32[16,16,512]{2,1,0:T(8,128)S(1)} %get-tuple-element.53.g.refs_1_, ...), custom_call_target="tpu_custom_call" | custom-call | tf_op jit(solution)/shard_map/prepare/pallas_call | solution.py:24
  23.1 2.4 %collective-permute-done.12.refs_12_ = f32[80,128]{1,0:T(8,128)S(1)} collective-permute-done((f32[80,128]{1,0:T(8,128)S(1)}, f32[80,128]{1,0:T(8,128)S(1)}, u32[]{:S(2)}, u32[]{:S(2)}) %collective-permute-start.12) | collective-permute-done | bytes 40992 | tf_op jit(solution)/shard_map/ppermute | solution.py:546
  25.5 2.2 %finish.1 = (f32[16,16,512]{2,1,0:T(8,128)}, f32[4,16,128]{2,1,0:T(8,128)}) custom-call(f32[16,16,512]{2,1,0:T(8,128)S(1)} %get-tuple-element.52.f.refs_0_, f32[16,16,512]{2,1,0:T(8,128)S(1)} %get-tuple-element.53.g.refs_1_, f32[18,16,512]{2,1,0:T(8,128)S(1)} %get-tuple-element.73.refs_2_, f32[16,512]{1,0:T(8,128)S(1)} %get-tuple-element.74.refs_3_, ...), custom_call_target="tpu_custom_call" | custom-call | tf_op jit(solution)/shard_map/finish/pallas_call | solution.py:24
  (23 shorter events, 0.2 us)
Async XLA Ops:
  0.6 7.8 %copy-start = (f32[16,16,512]{2,1,0:T(8,128)S(1)}, f32[16,16,512]{2,1,0:T(8,128)}, u32[]{:S(2)}) copy-start(f32[16,16,512]{2,1,0:T(8,128)} %source.1) | copy-start | bytes 1572868
  0.6 7.8 %copy-start.1 = (f32[16,16,512]{2,1,0:T(8,128)S(1)}, f32[16,16,512]{2,1,0:T(8,128)}, u32[]{:S(2)}) copy-start(f32[16,16,512]{2,1,0:T(8,128)} %reaction.1) | copy-start | bytes 1572868
  0.7 7.8 %copy-start.2 = (s32[16,16,512]{2,1,0:T(8,128)S(1)}, s32[16,16,512]{2,1,0:T(8,128)}, u32[]{:S(2)}) copy-start(s32[16,16,512]{2,1,0:T(8,128)} %kind.1) | copy-start | bytes 1572868
  0.7 7.8 %copy-start.3 = (s32[16,16,512]{2,1,0:T(8,128)S(1)}, s32[16,16,512]{2,1,0:T(8,128)}, u32[]{:S(2)}) copy-start(s32[16,16,512]{2,1,0:T(8,128)} %disk_id.1) | copy-start | bytes 1572868
  0.7 7.8 %copy-start.4 = (s32[16,16,512]{2,1,0:T(8,128)S(1)}, s32[16,16,512]{2,1,0:T(8,128)}, u32[]{:S(2)}) copy-start(s32[16,16,512]{2,1,0:T(8,128)} %disk_mask.1) | copy-start | bytes 1572868
  2.3 8.4 %collective-permute-start = (f32[128,128]{1,0:T(8,128)S(1)}, f32[128,128]{1,0:T(8,128)S(1)}, u32[]{:S(2)}, u32[]{:S(2)}) collective-permute-start(f32[128,128]{1,0:T(8,128)S(1)} %get-tuple-element.42), channel_id=1, source_target_pairs={{0,3},{1,2},{2,1},{3,0},{4,7},{5,6},{6,5},{7,4},{8,11},{9,10},{10,... | collective-permute-start | bytes 196616 | tf_op jit(solution)/shard_map/ppermute | solution.py:546
  6.2 4.5 %collective-permute-start.1 = (f32[128,128]{1,0:T(8,128)S(1)}, f32[128,128]{1,0:T(8,128)S(1)}, u32[]{:S(2)}, u32[]{:S(2)}) collective-permute-start(f32[128,128]{1,0:T(8,128)S(1)} %get-tuple-element.43), channel_id=1, source_target_pairs={{0,1},{1,0},{2,3},{3,2},{4,5},{5,4},{6,7},{7,6},{8,9},{9,8},{10,11... | collective-permute-start | bytes 196616 | tf_op jit(solution)/shard_map/ppermute | solution.py:546
  6.8 1.7 %copy-start.5 = (f32[120]{0:T(128)S(1)}, f32[120]{0:T(128)}, u32[]{:S(2)}) copy-start(f32[120]{0:T(128)} %param.11) | copy-start | bytes 1444
  6.8 3.9 %collective-permute-start.2 = (f32[64,128]{1,0:T(8,128)S(1)}, f32[64,128]{1,0:T(8,128)S(1)}, u32[]{:S(2)}, u32[]{:S(2)}) collective-permute-start(f32[64,128]{1,0:T(8,128)S(1)} %get-tuple-element.44), channel_id=1, source_target_pairs={{0,2},{1,3},{2,0},{3,1},{4,8},{5,9},{6,10},{7,11},{8,4},{9,5},{10,... | collective-permute-start | bytes 98312 | tf_op jit(solution)/shard_map/ppermute | solution.py:546
  6.9 3.8 %collective-permute-start.3 = (f32[64,128]{1,0:T(8,128)S(1)}, f32[64,128]{1,0:T(8,128)S(1)}, u32[]{:S(2)}, u32[]{:S(2)}) collective-permute-start(f32[64,128]{1,0:T(8,128)S(1)} %get-tuple-element.45), channel_id=1, source_target_pairs={{0,4},{1,5},{2,6},{3,7},{4,0},{5,1},{6,2},{7,3},{8,12},{9,13},{10,... | collective-permute-start | bytes 98312 | tf_op jit(solution)/shard_map/ppermute | solution.py:546
  11.1 1.4 %collective-permute-start.4 = (f32[224,128]{1,0:T(8,128)S(1)}, f32[224,128]{1,0:T(8,128)S(1)}, u32[]{:S(2)}, u32[]{:S(2)}) collective-permute-start(f32[224,128]{1,0:T(8,128)S(1)} %get-tuple-element.64), channel_id=1, source_target_pairs={{0,4},{1,5},{2,6},{3,7},{4,0},{5,1},{6,2},{7,3},{8,12},{9,13},{10,... | collective-permute-start | bytes 344072 | tf_op jit(solution)/shard_map/ppermute | solution.py:546
  12.6 4.2 %collective-permute-start.5 = (f32[112,128]{1,0:T(8,128)S(1)}, f32[112,128]{1,0:T(8,128)S(1)}, u32[]{:S(2)}, u32[]{:S(2)}) collective-permute-start(f32[112,128]{1,0:T(8,128)S(1)} %get-tuple-element.68), channel_id=1, source_target_pairs={{0,2},{1,3},{2,0},{3,1},{4,8},{5,9},{6,10},{7,11},{8,4},{9,5},{10,... | collective-permute-start | bytes 172040 | tf_op jit(solution)/shard_map/ppermute | solution.py:546
  13.1 7.5 %collective-permute-start.7 = (f32[192,128]{1,0:T(8,128)S(1)}, f32[192,128]{1,0:T(8,128)S(1)}, u32[]{:S(2)}, u32[]{:S(2)}) collective-permute-start(f32[192,128]{1,0:T(8,128)S(1)} %get-tuple-element.71), channel_id=1, source_target_pairs={{0,1},{1,0},{2,3},{3,2},{4,5},{5,4},{6,7},{7,6},{8,9},{9,8},{10,11... | collective-permute-start | bytes 294920 | tf_op jit(solution)/shard_map/ppermute | solution.py:546
  14.6 7.1 %collective-permute-start.8 = (f32[192,128]{1,0:T(8,128)S(1)}, f32[192,128]{1,0:T(8,128)S(1)}, u32[]{:S(2)}, u32[]{:S(2)}) collective-permute-start(f32[192,128]{1,0:T(8,128)S(1)} %get-tuple-element.72), channel_id=1, source_target_pairs={{0,3},{1,2},{2,1},{3,0},{4,7},{5,6},{6,5},{7,4},{8,11},{9,10},{10,... | collective-permute-start | bytes 294920 | tf_op jit(solution)/shard_map/ppermute | solution.py:546
  16.8 1.3 %collective-permute-start.9 = (f32[40,128]{1,0:T(8,128)S(1)}, f32[40,128]{1,0:T(8,128)S(1)}, u32[]{:S(2)}, u32[]{:S(2)}) collective-permute-start(f32[40,128]{1,0:T(8,128)S(1)} %get-tuple-element.78.full), channel_id=1, source_target_pairs={{0,4},{1,5},{2,6},{3,7},{4,0},{5,1},{6,2},{7,3},{8,12},{9,13},{10,... | collective-permute-start | bytes 61448 | tf_op jit(solution)/shard_map/ppermute | solution.py:546
  16.9 5.6 %collective-permute-start.6 = (f32[152,128]{1,0:T(8,128)S(1)}, f32[152,128]{1,0:T(8,128)S(1)}, u32[]{:S(2)}, u32[]{:S(2)}) collective-permute-start(f32[152,128]{1,0:T(8,128)S(1)} %get-tuple-element.70), channel_id=1, source_target_pairs={{0,2},{1,3},{2,0},{3,1},{4,8},{5,9},{6,10},{7,11},{8,4},{9,5},{10,... | collective-permute-start | bytes 233480 | tf_op jit(solution)/shard_map/ppermute | solution.py:546
  18.1 7.4 %collective-permute-start.11 = (f32[136,128]{1,0:T(8,128)S(1)}, f32[136,128]{1,0:T(8,128)S(1)}, u32[]{:S(2)}, u32[]{:S(2)}) collective-permute-start(f32[136,128]{1,0:T(8,128)S(1)} %get-tuple-element.80.refs_9_), channel_id=1, source_target_pairs={{0,2},{1,3},{2,0},{3,1},{4,6},{5,7},{6,4},{7,5},{8,10},{9,11},{10,... | collective-permute-start | bytes 208904 | tf_op jit(solution)/shard_map/ppermute | solution.py:546
  19.1 4.0 %collective-permute-start.10 = (f32[80,128]{1,0:T(8,128)S(1)}, f32[80,128]{1,0:T(8,128)S(1)}, u32[]{:S(2)}, u32[]{:S(2)}) collective-permute-start(f32[80,128]{1,0:T(8,128)S(1)} %get-tuple-element.81), channel_id=1, source_target_pairs={{0,1},{1,0},{2,3},{3,2},{4,5},{5,4},{6,7},{7,6},{8,9},{9,8},{10,11... | collective-permute-start | bytes 122888 | tf_op jit(solution)/shard_map/ppermute | solution.py:546
  20.6 4.9 %collective-permute-start.12 = (f32[80,128]{1,0:T(8,128)S(1)}, f32[80,128]{1,0:T(8,128)S(1)}, u32[]{:S(2)}, u32[]{:S(2)}) collective-permute-start(f32[80,128]{1,0:T(8,128)S(1)} %get-tuple-element.81), channel_id=1, source_target_pairs={{0,3},{1,2},{2,1},{3,0},{4,7},{5,6},{6,5},{7,4},{8,11},{9,10},{10,... | collective-permute-start | bytes 122888 | tf_op jit(solution)/shard_map/ppermute | solution.py:546

commit v14 on v13

--- a/solution.py
+++ b/solution.py
@@ -17,7 +17,7 @@
 
 HBM = pl.BlockSpec(memory_space=pltpu.HBM)
 MORE = 152
-FACES = 192
+FACES = 184
 
 
 def call(kernel, outs, *args, scratch=(), name=None, in_specs=None, out_specs=None):
@@ -396,7 +396,7 @@
 
     def finish(*refs):
         f, g, u, u_low, u_high, g_x, g_y, s_row, s_odd = refs[:9]
-        windows = refs[9 : 9 + ny]
+        windows = refs[9 : 9 + ny][::-1]
         pressure, coarse = refs[9 + ny : 11 + ny]
         every, res, diag, inv, one, two, sol, C, U, ul, uh, result, slab_out, sems = refs[11 + ny :]
         x_at, y_at, x_even, y_even = where_am_i()
@@ -609,7 +609,7 @@
         pressure, coarse = call(
             finish,
             [field, (4, planes, 128)],
-            f, g, *prepared, s_row, s_odd, *windows,
+            f, g, *prepared, s_row, s_odd, *windows[::-1],
             scratch=[(ny, 136, 128)]
             + [(planes, 16, 128)] * 3
             + [(planes + 2, 16, 128)] * 3

time: 27.8 us -> 27.5 us (0.989)
  waiting for transfers between devices: 6.49 us -> 6.13 us
    ppermute x13, waiting for transfers between devices: 6.49 us -> 6.13 us  [swap(): return lax.ppermute(array, axes, pairs)]
  transfers between devices with their start and end apart: 13 -> 13, of which waited for: 6 -> 7; matrix products, arithmetic and copies ran while one was open for 0% -> 0% of each run, Pallas kernels for 8% -> 8%
where the time goes in v14:
time: 27.5 us; the launch traced here: 27.3 us
  starting transfers between devices  13.9 us (51%)
  Pallas kernels  6.47 us (24%)
  waiting for transfers between devices  6.13 us (22%)
  between operations  0.77 us (3%)
    ppermute x13, starting transfers between devices, swap(): return lax.ppermute(array, axes, pairs)  13.9 us
    pallas_call x9, Pallas kernels, call(): pl.pallas_call(kernel, out_shape=[jax.ShapeDtypeStruct(s, F32) for s in o...  6.47 us
    ppermute x13, waiting for transfers between devices, swap(): return lax.ppermute(array, axes, pairs)  6.13 us
  transfers between devices with their start and end apart: 13, of which 7 were waited for; matrix products, arithmetic and copies ran while one was open for 0% of the time, Pallas kernels for 8%

profile of v14, /device:TPU:0, one launch (start us, length us, event | category | flops | bytes accessed | tf_op | source)
XLA Modules:
  0.0 27.3 jit_solution(4616129043421995980)
XLA Ops:
  0.7 1.6 %faces.1 = (f32[64,128]{1,0:T(8,128)S(1)}, f32[64,128]{1,0:T(8,128)S(1)}, f32[128,128]{1,0:T(8,128)S(1)}, f32[128,128]{1,0:T(8,128)S(1)}) custom-call(f32[16,16,512]{2,1,0:T(8,128)} %source.1, f32[16,16,512]{2,1,0:T(8,128)} %reaction.1, s32[16,16,512]{2,1,0:T(8,128)} %kind.1, s32[16,16,512]{2,1,0:T(8,128)} %disk_id.1, s32[16,16,512]{2,1,0:T(8,128)} %disk_mask.1, ...), custom_call_target="tpu_custom_call" | custom-call | tf_op jit(solution)/shard_map/faces/pallas_call | solution.py:24
  2.3 4.0 %collective-permute-start = (f32[128,128]{1,0:T(8,128)S(1)}, f32[128,128]{1,0:T(8,128)S(1)}, u32[]{:S(2)}, u32[]{:S(2)}) collective-permute-start(f32[128,128]{1,0:T(8,128)S(1)} %get-tuple-element.42), channel_id=1, source_target_pairs={{0,3},{1,2},{2,1},{3,0},{4,7},{5,6},{6,5},{7,4},{8,11},{9,10},{10,... | collective-permute-start | bytes 196616 | tf_op jit(solution)/shard_map/ppermute | solution.py:546
  6.2 0.5 %collective-permute-start.1 = (f32[128,128]{1,0:T(8,128)S(1)}, f32[128,128]{1,0:T(8,128)S(1)}, u32[]{:S(2)}, u32[]{:S(2)}) collective-permute-start(f32[128,128]{1,0:T(8,128)S(1)} %get-tuple-element.43), channel_id=1, source_target_pairs={{0,1},{1,0},{2,3},{3,2},{4,5},{5,4},{6,7},{7,6},{8,9},{9,8},{10,11... | collective-permute-start | bytes 196616 | tf_op jit(solution)/shard_map/ppermute | solution.py:546
  6.8 0.1 collective-permute-start.2
  6.9 1.6 %collective-permute-start.3 = (f32[64,128]{1,0:T(8,128)S(1)}, f32[64,128]{1,0:T(8,128)S(1)}, u32[]{:S(2)}, u32[]{:S(2)}) collective-permute-start(f32[64,128]{1,0:T(8,128)S(1)} %get-tuple-element.45), channel_id=1, source_target_pairs={{0,4},{1,5},{2,6},{3,7},{4,0},{5,1},{6,2},{7,3},{8,12},{9,13},{10,... | collective-permute-start | bytes 98312 | tf_op jit(solution)/shard_map/ppermute | solution.py:546
  8.5 0.9 %set_up.1 = (f32[16,16,512]{2,1,0:T(8,128)S(1)}, f32[16,16,512]{2,1,0:T(8,128)S(1)}, f32[16,16,512]{2,1,0:T(8,128)S(1)}, f32[16,128]{1,0:T(8,128)S(1)}, f32[16,1...) custom-call(f32[16,16,512]{2,1,0:T(8,128)S(1)} %copy-done, f32[16,16,512]{2,1,0:T(8,128)S(1)} %copy-done.1, ...), custom_call_target="tpu_custom_call" | custom-call | tf_op jit(solution)/shard_map/set_up/pallas_call | solution.py:24
  9.4 1.3 %collective-permute-done.2.chip.a_chip = f32[64,128]{1,0:T(8,128)S(1)} collective-permute-done((f32[64,128]{1,0:T(8,128)S(1)}, f32[64,128]{1,0:T(8,128)S(1)}, u32[]{:S(2)}, u32[]{:S(2)}) %collective-permute-start.2) | collective-permute-done | bytes 32800 | tf_op jit(solution)/shard_map/ppermute | solution.py:546
  10.7 0.4 %early.1 = (f32[224,128]{1,0:T(8,128)S(1)}, f32[16,128]{1,0:T(8,128)S(1)}, f32[32,512]{1,0:T(8,128)S(1)}) custom-call(f32[16,16,512]{2,1,0:T(8,128)S(1)} %get-tuple-element.56.inner, f32[16,16,512]{2,1,0:T(8,128)S(1)} %get-tuple-element.53.g.refs_1_, f32[4,16,512]{2,1,0:T(8,128)S(1)} %get-tuple-element.57.rows, f32[16,128]{1,0:T(8,128)S(1)} %get-tuple-element.55.absorb, ...), custom_call_target="tpu_custom_call" | custom-call | tf_op jit(solution)/shard_map/early/pallas_call | solution.py:24
  11.2 0.8 %restrict.1 = (f32[16,16,512]{2,1,0:T(8,128)S(1)}, f32[40,128]{1,0:T(8,128)S(1)}, f32[32,512]{1,0:T(8,128)S(1)}) custom-call(f32[16,16,512]{2,1,0:T(8,128)S(1)} %get-tuple-element.52.f.refs_0_, f32[16,16,512]{2,1,0:T(8,128)S(1)} %get-tuple-element.53.g.refs_1_, f32[16,16,512]{2,1,0:T(8,128)S(1)} %get-tuple-element.54.d, ...), custom_call_target="tpu_custom_call" | custom-call | tf_op jit(solution)/shard_map/restrict/pallas_call | solution.py:24
  12.0 0.5 %collective-permute-done.4.core.s_core = f32[224,128]{1,0:T(8,128)S(1)} collective-permute-done((f32[224,128]{1,0:T(8,128)S(1)}, f32[224,128]{1,0:T(8,128)S(1)}, u32[]{:S(2)}, u32[]{:S(2)}) %collective-permute-start.4) | collective-permute-done | bytes 114720 | tf_op jit(solution)/shard_map/ppermute | solution.py:546
  12.6 0.5 %collective-permute-start.5 = (f32[112,128]{1,0:T(8,128)S(1)}, f32[112,128]{1,0:T(8,128)S(1)}, u32[]{:S(2)}, u32[]{:S(2)}) collective-permute-start(f32[112,128]{1,0:T(8,128)S(1)} %get-tuple-element.68), channel_id=1, source_target_pairs={{0,2},{1,3},{2,0},{3,1},{4,8},{5,9},{6,10},{7,11},{8,4},{9,5},{10,... | collective-permute-start | bytes 172040 | tf_op jit(solution)/shard_map/ppermute | solution.py:546
  13.1 1.6 %collective-permute-start.7 = (f32[184,128]{1,0:T(8,128)S(1)}, f32[184,128]{1,0:T(8,128)S(1)}, u32[]{:S(2)}, u32[]{:S(2)}) collective-permute-start(f32[184,128]{1,0:T(8,128)S(1)} %get-tuple-element.71), channel_id=1, source_target_pairs={{0,1},{1,0},{2,3},{3,2},{4,5},{5,4},{6,7},{7,6},{8,9},{9,8},{10,11... | collective-permute-start | bytes 282632 | tf_op jit(solution)/shard_map/ppermute | solution.py:546
  14.6 1.5 %collective-permute-start.8 = (f32[184,128]{1,0:T(8,128)S(1)}, f32[184,128]{1,0:T(8,128)S(1)}, u32[]{:S(2)}, u32[]{:S(2)}) collective-permute-start(f32[184,128]{1,0:T(8,128)S(1)} %get-tuple-element.72), channel_id=1, source_target_pairs={{0,3},{1,2},{2,1},{3,0},{4,7},{5,6},{6,5},{7,4},{8,11},{9,10},{10,... | collective-permute-start | bytes 282632 | tf_op jit(solution)/shard_map/ppermute | solution.py:546
  16.1 0.7 %collective-permute-done.5.chip.s_chip = f32[112,128]{1,0:T(8,128)S(1)} collective-permute-done((f32[112,128]{1,0:T(8,128)S(1)}, f32[112,128]{1,0:T(8,128)S(1)}, u32[]{:S(2)}, u32[]{:S(2)}) %collective-permute-start.5) | collective-permute-done | bytes 57376 | tf_op jit(solution)/shard_map/ppermute | solution.py:546
  16.9 0.5 %collective-permute-start.6 = (f32[152,128]{1,0:T(8,128)S(1)}, f32[152,128]{1,0:T(8,128)S(1)}, u32[]{:S(2)}, u32[]{:S(2)}) collective-permute-start(f32[152,128]{1,0:T(8,128)S(1)} %get-tuple-element.70), channel_id=1, source_target_pairs={{0,2},{1,3},{2,0},{3,1},{4,8},{5,9},{6,10},{7,11},{8,4},{9,5},{10,... | collective-permute-start | bytes 233480 | tf_op jit(solution)/shard_map/ppermute | solution.py:546
  17.4 0.7 %collective-permute-done.9.core = f32[40,128]{1,0:T(8,128)S(1)} collective-permute-done((f32[40,128]{1,0:T(8,128)S(1)}, f32[40,128]{1,0:T(8,128)S(1)}, u32[]{:S(2)}, u32[]{:S(2)}) %collective-permute-start.9) | collective-permute-done | bytes 20512 | tf_op jit(solution)/shard_map/ppermute | solution.py:546
  18.1 1.0 %collective-permute-start.11 = (f32[136,128]{1,0:T(8,128)S(1)}, f32[136,128]{1,0:T(8,128)S(1)}, u32[]{:S(2)}, u32[]{:S(2)}) collective-permute-start(f32[136,128]{1,0:T(8,128)S(1)} %get-tuple-element.81.refs_12_), channel_id=1, source_target_pairs={{0,2},{1,3},{2,0},{3,1},{4,6},{5,7},{6,4},{7,5},{8,10},{9,11},{10,... | collective-permute-start | bytes 208904 | tf_op jit(solution)/shard_map/ppermute | solution.py:546
  19.1 2.0 %collective-permute-start.10 = (f32[80,128]{1,0:T(8,128)S(1)}, f32[80,128]{1,0:T(8,128)S(1)}, u32[]{:S(2)}, u32[]{:S(2)}) collective-permute-start(f32[80,128]{1,0:T(8,128)S(1)} %get-tuple-element.80), channel_id=1, source_target_pairs={{0,3},{1,2},{2,1},{3,0},{4,7},{5,6},{6,5},{7,4},{8,11},{9,10},{10,... | collective-permute-start | bytes 122888 | tf_op jit(solution)/shard_map/ppermute | solution.py:546
  21.2 0.5 %collective-permute-start.12 = (f32[80,128]{1,0:T(8,128)S(1)}, f32[80,128]{1,0:T(8,128)S(1)}, u32[]{:S(2)}, u32[]{:S(2)}) collective-permute-start(f32[80,128]{1,0:T(8,128)S(1)} %get-tuple-element.80), channel_id=1, source_target_pairs={{0,1},{1,0},{2,3},{3,2},{4,5},{5,4},{6,7},{7,6},{8,9},{9,8},{10,11... | collective-permute-start | bytes 122888 | tf_op jit(solution)/shard_map/ppermute | solution.py:546
  21.7 1.0 %collective-permute-done.6.s_more = f32[152,128]{1,0:T(8,128)S(1)} collective-permute-done((f32[152,128]{1,0:T(8,128)S(1)}, f32[152,128]{1,0:T(8,128)S(1)}, u32[]{:S(2)}, u32[]{:S(2)}) %collective-permute-start.6) | collective-permute-done | bytes 77856 | tf_op jit(solution)/shard_map/ppermute | solution.py:546
  22.7 0.5 %prepare.1 = (f32[18,16,512]{2,1,0:T(8,128)S(1)}, f32[16,512]{1,0:T(8,128)S(1)}, f32[16,512]{1,0:T(8,128)S(1)}, f32[2,16,512]{2,1,0:T(8,128)S(1)}, f32[2,16,512]{2,1,0:T(8,128)S(1)}) custom-call(f32[16,16,512]{2,1,0:T(8,128)S(1)} %get-tuple-element.52.f.refs_0_, f32[16,16,512]{2,1,0:T(8,128)S(1)} %get-tuple-element.53.g.refs_1_, ...), custom_call_target="tpu_custom_call" | custom-call | tf_op jit(solution)/shard_map/prepare/pallas_call | solution.py:24
  23.3 0.9 %collective-permute-done.10.refs_9_ = f32[80,128]{1,0:T(8,128)S(1)} collective-permute-done((f32[80,128]{1,0:T(8,128)S(1)}, f32[80,128]{1,0:T(8,128)S(1)}, u32[]{:S(2)}, u32[]{:S(2)}) %collective-permute-start.10) | collective-permute-done | bytes 40992 | tf_op jit(solution)/shard_map/ppermute | solution.py:546
  24.2 1.0 %collective-permute-done.12.refs_11_ = f32[80,128]{1,0:T(8,128)S(1)} collective-permute-done((f32[80,128]{1,0:T(8,128)S(1)}, f32[80,128]{1,0:T(8,128)S(1)}, u32[]{:S(2)}, u32[]{:S(2)}) %collective-permute-start.12) | collective-permute-done | bytes 40992 | tf_op jit(solution)/shard_map/ppermute | solution.py:546
  25.2 2.2 %finish.1 = (f32[16,16,512]{2,1,0:T(8,128)}, f32[4,16,128]{2,1,0:T(8,128)}) custom-call(f32[16,16,512]{2,1,0:T(8,128)S(1)} %get-tuple-element.52.f.refs_0_, f32[16,16,512]{2,1,0:T(8,128)S(1)} %get-tuple-element.53.g.refs_1_, f32[18,16,512]{2,1,0:T(8,128)S(1)} %get-tuple-element.73.refs_2_, f32[16,512]{1,0:T(8,128)S(1)} %get-tuple-element.74.refs_3_, ...), custom_call_target="tpu_custom_call" | custom-call | tf_op jit(solution)/shard_map/finish/pallas_call | solution.py:24
  (23 shorter events, 0.3 us)
Async XLA Ops:
  0.6 7.8 %copy-start = (f32[16,16,512]{2,1,0:T(8,128)S(1)}, f32[16,16,512]{2,1,0:T(8,128)}, u32[]{:S(2)}) copy-start(f32[16,16,512]{2,1,0:T(8,128)} %source.1) | copy-start | bytes 1572868
  0.6 7.8 %copy-start.1 = (f32[16,16,512]{2,1,0:T(8,128)S(1)}, f32[16,16,512]{2,1,0:T(8,128)}, u32[]{:S(2)}) copy-start(f32[16,16,512]{2,1,0:T(8,128)} %reaction.1) | copy-start | bytes 1572868
  0.7 7.8 %copy-start.2 = (s32[16,16,512]{2,1,0:T(8,128)S(1)}, s32[16,16,512]{2,1,0:T(8,128)}, u32[]{:S(2)}) copy-start(s32[16,16,512]{2,1,0:T(8,128)} %kind.1) | copy-start | bytes 1572868
  0.7 7.8 %copy-start.3 = (s32[16,16,512]{2,1,0:T(8,128)S(1)}, s32[16,16,512]{2,1,0:T(8,128)}, u32[]{:S(2)}) copy-start(s32[16,16,512]{2,1,0:T(8,128)} %disk_id.1) | copy-start | bytes 1572868
  0.7 7.8 %copy-start.4 = (s32[16,16,512]{2,1,0:T(8,128)S(1)}, s32[16,16,512]{2,1,0:T(8,128)}, u32[]{:S(2)}) copy-start(s32[16,16,512]{2,1,0:T(8,128)} %disk_mask.1) | copy-start | bytes 1572868
  2.3 8.4 %collective-permute-start = (f32[128,128]{1,0:T(8,128)S(1)}, f32[128,128]{1,0:T(8,128)S(1)}, u32[]{:S(2)}, u32[]{:S(2)}) collective-permute-start(f32[128,128]{1,0:T(8,128)S(1)} %get-tuple-element.42), channel_id=1, source_target_pairs={{0,3},{1,2},{2,1},{3,0},{4,7},{5,6},{6,5},{7,4},{8,11},{9,10},{10,... | collective-permute-start | bytes 196616 | tf_op jit(solution)/shard_map/ppermute | solution.py:546
  6.2 4.5 %collective-permute-start.1 = (f32[128,128]{1,0:T(8,128)S(1)}, f32[128,128]{1,0:T(8,128)S(1)}, u32[]{:S(2)}, u32[]{:S(2)}) collective-permute-start(f32[128,128]{1,0:T(8,128)S(1)} %get-tuple-element.43), channel_id=1, source_target_pairs={{0,1},{1,0},{2,3},{3,2},{4,5},{5,4},{6,7},{7,6},{8,9},{9,8},{10,11... | collective-permute-start | bytes 196616 | tf_op jit(solution)/shard_map/ppermute | solution.py:546
  6.8 1.7 %copy-start.5 = (f32[120]{0:T(128)S(1)}, f32[120]{0:T(128)}, u32[]{:S(2)}) copy-start(f32[120]{0:T(128)} %param.11) | copy-start | bytes 1444
  6.8 3.9 %collective-permute-start.2 = (f32[64,128]{1,0:T(8,128)S(1)}, f32[64,128]{1,0:T(8,128)S(1)}, u32[]{:S(2)}, u32[]{:S(2)}) collective-permute-start(f32[64,128]{1,0:T(8,128)S(1)} %get-tuple-element.44), channel_id=1, source_target_pairs={{0,2},{1,3},{2,0},{3,1},{4,8},{5,9},{6,10},{7,11},{8,4},{9,5},{10,... | collective-permute-start | bytes 98312 | tf_op jit(solution)/shard_map/ppermute | solution.py:546
  6.9 3.8 %collective-permute-start.3 = (f32[64,128]{1,0:T(8,128)S(1)}, f32[64,128]{1,0:T(8,128)S(1)}, u32[]{:S(2)}, u32[]{:S(2)}) collective-permute-start(f32[64,128]{1,0:T(8,128)S(1)} %get-tuple-element.45), channel_id=1, source_target_pairs={{0,4},{1,5},{2,6},{3,7},{4,0},{5,1},{6,2},{7,3},{8,12},{9,13},{10,... | collective-permute-start | bytes 98312 | tf_op jit(solution)/shard_map/ppermute | solution.py:546
  11.1 1.4 %collective-permute-start.4 = (f32[224,128]{1,0:T(8,128)S(1)}, f32[224,128]{1,0:T(8,128)S(1)}, u32[]{:S(2)}, u32[]{:S(2)}) collective-permute-start(f32[224,128]{1,0:T(8,128)S(1)} %get-tuple-element.64), channel_id=1, source_target_pairs={{0,4},{1,5},{2,6},{3,7},{4,0},{5,1},{6,2},{7,3},{8,12},{9,13},{10,... | collective-permute-start | bytes 344072 | tf_op jit(solution)/shard_map/ppermute | solution.py:546
  12.6 4.2 %collective-permute-start.5 = (f32[112,128]{1,0:T(8,128)S(1)}, f32[112,128]{1,0:T(8,128)S(1)}, u32[]{:S(2)}, u32[]{:S(2)}) collective-permute-start(f32[112,128]{1,0:T(8,128)S(1)} %get-tuple-element.68), channel_id=1, source_target_pairs={{0,2},{1,3},{2,0},{3,1},{4,8},{5,9},{6,10},{7,11},{8,4},{9,5},{10,... | collective-permute-start | bytes 172040 | tf_op jit(solution)/shard_map/ppermute | solution.py:546
  13.1 8.1 %collective-permute-start.7 = (f32[184,128]{1,0:T(8,128)S(1)}, f32[184,128]{1,0:T(8,128)S(1)}, u32[]{:S(2)}, u32[]{:S(2)}) collective-permute-start(f32[184,128]{1,0:T(8,128)S(1)} %get-tuple-element.71), channel_id=1, source_target_pairs={{0,1},{1,0},{2,3},{3,2},{4,5},{5,4},{6,7},{7,6},{8,9},{9,8},{10,11... | collective-permute-start | bytes 282632 | tf_op jit(solution)/shard_map/ppermute | solution.py:546
  14.6 7.1 %collective-permute-start.8 = (f32[184,128]{1,0:T(8,128)S(1)}, f32[184,128]{1,0:T(8,128)S(1)}, u32[]{:S(2)}, u32[]{:S(2)}) collective-permute-start(f32[184,128]{1,0:T(8,128)S(1)} %get-tuple-element.72), channel_id=1, source_target_pairs={{0,3},{1,2},{2,1},{3,0},{4,7},{5,6},{6,5},{7,4},{8,11},{9,10},{10,... | collective-permute-start | bytes 282632 | tf_op jit(solution)/shard_map/ppermute | solution.py:546
  16.9 1.3 %collective-permute-start.9 = (f32[40,128]{1,0:T(8,128)S(1)}, f32[40,128]{1,0:T(8,128)S(1)}, u32[]{:S(2)}, u32[]{:S(2)}) collective-permute-start(f32[40,128]{1,0:T(8,128)S(1)} %get-tuple-element.78.full), channel_id=1, source_target_pairs={{0,4},{1,5},{2,6},{3,7},{4,0},{5,1},{6,2},{7,3},{8,12},{9,13},{10,... | collective-permute-start | bytes 61448 | tf_op jit(solution)/shard_map/ppermute | solution.py:546
  16.9 5.8 %collective-permute-start.6 = (f32[152,128]{1,0:T(8,128)S(1)}, f32[152,128]{1,0:T(8,128)S(1)}, u32[]{:S(2)}, u32[]{:S(2)}) collective-permute-start(f32[152,128]{1,0:T(8,128)S(1)} %get-tuple-element.70), channel_id=1, source_target_pairs={{0,2},{1,3},{2,0},{3,1},{4,8},{5,9},{6,10},{7,11},{8,4},{9,5},{10,... | collective-permute-start | bytes 233480 | tf_op jit(solution)/shard_map/ppermute | solution.py:546
  18.1 7.0 %collective-permute-start.11 = (f32[136,128]{1,0:T(8,128)S(1)}, f32[136,128]{1,0:T(8,128)S(1)}, u32[]{:S(2)}, u32[]{:S(2)}) collective-permute-start(f32[136,128]{1,0:T(8,128)S(1)} %get-tuple-element.81.refs_12_), channel_id=1, source_target_pairs={{0,2},{1,3},{2,0},{3,1},{4,6},{5,7},{6,4},{7,5},{8,10},{9,11},{10,... | collective-permute-start | bytes 208904 | tf_op jit(solution)/shard_map/ppermute | solution.py:546
  19.1 5.1 %collective-permute-start.10 = (f32[80,128]{1,0:T(8,128)S(1)}, f32[80,128]{1,0:T(8,128)S(1)}, u32[]{:S(2)}, u32[]{:S(2)}) collective-permute-start(f32[80,128]{1,0:T(8,128)S(1)} %get-tuple-element.80), channel_id=1, source_target_pairs={{0,3},{1,2},{2,1},{3,0},{4,7},{5,6},{6,5},{7,4},{8,11},{9,10},{10,... | collective-permute-start | bytes 122888 | tf_op jit(solution)/shard_map/ppermute | solution.py:546
  21.2 4.0 %collective-permute-start.12 = (f32[80,128]{1,0:T(8,128)S(1)}, f32[80,128]{1,0:T(8,128)S(1)}, u32[]{:S(2)}, u32[]{:S(2)}) collective-permute-start(f32[80,128]{1,0:T(8,128)S(1)} %get-tuple-element.80), channel_id=1, source_target_pairs={{0,1},{1,0},{2,3},{3,2},{4,5},{5,4},{6,7},{7,6},{8,9},{9,8},{10,11... | collective-permute-start | bytes 122888 | tf_op jit(solution)/shard_map/ppermute | solution.py:546

commit v15 on v14

--- a/solution.py
+++ b/solution.py
@@ -541,6 +541,9 @@
     core_pairs, chip_pairs = pairs_core(nx, ny), pairs_chip(nx, ny)
     row_pairs = [pairs_row(nx, ny, step) for step in range(1, ny)]
     odd_pairs = pairs_odd(nx, ny)
+    inner_pairs = [
+        (a, b) if 0 < a % ny < ny - 1 else (a, ((a // ny) ^ 1) * ny + a % ny) for a, b in odd_pairs
+    ]
 
     def swap(array, pairs):
         return lax.ppermute(array, axes, pairs)
@@ -559,7 +562,7 @@
             name="faces",
         )
         a_core, a_chip = swap(core, core_pairs), swap(chip, chip_pairs)
-        a_odd, a_row = swap(odd, odd_pairs), swap(row, row_pairs[0])
+        a_odd, a_row = swap(odd, inner_pairs), swap(row, row_pairs[0])
         f, g, d, absorb, inner, rows = call(
             set_up, [field, field, field, (16, 128), field, (4, 16, 512)], *inputs, scratch=[(64, 512)], name="set_up"
         )

time: 27.5 us -> 26.9 us (0.978)
  waiting for transfers between devices: 6.13 us -> 5.56 us
    ppermute x13, waiting for transfers between devices: 6.13 us -> 5.56 us  [swap(): return lax.ppermute(array, axes, pairs)]
where the time goes in v15:
time: 26.9 us; the launch traced here: 26.7 us
  starting transfers between devices  13.9 us (52%)
  Pallas kernels  6.47 us (24%)
  waiting for transfers between devices  5.56 us (21%)
  between operations  0.77 us (3%)
    ppermute x13, starting transfers between devices, swap(): return lax.ppermute(array, axes, pairs)  13.9 us
    pallas_call x9, Pallas kernels, call(): pl.pallas_call(kernel, out_shape=[jax.ShapeDtypeStruct(s, F32) for s in o...  6.47 us
    ppermute x13, waiting for transfers between devices, swap(): return lax.ppermute(array, axes, pairs)  5.56 us
  transfers between devices with their start and end apart: 13, of which 7 were waited for; matrix products, arithmetic and copies ran while one was open for 0% of the time, Pallas kernels for 8%

profile of v15, /device:TPU:0, one launch (start us, length us, event | category | flops | bytes accessed | tf_op | source)
XLA Modules:
  0.0 26.7 jit_solution(10873868816380081343)
XLA Ops:
  0.7 1.6 %faces.1 = (f32[64,128]{1,0:T(8,128)S(1)}, f32[64,128]{1,0:T(8,128)S(1)}, f32[128,128]{1,0:T(8,128)S(1)}, f32[128,128]{1,0:T(8,128)S(1)}) custom-call(f32[16,16,512]{2,1,0:T(8,128)} %source.1, f32[16,16,512]{2,1,0:T(8,128)} %reaction.1, s32[16,16,512]{2,1,0:T(8,128)} %kind.1, s32[16,16,512]{2,1,0:T(8,128)} %disk_id.1, s32[16,16,512]{2,1,0:T(8,128)} %disk_mask.1, ...), custom_call_target="tpu_custom_call" | custom-call | tf_op jit(solution)/shard_map/faces/pallas_call | solution.py:24
  2.3 0.5 %collective-permute-start = (f32[128,128]{1,0:T(8,128)S(1)}, f32[128,128]{1,0:T(8,128)S(1)}, u32[]{:S(2)}, u32[]{:S(2)}) collective-permute-start(f32[128,128]{1,0:T(8,128)S(1)} %get-tuple-element.42), channel_id=1, source_target_pairs={{0,4},{1,2},{2,1},{3,7},{4,0},{5,6},{6,5},{7,3},{8,12},{9,10},{10,... | collective-permute-start | bytes 196616 | tf_op jit(solution)/shard_map/ppermute | solution.py:549
  2.8 4.0 %collective-permute-start.1 = (f32[128,128]{1,0:T(8,128)S(1)}, f32[128,128]{1,0:T(8,128)S(1)}, u32[]{:S(2)}, u32[]{:S(2)}) collective-permute-start(f32[128,128]{1,0:T(8,128)S(1)} %get-tuple-element.43), channel_id=1, source_target_pairs={{0,1},{1,0},{2,3},{3,2},{4,5},{5,4},{6,7},{7,6},{8,9},{9,8},{10,11... | collective-permute-start | bytes 196616 | tf_op jit(solution)/shard_map/ppermute | solution.py:549
  6.8 0.1 collective-permute-start.2
  6.9 1.6 %collective-permute-start.3 = (f32[64,128]{1,0:T(8,128)S(1)}, f32[64,128]{1,0:T(8,128)S(1)}, u32[]{:S(2)}, u32[]{:S(2)}) collective-permute-start(f32[64,128]{1,0:T(8,128)S(1)} %get-tuple-element.45), channel_id=1, source_target_pairs={{0,4},{1,5},{2,6},{3,7},{4,0},{5,1},{6,2},{7,3},{8,12},{9,13},{10,... | collective-permute-start | bytes 98312 | tf_op jit(solution)/shard_map/ppermute | solution.py:549
  8.5 0.9 %set_up.1 = (f32[16,16,512]{2,1,0:T(8,128)S(1)}, f32[16,16,512]{2,1,0:T(8,128)S(1)}, f32[16,16,512]{2,1,0:T(8,128)S(1)}, f32[16,128]{1,0:T(8,128)S(1)}, f32[16,1...) custom-call(f32[16,16,512]{2,1,0:T(8,128)S(1)} %copy-done, f32[16,16,512]{2,1,0:T(8,128)S(1)} %copy-done.1, ...), custom_call_target="tpu_custom_call" | custom-call | tf_op jit(solution)/shard_map/set_up/pallas_call | solution.py:24
  9.4 1.3 %collective-permute-done.2.chip.a_chip = f32[64,128]{1,0:T(8,128)S(1)} collective-permute-done((f32[64,128]{1,0:T(8,128)S(1)}, f32[64,128]{1,0:T(8,128)S(1)}, u32[]{:S(2)}, u32[]{:S(2)}) %collective-permute-start.2) | collective-permute-done | bytes 32800 | tf_op jit(solution)/shard_map/ppermute | solution.py:549
  10.7 0.4 %early.1 = (f32[224,128]{1,0:T(8,128)S(1)}, f32[16,128]{1,0:T(8,128)S(1)}, f32[32,512]{1,0:T(8,128)S(1)}) custom-call(f32[16,16,512]{2,1,0:T(8,128)S(1)} %get-tuple-element.56.inner, f32[16,16,512]{2,1,0:T(8,128)S(1)} %get-tuple-element.53.g.refs_1_, f32[4,16,512]{2,1,0:T(8,128)S(1)} %get-tuple-element.57.rows, f32[16,128]{1,0:T(8,128)S(1)} %get-tuple-element.55.absorb, ...), custom_call_target="tpu_custom_call" | custom-call | tf_op jit(solution)/shard_map/early/pallas_call | solution.py:24
  11.2 0.8 %restrict.1 = (f32[16,16,512]{2,1,0:T(8,128)S(1)}, f32[40,128]{1,0:T(8,128)S(1)}, f32[32,512]{1,0:T(8,128)S(1)}) custom-call(f32[16,16,512]{2,1,0:T(8,128)S(1)} %get-tuple-element.52.f.refs_0_, f32[16,16,512]{2,1,0:T(8,128)S(1)} %get-tuple-element.53.g.refs_1_, f32[16,16,512]{2,1,0:T(8,128)S(1)} %get-tuple-element.54.d, ...), custom_call_target="tpu_custom_call" | custom-call | tf_op jit(solution)/shard_map/restrict/pallas_call | solution.py:24
  12.0 0.5 %collective-permute-done.4.core.s_core = f32[224,128]{1,0:T(8,128)S(1)} collective-permute-done((f32[224,128]{1,0:T(8,128)S(1)}, f32[224,128]{1,0:T(8,128)S(1)}, u32[]{:S(2)}, u32[]{:S(2)}) %collective-permute-start.4) | collective-permute-done | bytes 114720 | tf_op jit(solution)/shard_map/ppermute | solution.py:549
  12.6 0.5 %collective-permute-start.5 = (f32[112,128]{1,0:T(8,128)S(1)}, f32[112,128]{1,0:T(8,128)S(1)}, u32[]{:S(2)}, u32[]{:S(2)}) collective-permute-start(f32[112,128]{1,0:T(8,128)S(1)} %get-tuple-element.68), channel_id=1, source_target_pairs={{0,2},{1,3},{2,0},{3,1},{4,8},{5,9},{6,10},{7,11},{8,4},{9,5},{10,... | collective-permute-start | bytes 172040 | tf_op jit(solution)/shard_map/ppermute | solution.py:549
  13.0 1.6 %collective-permute-start.7 = (f32[184,128]{1,0:T(8,128)S(1)}, f32[184,128]{1,0:T(8,128)S(1)}, u32[]{:S(2)}, u32[]{:S(2)}) collective-permute-start(f32[184,128]{1,0:T(8,128)S(1)} %get-tuple-element.71), channel_id=1, source_target_pairs={{0,1},{1,0},{2,3},{3,2},{4,5},{5,4},{6,7},{7,6},{8,9},{9,8},{10,11... | collective-permute-start | bytes 282632 | tf_op jit(solution)/shard_map/ppermute | solution.py:549
  14.6 1.5 %collective-permute-start.8 = (f32[184,128]{1,0:T(8,128)S(1)}, f32[184,128]{1,0:T(8,128)S(1)}, u32[]{:S(2)}, u32[]{:S(2)}) collective-permute-start(f32[184,128]{1,0:T(8,128)S(1)} %get-tuple-element.72), channel_id=1, source_target_pairs={{0,3},{1,2},{2,1},{3,0},{4,7},{5,6},{6,5},{7,4},{8,11},{9,10},{10,... | collective-permute-start | bytes 282632 | tf_op jit(solution)/shard_map/ppermute | solution.py:549
  16.1 0.7 %collective-permute-done.5.chip.s_chip = f32[112,128]{1,0:T(8,128)S(1)} collective-permute-done((f32[112,128]{1,0:T(8,128)S(1)}, f32[112,128]{1,0:T(8,128)S(1)}, u32[]{:S(2)}, u32[]{:S(2)}) %collective-permute-start.5) | collective-permute-done | bytes 57376 | tf_op jit(solution)/shard_map/ppermute | solution.py:549
  16.9 0.5 %collective-permute-start.6 = (f32[152,128]{1,0:T(8,128)S(1)}, f32[152,128]{1,0:T(8,128)S(1)}, u32[]{:S(2)}, u32[]{:S(2)}) collective-permute-start(f32[152,128]{1,0:T(8,128)S(1)} %get-tuple-element.70), channel_id=1, source_target_pairs={{0,2},{1,3},{2,0},{3,1},{4,8},{5,9},{6,10},{7,11},{8,4},{9,5},{10,... | collective-permute-start | bytes 233480 | tf_op jit(solution)/shard_map/ppermute | solution.py:549
  17.4 0.7 %collective-permute-done.9.core = f32[40,128]{1,0:T(8,128)S(1)} collective-permute-done((f32[40,128]{1,0:T(8,128)S(1)}, f32[40,128]{1,0:T(8,128)S(1)}, u32[]{:S(2)}, u32[]{:S(2)}) %collective-permute-start.9) | collective-permute-done | bytes 20512 | tf_op jit(solution)/shard_map/ppermute | solution.py:549
  18.1 1.0 %collective-permute-start.11 = (f32[136,128]{1,0:T(8,128)S(1)}, f32[136,128]{1,0:T(8,128)S(1)}, u32[]{:S(2)}, u32[]{:S(2)}) collective-permute-start(f32[136,128]{1,0:T(8,128)S(1)} %get-tuple-element.81.refs_12_), channel_id=1, source_target_pairs={{0,2},{1,3},{2,0},{3,1},{4,6},{5,7},{6,4},{7,5},{8,10},{9,11},{10,... | collective-permute-start | bytes 208904 | tf_op jit(solution)/shard_map/ppermute | solution.py:549
  19.1 1.4 %collective-permute-start.10 = (f32[80,128]{1,0:T(8,128)S(1)}, f32[80,128]{1,0:T(8,128)S(1)}, u32[]{:S(2)}, u32[]{:S(2)}) collective-permute-start(f32[80,128]{1,0:T(8,128)S(1)} %get-tuple-element.80), channel_id=1, source_target_pairs={{0,3},{1,2},{2,1},{3,0},{4,7},{5,6},{6,5},{7,4},{8,11},{9,10},{10,... | collective-permute-start | bytes 122888 | tf_op jit(solution)/shard_map/ppermute | solution.py:549
  20.6 1.1 %collective-permute-start.12 = (f32[80,128]{1,0:T(8,128)S(1)}, f32[80,128]{1,0:T(8,128)S(1)}, u32[]{:S(2)}, u32[]{:S(2)}) collective-permute-start(f32[80,128]{1,0:T(8,128)S(1)} %get-tuple-element.80), channel_id=1, source_target_pairs={{0,1},{1,0},{2,3},{3,2},{4,5},{5,4},{6,7},{7,6},{8,9},{9,8},{10,11... | collective-permute-start | bytes 122888 | tf_op jit(solution)/shard_map/ppermute | solution.py:549
  21.7 0.4 %collective-permute-done.6.s_more = f32[152,128]{1,0:T(8,128)S(1)} collective-permute-done((f32[152,128]{1,0:T(8,128)S(1)}, f32[152,128]{1,0:T(8,128)S(1)}, u32[]{:S(2)}, u32[]{:S(2)}) %collective-permute-start.6) | collective-permute-done | bytes 77856 | tf_op jit(solution)/shard_map/ppermute | solution.py:549
  22.1 0.5 %prepare.1 = (f32[18,16,512]{2,1,0:T(8,128)S(1)}, f32[16,512]{1,0:T(8,128)S(1)}, f32[16,512]{1,0:T(8,128)S(1)}, f32[2,16,512]{2,1,0:T(8,128)S(1)}, f32[2,16,512]{2,1,0:T(8,128)S(1)}) custom-call(f32[16,16,512]{2,1,0:T(8,128)S(1)} %get-tuple-element.52.f.refs_0_, f32[16,16,512]{2,1,0:T(8,128)S(1)} %get-tuple-element.53.g.refs_1_, ...), custom_call_target="tpu_custom_call" | custom-call | tf_op jit(solution)/shard_map/prepare/pallas_call | solution.py:24
  22.7 1.5 %collective-permute-done.10.refs_9_ = f32[80,128]{1,0:T(8,128)S(1)} collective-permute-done((f32[80,128]{1,0:T(8,128)S(1)}, f32[80,128]{1,0:T(8,128)S(1)}, u32[]{:S(2)}, u32[]{:S(2)}) %collective-permute-start.10) | collective-permute-done | bytes 40992 | tf_op jit(solution)/shard_map/ppermute | solution.py:549
  24.2 0.4 %collective-permute-done.12.refs_11_ = f32[80,128]{1,0:T(8,128)S(1)} collective-permute-done((f32[80,128]{1,0:T(8,128)S(1)}, f32[80,128]{1,0:T(8,128)S(1)}, u32[]{:S(2)}, u32[]{:S(2)}) %collective-permute-start.12) | collective-permute-done | bytes 40992 | tf_op jit(solution)/shard_map/ppermute | solution.py:549
  24.6 2.2 %finish.1 = (f32[16,16,512]{2,1,0:T(8,128)}, f32[4,16,128]{2,1,0:T(8,128)}) custom-call(f32[16,16,512]{2,1,0:T(8,128)S(1)} %get-tuple-element.52.f.refs_0_, f32[16,16,512]{2,1,0:T(8,128)S(1)} %get-tuple-element.53.g.refs_1_, f32[18,16,512]{2,1,0:T(8,128)S(1)} %get-tuple-element.73.refs_2_, f32[16,512]{1,0:T(8,128)S(1)} %get-tuple-element.74.refs_3_, ...), custom_call_target="tpu_custom_call" | custom-call | tf_op jit(solution)/shard_map/finish/pallas_call | solution.py:24
  (23 shorter events, 0.3 us)
Async XLA Ops:
  0.6 7.8 %copy-start = (f32[16,16,512]{2,1,0:T(8,128)S(1)}, f32[16,16,512]{2,1,0:T(8,128)}, u32[]{:S(2)}) copy-start(f32[16,16,512]{2,1,0:T(8,128)} %source.1) | copy-start | bytes 1572868
  0.6 7.8 %copy-start.1 = (f32[16,16,512]{2,1,0:T(8,128)S(1)}, f32[16,16,512]{2,1,0:T(8,128)}, u32[]{:S(2)}) copy-start(f32[16,16,512]{2,1,0:T(8,128)} %reaction.1) | copy-start | bytes 1572868
  0.7 7.8 %copy-start.2 = (s32[16,16,512]{2,1,0:T(8,128)S(1)}, s32[16,16,512]{2,1,0:T(8,128)}, u32[]{:S(2)}) copy-start(s32[16,16,512]{2,1,0:T(8,128)} %kind.1) | copy-start | bytes 1572868
  0.7 7.8 %copy-start.3 = (s32[16,16,512]{2,1,0:T(8,128)S(1)}, s32[16,16,512]{2,1,0:T(8,128)}, u32[]{:S(2)}) copy-start(s32[16,16,512]{2,1,0:T(8,128)} %disk_id.1) | copy-start | bytes 1572868
  0.7 7.8 %copy-start.4 = (s32[16,16,512]{2,1,0:T(8,128)S(1)}, s32[16,16,512]{2,1,0:T(8,128)}, u32[]{:S(2)}) copy-start(s32[16,16,512]{2,1,0:T(8,128)} %disk_mask.1) | copy-start | bytes 1572868
  2.3 8.4 %collective-permute-start = (f32[128,128]{1,0:T(8,128)S(1)}, f32[128,128]{1,0:T(8,128)S(1)}, u32[]{:S(2)}, u32[]{:S(2)}) collective-permute-start(f32[128,128]{1,0:T(8,128)S(1)} %get-tuple-element.42), channel_id=1, source_target_pairs={{0,4},{1,2},{2,1},{3,7},{4,0},{5,6},{6,5},{7,3},{8,12},{9,10},{10,... | collective-permute-start | bytes 196616 | tf_op jit(solution)/shard_map/ppermute | solution.py:549
  2.8 7.9 %collective-permute-start.1 = (f32[128,128]{1,0:T(8,128)S(1)}, f32[128,128]{1,0:T(8,128)S(1)}, u32[]{:S(2)}, u32[]{:S(2)}) collective-permute-start(f32[128,128]{1,0:T(8,128)S(1)} %get-tuple-element.43), channel_id=1, source_target_pairs={{0,1},{1,0},{2,3},{3,2},{4,5},{5,4},{6,7},{7,6},{8,9},{9,8},{10,11... | collective-permute-start | bytes 196616 | tf_op jit(solution)/shard_map/ppermute | solution.py:549
  6.8 1.7 %copy-start.5 = (f32[120]{0:T(128)S(1)}, f32[120]{0:T(128)}, u32[]{:S(2)}) copy-start(f32[120]{0:T(128)} %param.11) | copy-start | bytes 1444
  6.8 3.9 %collective-permute-start.2 = (f32[64,128]{1,0:T(8,128)S(1)}, f32[64,128]{1,0:T(8,128)S(1)}, u32[]{:S(2)}, u32[]{:S(2)}) collective-permute-start(f32[64,128]{1,0:T(8,128)S(1)} %get-tuple-element.44), channel_id=1, source_target_pairs={{0,2},{1,3},{2,0},{3,1},{4,8},{5,9},{6,10},{7,11},{8,4},{9,5},{10,... | collective-permute-start | bytes 98312 | tf_op jit(solution)/shard_map/ppermute | solution.py:549
  6.9 3.8 %collective-permute-start.3 = (f32[64,128]{1,0:T(8,128)S(1)}, f32[64,128]{1,0:T(8,128)S(1)}, u32[]{:S(2)}, u32[]{:S(2)}) collective-permute-start(f32[64,128]{1,0:T(8,128)S(1)} %get-tuple-element.45), channel_id=1, source_target_pairs={{0,4},{1,5},{2,6},{3,7},{4,0},{5,1},{6,2},{7,3},{8,12},{9,13},{10,... | collective-permute-start | bytes 98312 | tf_op jit(solution)/shard_map/ppermute | solution.py:549
  11.1 1.4 %collective-permute-start.4 = (f32[224,128]{1,0:T(8,128)S(1)}, f32[224,128]{1,0:T(8,128)S(1)}, u32[]{:S(2)}, u32[]{:S(2)}) collective-permute-start(f32[224,128]{1,0:T(8,128)S(1)} %get-tuple-element.64), channel_id=1, source_target_pairs={{0,4},{1,5},{2,6},{3,7},{4,0},{5,1},{6,2},{7,3},{8,12},{9,13},{10,... | collective-permute-start | bytes 344072 | tf_op jit(solution)/shard_map/ppermute | solution.py:549
  12.6 4.2 %collective-permute-start.5 = (f32[112,128]{1,0:T(8,128)S(1)}, f32[112,128]{1,0:T(8,128)S(1)}, u32[]{:S(2)}, u32[]{:S(2)}) collective-permute-start(f32[112,128]{1,0:T(8,128)S(1)} %get-tuple-element.68), channel_id=1, source_target_pairs={{0,2},{1,3},{2,0},{3,1},{4,8},{5,9},{6,10},{7,11},{8,4},{9,5},{10,... | collective-permute-start | bytes 172040 | tf_op jit(solution)/shard_map/ppermute | solution.py:549
  13.0 7.5 %collective-permute-start.7 = (f32[184,128]{1,0:T(8,128)S(1)}, f32[184,128]{1,0:T(8,128)S(1)}, u32[]{:S(2)}, u32[]{:S(2)}) collective-permute-start(f32[184,128]{1,0:T(8,128)S(1)} %get-tuple-element.71), channel_id=1, source_target_pairs={{0,1},{1,0},{2,3},{3,2},{4,5},{5,4},{6,7},{7,6},{8,9},{9,8},{10,11... | collective-permute-start | bytes 282632 | tf_op jit(solution)/shard_map/ppermute | solution.py:549
  14.6 7.1 %collective-permute-start.8 = (f32[184,128]{1,0:T(8,128)S(1)}, f32[184,128]{1,0:T(8,128)S(1)}, u32[]{:S(2)}, u32[]{:S(2)}) collective-permute-start(f32[184,128]{1,0:T(8,128)S(1)} %get-tuple-element.72), channel_id=1, source_target_pairs={{0,3},{1,2},{2,1},{3,0},{4,7},{5,6},{6,5},{7,4},{8,11},{9,10},{10,... | collective-permute-start | bytes 282632 | tf_op jit(solution)/shard_map/ppermute | solution.py:549
  16.9 1.3 %collective-permute-start.9 = (f32[40,128]{1,0:T(8,128)S(1)}, f32[40,128]{1,0:T(8,128)S(1)}, u32[]{:S(2)}, u32[]{:S(2)}) collective-permute-start(f32[40,128]{1,0:T(8,128)S(1)} %get-tuple-element.78.full), channel_id=1, source_target_pairs={{0,4},{1,5},{2,6},{3,7},{4,0},{5,1},{6,2},{7,3},{8,12},{9,13},{10,... | collective-permute-start | bytes 61448 | tf_op jit(solution)/shard_map/ppermute | solution.py:549
  16.9 5.2 %collective-permute-start.6 = (f32[152,128]{1,0:T(8,128)S(1)}, f32[152,128]{1,0:T(8,128)S(1)}, u32[]{:S(2)}, u32[]{:S(2)}) collective-permute-start(f32[152,128]{1,0:T(8,128)S(1)} %get-tuple-element.70), channel_id=1, source_target_pairs={{0,2},{1,3},{2,0},{3,1},{4,8},{5,9},{6,10},{7,11},{8,4},{9,5},{10,... | collective-permute-start | bytes 233480 | tf_op jit(solution)/shard_map/ppermute | solution.py:549
  18.1 6.4 %collective-permute-start.11 = (f32[136,128]{1,0:T(8,128)S(1)}, f32[136,128]{1,0:T(8,128)S(1)}, u32[]{:S(2)}, u32[]{:S(2)}) collective-permute-start(f32[136,128]{1,0:T(8,128)S(1)} %get-tuple-element.81.refs_12_), channel_id=1, source_target_pairs={{0,2},{1,3},{2,0},{3,1},{4,6},{5,7},{6,4},{7,5},{8,10},{9,11},{10,... | collective-permute-start | bytes 208904 | tf_op jit(solution)/shard_map/ppermute | solution.py:549
  19.1 5.1 %collective-permute-start.10 = (f32[80,128]{1,0:T(8,128)S(1)}, f32[80,128]{1,0:T(8,128)S(1)}, u32[]{:S(2)}, u32[]{:S(2)}) collective-permute-start(f32[80,128]{1,0:T(8,128)S(1)} %get-tuple-element.80), channel_id=1, source_target_pairs={{0,3},{1,2},{2,1},{3,0},{4,7},{5,6},{6,5},{7,4},{8,11},{9,10},{10,... | collective-permute-start | bytes 122888 | tf_op jit(solution)/shard_map/ppermute | solution.py:549
  20.6 4.0 %collective-permute-start.12 = (f32[80,128]{1,0:T(8,128)S(1)}, f32[80,128]{1,0:T(8,128)S(1)}, u32[]{:S(2)}, u32[]{:S(2)}) collective-permute-start(f32[80,128]{1,0:T(8,128)S(1)} %get-tuple-element.80), channel_id=1, source_target_pairs={{0,1},{1,0},{2,3},{3,2},{4,5},{5,4},{6,7},{7,6},{8,9},{9,8},{10,11... | collective-permute-start | bytes 122888 | tf_op jit(solution)/shard_map/ppermute | solution.py:549

commit v16 on v15

--- a/solution.py
+++ b/solution.py
@@ -566,8 +566,8 @@
         f, g, d, absorb, inner, rows = call(
             set_up, [field, field, field, (16, 128), field, (4, 16, 512)], *inputs, scratch=[(64, 512)], name="set_up"
         )
-        a_odd, a_row, a_chip, a_core, f, g, d, absorb, inner, rows = lax.optimization_barrier(
-            (a_odd, a_row, a_chip, a_core, f, g, d, absorb, inner, rows)
+        a_row, a_odd, a_chip, a_core, f, g, d, absorb, inner, rows = lax.optimization_barrier(
+            (a_row, a_odd, a_chip, a_core, f, g, d, absorb, inner, rows)
         )
         to_core, sums, y_faces = call(
             early,

time: 26.9 us -> 27.5 us (1.022)
  starting transfers between devices: 13.9 us -> 15.1 us
  waiting for transfers between devices: 5.56 us -> 4.98 us
    ppermute x13, starting transfers between devices: 13.9 us -> 15.1 us  [swap(): return lax.ppermute(array, axes, pairs)]
    ppermute x13, waiting for transfers between devices: 5.56 us -> 4.98 us  [swap(): return lax.ppermute(array, axes, pairs)]
  transfers between devices with their start and end apart: 13 -> 13, of which waited for: 7 -> 6; matrix products, arithmetic and copies ran while one was open for 0% -> 0% of each run, Pallas kernels for 8% -> 8%
where the time goes in v16:
time: 27.5 us; the launch traced here: 27.3 us
  starting transfers between devices  15.1 us (55%)
  Pallas kernels  6.47 us (24%)
  waiting for transfers between devices  4.98 us (18%)
  between operations  0.76 us (3%)
    ppermute x13, starting transfers between devices, swap(): return lax.ppermute(array, axes, pairs)  15.1 us
    pallas_call x9, Pallas kernels, call(): pl.pallas_call(kernel, out_shape=[jax.ShapeDtypeStruct(s, F32) for s in o...  6.47 us
    ppermute x13, waiting for transfers between devices, swap(): return lax.ppermute(array, axes, pairs)  4.98 us
  transfers between devices with their start and end apart: 13, of which 6 were waited for; matrix products, arithmetic and copies ran while one was open for 0% of the time, Pallas kernels for 8%

profile of v16, /device:TPU:0, one launch (start us, length us, event | category | flops | bytes accessed | tf_op | source)
XLA Modules:
  0.0 27.3 jit_solution(5080401724869458840)
XLA Ops:
  0.7 1.6 %faces.1 = (f32[64,128]{1,0:T(8,128)S(1)}, f32[64,128]{1,0:T(8,128)S(1)}, f32[128,128]{1,0:T(8,128)S(1)}, f32[128,128]{1,0:T(8,128)S(1)}) custom-call(f32[16,16,512]{2,1,0:T(8,128)} %source.1, f32[16,16,512]{2,1,0:T(8,128)} %reaction.1, s32[16,16,512]{2,1,0:T(8,128)} %kind.1, s32[16,16,512]{2,1,0:T(8,128)} %disk_id.1, s32[16,16,512]{2,1,0:T(8,128)} %disk_mask.1, ...), custom_call_target="tpu_custom_call" | custom-call | tf_op jit(solution)/shard_map/faces/pallas_call | solution.py:24
  2.3 3.0 %collective-permute-start = (f32[128,128]{1,0:T(8,128)S(1)}, f32[128,128]{1,0:T(8,128)S(1)}, u32[]{:S(2)}, u32[]{:S(2)}) collective-permute-start(f32[128,128]{1,0:T(8,128)S(1)} %get-tuple-element.42), channel_id=1, source_target_pairs={{0,1},{1,0},{2,3},{3,2},{4,5},{5,4},{6,7},{7,6},{8,9},{9,8},{10,11... | collective-permute-start | bytes 196616 | tf_op jit(solution)/shard_map/ppermute | solution.py:549
  5.3 1.5 %collective-permute-start.2 = (f32[64,128]{1,0:T(8,128)S(1)}, f32[64,128]{1,0:T(8,128)S(1)}, u32[]{:S(2)}, u32[]{:S(2)}) collective-permute-start(f32[64,128]{1,0:T(8,128)S(1)} %get-tuple-element.44), channel_id=1, source_target_pairs={{0,2},{1,3},{2,0},{3,1},{4,8},{5,9},{6,10},{7,11},{8,4},{9,5},{10,... | collective-permute-start | bytes 98312 | tf_op jit(solution)/shard_map/ppermute | solution.py:549
  6.8 0.2 collective-permute-start.3
  7.0 0.9 %set_up.1 = (f32[16,16,512]{2,1,0:T(8,128)S(1)}, f32[16,16,512]{2,1,0:T(8,128)S(1)}, f32[16,16,512]{2,1,0:T(8,128)S(1)}, f32[16,128]{1,0:T(8,128)S(1)}, f32[16,1...) custom-call(f32[16,16,512]{2,1,0:T(8,128)S(1)} %copy-done, f32[16,16,512]{2,1,0:T(8,128)S(1)} %copy-done.1, ...), custom_call_target="tpu_custom_call" | custom-call | tf_op jit(solution)/shard_map/set_up/pallas_call | solution.py:24
  7.9 1.3 %collective-permute-done.2.chip.a_chip = f32[64,128]{1,0:T(8,128)S(1)} collective-permute-done((f32[64,128]{1,0:T(8,128)S(1)}, f32[64,128]{1,0:T(8,128)S(1)}, u32[]{:S(2)}, u32[]{:S(2)}) %collective-permute-start.2) | collective-permute-done | bytes 32800 | tf_op jit(solution)/shard_map/ppermute | solution.py:549
  9.2 0.4 %early.1 = (f32[224,128]{1,0:T(8,128)S(1)}, f32[16,128]{1,0:T(8,128)S(1)}, f32[32,512]{1,0:T(8,128)S(1)}) custom-call(f32[16,16,512]{2,1,0:T(8,128)S(1)} %get-tuple-element.56.inner, f32[16,16,512]{2,1,0:T(8,128)S(1)} %get-tuple-element.53.g.refs_1_, f32[4,16,512]{2,1,0:T(8,128)S(1)} %get-tuple-element.57.rows, f32[16,128]{1,0:T(8,128)S(1)} %get-tuple-element.55.absorb, ...), custom_call_target="tpu_custom_call" | custom-call | tf_op jit(solution)/shard_map/early/pallas_call | solution.py:24
  9.7 0.2 collective-permute-start.4
  9.8 0.8 %restrict.1 = (f32[16,16,512]{2,1,0:T(8,128)S(1)}, f32[40,128]{1,0:T(8,128)S(1)}, f32[32,512]{1,0:T(8,128)S(1)}) custom-call(f32[16,16,512]{2,1,0:T(8,128)S(1)} %get-tuple-element.52.f.refs_0_, f32[16,16,512]{2,1,0:T(8,128)S(1)} %get-tuple-element.53.g.refs_1_, f32[16,16,512]{2,1,0:T(8,128)S(1)} %get-tuple-element.54.d, ...), custom_call_target="tpu_custom_call" | custom-call | tf_op jit(solution)/shard_map/restrict/pallas_call | solution.py:24
  10.6 0.4 %collective-permute-done.4.core.s_core = f32[224,128]{1,0:T(8,128)S(1)} collective-permute-done((f32[224,128]{1,0:T(8,128)S(1)}, f32[224,128]{1,0:T(8,128)S(1)}, u32[]{:S(2)}, u32[]{:S(2)}) %collective-permute-start.4) | collective-permute-done | bytes 114720 | tf_op jit(solution)/shard_map/ppermute | solution.py:549
  11.1 2.8 %collective-permute-start.5 = (f32[112,128]{1,0:T(8,128)S(1)}, f32[112,128]{1,0:T(8,128)S(1)}, u32[]{:S(2)}, u32[]{:S(2)}) collective-permute-start(f32[112,128]{1,0:T(8,128)S(1)} %get-tuple-element.68), channel_id=1, source_target_pairs={{0,2},{1,3},{2,0},{3,1},{4,8},{5,9},{6,10},{7,11},{8,4},{9,5},{10,... | collective-permute-start | bytes 172040 | tf_op jit(solution)/shard_map/ppermute | solution.py:549
  13.9 0.3 %collective-permute-start.7 = (f32[184,128]{1,0:T(8,128)S(1)}, f32[184,128]{1,0:T(8,128)S(1)}, u32[]{:S(2)}, u32[]{:S(2)}) collective-permute-start(f32[184,128]{1,0:T(8,128)S(1)} %get-tuple-element.71), channel_id=1, source_target_pairs={{0,1},{1,0},{2,3},{3,2},{4,5},{5,4},{6,7},{7,6},{8,9},{9,8},{10,11... | collective-permute-start | bytes 282632 | tf_op jit(solution)/shard_map/ppermute | solution.py:549
  14.2 1.4 %collective-permute-start.8 = (f32[184,128]{1,0:T(8,128)S(1)}, f32[184,128]{1,0:T(8,128)S(1)}, u32[]{:S(2)}, u32[]{:S(2)}) collective-permute-start(f32[184,128]{1,0:T(8,128)S(1)} %get-tuple-element.72), channel_id=1, source_target_pairs={{0,3},{1,2},{2,1},{3,0},{4,7},{5,6},{6,5},{7,4},{8,11},{9,10},{10,... | collective-permute-start | bytes 282632 | tf_op jit(solution)/shard_map/ppermute | solution.py:549
  15.6 0.5 %collective-permute-done.5.chip.s_chip = f32[112,128]{1,0:T(8,128)S(1)} collective-permute-done((f32[112,128]{1,0:T(8,128)S(1)}, f32[112,128]{1,0:T(8,128)S(1)}, u32[]{:S(2)}, u32[]{:S(2)}) %collective-permute-start.5) | collective-permute-done | bytes 57376 | tf_op jit(solution)/shard_map/ppermute | solution.py:549
  16.1 0.5 %collective-permute-start.9 = (f32[40,128]{1,0:T(8,128)S(1)}, f32[40,128]{1,0:T(8,128)S(1)}, u32[]{:S(2)}, u32[]{:S(2)}) collective-permute-start(f32[40,128]{1,0:T(8,128)S(1)} %get-tuple-element.78.full), channel_id=1, source_target_pairs={{0,4},{1,5},{2,6},{3,7},{4,0},{5,1},{6,2},{7,3},{8,12},{9,13},{10,... | collective-permute-start | bytes 61448 | tf_op jit(solution)/shard_map/ppermute | solution.py:549
  16.6 1.7 %collective-permute-start.6 = (f32[152,128]{1,0:T(8,128)S(1)}, f32[152,128]{1,0:T(8,128)S(1)}, u32[]{:S(2)}, u32[]{:S(2)}) collective-permute-start(f32[152,128]{1,0:T(8,128)S(1)} %get-tuple-element.70), channel_id=1, source_target_pairs={{0,2},{1,3},{2,0},{3,1},{4,8},{5,9},{6,10},{7,11},{8,4},{9,5},{10,... | collective-permute-start | bytes 233480 | tf_op jit(solution)/shard_map/ppermute | solution.py:549
  18.3 1.2 %collective-permute-start.11 = (f32[136,128]{1,0:T(8,128)S(1)}, f32[136,128]{1,0:T(8,128)S(1)}, u32[]{:S(2)}, u32[]{:S(2)}) collective-permute-start(f32[136,128]{1,0:T(8,128)S(1)} %get-tuple-element.81.refs_12_), channel_id=1, source_target_pairs={{0,2},{1,3},{2,0},{3,1},{4,6},{5,7},{6,4},{7,5},{8,10},{9,11},{10,... | collective-permute-start | bytes 208904 | tf_op jit(solution)/shard_map/ppermute | solution.py:549
  19.5 1.7 %collective-permute-start.10 = (f32[80,128]{1,0:T(8,128)S(1)}, f32[80,128]{1,0:T(8,128)S(1)}, u32[]{:S(2)}, u32[]{:S(2)}) collective-permute-start(f32[80,128]{1,0:T(8,128)S(1)} %get-tuple-element.80), channel_id=1, source_target_pairs={{0,3},{1,2},{2,1},{3,0},{4,7},{5,6},{6,5},{7,4},{8,11},{9,10},{10,... | collective-permute-start | bytes 122888 | tf_op jit(solution)/shard_map/ppermute | solution.py:549
  21.2 0.7 %collective-permute-start.12 = (f32[80,128]{1,0:T(8,128)S(1)}, f32[80,128]{1,0:T(8,128)S(1)}, u32[]{:S(2)}, u32[]{:S(2)}) collective-permute-start(f32[80,128]{1,0:T(8,128)S(1)} %get-tuple-element.80), channel_id=1, source_target_pairs={{0,1},{1,0},{2,3},{3,2},{4,5},{5,4},{6,7},{7,6},{8,9},{9,8},{10,11... | collective-permute-start | bytes 122888 | tf_op jit(solution)/shard_map/ppermute | solution.py:549
  21.8 0.9 %collective-permute-done.6.s_more = f32[152,128]{1,0:T(8,128)S(1)} collective-permute-done((f32[152,128]{1,0:T(8,128)S(1)}, f32[152,128]{1,0:T(8,128)S(1)}, u32[]{:S(2)}, u32[]{:S(2)}) %collective-permute-start.6) | collective-permute-done | bytes 77856 | tf_op jit(solution)/shard_map/ppermute | solution.py:549
  22.8 0.5 %prepare.1 = (f32[18,16,512]{2,1,0:T(8,128)S(1)}, f32[16,512]{1,0:T(8,128)S(1)}, f32[16,512]{1,0:T(8,128)S(1)}, f32[2,16,512]{2,1,0:T(8,128)S(1)}, f32[2,16,512]{2,1,0:T(8,128)S(1)}) custom-call(f32[16,16,512]{2,1,0:T(8,128)S(1)} %get-tuple-element.52.f.refs_0_, f32[16,16,512]{2,1,0:T(8,128)S(1)} %get-tuple-element.53.g.refs_1_, ...), custom_call_target="tpu_custom_call" | custom-call | tf_op jit(solution)/shard_map/prepare/pallas_call | solution.py:24
  23.3 1.1 %collective-permute-done.10.refs_9_ = f32[80,128]{1,0:T(8,128)S(1)} collective-permute-done((f32[80,128]{1,0:T(8,128)S(1)}, f32[80,128]{1,0:T(8,128)S(1)}, u32[]{:S(2)}, u32[]{:S(2)}) %collective-permute-start.10) | collective-permute-done | bytes 40992 | tf_op jit(solution)/shard_map/ppermute | solution.py:549
  24.4 0.8 %collective-permute-done.12.refs_11_ = f32[80,128]{1,0:T(8,128)S(1)} collective-permute-done((f32[80,128]{1,0:T(8,128)S(1)}, f32[80,128]{1,0:T(8,128)S(1)}, u32[]{:S(2)}, u32[]{:S(2)}) %collective-permute-start.12) | collective-permute-done | bytes 40992 | tf_op jit(solution)/shard_map/ppermute | solution.py:549
  25.2 2.2 %finish.1 = (f32[16,16,512]{2,1,0:T(8,128)}, f32[4,16,128]{2,1,0:T(8,128)}) custom-call(f32[16,16,512]{2,1,0:T(8,128)S(1)} %get-tuple-element.52.f.refs_0_, f32[16,16,512]{2,1,0:T(8,128)S(1)} %get-tuple-element.53.g.refs_1_, f32[18,16,512]{2,1,0:T(8,128)S(1)} %get-tuple-element.73.refs_2_, f32[16,512]{1,0:T(8,128)S(1)} %get-tuple-element.74.refs_3_, ...), custom_call_target="tpu_custom_call" | custom-call | tf_op jit(solution)/shard_map/finish/pallas_call | solution.py:24
  (23 shorter events, 0.1 us)
Async XLA Ops:
  0.6 6.4 %copy-start = (f32[16,16,512]{2,1,0:T(8,128)S(1)}, f32[16,16,512]{2,1,0:T(8,128)}, u32[]{:S(2)}) copy-start(f32[16,16,512]{2,1,0:T(8,128)} %source.1) | copy-start | bytes 1572868
  0.6 6.3 %copy-start.1 = (f32[16,16,512]{2,1,0:T(8,128)S(1)}, f32[16,16,512]{2,1,0:T(8,128)}, u32[]{:S(2)}) copy-start(f32[16,16,512]{2,1,0:T(8,128)} %reaction.1) | copy-start | bytes 1572868
  0.7 6.3 %copy-start.2 = (s32[16,16,512]{2,1,0:T(8,128)S(1)}, s32[16,16,512]{2,1,0:T(8,128)}, u32[]{:S(2)}) copy-start(s32[16,16,512]{2,1,0:T(8,128)} %kind.1) | copy-start | bytes 1572868
  0.7 6.3 %copy-start.3 = (s32[16,16,512]{2,1,0:T(8,128)S(1)}, s32[16,16,512]{2,1,0:T(8,128)}, u32[]{:S(2)}) copy-start(s32[16,16,512]{2,1,0:T(8,128)} %disk_id.1) | copy-start | bytes 1572868
  0.7 6.3 %copy-start.4 = (s32[16,16,512]{2,1,0:T(8,128)S(1)}, s32[16,16,512]{2,1,0:T(8,128)}, u32[]{:S(2)}) copy-start(s32[16,16,512]{2,1,0:T(8,128)} %disk_mask.1) | copy-start | bytes 1572868
  2.3 6.9 %collective-permute-start = (f32[128,128]{1,0:T(8,128)S(1)}, f32[128,128]{1,0:T(8,128)S(1)}, u32[]{:S(2)}, u32[]{:S(2)}) collective-permute-start(f32[128,128]{1,0:T(8,128)S(1)} %get-tuple-element.42), channel_id=1, source_target_pairs={{0,1},{1,0},{2,3},{3,2},{4,5},{5,4},{6,7},{7,6},{8,9},{9,8},{10,11... | collective-permute-start | bytes 196616 | tf_op jit(solution)/shard_map/ppermute | solution.py:549
  5.3 3.9 %collective-permute-start.1 = (f32[128,128]{1,0:T(8,128)S(1)}, f32[128,128]{1,0:T(8,128)S(1)}, u32[]{:S(2)}, u32[]{:S(2)}) collective-permute-start(f32[128,128]{1,0:T(8,128)S(1)} %get-tuple-element.43), channel_id=1, source_target_pairs={{0,4},{1,2},{2,1},{3,7},{4,0},{5,6},{6,5},{7,3},{8,12},{9,10},{10,... | collective-permute-start | bytes 196616 | tf_op jit(solution)/shard_map/ppermute | solution.py:549
  5.3 1.7 %copy-start.5 = (f32[120]{0:T(128)S(1)}, f32[120]{0:T(128)}, u32[]{:S(2)}) copy-start(f32[120]{0:T(128)} %param.11) | copy-start | bytes 1444
  5.3 3.9 %collective-permute-start.2 = (f32[64,128]{1,0:T(8,128)S(1)}, f32[64,128]{1,0:T(8,128)S(1)}, u32[]{:S(2)}, u32[]{:S(2)}) collective-permute-start(f32[64,128]{1,0:T(8,128)S(1)} %get-tuple-element.44), channel_id=1, source_target_pairs={{0,2},{1,3},{2,0},{3,1},{4,8},{5,9},{6,10},{7,11},{8,4},{9,5},{10,... | collective-permute-start | bytes 98312 | tf_op jit(solution)/shard_map/ppermute | solution.py:549
  6.8 2.4 %collective-permute-start.3 = (f32[64,128]{1,0:T(8,128)S(1)}, f32[64,128]{1,0:T(8,128)S(1)}, u32[]{:S(2)}, u32[]{:S(2)}) collective-permute-start(f32[64,128]{1,0:T(8,128)S(1)} %get-tuple-element.45), channel_id=1, source_target_pairs={{0,4},{1,5},{2,6},{3,7},{4,0},{5,1},{6,2},{7,3},{8,12},{9,13},{10,... | collective-permute-start | bytes 98312 | tf_op jit(solution)/shard_map/ppermute | solution.py:549
  9.7 1.4 %collective-permute-start.4 = (f32[224,128]{1,0:T(8,128)S(1)}, f32[224,128]{1,0:T(8,128)S(1)}, u32[]{:S(2)}, u32[]{:S(2)}) collective-permute-start(f32[224,128]{1,0:T(8,128)S(1)} %get-tuple-element.64), channel_id=1, source_target_pairs={{0,4},{1,5},{2,6},{3,7},{4,0},{5,1},{6,2},{7,3},{8,12},{9,13},{10,... | collective-permute-start | bytes 344072 | tf_op jit(solution)/shard_map/ppermute | solution.py:549
  11.1 5.0 %collective-permute-start.5 = (f32[112,128]{1,0:T(8,128)S(1)}, f32[112,128]{1,0:T(8,128)S(1)}, u32[]{:S(2)}, u32[]{:S(2)}) collective-permute-start(f32[112,128]{1,0:T(8,128)S(1)} %get-tuple-element.68), channel_id=1, source_target_pairs={{0,2},{1,3},{2,0},{3,1},{4,8},{5,9},{6,10},{7,11},{8,4},{9,5},{10,... | collective-permute-start | bytes 172040 | tf_op jit(solution)/shard_map/ppermute | solution.py:549
  13.9 7.3 %collective-permute-start.7 = (f32[184,128]{1,0:T(8,128)S(1)}, f32[184,128]{1,0:T(8,128)S(1)}, u32[]{:S(2)}, u32[]{:S(2)}) collective-permute-start(f32[184,128]{1,0:T(8,128)S(1)} %get-tuple-element.71), channel_id=1, source_target_pairs={{0,1},{1,0},{2,3},{3,2},{4,5},{5,4},{6,7},{7,6},{8,9},{9,8},{10,11... | collective-permute-start | bytes 282632 | tf_op jit(solution)/shard_map/ppermute | solution.py:549
  14.2 7.6 %collective-permute-start.8 = (f32[184,128]{1,0:T(8,128)S(1)}, f32[184,128]{1,0:T(8,128)S(1)}, u32[]{:S(2)}, u32[]{:S(2)}) collective-permute-start(f32[184,128]{1,0:T(8,128)S(1)} %get-tuple-element.72), channel_id=1, source_target_pairs={{0,3},{1,2},{2,1},{3,0},{4,7},{5,6},{6,5},{7,4},{8,11},{9,10},{10,... | collective-permute-start | bytes 282632 | tf_op jit(solution)/shard_map/ppermute | solution.py:549
  16.1 2.2 %collective-permute-start.9 = (f32[40,128]{1,0:T(8,128)S(1)}, f32[40,128]{1,0:T(8,128)S(1)}, u32[]{:S(2)}, u32[]{:S(2)}) collective-permute-start(f32[40,128]{1,0:T(8,128)S(1)} %get-tuple-element.78.full), channel_id=1, source_target_pairs={{0,4},{1,5},{2,6},{3,7},{4,0},{5,1},{6,2},{7,3},{8,12},{9,13},{10,... | collective-permute-start | bytes 61448 | tf_op jit(solution)/shard_map/ppermute | solution.py:549
  16.6 6.2 %collective-permute-start.6 = (f32[152,128]{1,0:T(8,128)S(1)}, f32[152,128]{1,0:T(8,128)S(1)}, u32[]{:S(2)}, u32[]{:S(2)}) collective-permute-start(f32[152,128]{1,0:T(8,128)S(1)} %get-tuple-element.70), channel_id=1, source_target_pairs={{0,2},{1,3},{2,0},{3,1},{4,8},{5,9},{6,10},{7,11},{8,4},{9,5},{10,... | collective-permute-start | bytes 233480 | tf_op jit(solution)/shard_map/ppermute | solution.py:549
  18.3 6.9 %collective-permute-start.11 = (f32[136,128]{1,0:T(8,128)S(1)}, f32[136,128]{1,0:T(8,128)S(1)}, u32[]{:S(2)}, u32[]{:S(2)}) collective-permute-start(f32[136,128]{1,0:T(8,128)S(1)} %get-tuple-element.81.refs_12_), channel_id=1, source_target_pairs={{0,2},{1,3},{2,0},{3,1},{4,6},{5,7},{6,4},{7,5},{8,10},{9,11},{10,... | collective-permute-start | bytes 208904 | tf_op jit(solution)/shard_map/ppermute | solution.py:549
  19.5 4.9 %collective-permute-start.10 = (f32[80,128]{1,0:T(8,128)S(1)}, f32[80,128]{1,0:T(8,128)S(1)}, u32[]{:S(2)}, u32[]{:S(2)}) collective-permute-start(f32[80,128]{1,0:T(8,128)S(1)} %get-tuple-element.80), channel_id=1, source_target_pairs={{0,3},{1,2},{2,1},{3,0},{4,7},{5,6},{6,5},{7,4},{8,11},{9,10},{10,... | collective-permute-start | bytes 122888 | tf_op jit(solution)/shard_map/ppermute | solution.py:549
  21.2 4.0 %collective-permute-start.12 = (f32[80,128]{1,0:T(8,128)S(1)}, f32[80,128]{1,0:T(8,128)S(1)}, u32[]{:S(2)}, u32[]{:S(2)}) collective-permute-start(f32[80,128]{1,0:T(8,128)S(1)} %get-tuple-element.80), channel_id=1, source_target_pairs={{0,1},{1,0},{2,3},{3,2},{4,5},{5,4},{6,7},{7,6},{8,9},{9,8},{10,11... | collective-permute-start | bytes 122888 | tf_op jit(solution)/shard_map/ppermute | solution.py:549
